TPU v7x, 256 devices: a whole 4x4x8 slice. The times are simulated.
256 devices in a mesh: row: 32 (over y, x, core), col: 8 (over z).
Axes of the slice: x: 4, y: 4, z: 8, core: 2. Of those that a mesh axis runs over, the one named last changes fastest.
Arguments:
- queries: bfloat16 [4096, 32, 128], P('row', 'col'), may hold values from -96 to 96
- keys: bfloat16 [4096, 32, 128], P('row', 'col'), may hold values from -6 to 6
- values: bfloat16 [4096, 32, 128], P('row', 'col'), may hold values from -6 to 6
- out_grad: bfloat16 [4096, 32, 128], P('row', 'col'), may hold values from -24 to 24
- row_keep: int32 [4096], P('row'), may hold values 0 or 1
- row_lengths: int32 [4096], P('row'), may hold values from 8 to 32, as said below
Outputs:
- dq: bfloat16 [4096, 32, 128], P('row', 'col')
- dk: bfloat16 [4096, 32, 128], P('row', 'col')
- dv: bfloat16 [4096, 32, 128], P('row', 'col')
Inputs may be any that keep to these rules, and one draw needn't show every extreme that they name: Row r's cells in columns below row_lengths[r] are valid.
All inputs are finite; a program needn't handle non-finite values. No bound on the sum of `row_keep` on one device may be relied on, other than what follows from the above.
Results may differ from a plain program's by a relative error of at most 0.035.
Values may be sent and summed in bfloat16 or wider, within the bound.
No kernel may reach another device: no remote copies, remote signals or barrier semaphores. Data moves between devices by JAX's collectives and lax.ppermute only.
A program may use at most 64 MiB of HBM per device.

v0:
```python
import math

import jax
import jax.numpy as jnp
from jax import lax
from jax.sharding import PartitionSpec as P

SUMMARIES = 256


ROW_PAIR = (((1,), (1,)), ((), ()))
LEAD_PAIR = (((0,), (0,)), ((), ()))


def blank_cells(table, cell_keep):
    return jnp.where(cell_keep, table, jnp.zeros((), table.dtype))


def softmax_rows(logits):
    row_peak = jnp.max(logits, axis=-1, keepdims=True)
    lifted = jnp.exp(logits - row_peak)
    return lifted / jnp.sum(lifted, axis=-1, keepdims=True)


def group_means(flat_table, groups_dev, group_rows, flat_width):
    summed = jnp.sum(
        flat_table.reshape(groups_dev, group_rows, flat_width), axis=1, dtype=jnp.float32
    )
    return (summed / group_rows).astype(jnp.bfloat16)


def logit_grads(logit_sum, dprob_sum, key_flags, logit_scale):
    logits = jnp.where(key_flags[None, :] > 0, logit_sum * logit_scale, -1e30)
    probs = softmax_rows(logits)
    prob_bf = probs.astype(jnp.bfloat16)
    row_delta = jnp.sum(prob_bf.astype(jnp.float32) * dprob_sum, axis=1, keepdims=True)
    dlogit_bf = (logit_scale * probs * (dprob_sum - row_delta)).astype(jnp.bfloat16)
    return (dlogit_bf, prob_bf)


def shards(queries, keys, values, out_grad, row_keep, row_lengths):
    rows_dev, cols_dev, feature = queries.shape
    total_rows = rows_dev * lax.axis_size("row")
    total_cols = cols_dev * lax.axis_size("col")
    group_rows = total_rows // SUMMARIES
    groups_dev = rows_dev // group_rows
    flat_width = cols_dev * feature
    column_ids = lax.axis_index("col") * cols_dev + jnp.arange(cols_dev, dtype=jnp.int32)
    cell_keep = ((row_keep[:, None] == 1) & (column_ids[None, :] < row_lengths[:, None]))[
        :, :, None
    ]
    q_masked = blank_cells(queries, cell_keep)
    k_masked = blank_cells(keys, cell_keep)
    v_masked = blank_cells(values, cell_keep)
    g_masked = blank_cells(out_grad, cell_keep)
    q_flat = q_masked.reshape(rows_dev, flat_width)
    k_flat = k_masked.reshape(rows_dev, flat_width)
    v_flat = v_masked.reshape(rows_dev, flat_width)
    g_flat = g_masked.reshape(rows_dev, flat_width)
    logit_scale = 1.0 / math.sqrt(total_cols * feature)
    own_keys = group_means(k_flat, groups_dev, group_rows, flat_width)
    own_values = group_means(v_flat, groups_dev, group_rows, flat_width)
    own_flags = row_keep.astype(jnp.bfloat16)
    summary_keys, summary_values, key_flags = (
        lax.all_gather(own_keys, "row", axis=0, tiled=True),
        lax.all_gather(own_values, "row", axis=0, tiled=True),
        lax.all_gather(own_flags, "row", axis=0, tiled=True),
    )
    key_piece = lax.all_gather(k_flat, "row", axis=0, tiled=True)
    value_piece = lax.all_gather(v_flat, "row", axis=0, tiled=True)
    logit_piece = lax.dot_general(q_flat, key_piece, ROW_PAIR, preferred_element_type=jnp.float32)
    dprob_piece = lax.dot_general(g_flat, value_piece, ROW_PAIR, preferred_element_type=jnp.float32)
    logit_sum, dprob_sum = lax.psum((logit_piece, dprob_piece), "col")
    dlogit_bf, prob_bf = logit_grads(logit_sum, dprob_sum, key_flags, logit_scale)
    dq_rows = jnp.dot(
        dlogit_bf,
        lax.all_gather(k_flat, "row", axis=0, tiled=True),
        preferred_element_type=jnp.float32,
    )
    dlogit_cols, prob_cols = (
        lax.all_to_all(dlogit_bf, "row", split_axis=1, concat_axis=0, tiled=True),
        lax.all_to_all(prob_bf, "row", split_axis=1, concat_axis=0, tiled=True),
    )
    q_piece = lax.all_gather(q_flat, "row", axis=0, tiled=True)
    g_piece = lax.all_gather(g_flat, "row", axis=0, tiled=True)
    dk_rows = lax.dot_general(dlogit_cols, q_piece, LEAD_PAIR, preferred_element_type=jnp.float32)
    dv_rows = lax.dot_general(prob_cols, g_piece, LEAD_PAIR, preferred_element_type=jnp.float32)
    inv_root = 1.0 / math.sqrt(feature)
    sk_cells = summary_keys.reshape(SUMMARIES, cols_dev, feature)
    sv_cells = summary_values.reshape(SUMMARIES, cols_dev, feature)
    cross_logits = (
        jnp.einsum("rcd,scd->crs", q_masked, sk_cells, preferred_element_type=jnp.float32)
        * inv_root
    )
    cross_probs = softmax_rows(cross_logits)
    cross_bf = cross_probs.astype(jnp.bfloat16)
    cross_dprobs = jnp.einsum(
        "rcd,scd->crs", g_masked, sv_cells, preferred_element_type=jnp.float32
    )
    cross_delta = jnp.sum(cross_bf.astype(jnp.float32) * cross_dprobs, axis=-1, keepdims=True)
    cross_dlogit = (inv_root * cross_probs * (cross_dprobs - cross_delta)).astype(jnp.bfloat16)
    dq_cross = jnp.einsum(
        "crs,scd->rcd", cross_dlogit, sk_cells, preferred_element_type=jnp.float32
    )
    dsum_keys = jnp.einsum(
        "crs,rcd->scd", cross_dlogit, q_masked, preferred_element_type=jnp.float32
    ).reshape(SUMMARIES, flat_width)
    dsum_values = jnp.einsum(
        "crs,rcd->scd", cross_bf, g_masked, preferred_element_type=jnp.float32
    ).reshape(SUMMARIES, flat_width)
    own_dkeys, own_dvalues = (
        lax.psum_scatter(dsum_keys, "row", scatter_dimension=0, tiled=True),
        lax.psum_scatter(dsum_values, "row", scatter_dimension=0, tiled=True),
    )

    def spread_groups(own_grads):
        widened = jnp.broadcast_to(own_grads[:, None, :], (groups_dev, group_rows, flat_width))
        return widened.reshape(rows_dev, cols_dev, feature) / group_rows

    grad_q = jnp.where(
        cell_keep, dq_rows.reshape(rows_dev, cols_dev, feature) + dq_cross, 0.0
    ).astype(jnp.bfloat16)
    grad_k = jnp.where(
        cell_keep, dk_rows.reshape(rows_dev, cols_dev, feature) + spread_groups(own_dkeys), 0.0
    ).astype(jnp.bfloat16)
    grad_v = jnp.where(
        cell_keep, dv_rows.reshape(rows_dev, cols_dev, feature) + spread_groups(own_dvalues), 0.0
    ).astype(jnp.bfloat16)
    return (grad_q, grad_k, grad_v)


def solution(mesh):
    return jax.shard_map(
        shards,
        mesh=mesh,
        in_specs=(
            P("row", "col", None),
            P("row", "col", None),
            P("row", "col", None),
            P("row", "col", None),
            P("row"),
            P("row"),
        ),
        out_specs=(P("row", "col", None), P("row", "col", None), P("row", "col", None)),
        check_vma=False,
    )
```

profile of v0, /device:TPU:1, one launch (start us, length us, event | category | flops | bytes accessed | tf_op | source)
XLA Modules:
  0.0 540.5 jit_solution(7852064781852054533)
XLA Ops:
  7.2 1.0 copy.48
  8.3 0.7 broadcast_compare_fusion
  8.9 1.0 copy.49
  10.0 1.0 copy.50
  11.0 1.0 copy.47
  12.0 0.7 compare_and_fusion
  12.8 0.7 broadcast_select_fusion.2
  13.5 0.0 all-gather.6.cloned.1.call-start
  13.6 0.7 all-gather.6.cloned.1.call-update
  14.3 57.8 %all-gather.8.cloned.1.call-done = bf16[4096,512]{0,1:T(8,128)(2,1)} async-done(((bf16[128,512]{0,1:T(8,128)(2,1)}), bf16[4096,512]{0,1:T(8,128)(2,1)}) %all-gather.8.cloned.1.call-update) | async-done | bytes 4194320 | tf_op jit(solution)/shard_map/all_gather | solution.py:70
  72.2 4.3 fusion.20
  76.5 52.6 %all-gather.6.cloned.1.call-done = bf16[4096,512]{0,1:T(8,128)(2,1)} async-done(((bf16[128,512]{0,1:T(8,128)(2,1)}), bf16[4096,512]{0,1:T(8,128)(2,1)}) %all-gather.6.cloned.1.call-update) | async-done | bytes 4194320 | tf_op jit(solution)/shard_map/all_gather | solution.py:69
  129.1 4.2 fusion.19
  133.4 0.0 reduce-scatter.7.cloned.1.call-start
  133.4 0.8 copy-done.7
  134.2 0.1 copy.51
  134.4 0.1 copy.55
  134.5 0.1 reshape.121
  134.7 24.2 %all_gather.25 = bf16[256,512]{1,0:T(8,128)(2,1)S(1)} all-gather(bf16[8,512]{1,0:T(8,128)(2,1)S(1)} %multiply_convert_fusion.3), channel_id=1, replica_groups=mesh['row'=32,'col'=8] {'row'}, dimensions={0}, use_global_device_ids=true | all-gather | bytes 270336 | tf_op jit(solution)/shard_map/all_gather | solution.py:65
  158.9 0.1 copy.52
  159.0 0.1 reshape.122
  159.2 22.7 %all_gather.26 = bf16[256,512]{1,0:T(8,128)(2,1)S(1)} all-gather(bf16[8,512]{1,0:T(8,128)(2,1)S(1)} %multiply_convert_fusion.2), channel_id=1, replica_groups=mesh['row'=32,'col'=8] {'row'}, dimensions={0}, use_global_device_ids=true | all-gather | bytes 270336 | tf_op jit(solution)/shard_map/all_gather | solution.py:66
  181.9 0.1 copy.56
  182.1 0.5 fusion.18
  182.5 0.4 multiply_reduce_fusion.1
  182.9 0.2 multiply_convert_fusion.1
  183.1 0.2 fusion.22
  183.3 1.0 copy.82
  184.4 0.0 reduce-scatter.9.cloned.1.call-start
  184.4 0.6 fusion.16
  185.1 1.0 copy.84
  186.1 0.5 all-gather.10.cloned.1.call-update
  186.7 0.7 all-gather.12.cloned.1.call-update
  187.4 20.4 %all-gather = bf16[32,1,128]{2,1,0:T(2,128)(2,1)S(1)} all-gather(bf16[1,1,128]{2,1,0:T(2,128)(2,1)S(1)} %convert_bitcast_fusion.1), channel_id=1, replica_groups=mesh['row'=32,'col'=8] {'row'}, dimensions={0}, use_global_device_ids=true | all-gather | bytes 8448 | tf_op jit(solution)/shard_map/all_gather | solution.py:67
  207.8 34.2 %all-reduce.3.cloned.1.call-done = (f32[128,4096]{1,0:T(8,128)}, f32[128,4096]{1,0:T(8,128)}) async-done(((f32[128,4096]{1,0:T(8,128)}, f32[128,4096]{1,0:T(8,128)}), (f32[128,4096]{1,0:T(8,128)}, f32[128,4096]{1,0:T(8,128)})) %all-reduce.3.cloned.1.call-update) | async-done | bytes 4194320 | tf_op jit(solution)/shard_map/psum | solution.py:73
  242.1 2.0 fusion.1
  244.1 0.2 copy-done
  244.3 0.6 fusion.3
  244.8 0.1 copy-done.1
  244.9 0.8 convert_bitcast_fusion
  245.8 0.8 multiply_convert_fusion
  246.6 1.3 copy_bitcast_fusion.1
  247.9 7.5 %all-to-all-start = ((bf16[128,32,128]{2,0,1:T(8,128)(2,1)}), bf16[128,32,128]{2,0,1:T(8,128)(2,1)S(1)}, u32[]{:S(2)}, u32[]{:S(2)}) async-start(bf16[128,32,128]{2,0,1:T(8,128)(2,1)} %copy_bitcast_fusion.1), calls=%async_computation | async-start | bytes 2097152 | tf_op jit(solution)/shard_map/all_to_all | solution.py:81
  255.4 71.7 %reduce-scatter.7.cloned.1.call-done = f32[8,512]{1,0:T(8,128)} async-done(((f32[256,512]{1,0:T(8,128)}), f32[8,512]{1,0:T(8,128)}) %reduce-scatter.7.cloned.1.call-update) | async-done | bytes 16400 | tf_op jit(solution)/shard_map/reduce_scatter | solution.py:112
  327.1 0.7 broadcast_multiply_fusion.1
  327.8 1.3 copy.91
  329.2 7.5 %all-to-all-start.1 = ((bf16[128,32,128]{2,0,1:T(8,128)(2,1)}), bf16[128,32,128]{2,0,1:T(8,128)(2,1)S(1)}, u32[]{:S(2)}, u32[]{:S(2)}) async-start(bf16[128,32,128]{2,0,1:T(8,128)(2,1)} %bitcast.75), calls=%async_computation.1 | async-start | bytes 2097152 | tf_op jit(solution)/shard_map/all_to_all | solution.py:82
  336.7 78.1 %reduce-scatter.9.cloned.1.call-done = f32[8,512]{1,0:T(8,128)} async-done(((f32[256,512]{1,0:T(8,128)}), f32[8,512]{1,0:T(8,128)}) %reduce-scatter.9.cloned.1.call-update) | async-done | bytes 16400 | tf_op jit(solution)/shard_map/reduce_scatter | solution.py:113
  414.8 0.7 broadcast_multiply_fusion
  415.5 0.7 broadcast_in_dim.82
  416.2 1.7 div.39
  417.9 1.8 copy.64
  419.7 0.7 broadcast_in_dim.83
  420.4 1.7 div.41
  422.2 1.8 copy.69
  423.9 3.5 fusion.21
  427.4 0.2 fusion.10
  427.7 0.8 copy.70
  428.5 44.6 %all-gather.10.cloned.1.call-done = bf16[4096,512]{0,1:T(8,128)(2,1)} async-done(((bf16[128,512]{0,1:T(8,128)(2,1)}), bf16[4096,512]{0,1:T(8,128)(2,1)}) %all-gather.10.cloned.1.call-update) | async-done | bytes 4194320 | tf_op jit(solution)/shard_map/all_gather | solution.py:84
  473.1 3.5 fusion.11
  476.6 0.8 copy.71
  477.4 52.0 %all-gather.12.cloned.1.call-done = bf16[4096,512]{0,1:T(8,128)(2,1)} async-done(((bf16[128,512]{0,1:T(8,128)(2,1)}), bf16[4096,512]{0,1:T(8,128)(2,1)}) %all-gather.12.cloned.1.call-update) | async-done | bytes 4194320 | tf_op jit(solution)/shard_map/all_gather | solution.py:85
  529.4 3.4 fusion.12
  532.9 0.8 copy.72
  (34 shorter events, 0.4 us)
Async XLA Ops:
  7.2 65.0 %all-gather.8.cloned.1.call-start = ((), (), s32[]{:S(2)}) async-start(), calls=%async_computation.5 | async-start | bytes 4325376 | tf_op jit(solution)/shard_map/all_gather | solution.py:70
  13.5 170.9 %copy-start.2 = (bf16[128,4,128]{0,2,1:T(8,128)(2,1)}, bf16[128,4,128]{0,2,1:T(8,128)(2,1)S(1)}, u32[]{:S(2)}) copy-start(bf16[128,4,128]{0,2,1:T(8,128)(2,1)S(1)} %get-tuple-element.19) | copy-start | bytes 393220
  13.5 170.9 %copy-start.5 = (bf16[128,4,128]{0,2,1:T(8,128)(2,1)}, bf16[128,4,128]{0,2,1:T(8,128)(2,1)S(1)}, u32[]{:S(2)}) copy-start(bf16[128,4,128]{0,2,1:T(8,128)(2,1)S(1)} %get-tuple-element.17) | copy-start | bytes 393220
  13.5 115.6 %all-gather.6.cloned.1.call-start = ((), (), s32[]{:S(2)}) async-start(), calls=%async_computation.4 | async-start | bytes 4325376 | tf_op jit(solution)/shard_map/all_gather | solution.py:69
  14.3 227.7 %all-reduce.3.cloned.1.call-start = ((), (), s32[]{:S(2)}) async-start(), calls=%async_computation.10 | async-start | bytes 8388608 | tf_op jit(solution)/shard_map/psum | solution.py:73
  133.3 0.9 copy-start.7
  133.3 1.0 copy-start.6
  133.4 193.8 %reduce-scatter.7.cloned.1.call-start = ((), (), s32[]{:S(2)}) async-start(), calls=%async_computation.8 | async-start | bytes 540672 | tf_op jit(solution)/shard_map/reduce_scatter | solution.py:112
  159.0 25.4 %copy-start.3 = (bf16[256,512]{0,1:T(8,128)(2,1)}, bf16[256,512]{0,1:T(8,128)(2,1)S(1)}, u32[]{:S(2)}) copy-start(bf16[256,512]{0,1:T(8,128)(2,1)S(1)} %copy.52) | copy-start | bytes 786436
  184.3 3.1 copy-start.9
  184.4 230.4 %reduce-scatter.9.cloned.1.call-start = ((), (), s32[]{:S(2)}) async-start(), calls=%async_computation.9 | async-start | bytes 540672 | tf_op jit(solution)/shard_map/reduce_scatter | solution.py:113
  186.1 287.0 %all-gather.10.cloned.1.call-start = ((), (), s32[]{:S(2)}) async-start(), calls=%async_computation.6 | async-start | bytes 4325376 | tf_op jit(solution)/shard_map/all_gather | solution.py:84
  186.7 342.8 %all-gather.12.cloned.1.call-start = ((), (), s32[]{:S(2)}) async-start(), calls=%async_computation.7 | async-start | bytes 4325376 | tf_op jit(solution)/shard_map/all_gather | solution.py:85
  242.1 2.2 copy-start
  242.1 2.9 copy-start.1
  247.9 81.3 %all-to-all-start = ((bf16[128,32,128]{2,0,1:T(8,128)(2,1)}), bf16[128,32,128]{2,0,1:T(8,128)(2,1)S(1)}, u32[]{:S(2)}, u32[]{:S(2)}) async-start(bf16[128,32,128]{2,0,1:T(8,128)(2,1)} %copy_bitcast_fusion.1), calls=%async_computation | async-start | bytes 2097152 | tf_op jit(solution)/shard_map/all_to_all | solution.py:81
  329.2 200.3 %all-to-all-start.1 = ((bf16[128,32,128]{2,0,1:T(8,128)(2,1)}), bf16[128,32,128]{2,0,1:T(8,128)(2,1)S(1)}, u32[]{:S(2)}, u32[]{:S(2)}) async-start(bf16[128,32,128]{2,0,1:T(8,128)(2,1)} %bitcast.75), calls=%async_computation.1 | async-start | bytes 2097152 | tf_op jit(solution)/shard_map/all_to_all | solution.py:82
  423.9 3.5 copy-start.4
  473.1 56.4 %copy-start.8 = (f32[128,4,128]{0,2,1:T(8,128)S(1)}, f32[128,4,128]{0,2,1:T(8,128)}, u32[]{:S(2)}) copy-start(f32[128,4,128]{0,2,1:T(8,128)} %copy.69) | copy-start | bytes 786436
Sparse Core Ops, SparseCore 0:
  13.7 58.4 all-gather.7
  75.2 53.8 all-gather.5
  133.5 108.5 all-reduce.2
  245.6 81.4 reduce-scatter.6
  330.7 84.0 reduce-scatter.8
  417.1 55.9 all-gather.9
  475.5 53.8 all-gather.11
where the time goes:
time: 541 us
  waiting for transfers between devices  393 us (73%)
  blocking collectives  67.3 us (12%)
  local copies, waits for them, and re-layouts  21.4 us (4%)
  matrix products  20.8 us (4%)
  starting transfers between devices  15.3 us (3%)
  between operations  14.4 us (3%)
  other arithmetic  8.17 us (2%)
    reduce_scatter x1, waiting for transfers between devices, shards(): lax.psum_scatter(dsum_values, 'row', scatter_dimension=0, tiled=True)  78.1 us
    reduce_scatter x1, waiting for transfers between devices, shards(): lax.psum_scatter(dsum_keys, 'row', scatter_dimension=0, tiled=True)  71.7 us
    all_gather x1, waiting for transfers between devices, shards(): value_piece = lax.all_gather(v_flat, 'row', axis=0, tiled=True)  57.8 us
    all_gather x1, waiting for transfers between devices, shards(): key_piece = lax.all_gather(k_flat, 'row', axis=0, tiled=True)  52.6 us
    all_gather x1, waiting for transfers between devices, shards(): g_piece = lax.all_gather(g_flat, 'row', axis=0, tiled=True)  52 us
    all_gather x1, waiting for transfers between devices, shards(): q_piece = lax.all_gather(q_flat, 'row', axis=0, tiled=True)  44.6 us
    psum x1, waiting for transfers between devices, shards(): logit_sum, dprob_sum = lax.psum((logit_piece, dprob_piece), 'col')  34.2 us
    all_gather x1, blocking collectives, shards(): lax.all_gather(own_keys, 'row', axis=0, tiled=True)  24.2 us
  transfers between devices with their start and end apart: 9, of which 7 were waited for; matrix products, arithmetic and copies ran while one was open for 6% of the time, Pallas kernels for 0%

commit v1 on v0

v1 whole, which is shorter than its diff:
```python
import math

import jax
import jax.numpy as jnp
from jax import lax
from jax.sharding import PartitionSpec as P

SUMMARIES = 256
BLOCKS = 8

ROW_PAIR = (((1,), (1,)), ((), ()))
LEAD_PAIR = (((0,), (0,)), ((), ()))


def dot_f32(left, right, dims=(((1,), (0,)), ((), ()))):
    return lax.dot_general(left, right, dims, preferred_element_type=jnp.float32)


def merge_stats(stats):
    peak = jnp.max(stats[:, 0], axis=0)
    weight = jnp.exp(stats[:, 0] - peak)
    total = jnp.sum(weight * stats[:, 1], axis=0)
    delta = jnp.sum(weight * stats[:, 2], axis=0) / total
    return peak, total, delta


def shards(queries, keys, values, out_grad, row_keep, row_lengths):
    rows_dev, cols_dev, feature = queries.shape
    row_axis = lax.axis_size("row")
    total_rows = rows_dev * row_axis
    total_cols = cols_dev * lax.axis_size("col")
    group_rows = total_rows // SUMMARIES
    flat_width = cols_dev * feature
    near = [[y * BLOCKS + i for i in range(BLOCKS)] for y in range(row_axis // BLOCKS)]
    far = [[y * BLOCKS + i for y in range(row_axis // BLOCKS)] for i in range(BLOCKS)]
    bands = row_axis // BLOCKS
    block_keys = bands * rows_dev
    column_ids = lax.axis_index("col") * cols_dev + jnp.arange(cols_dev, dtype=jnp.int32)
    cell_keep = (row_keep[:, None] == 1) & (column_ids[None, :] < row_lengths[:, None])
    keep_flat = jnp.broadcast_to(cell_keep[:, :, None], queries.shape).reshape(
        rows_dev, flat_width
    )
    zero = jnp.zeros((), queries.dtype)

    def masked(table):
        return jnp.where(keep_flat, table.reshape(rows_dev, flat_width), zero)

    q_flat, k_flat, v_flat, g_flat = (
        masked(queries),
        masked(keys),
        masked(values),
        masked(out_grad),
    )
    logit_scale = 1.0 / math.sqrt(total_cols * feature)
    inv_root = 1.0 / math.sqrt(feature)

    k_blk = lax.all_gather(k_flat, "row", axis=0, tiled=True, axis_index_groups=far)
    q_blk = lax.all_gather(q_flat, "row", axis=0, tiled=True, axis_index_groups=near)
    logit_piece = dot_f32(q_blk, k_blk, ROW_PAIR)
    logit_sum = lax.psum_scatter(logit_piece, "col", scatter_dimension=0, tiled=True)

    flag_row = jnp.pad(
        row_keep.astype(jnp.bfloat16)[None, :], ((0, 15), (0, flat_width - rows_dev))
    )
    v_pay = jnp.concatenate([v_flat, flag_row], axis=0)
    v_all = lax.all_gather(v_pay, "row", axis=0, tiled=False, axis_index_groups=far)
    v_blk = v_all[:, :rows_dev].reshape(block_keys, flat_width)
    key_flags = v_all[:, rows_dev, :rows_dev].reshape(block_keys)
    g_blk = lax.all_gather(g_flat, "row", axis=0, tiled=True, axis_index_groups=near)
    dprob_piece = dot_f32(g_blk, v_blk, ROW_PAIR)
    dprob_sum = lax.psum_scatter(dprob_piece, "col", scatter_dimension=0, tiled=True)

    tokens = block_keys // group_rows

    def pooled(blk):
        summed = jnp.sum(
            blk.reshape(tokens, group_rows, flat_width), axis=1, dtype=jnp.float32
        )
        return (summed / group_rows).astype(jnp.bfloat16)

    sum_k, sum_v = pooled(k_blk), pooled(v_blk)
    cross_exp, cross_dp, cross_stats = [], [], []
    for c in range(cols_dev):
        lanes = slice(c * feature, (c + 1) * feature)
        cl = dot_f32(sum_k[:, lanes], q_blk[:, lanes], ROW_PAIR) * inv_root
        dp = dot_f32(sum_v[:, lanes], g_blk[:, lanes], ROW_PAIR)
        peak = jnp.max(cl, axis=0)
        lifted = jnp.exp(cl - peak[None, :])
        cross_exp.append(lifted)
        cross_dp.append(dp)
        cross_stats.append(
            jnp.stack([peak, jnp.sum(lifted, axis=0), jnp.sum(lifted * dp, axis=0)])
        )
    own_stats = jnp.stack(cross_stats, axis=1)
    all_stats = lax.all_gather(own_stats, "row", axis=0, tiled=False, axis_index_groups=near)
    c_peak, c_total, c_delta = merge_stats(all_stats)
    dq_cross, dk_sum, dv_sum = [], [], []
    for c in range(cols_dev):
        lanes = slice(c * feature, (c + 1) * feature)
        weight = jnp.exp(own_stats[0, c] - c_peak[c]) / c_total[c]
        probs = cross_exp[c] * weight[None, :]
        prob_bf = probs.astype(jnp.bfloat16)
        dl_bf = (inv_root * probs * (cross_dp[c] - c_delta[c][None, :])).astype(jnp.bfloat16)
        dq_cross.append(dot_f32(dl_bf, sum_k[:, lanes], LEAD_PAIR))
        dk_sum.append(dot_f32(dl_bf, q_blk[:, lanes]))
        dv_sum.append(dot_f32(prob_bf, g_blk[:, lanes]))

    def spread(pieces):
        wide = jnp.concatenate(pieces, axis=1) / group_rows
        return jnp.broadcast_to(wide[:, None, :], (tokens, group_rows, flat_width)).reshape(
            block_keys, flat_width
        )

    logits = jnp.where(key_flags[None, :] > 0, logit_sum * logit_scale, -1e30)
    r_peak = jnp.max(logits, axis=1)
    lifted = jnp.exp(logits - r_peak[:, None])
    r_stats = jnp.stack(
        [r_peak, jnp.sum(lifted, axis=1), jnp.sum(lifted * dprob_sum, axis=1)]
    )
    m_peak, m_total, m_delta = merge_stats(
        lax.all_gather(r_stats, "row", axis=0, tiled=False, axis_index_groups=near)
    )
    probs = lifted * (jnp.exp(r_peak - m_peak) / m_total)[:, None]
    dlogit = logit_scale * probs * (dprob_sum - m_delta[:, None])
    both = jnp.concatenate([probs.astype(jnp.bfloat16), dlogit.astype(jnp.bfloat16)], axis=1)
    both_blk = lax.all_gather(both, "col", axis=0, tiled=True)
    prob_blk, dlogit_blk = both_blk[:, :block_keys], both_blk[:, block_keys:]

    dq_part = dot_f32(dlogit_blk, k_blk) + jnp.concatenate(dq_cross, axis=1)
    dk_part = dot_f32(dlogit_blk, q_blk, LEAD_PAIR) + spread(dk_sum)
    dv_part = dot_f32(prob_blk, g_blk, LEAD_PAIR) + spread(dv_sum)

    def reduce_parts(parts, groups):
        moved = lax.all_to_all(
            parts, "row", split_axis=0, concat_axis=0, tiled=True, axis_index_groups=groups
        )
        return jnp.sum(
            moved.reshape(len(groups[0]), -1, moved.shape[-1]), axis=0, dtype=jnp.float32
        )

    def finished(total):
        return (
            jnp.where(keep_flat, total, 0.0)
            .astype(jnp.bfloat16)
            .reshape(rows_dev, cols_dev, feature)
        )

    grad_q = finished(reduce_parts(dq_part.astype(jnp.bfloat16), near))
    kv = reduce_parts(jnp.concatenate([dk_part, dv_part], axis=1).astype(jnp.bfloat16), far)
    return (grad_q, finished(kv[:, :flat_width]), finished(kv[:, flat_width:]))


def solution(mesh):
    return jax.shard_map(
        shards,
        mesh=mesh,
        in_specs=(
            P("row", "col", None),
            P("row", "col", None),
            P("row", "col", None),
            P("row", "col", None),
            P("row"),
            P("row"),
        ),
        out_specs=(P("row", "col", None), P("row", "col", None), P("row", "col", None)),
        check_vma=False,
    )
```

time: 541 us -> 264 us (0.49)
  waiting for transfers between devices: 393 us -> 140 us
  local copies, waits for them, and re-layouts: 21.4 us -> 2.74 us
  blocking collectives: 67.3 us -> 53.4 us
  other arithmetic: 8.17 us -> 19.9 us
    all_gather x4 -> x3, waiting for transfers between devices: 207 us -> 59.2 us  [the longest x1 28.9 us: shards(): both_blk = lax.all_gather(both, 'col', axis=0, tiled=True)]
    reduce_scatter x2, waiting for transfers between devices: 150 us -> 59.5 us  [the longest x1 41.6 us: shards(): lax.psum_scatter(dprob_piece, 'col', scatter_dimension=0, tiled=True)]
    psum x1 -> x0, waiting for transfers between devices: 34.2 us -> none  [shards(): logit_sum, dprob_sum = lax.psum((logit_piece, dprob_piece), 'col')]
    all_to_all x2, waiting for transfers between devices: 0.01 us -> 20.2 us  [reduce_parts(): lax.all_to_all(parts, 'row', split_axis=0, concat_axis=0, tiled=True, axi...]
    all_gather x3 -> x4, blocking collectives: 67.3 us -> 53.4 us  [the longest x1 16.4 us: shards(): lax.all_gather(r_stats, 'row', axis=0, tiled=False, axis_index_groups=near)]
    unnamed x29 -> x20, local copies, waits for them, and re-layouts: 9.62 us -> 0.04 us
    div x4 -> x0, local copies, waits for them, and re-layouts: 7.01 us -> none  [spread_groups(): return widened.reshape(rows_dev, cols_dev, feature) / group_rows]
    dot_general x8 -> x25, matrix products: 16.9 us -> 18.4 us  [dot_f32(): lax.dot_general(left, right, dims, preferred_element_type=jnp.float32)]
  transfers between devices with their start and end apart: 9 -> 7, of which waited for: 7 -> 7; matrix products, arithmetic and copies ran while one was open for 6% -> 10% of each run, Pallas kernels for 0% -> 0%
where the time goes in v1:
time: 264 us; the launch traced here: 263 us
  waiting for transfers between devices  140 us (53%)
  blocking collectives  53.4 us (20%)
  other arithmetic  19.9 us (8%)
  matrix products  18.4 us (7%)
  starting transfers between devices  14.5 us (5%)
  between operations  14.2 us (5%)
  local copies, waits for them, and re-layouts  2.74 us (1%)
    reduce_scatter x1, waiting for transfers between devices, shards(): lax.psum_scatter(dprob_piece, 'col', scatter_dimension=0, tiled=True)  41.6 us
    all_gather x1, waiting for transfers between devices, shards(): both_blk = lax.all_gather(both, 'col', axis=0, tiled=True)  28.9 us
    all_to_all x2, waiting for transfers between devices, reduce_parts(): lax.all_to_all(parts, 'row', split_axis=0, concat_axis=0, tiled=True, axi...  20.2 us
    dot_general x25, matrix products, dot_f32(): lax.dot_general(left, right, dims, preferred_element_type=jnp.float32)  18.4 us
    reduce_scatter x1, waiting for transfers between devices, shards(): lax.psum_scatter(logit_piece, 'col', scatter_dimension=0, tiled=True)  17.8 us
    all_gather x1, waiting for transfers between devices, shards(): lax.all_gather(q_flat, 'row', axis=0, tiled=True, axis_index_groups=near)  16.9 us
    all_gather x1, blocking collectives, shards(): lax.all_gather(r_stats, 'row', axis=0, tiled=False, axis_index_groups=near)  16.4 us
    all_to_all x2, starting transfers between devices, reduce_parts(): lax.all_to_all(parts, 'row', split_axis=0, concat_axis=0, tiled=True, axi...  14.3 us
  transfers between devices with their start and end apart: 7, of which 7 were waited for; matrix products, arithmetic and copies ran while one was open for 10% of the time, Pallas kernels for 0%

profile of v1, /device:TPU:1, one launch (start us, length us, event | category | flops | bytes accessed | tf_op | source)
XLA Modules:
  0.0 262.9 jit_solution(8420967507755928658)
XLA Ops:
  7.2 0.7 broadcast_compare_fusion
  7.9 0.7 compare_and_fusion
  8.8 0.2 broadcast_in_dim.36
  9.0 1.9 bitcast_select_fusion.1
  10.9 0.7 all-gather.10.cloned.1.call-update
  11.7 12.6 %all_gather.33 = bf16[512,512]{1,0:T(8,128)(2,1)S(1)} all-gather(bf16[128,512]{1,0:T(8,128)(2,1)S(1)} %get-tuple-element.21), channel_id=1, replica_groups={{0,64,128,192},{8,72,136,200},{16,80,144,208},{24,88,152,216},{32,96,16..., dimensions={0}, use_global_device_ids=true | all-gather | bytes 655360 | tf_op jit(solution)/shard_map/all_gather | solution.py:57
  24.3 16.9 %all-gather.8.cloned.1.call-done = bf16[1024,512]{1,0:T(8,128)(2,1)} async-done(((bf16[128,512]{1,0:T(8,128)(2,1)}), bf16[1024,512]{1,0:T(8,128)(2,1)}) %all-gather.8.cloned.1.call-update) | async-done | bytes 1048592 | tf_op jit(solution)/shard_map/all_gather | solution.py:58
  41.1 3.3 %fusion.83 = f32[1024,512]{1,0:T(8,128)} fusion(bf16[1024,512]{1,0:T(8,128)(2,1)} %all-gather.8.cloned.1.call-done, bf16[512,512]{1,0:T(8,128)(2,1)S(1)} %all_gather.33), kind=kOutput, calls=%fused_computation.156 | convolution fusion | flops 536870912 | bytes 3670016 | tf_op jit(solution)/shard_map/dot_general | solution.py:16
  44.6 11.4 %all-gather = bf16[576,512]{1,0:T(8,128)(2,1)S(1)} all-gather(bf16[144,512]{1,0:T(8,128)(2,1)S(1)} %fusion.38), channel_id=2, replica_groups={{0,64,128,192},{8,72,136,200},{16,80,144,208},{24,88,152,216},{32,96,16..., dimensions={0}, use_global_device_ids=true | all-gather | bytes 737280 | tf_op jit(solution)/shard_map/all_gather | solution.py:66
  56.0 13.4 %all-gather.10.cloned.1.call-done = bf16[1024,512]{1,0:T(8,128)(2,1)} async-done(((bf16[128,512]{1,0:T(8,128)(2,1)}), bf16[1024,512]{1,0:T(8,128)(2,1)}) %all-gather.10.cloned.1.call-update) | async-done | bytes 1048592 | tf_op jit(solution)/shard_map/all_gather | solution.py:69
  69.4 3.3 %fusion.84 = f32[1024,512]{1,0:T(8,128)} fusion(bf16[1024,512]{1,0:T(8,128)(2,1)} %all-gather.10.cloned.1.call-done, bf16[512,512]{1,0:T(8,128)(2,1)S(1)} %bitcast.114), kind=kOutput, calls=%fused_computation.157 | convolution fusion | flops 536870912 | bytes 3670016 | tf_op jit(solution)/shard_map/dot_general | solution.py:16
  72.7 1.4 compare_reduce_fusion
  74.2 0.2 convert_reduce_fusion.3
  74.4 0.2 convert_reduce_fusion.2
  74.6 0.2 fusion.82
  74.8 0.2 fusion.44
  75.1 0.2 fusion.81
  75.3 0.2 fusion.45
  75.6 0.2 fusion.80
  75.8 0.9 fusion.46
  76.7 0.2 fusion.79
  76.9 0.9 fusion.47
  77.8 13.1 %all-gather.2 = f32[24,4,1024]{2,1,0:T(4,128)S(1)} all-gather(f32[3,4,1024]{2,1,0:T(4,128)S(1)} %pad_maximum_fusion.2), channel_id=4, replica_groups={{0,8,16,24,32,40,48,56},{64,72,80,88,96,104,112,120},{128,136,144,152,1..., dimensions={0}, use_global_device_ids=true | all-gather | bytes 442368 | tf_op jit(solution)/shard_map/all_gather | solution.py:95
  91.0 0.6 slice_divide_fusion.3
  91.7 17.8 %reduce-scatter.3.cloned.1.call-done = f32[128,512]{1,0:T(8,128)} async-done(((f32[1024,512]{1,0:T(8,128)}), f32[128,512]{1,0:T(8,128)}) %reduce-scatter.3.cloned.1.call-update) | async-done | bytes 262160 | tf_op jit(solution)/shard_map/reduce_scatter | solution.py:60
  109.5 1.7 fusion.9
  111.2 41.6 %reduce-scatter.5.cloned.1.call-done = f32[128,512]{1,0:T(8,128)} async-done(((f32[1024,512]{1,0:T(8,128)}), f32[128,512]{1,0:T(8,128)}) %reduce-scatter.5.cloned.1.call-update) | async-done | bytes 262160 | tf_op jit(solution)/shard_map/reduce_scatter | solution.py:71
  152.8 1.2 fusion.76
  154.1 0.7 maximum_bitcast_fusion.3
  154.8 16.4 %all-gather.3 = f32[8,3,128]{2,1,0:T(4,128)S(1)} all-gather(f32[1,3,128]{2,1,0:T(4,128)S(1)} %maximum_bitcast_fusion.3), channel_id=3, replica_groups={{0,8,16,24,32,40,48,56},{64,72,80,88,96,104,112,120},{128,136,144,152,1..., dimensions={0}, use_global_device_ids=true | all-gather | bytes 13824 | tf_op jit(solution)/shard_map/all_gather | solution.py:121
  171.1 0.6 fusion.77
  171.8 1.2 reduce_max.64
  173.0 0.7 multiply_reduce_fusion.6
  173.7 0.7 exponential_divide_fusion
  174.4 1.2 multiply_convert_fusion.1
  175.6 0.8 pad_maximum_fusion.1
  176.4 0.8 multiply_convert_fusion.5
  177.2 0.7 multiply_convert_fusion.4
  177.9 0.9 multiply_convert_fusion.3
  178.9 0.9 multiply_convert_fusion.2
  179.8 0.2 fusion.35
  180.0 0.2 fusion.28
  180.1 0.2 fusion.21
  180.5 0.2 fusion.17
  180.7 0.2 fusion.24
  180.9 0.2 fusion.31
  181.1 0.2 fusion.10
  181.3 0.3 fusion.69
  181.5 1.1 fusion.66
  182.6 28.9 %all-gather.12.cloned.1.call-done = bf16[1024,1024]{1,0:T(8,128)(2,1)} async-done(((bf16[128,1024]{1,0:T(8,128)(2,1)}), bf16[1024,1024]{1,0:T(8,128)(2,1)}) %all-gather.12.cloned.1.call-update) | async-done | bytes 2097168 | tf_op jit(solution)/shard_map/all_gather | solution.py:126
  211.6 2.1 fusion.1
  213.8 0.8 fusion.2
  214.6 1.1 pad_maximum_fusion
  215.7 4.1 %all-to-all-start.1 = ((bf16[4,128,1024]{2,1,0:T(8,128)(2,1)}), bf16[4,128,1024]{2,1,0:T(8,128)(2,1)S(1)}, u32[]{:S(2)}, u32[]{:S(2)}) async-start(bf16[4,128,1024]{2,1,0:T(8,128)(2,1)} %pad_maximum_fusion), calls=%async_computation.3 | async-start | bytes 2097152 | tf_op jit(solution)/shard_map/all_to_all | solution.py:134
  219.9 0.2 fusion.63
  220.1 0.3 fusion.60
  220.4 2.9 %fusion = bf16[1024,512]{1,0:T(8,128)(2,1)} fusion(f32[1024,128]{1,0:T(8,128)S(1)} %fusion.60, f32[1024,128]{1,0:T(8,128)S(1)} %fusion.63, f32[1024,128]{1,0:T(8,128)S(1)} %copy-done.3, f32[1024,128]{1,0:T(8,128)S(1)} %fusion.69, bf16[512,512]{1,0:T(8,128)(2,1)S(1)} %all_gather.33, bf16[1024,1024]{1,0:T(8,128)(2,1)} %all-gather.12.cloned.1.call-done), kind=kOutput, calls=%fused_computation.1 | convolution fusion | flops 539492352 | bytes 4718592 | tf_op jit(solution)/shard_map/dot_general | solution.py:16
  223.3 6.8 %all-to-all-done.1 = bf16[4,128,1024]{2,1,0:T(8,128)(2,1)S(1)} async-done(((bf16[4,128,1024]{2,1,0:T(8,128)(2,1)}), bf16[4,128,1024]{2,1,0:T(8,128)(2,1)S(1)}, u32[]{:S(2)}, u32[]{:S(2)}) %all-to-all-start.1) | async-done | bytes 1048608 | tf_op jit(solution)/shard_map/all_to_all | solution.py:134
  230.1 10.1 %all-to-all-start = ((bf16[8,128,512]{2,1,0:T(8,128)(2,1)}), bf16[8,128,512]{2,1,0:T(8,128)(2,1)S(1)}, u32[]{:S(2)}, u32[]{:S(2)}) async-start(bf16[8,128,512]{2,1,0:T(8,128)(2,1)} %bitcast.120), calls=%async_computation.2 | async-start | bytes 2097152 | tf_op jit(solution)/shard_map/all_to_all | solution.py:134
  240.2 0.2 convert_reduce_fusion
  240.4 0.7 reshape.208
  241.1 0.7 reshape.209
  241.8 13.5 %all-to-all-done = bf16[8,128,512]{2,1,0:T(8,128)(2,1)S(1)} async-done(((bf16[8,128,512]{2,1,0:T(8,128)(2,1)}), bf16[8,128,512]{2,1,0:T(8,128)(2,1)S(1)}, u32[]{:S(2)}, u32[]{:S(2)}) %all-to-all-start) | async-done | bytes 1048608 | tf_op jit(solution)/shard_map/all_to_all | solution.py:134
  255.5 0.9 select_convert_fusion
  (57 shorter events, 1.5 us)
Async XLA Ops:
  7.2 34.0 %all-gather.8.cloned.1.call-start = ((), (), s32[]{:S(2)}) async-start(), calls=%async_computation.4 | async-start | bytes 1179648 | tf_op jit(solution)/shard_map/all_gather | solution.py:58
  10.9 58.5 %all-gather.10.cloned.1.call-start = ((), (), s32[]{:S(2)}) async-start(), calls=%async_computation.6 | async-start | bytes 1179648 | tf_op jit(solution)/shard_map/all_gather | solution.py:69
  11.6 97.9 %reduce-scatter.3.cloned.1.call-start = ((), (), s32[]{:S(2)}) async-start(), calls=%async_computation.5 | async-start | bytes 2359296 | tf_op jit(solution)/shard_map/reduce_scatter | solution.py:60
  24.3 20.2 %copy-start.9 = (s32[128]{0:T(128)S(1)}, s32[128]{0:T(128)}, u32[]{:S(2)}) copy-start(s32[128]{0:T(128)} %param.10) | copy-start | bytes 1540
  44.5 108.3 %reduce-scatter.5.cloned.1.call-start = ((), (), s32[]{:S(2)}) async-start(), calls=%async_computation.7 | async-start | bytes 2359296 | tf_op jit(solution)/shard_map/reduce_scatter | solution.py:71
  55.9 13.5 %copy-start.2 = (bf16[576,512]{1,0:T(8,128)(2,1)}, bf16[576,512]{1,0:T(8,128)(2,1)S(1)}, u32[]{:S(2)}) copy-start(bf16[576,512]{1,0:T(8,128)(2,1)S(1)} %all-gather) | copy-start | bytes 1769476
  72.7 1.9 copy-start
  72.7 2.1 copy-start.1
  72.7 138.8 %all-gather.12.cloned.1.call-start = ((), (), s32[]{:S(2)}) async-start(), calls=%async_computation.8 | async-start | bytes 2359296 | tf_op jit(solution)/shard_map/all_gather | solution.py:126
  176.4 4.1 %copy-start.7 = (f32[1,1024]{1,0:T(1,128)S(1)}, f32[1,1024]{1,0:T(1,128)}, u32[]{:S(2)}) copy-start(f32[1,1024]{1,0:T(1,128)} %get-tuple-element.27) | copy-start | bytes 12292
  176.4 4.3 %copy-start.6 = (f32[1,1024]{1,0:T(1,128)S(1)}, f32[1,1024]{1,0:T(1,128)}, u32[]{:S(2)}) copy-start(f32[1,1024]{1,0:T(1,128)} %get-tuple-element.28) | copy-start | bytes 12292
  176.4 4.5 %copy-start.5 = (f32[1,1024]{1,0:T(1,128)S(1)}, f32[1,1024]{1,0:T(1,128)}, u32[]{:S(2)}) copy-start(f32[1,1024]{1,0:T(1,128)} %get-tuple-element.25) | copy-start | bytes 12292
  176.4 4.7 %copy-start.4 = (f32[1,1024]{1,0:T(1,128)S(1)}, f32[1,1024]{1,0:T(1,128)}, u32[]{:S(2)}) copy-start(f32[1,1024]{1,0:T(1,128)} %get-tuple-element.26) | copy-start | bytes 12292
  211.6 2.2 copy-start.8
  215.7 4.7 %copy-start.3 = (f32[1024,128]{1,0:T(8,128)S(1)}, f32[1024,128]{1,0:T(8,128)}, u32[]{:S(2)}) copy-start(f32[1024,128]{1,0:T(8,128)} %fusion.66) | copy-start | bytes 1572868
  215.7 14.3 %all-to-all-start.1 = ((bf16[4,128,1024]{2,1,0:T(8,128)(2,1)}), bf16[4,128,1024]{2,1,0:T(8,128)(2,1)S(1)}, u32[]{:S(2)}, u32[]{:S(2)}) async-start(bf16[4,128,1024]{2,1,0:T(8,128)(2,1)} %pad_maximum_fusion), calls=%async_computation.3 | async-start | bytes 2097152 | tf_op jit(solution)/shard_map/all_to_all | solution.py:134
  230.1 25.2 %all-to-all-start = ((bf16[8,128,512]{2,1,0:T(8,128)(2,1)}), bf16[8,128,512]{2,1,0:T(8,128)(2,1)S(1)}, u32[]{:S(2)}, u32[]{:S(2)}) async-start(bf16[8,128,512]{2,1,0:T(8,128)(2,1)} %bitcast.120), calls=%async_computation.2 | async-start | bytes 2097152 | tf_op jit(solution)/shard_map/all_to_all | solution.py:134
Sparse Core Ops, SparseCore 0:
  11.0 30.0 all-gather.7
  43.6 25.7 all-gather.9
  72.0 37.5 reduce-scatter.2
  111.9 40.8 reduce-scatter.4
  176.5 34.9 all-gather.11

commit v2 on v1

v2 whole, which is shorter than its diff:
```python
import math

import jax
import jax.numpy as jnp
from jax import lax
from jax.experimental.layout import Layout, with_layout_constraint
from jax.sharding import PartitionSpec as P

SUMMARIES = 256
XS = 4

ROW_PAIR = (((1,), (1,)), ((), ()))
LEAD_PAIR = (((0,), (0,)), ((), ()))
PLAIN = (((1,), (0,)), ((), ()))


def dot_f32(left, right, dims=PLAIN):
    return lax.dot_general(left, right, dims, preferred_element_type=jnp.float32)


def merge_stats(stats):
    peak = jnp.max(stats[:, 0], axis=0)
    weight = jnp.exp(stats[:, 0] - peak)
    total = jnp.sum(weight * stats[:, 1], axis=0)
    delta = jnp.sum(weight * stats[:, 2], axis=0) / total
    return peak, total, delta


def shards(queries, keys, values, out_grad, row_keep, row_lengths):
    rows_dev, cols_dev, feature = queries.shape
    row_axis = lax.axis_size("row")
    ys = row_axis // (2 * XS)
    near_size = 2 * XS
    total_rows = rows_dev * row_axis
    total_cols = cols_dev * lax.axis_size("col")
    group_rows = total_rows // SUMMARIES
    flat_width = cols_dev * feature
    block_rows = near_size * rows_dev
    block_keys = ys * rows_dev
    near = [[y * near_size + i for i in range(near_size)] for y in range(ys)]
    place = lax.axis_index("row")
    own_x = (place // 2) % XS
    own_core = place % 2

    def at(y, x, core):
        return ((y % ys) * XS + x % XS) * 2 + core

    cells = [(y, x, c) for y in range(ys) for x in range(XS) for c in range(2)]

    def shift_y(table, step):
        return lax.ppermute(table, "row", [(at(y, x, c), at(y + step, x, c)) for y, x, c in cells])

    def shift_x(table, step):
        return lax.ppermute(table, "row", [(at(y, x, c), at(y, x + step, c)) for y, x, c in cells])

    def swap_core(table):
        return lax.ppermute(table, "row", [(at(y, x, c), at(y, x, 1 - c)) for y, x, c in cells])

    def by_core(own, other):
        first = jnp.where(own_core == 0, own, other)
        second = jnp.where(own_core == 0, other, own)
        return first, second

    column_ids = lax.axis_index("col") * cols_dev + jnp.arange(cols_dev, dtype=jnp.int32)
    cell_keep = (row_keep[:, None] == 1) & (column_ids[None, :] < row_lengths[:, None])
    keep_flat = jnp.broadcast_to(cell_keep[:, :, None], queries.shape).reshape(
        rows_dev, flat_width
    )
    zero = jnp.zeros((), queries.dtype)

    def masked(table):
        flat = jnp.where(keep_flat, table.reshape(rows_dev, flat_width), zero)
        return with_layout_constraint(flat, Layout((0, 1)))

    def key_block(table):
        return [table] + [shift_y(table, s) for s in range(1, ys)]

    def query_block(table):
        pieces = [table] + [shift_x(table, s) for s in range(1, XS)]
        line = jnp.zeros((XS,) + table.shape, table.dtype)
        for s, piece in enumerate(pieces):
            line = lax.dynamic_update_slice(line, piece[None], ((own_x - s) % XS, 0, 0))
        pair = jnp.stack(by_core(line, swap_core(line)), axis=1)
        return pair.reshape(block_rows, flat_width)

    logit_scale = 1.0 / math.sqrt(total_cols * feature)
    inv_root = 1.0 / math.sqrt(feature)

    q_flat, k_flat = masked(queries), masked(keys)
    k_blk = jnp.concatenate(key_block(k_flat), axis=0)
    q_blk = query_block(q_flat)
    logit_piece = dot_f32(q_blk, k_blk, ROW_PAIR)
    keep_flat, _ = lax.optimization_barrier((keep_flat, logit_piece))
    logit_sum = lax.psum_scatter(logit_piece, "col", scatter_dimension=0, tiled=True)

    v_flat, g_flat = masked(values), masked(out_grad)
    flag_row = jnp.pad(
        row_keep.astype(jnp.bfloat16)[None, :], ((0, 15), (0, flat_width - rows_dev))
    )
    v_pieces = key_block(jnp.concatenate([v_flat, flag_row], axis=0))
    v_blk = jnp.concatenate([p[:rows_dev] for p in v_pieces], axis=0)
    key_flags = jnp.concatenate([p[rows_dev, :rows_dev] for p in v_pieces])
    g_blk = query_block(g_flat)
    dprob_piece = dot_f32(g_blk, v_blk, ROW_PAIR).astype(jnp.bfloat16)
    dprob_parts = lax.all_to_all(dprob_piece, "col", split_axis=0, concat_axis=0, tiled=True)

    tokens = block_keys // group_rows

    def pooled(blk):
        summed = jnp.sum(
            blk.reshape(tokens, group_rows, flat_width), axis=1, dtype=jnp.float32
        )
        return (summed / group_rows).astype(jnp.bfloat16)

    sum_k, sum_v = pooled(k_blk), pooled(v_blk)
    cross_exp, cross_dp, cross_stats = [], [], []
    for c in range(cols_dev):
        lanes = slice(c * feature, (c + 1) * feature)
        cl = dot_f32(sum_k[:, lanes], q_blk[:, lanes], ROW_PAIR) * inv_root
        dp = dot_f32(sum_v[:, lanes], g_blk[:, lanes], ROW_PAIR)
        peak = jnp.max(cl, axis=0)
        lifted = jnp.exp(cl - peak[None, :])
        cross_exp.append(lifted)
        cross_dp.append(dp)
        cross_stats.append(
            jnp.stack([peak, jnp.sum(lifted, axis=0), jnp.sum(lifted * dp, axis=0)])
        )
    own_stats = jnp.stack(cross_stats, axis=1)
    all_stats = lax.all_gather(own_stats, "row", axis=0, tiled=False, axis_index_groups=near)
    c_peak, c_total, c_delta = merge_stats(all_stats)
    dq_cross, dk_sum, dv_sum = [], [], []
    for c in range(cols_dev):
        lanes = slice(c * feature, (c + 1) * feature)
        weight = jnp.exp(own_stats[0, c] - c_peak[c]) / c_total[c]
        probs = cross_exp[c] * weight[None, :]
        prob_bf = probs.astype(jnp.bfloat16)
        dl_bf = (inv_root * probs * (cross_dp[c] - c_delta[c][None, :])).astype(jnp.bfloat16)
        dq_cross.append(dot_f32(dl_bf, sum_k[:, lanes], LEAD_PAIR))
        dk_sum.append(dot_f32(dl_bf, q_blk[:, lanes]))
        dv_sum.append(dot_f32(prob_bf, g_blk[:, lanes]))
    dq_cross = jnp.concatenate(dq_cross, axis=1)
    dk_sum = jnp.concatenate(dk_sum, axis=1) / group_rows
    dv_sum = jnp.concatenate(dv_sum, axis=1) / group_rows
    logit_sum, dq_cross, dk_sum, dv_sum = lax.optimization_barrier(
        (logit_sum, dq_cross, dk_sum, dv_sum)
    )

    def spread(wide):
        return jnp.broadcast_to(wide[:, None, :], (tokens, group_rows, flat_width)).reshape(
            block_keys, flat_width
        )

    dprob_sum = jnp.sum(
        dprob_parts.reshape(-1, block_rows // lax.axis_size("col"), block_keys),
        axis=0,
        dtype=jnp.float32,
    )
    logits = jnp.where(key_flags[None, :] > 0, logit_sum * logit_scale, -1e30)
    peak = jnp.max(logits, axis=1)
    lifted = jnp.exp(logits - peak[:, None])
    total = jnp.sum(lifted, axis=1)
    weighted = jnp.sum(lifted * dprob_sum, axis=1)
    delta = weighted / total
    lift_bf = lifted.astype(jnp.bfloat16)
    tilt_bf = (lifted * (dprob_sum - delta[:, None])).astype(jnp.bfloat16)
    lift_blk = lax.all_gather(lift_bf, "col", axis=0, tiled=True).astype(jnp.float32)
    tilt_blk = lax.all_gather(tilt_bf, "col", axis=0, tiled=True).astype(jnp.float32)
    m_peak, m_total, m_delta = merge_stats(
        lax.all_gather(
            jnp.stack([peak, total, weighted]),
            "row",
            axis=0,
            tiled=False,
            axis_index_groups=near,
        )
    )
    scaling = jnp.stack([jnp.exp(peak - m_peak) / m_total, m_delta - delta])
    scaling = lax.all_gather(scaling, "col", axis=1, tiled=True)
    weight, offset = scaling[0][:, None], scaling[1][:, None]
    prob_blk = (lift_blk * weight).astype(jnp.bfloat16)
    dlogit_blk = (logit_scale * weight * (tilt_blk - lift_blk * offset)).astype(jnp.bfloat16)

    def reduce_keys(part):
        part = part.astype(jnp.bfloat16).reshape(ys, rows_dev, flat_width)
        moved = [part[0]] + [shift_y(part[s], -s) for s in range(1, ys)]
        return sum(m.astype(jnp.float32) for m in moved)

    def reduce_queries(part):
        part = part.astype(jnp.bfloat16).reshape(XS, 2, rows_dev, flat_width)
        own, other = by_core(part[:, 0], part[:, 1])
        line = (own.astype(jnp.float32) + swap_core(other).astype(jnp.float32)).astype(
            jnp.bfloat16
        )

        def piece(s):
            return lax.dynamic_index_in_dim(line, (own_x - s) % XS, axis=0, keepdims=False)

        moved = [piece(0)] + [shift_x(piece(s), -s) for s in range(1, XS)]
        return sum(m.astype(jnp.float32) for m in moved)

    def finished(rows):
        return (
            jnp.where(keep_flat, rows, 0.0)
            .astype(jnp.bfloat16)
            .reshape(rows_dev, cols_dev, feature)
        )

    grad_v = finished(reduce_keys(dot_f32(prob_blk, g_blk, LEAD_PAIR) + spread(dv_sum)))
    grad_q = finished(reduce_queries(dot_f32(dlogit_blk, k_blk) + dq_cross))
    grad_k = finished(reduce_keys(dot_f32(dlogit_blk, q_blk, LEAD_PAIR) + spread(dk_sum)))
    return (grad_q, grad_k, grad_v)


def solution(mesh):
    return jax.shard_map(
        shards,
        mesh=mesh,
        in_specs=(
            P("row", "col", None),
            P("row", "col", None),
            P("row", "col", None),
            P("row", "col", None),
            P("row"),
            P("row"),
        ),
        out_specs=(P("row", "col", None), P("row", "col", None), P("row", "col", None)),
        check_vma=False,
    )
```

time: 264 us -> 227 us (0.86)
  waiting for transfers between devices: 140 us -> 88.3 us
  starting transfers between devices: 14.5 us -> 44.5 us
  blocking collectives: 53.4 us -> 37 us
  other arithmetic: 19.9 us -> 15.2 us
  local copies, waits for them, and re-layouts: 2.74 us -> 6.18 us
    reduce_scatter x1 -> x0, waiting for transfers between devices: 41.6 us -> none  [shards(): lax.psum_scatter(dprob_piece, 'col', scatter_dimension=0, tiled=True)]
    ppermute x0 -> x24, starting transfers between devices: none -> 36.2 us  [the longest x9 14.4 us: shift_x(): lax.ppermute(table, 'row', [(at(y, x, c), at(y, x + step, c)) for y, x, c...]
    ppermute x0 -> x24, waiting for transfers between devices: none -> 24.5 us  [the longest x12 15.1 us: shift_y(): lax.ppermute(table, 'row', [(at(y, x, c), at(y + step, x, c)) for y, x, c...]
    all_gather x3 -> x2, blocking collectives: 40.4 us -> 22.2 us  [the longest x1 11.5 us: shards(): lax.all_gather(jnp.stack([peak, total, weighted]), 'row', axis=0, tiled=F...]
    reduce_scatter x1, waiting for transfers between devices: 17.8 us -> 0.02 us  [shards(): lax.psum_scatter(logit_piece, 'col', scatter_dimension=0, tiled=True)]
    all_gather x3 -> x2, waiting for transfers between devices: 59.2 us -> 43 us  [the longest x1 39.5 us: shards(): lax.all_gather(lift_bf, 'col', axis=0, tiled=True).astype(jnp.float32)]
    all_to_all x2 -> x1, starting transfers between devices: 14.3 us -> 8.19 us  [shards(): lax.all_to_all(dprob_piece, 'col', split_axis=0, concat_axis=0, tiled=True)]
    all_to_all x2 -> x1, waiting for transfers between devices: 20.2 us -> 20 us  [shards(): lax.all_to_all(dprob_piece, 'col', split_axis=0, concat_axis=0, tiled=True)]
  transfers between devices with their start and end apart: 7 -> 28, of which waited for: 7 -> 13; matrix products, arithmetic and copies ran while one was open for 10% -> 9% of each run, Pallas kernels for 0% -> 0%
where the time goes in v2:
time: 227 us; the launch traced here: 223 us
  waiting for transfers between devices  88.3 us (39%)
  starting transfers between devices  44.5 us (20%)
  blocking collectives  37 us (16%)
  matrix products  17.5 us (8%)
  other arithmetic  15.2 us (7%)
  between operations  14.6 us (6%)
  local copies, waits for them, and re-layouts  6.18 us (3%)
    all_gather x1, waiting for transfers between devices, shards(): lax.all_gather(lift_bf, 'col', axis=0, tiled=True).astype(jnp.float32)  39.5 us
    all_to_all x1, waiting for transfers between devices, shards(): lax.all_to_all(dprob_piece, 'col', split_axis=0, concat_axis=0, tiled=True)  20 us
    dot_general x25, matrix products, dot_f32(): lax.dot_general(left, right, dims, preferred_element_type=jnp.float32)  17.5 us
    ppermute x12, waiting for transfers between devices, shift_y(): lax.ppermute(table, 'row', [(at(y, x, c), at(y + step, x, c)) for y, x, c...  15.1 us
    all_gather x1, blocking collectives, shards(): lax.all_gather(own_stats, 'row', axis=0, tiled=False, axis_index_groups=n...  14.8 us
    ppermute x9, starting transfers between devices, shift_x(): lax.ppermute(table, 'row', [(at(y, x, c), at(y, x + step, c)) for y, x, c...  14.4 us
    ppermute x12, starting transfers between devices, shift_y(): lax.ppermute(table, 'row', [(at(y, x, c), at(y + step, x, c)) for y, x, c...  12.3 us
    all_gather x1, blocking collectives, shards(): lax.all_gather(jnp.stack([peak, total, weighted]), 'row', axis=0, tiled=F...  11.5 us
  transfers between devices with their start and end apart: 28, of which 13 were waited for; matrix products, arithmetic and copies ran while one was open for 9% of the time, Pallas kernels for 0%

profile of v2, /device:TPU:1, one launch (start us, length us, event | category | flops | bytes accessed | tf_op | source)
XLA Modules:
  0.0 223.4 jit_solution(16214101307348684247)
XLA Ops:
  7.3 0.7 broadcast_compare_fusion
  8.0 0.7 compare_and_fusion
  9.1 1.0 bitcast_dynamic-update-slice_fusion.7
  10.0 2.1 collective-permute-start
  12.2 2.5 %collective-permute-start.1 = (bf16[128,512]{1,0:T(8,128)(2,1)S(1)}, bf16[128,512]{1,0:T(8,128)(2,1)S(1)}, u32[]{:S(2)}, u32[]{:S(2)}) collective-permute-start(bf16[128,512]{1,0:T(8,128)(2,1)S(1)} %get-tuple-element.30), channel_id=1, source_target_pairs={{0,32},{8,40},{16,48},{24,56},{32,0},{40,8},{48,16},{56,24},{64,96... | collective-permute-start | bytes 393224 | tf_op jit(solution)/shard_map/ppermute | solution.py:54
  14.6 1.2 collective-permute-start.2
  15.8 4.5 %collective-permute-done.1 = bf16[128,512]{1,0:T(8,128)(2,1)S(1)} collective-permute-done((bf16[128,512]{1,0:T(8,128)(2,1)S(1)}, bf16[128,512]{1,0:T(8,128)(2,1)S(1)}, u32[]{:S(2)}, u32[]{:S(2)}) %collective-permute-start.1) | collective-permute-done | bytes 131104 | tf_op jit(solution)/shard_map/ppermute | solution.py:54
  20.4 2.0 collective-permute-start.3
  22.5 2.4 %collective-permute-start.6 = (bf16[128,512]{1,0:T(8,128)(2,1)S(1)}, bf16[128,512]{1,0:T(8,128)(2,1)S(1)}, u32[]{:S(2)}, u32[]{:S(2)}) collective-permute-start(bf16[128,512]{1,0:T(8,128)(2,1)S(1)} %bitcast_select_fusion.2), channel_id=1, source_target_pairs={{0,192},{8,200},{16,208},{24,216},{32,224},{40,232},{48,240},{56,2... | collective-permute-start | bytes 393224 | tf_op jit(solution)/shard_map/ppermute | solution.py:51
  25.2 0.7 collective-permute-start.4
  26.0 4.4 %collective-permute-done.6 = bf16[128,512]{1,0:T(8,128)(2,1)S(1)} collective-permute-done((bf16[128,512]{1,0:T(8,128)(2,1)S(1)}, bf16[128,512]{1,0:T(8,128)(2,1)S(1)}, u32[]{:S(2)}, u32[]{:S(2)}) %collective-permute-start.6) | collective-permute-done | bytes 131104 | tf_op jit(solution)/shard_map/ppermute | solution.py:51
  30.4 0.8 collective-permute-done.5
  31.2 3.4 %collective-permute-done.4 = bf16[128,512]{1,0:T(8,128)(2,1)S(1)} collective-permute-done((bf16[128,512]{1,0:T(8,128)(2,1)S(1)}, bf16[128,512]{1,0:T(8,128)(2,1)S(1)}, u32[]{:S(2)}, u32[]{:S(2)}) %collective-permute-start.4) | collective-permute-done | bytes 131104 | tf_op jit(solution)/shard_map/ppermute | solution.py:51
  35.7 2.1 fusion.85
  37.8 0.8 copy-done.16
  38.7 1.1 collective-permute-start.10
  39.8 2.1 collective-permute-start.11
  41.9 1.3 collective-permute-start.12
  45.2 2.7 %collective-permute-done.11 = bf16[128,512]{1,0:T(8,128)(2,1)S(1)} collective-permute-done((bf16[128,512]{1,0:T(8,128)(2,1)S(1)}, bf16[128,512]{1,0:T(8,128)(2,1)S(1)}, u32[]{:S(2)}, u32[]{:S(2)}) %collective-permute-start.11) | collective-permute-done | bytes 131104 | tf_op jit(solution)/shard_map/ppermute | solution.py:54
  47.9 1.7 collective-permute-start.13
  49.6 2.7 %collective-permute-done.7 = bf16[144,512]{1,0:T(8,128)(2,1)S(1)} collective-permute-done((bf16[144,512]{1,0:T(8,128)(2,1)S(1)}, bf16[144,512]{1,0:T(8,128)(2,1)S(1)}, u32[]{:S(2)}, u32[]{:S(2)}) %collective-permute-start.7) | collective-permute-done | bytes 147488 | tf_op jit(solution)/shard_map/ppermute | solution.py:51
  53.4 1.7 convolution_convert_fusion
  55.1 0.9 fusion.52
  56.0 0.9 fusion.51
  56.9 0.9 fusion.50
  57.9 0.8 fusion.49
  58.8 14.8 %all-gather = f32[24,4,1024]{2,1,0:T(4,128)S(1)} all-gather(f32[3,4,1024]{2,1,0:T(4,128)S(1)} %pad_maximum_fusion.5), channel_id=2, replica_groups={{0,8,16,24,32,40,48,56},{64,72,80,88,96,104,112,120},{128,136,144,152,1..., dimensions={0}, use_global_device_ids=true | all-gather | bytes 442368 | tf_op jit(solution)/shard_map/all_gather | solution.py:129
  73.7 0.6 slice_divide_fusion.3
  74.4 0.6 fusion.91
  75.0 8.2 %all-to-all-start = ((bf16[8,128,512]{2,1,0:T(8,128)(2,1)}), bf16[8,128,512]{2,1,0:T(8,128)(2,1)S(1)}, u32[]{:S(2)}, u32[]{:S(2)}) async-start(bf16[8,128,512]{2,1,0:T(8,128)(2,1)} %bitcast.216), calls=%async_computation.1 | async-start | bytes 2097152 | tf_op jit(solution)/shard_map/all_to_all | solution.py:105
  83.3 1.0 multiply_convert_fusion.3
  84.3 1.0 multiply_convert_fusion.4
  85.3 0.9 multiply_convert_fusion.1
  86.6 0.9 fusion.29
  88.1 0.6 maximum_multiply_fusion.1
  89.1 0.6 maximum_multiply_fusion
  90.8 1.6 pad_maximum_fusion
  92.4 20.0 %all-to-all-done = bf16[8,128,512]{2,1,0:T(8,128)(2,1)S(1)} async-done(((bf16[8,128,512]{2,1,0:T(8,128)(2,1)}), bf16[8,128,512]{2,1,0:T(8,128)(2,1)S(1)}, u32[]{:S(2)}, u32[]{:S(2)}) %all-to-all-start) | async-done | bytes 1048608 | tf_op jit(solution)/shard_map/all_to_all | solution.py:105
  112.6 1.1 fusion.14
  113.7 1.2 fusion.84
  114.9 1.8 multiply_convert_fusion
  116.7 0.7 all-gather.8.cloned.1.call-update
  117.4 11.5 %all-gather.2 = f32[8,3,128]{2,1,0:T(4,128)S(1)} all-gather(f32[1,3,128]{2,1,0:T(4,128)S(1)} %maximum_bitcast_fusion.3), channel_id=3, replica_groups={{0,8,16,24,32,40,48,56},{64,72,80,88,96,104,112,120},{128,136,144,152,1..., dimensions={0}, use_global_device_ids=true | all-gather | bytes 13824 | tf_op jit(solution)/shard_map/all_gather | solution.py:169
  129.0 10.7 %all_gather.25 = f32[2,1024]{1,0:T(2,128)S(1)} all-gather(f32[2,128]{1,0:T(2,128)S(1)} %pad_maximum_fusion.7), channel_id=1, replica_groups=mesh['row'=32,'col'=8] {'col'}, dimensions={1}, use_global_device_ids=true | all-gather | bytes 9216 | tf_op jit(solution)/shard_map/all_gather | solution.py:178
  139.7 3.5 %all-gather.6.cloned.1.call-done = bf16[1024,512]{1,0:T(8,128)(2,1)} async-done(((bf16[128,512]{1,0:T(8,128)(2,1)}), bf16[1024,512]{1,0:T(8,128)(2,1)}) %all-gather.6.cloned.1.call-update) | async-done | bytes 1048592 | tf_op jit(solution)/shard_map/all_gather | solution.py:167
  143.2 39.5 %all-gather.8.cloned.1.call-done = bf16[1024,512]{1,0:T(8,128)(2,1)} async-done(((bf16[128,512]{1,0:T(8,128)(2,1)}), bf16[1024,512]{1,0:T(8,128)(2,1)}) %all-gather.8.cloned.1.call-update) | async-done | bytes 1048592 | tf_op jit(solution)/shard_map/all_gather | solution.py:166
  182.7 4.4 %add_convert_fusion = bf16[1024,512]{0,1:T(8,128)(2,1)} fusion(f32[1024,512]{0,1:T(8,128)} %pad_maximum_fusion, bf16[128,512]{1,0:T(8,128)(2,1)} %copy-done.6, bf16[128,512]{1,0:T(8,128)(2,1)} %copy-done.7, bf16[128,512]{1,0:T(8,128)(2,1)} %copy-done.8, bf16[128,512]{1,0:T(8,128)(2,1)S(1)} %copy-done.3, bf16[1024,512]{1,0:T(8,128)(2,1)} %all-gather.8.cloned.1.call-done, ...), kind=kOutput, calls=%fused_computation.7 | convolution fusion | flops 543162368 | bytes 5775360 | tf_op jit(solution)/shard_map/dot_general | solution.py:18
  187.1 1.5 copy.57
  188.8 5.9 %collective-permute-start.14 = (bf16[4,128,512]{2,1,0:T(8,128)(2,1)S(1)}, bf16[4,128,512]{2,1,0:T(8,128)(2,1)S(1)}, u32[]{:S(2)}, u32[]{:S(2)}) collective-permute-start(bf16[4,128,512]{2,1,0:T(8,128)(2,1)S(1)} %select_bitcast_fusion), channel_id=1, source_target_pairs={{0,8},{8,0},{16,24},{24,16},{32,40},{40,32},{48,56},{56,48},{64,72... | collective-permute-start | bytes 1572872 | tf_op jit(solution)/shard_map/ppermute | solution.py:57
  194.8 1.2 fusion.4
  196.0 2.5 %collective-permute-start.18 = (bf16[128,512]{1,0:T(8,128)(2,1)S(1)}, bf16[128,512]{1,0:T(8,128)(2,1)S(1)}, u32[]{:S(2)}, u32[]{:S(2)}) collective-permute-start(bf16[128,512]{1,0:T(8,128)(2,1)S(1)} %get-tuple-element.38), channel_id=1, source_target_pairs={{0,192},{8,200},{16,208},{24,216},{32,224},{40,232},{48,240},{56,2... | collective-permute-start | bytes 393224 | tf_op jit(solution)/shard_map/ppermute | solution.py:51
  198.5 1.7 collective-permute-start.19
  200.4 0.8 fusion.5
  201.3 1.0 collective-permute-start.21
  202.3 0.9 collective-permute-start.23
  203.4 1.6 collective-permute-start.22
  205.0 0.7 collective-permute-done.20
  205.7 2.4 %collective-permute-start.15 = (bf16[128,512]{1,0:T(8,128)(2,1)S(1)}, bf16[128,512]{1,0:T(8,128)(2,1)S(1)}, u32[]{:S(2)}, u32[]{:S(2)}) collective-permute-start(bf16[128,512]{1,0:T(8,128)(2,1)S(1)} %get-tuple-element.41), channel_id=1, source_target_pairs={{0,48},{8,56},{16,0},{24,8},{32,16},{40,24},{48,32},{56,40},{64,11... | collective-permute-start | bytes 393224 | tf_op jit(solution)/shard_map/ppermute | solution.py:54
  208.1 1.8 collective-permute-start.16
  209.8 3.1 %collective-permute-done.23 = bf16[128,512]{1,0:T(8,128)(2,1)S(1)} collective-permute-done((bf16[128,512]{1,0:T(8,128)(2,1)S(1)}, bf16[128,512]{1,0:T(8,128)(2,1)S(1)}, u32[]{:S(2)}, u32[]{:S(2)}) %collective-permute-start.23) | collective-permute-done | bytes 131104 | tf_op jit(solution)/shard_map/ppermute | solution.py:51
  212.9 1.6 collective-permute-done.17
  214.8 0.7 reshape.250
  215.4 0.7 reshape.248
  216.1 0.7 reshape.246
  (155 shorter events, 8.8 us)
Async XLA Ops:
  7.2 18.8 %copy-start.24 = (s32[128]{0:T(128)S(1)}, s32[128]{0:T(128)}, u32[]{:S(2)}) copy-start(s32[128]{0:T(128)} %param.10) | copy-start | bytes 1540
  7.2 15.2 %copy-start.14 = (bf16[128,4,128]{2,1,0:T(4,128)(2,1)S(1)}, bf16[128,4,128]{2,1,0:T(4,128)(2,1)}, u32[]{:S(2)}) copy-start(bf16[128,4,128]{2,1,0:T(4,128)(2,1)} %param.7) | copy-start | bytes 393220
  7.2 105.4 %reduce-scatter.2.cloned.1.call-start = ((), (), s32[]{:S(2)}) async-start(), calls=%async_computation.2 | async-start | bytes 2359296 | tf_op jit(solution)/shard_map/reduce_scatter | solution.py:94
  10.0 5.7 %collective-permute-start = (bf16[128,512]{1,0:T(8,128)(2,1)S(1)}, bf16[128,512]{1,0:T(8,128)(2,1)S(1)}, u32[]{:S(2)}, u32[]{:S(2)}) collective-permute-start(bf16[128,512]{1,0:T(8,128)(2,1)S(1)} %get-tuple-element.30), channel_id=1, source_target_pairs={{0,16},{8,24},{16,32},{24,40},{32,48},{40,56},{48,0},{56,8},{64,80... | collective-permute-start | bytes 393224 | tf_op jit(solution)/shard_map/ppermute | solution.py:54
  12.2 8.2 %collective-permute-start.1 = (bf16[128,512]{1,0:T(8,128)(2,1)S(1)}, bf16[128,512]{1,0:T(8,128)(2,1)S(1)}, u32[]{:S(2)}, u32[]{:S(2)}) collective-permute-start(bf16[128,512]{1,0:T(8,128)(2,1)S(1)} %get-tuple-element.30), channel_id=1, source_target_pairs={{0,32},{8,40},{16,48},{24,56},{32,0},{40,8},{48,16},{56,24},{64,96... | collective-permute-start | bytes 393224 | tf_op jit(solution)/shard_map/ppermute | solution.py:54
  14.6 5.7 %collective-permute-start.2 = (bf16[128,512]{1,0:T(8,128)(2,1)S(1)}, bf16[128,512]{1,0:T(8,128)(2,1)S(1)}, u32[]{:S(2)}, u32[]{:S(2)}) collective-permute-start(bf16[128,512]{1,0:T(8,128)(2,1)S(1)} %get-tuple-element.30), channel_id=1, source_target_pairs={{0,48},{8,56},{16,0},{24,8},{32,16},{40,24},{48,32},{56,40},{64,11... | collective-permute-start | bytes 393224 | tf_op jit(solution)/shard_map/ppermute | solution.py:54
  20.4 14.5 %collective-permute-start.3 = (bf16[4,128,512]{2,1,0:T(8,128)(2,1)S(1)}, bf16[4,128,512]{2,1,0:T(8,128)(2,1)S(1)}, u32[]{:S(2)}, u32[]{:S(2)}) collective-permute-start(bf16[4,128,512]{2,1,0:T(8,128)(2,1)S(1)} %bitcast_dynamic-update-slice_fusion.4), channel_id=1, source_target_pairs={{0,8},{8,0},{16,24},{24,16},{32,40},{40,32},{48,56},{56,48},{64,72... | collective-permute-start | bytes 1572872 | tf_op jit(solution)/shard_map/ppermute | solution.py:57
  22.5 13.2 %copy-start.2 = (bf16[128,512]{1,0:T(8,128)(2,1)}, bf16[128,512]{1,0:T(8,128)(2,1)S(1)}, u32[]{:S(2)}) copy-start(bf16[128,512]{1,0:T(8,128)(2,1)S(1)} %bitcast_select_fusion.2) | copy-start | bytes 393220
  22.5 8.0 %collective-permute-start.6 = (bf16[128,512]{1,0:T(8,128)(2,1)S(1)}, bf16[128,512]{1,0:T(8,128)(2,1)S(1)}, u32[]{:S(2)}, u32[]{:S(2)}) collective-permute-start(bf16[128,512]{1,0:T(8,128)(2,1)S(1)} %bitcast_select_fusion.2), channel_id=1, source_target_pairs={{0,192},{8,200},{16,208},{24,216},{32,224},{40,232},{48,240},{56,2... | collective-permute-start | bytes 393224 | tf_op jit(solution)/shard_map/ppermute | solution.py:51
  24.9 6.3 %collective-permute-start.5 = (bf16[128,512]{1,0:T(8,128)(2,1)S(1)}, bf16[128,512]{1,0:T(8,128)(2,1)S(1)}, u32[]{:S(2)}, u32[]{:S(2)}) collective-permute-start(bf16[128,512]{1,0:T(8,128)(2,1)S(1)} %bitcast_select_fusion.2), channel_id=1, source_target_pairs={{0,128},{8,136},{16,144},{24,152},{32,160},{40,168},{48,176},{56,1... | collective-permute-start | bytes 393224 | tf_op jit(solution)/shard_map/ppermute | solution.py:51
  25.2 9.4 %collective-permute-start.4 = (bf16[128,512]{1,0:T(8,128)(2,1)S(1)}, bf16[128,512]{1,0:T(8,128)(2,1)S(1)}, u32[]{:S(2)}, u32[]{:S(2)}) collective-permute-start(bf16[128,512]{1,0:T(8,128)(2,1)S(1)} %bitcast_select_fusion.2), channel_id=1, source_target_pairs={{0,64},{8,72},{16,80},{24,88},{32,96},{40,104},{48,112},{56,120},{... | collective-permute-start | bytes 393224 | tf_op jit(solution)/shard_map/ppermute | solution.py:51
  26.0 17.3 %copy-start.4 = (pred[16,8,4,128]{3,1,2,0:T(8,128)(4,1)}, pred[16,8,4,128]{3,1,2,0:T(8,128)(4,1)S(1)}, u32[]{:S(2)}) copy-start(pred[16,8,4,128]{3,1,2,0:T(8,128)(4,1)S(1)} %copy.88) | copy-start | bytes 196612
  30.4 5.2 %copy-start.6 = (bf16[128,512]{1,0:T(8,128)(2,1)}, bf16[128,512]{1,0:T(8,128)(2,1)S(1)}, u32[]{:S(2)}) copy-start(bf16[128,512]{1,0:T(8,128)(2,1)S(1)} %collective-permute-done.6) | copy-start | bytes 393220
  31.2 4.5 %copy-start.7 = (bf16[128,512]{1,0:T(8,128)(2,1)}, bf16[128,512]{1,0:T(8,128)(2,1)S(1)}, u32[]{:S(2)}) copy-start(bf16[128,512]{1,0:T(8,128)(2,1)S(1)} %collective-permute-done.5) | copy-start | bytes 393220
  34.6 1.1 copy-start.8
  34.8 9.0 %copy-start.10 = (bf16[32,512]{1,0:T(8,128)(2,1)}, bf16[32,512]{1,0:T(8,128)(2,1)S(1)}, u32[]{:S(2)}) copy-start(bf16[32,512]{1,0:T(8,128)(2,1)S(1)} %multiply_convert_fusion.14) | copy-start | bytes 98308
  37.8 0.9 copy-start.16
  37.8 5.5 %copy-start.15 = (bf16[128,4,128]{2,1,0:T(4,128)(2,1)S(1)}, bf16[128,4,128]{2,1,0:T(4,128)(2,1)}, u32[]{:S(2)}) copy-start(bf16[128,4,128]{2,1,0:T(4,128)(2,1)} %param.8) | copy-start | bytes 393220
  38.7 5.9 %collective-permute-start.10 = (bf16[128,512]{1,0:T(8,128)(2,1)S(1)}, bf16[128,512]{1,0:T(8,128)(2,1)S(1)}, u32[]{:S(2)}, u32[]{:S(2)}) collective-permute-start(bf16[128,512]{1,0:T(8,128)(2,1)S(1)} %get-tuple-element.28), channel_id=1, source_target_pairs={{0,16},{8,24},{16,32},{24,40},{32,48},{40,56},{48,0},{56,8},{64,80... | collective-permute-start | bytes 393224 | tf_op jit(solution)/shard_map/ppermute | solution.py:54
  39.8 8.0 %collective-permute-start.11 = (bf16[128,512]{1,0:T(8,128)(2,1)S(1)}, bf16[128,512]{1,0:T(8,128)(2,1)S(1)}, u32[]{:S(2)}, u32[]{:S(2)}) collective-permute-start(bf16[128,512]{1,0:T(8,128)(2,1)S(1)} %get-tuple-element.28), channel_id=1, source_target_pairs={{0,32},{8,40},{16,48},{24,56},{32,0},{40,8},{48,16},{56,24},{64,96... | collective-permute-start | bytes 393224 | tf_op jit(solution)/shard_map/ppermute | solution.py:54
  41.9 5.9 %collective-permute-start.12 = (bf16[128,512]{1,0:T(8,128)(2,1)S(1)}, bf16[128,512]{1,0:T(8,128)(2,1)S(1)}, u32[]{:S(2)}, u32[]{:S(2)}) collective-permute-start(bf16[128,512]{1,0:T(8,128)(2,1)S(1)} %get-tuple-element.28), channel_id=1, source_target_pairs={{0,48},{8,56},{16,0},{24,8},{32,16},{40,24},{48,32},{56,40},{64,11... | collective-permute-start | bytes 393224 | tf_op jit(solution)/shard_map/ppermute | solution.py:54
  43.3 6.3 %collective-permute-start.9 = (bf16[144,512]{1,0:T(8,128)(2,1)S(1)}, bf16[144,512]{1,0:T(8,128)(2,1)S(1)}, u32[]{:S(2)}, u32[]{:S(2)}) collective-permute-start(bf16[144,512]{1,0:T(8,128)(2,1)S(1)} %fusion.43), channel_id=1, source_target_pairs={{0,192},{8,200},{16,208},{24,216},{32,224},{40,232},{48,240},{56,2... | collective-permute-start | bytes 442376 | tf_op jit(solution)/shard_map/ppermute | solution.py:51
  43.4 6.2 %collective-permute-start.8 = (bf16[144,512]{1,0:T(8,128)(2,1)S(1)}, bf16[144,512]{1,0:T(8,128)(2,1)S(1)}, u32[]{:S(2)}, u32[]{:S(2)}) collective-permute-start(bf16[144,512]{1,0:T(8,128)(2,1)S(1)} %fusion.43), channel_id=1, source_target_pairs={{0,128},{8,136},{16,144},{24,152},{32,160},{40,168},{48,176},{56,1... | collective-permute-start | bytes 442376 | tf_op jit(solution)/shard_map/ppermute | solution.py:51
  44.0 13.8 %copy-start = (f32[32,1024]{1,0:T(8,128)}, f32[32,1024]{1,0:T(8,128)S(1)}, u32[]{:S(2)}) copy-start(f32[32,1024]{1,0:T(8,128)S(1)} %get-tuple-element.76) | copy-start | bytes 393220
  44.6 7.8 %collective-permute-start.7 = (bf16[144,512]{1,0:T(8,128)(2,1)S(1)}, bf16[144,512]{1,0:T(8,128)(2,1)S(1)}, u32[]{:S(2)}, u32[]{:S(2)}) collective-permute-start(bf16[144,512]{1,0:T(8,128)(2,1)S(1)} %fusion.43), channel_id=1, source_target_pairs={{0,64},{8,72},{16,80},{24,88},{32,96},{40,104},{48,112},{56,120},{... | collective-permute-start | bytes 442376 | tf_op jit(solution)/shard_map/ppermute | solution.py:51
  47.9 5.2 %collective-permute-start.13 = (bf16[4,128,512]{2,1,0:T(8,128)(2,1)S(1)}, bf16[4,128,512]{2,1,0:T(8,128)(2,1)S(1)}, u32[]{:S(2)}, u32[]{:S(2)}) collective-permute-start(bf16[4,128,512]{2,1,0:T(8,128)(2,1)S(1)} %bitcast_dynamic-update-slice_fusion), channel_id=1, source_target_pairs={{0,8},{8,0},{16,24},{24,16},{32,40},{40,32},{48,56},{56,48},{64,72... | collective-permute-start | bytes 1572872 | tf_op jit(solution)/shard_map/ppermute | solution.py:57
  75.0 37.4 %all-to-all-start = ((bf16[8,128,512]{2,1,0:T(8,128)(2,1)}), bf16[8,128,512]{2,1,0:T(8,128)(2,1)S(1)}, u32[]{:S(2)}, u32[]{:S(2)}) async-start(bf16[8,128,512]{2,1,0:T(8,128)(2,1)} %bitcast.216), calls=%async_computation.1 | async-start | bytes 2097152 | tf_op jit(solution)/shard_map/all_to_all | solution.py:105
  83.2 60.0 %all-gather.6.cloned.1.call-start = ((), (), s32[]{:S(2)}) async-start(), calls=%async_computation.3 | async-start | bytes 1179648 | tf_op jit(solution)/shard_map/all_gather | solution.py:167
  83.2 4.3 %copy-start.1 = (f32[32,1024]{1,0:T(8,128)S(1)}, f32[32,1024]{1,0:T(8,128)}, u32[]{:S(2)}) copy-start(f32[32,1024]{1,0:T(8,128)} %copy-done) | copy-start | bytes 393220
  83.3 4.3 %copy-start.19 = (f32[1,1024]{1,0:T(1,128)S(1)}, f32[1,1024]{1,0:T(1,128)}, u32[]{:S(2)}) copy-start(f32[1,1024]{1,0:T(1,128)} %get-tuple-element.49) | copy-start | bytes 12292
  83.3 4.4 %copy-start.18 = (f32[1,1024]{1,0:T(1,128)S(1)}, f32[1,1024]{1,0:T(1,128)}, u32[]{:S(2)}) copy-start(f32[1,1024]{1,0:T(1,128)} %get-tuple-element.50) | copy-start | bytes 12292
  83.3 4.6 %copy-start.17 = (f32[1,1024]{1,0:T(1,128)S(1)}, f32[1,1024]{1,0:T(1,128)}, u32[]{:S(2)}) copy-start(f32[1,1024]{1,0:T(1,128)} %get-tuple-element.51) | copy-start | bytes 12292
  83.3 4.8 %copy-start.9 = (f32[32,1024]{1,0:T(8,128)S(1)}, f32[32,1024]{1,0:T(8,128)}, u32[]{:S(2)}) copy-start(f32[32,1024]{1,0:T(8,128)} %get-tuple-element.71) | copy-start | bytes 393220
  83.3 4.8 %copy-start.20 = (f32[1,1024]{1,0:T(1,128)S(1)}, f32[1,1024]{1,0:T(1,128)}, u32[]{:S(2)}) copy-start(f32[1,1024]{1,0:T(1,128)} %get-tuple-element.58) | copy-start | bytes 12292
  84.3 5.4 %copy-start.11 = (bf16[32,512]{1,0:T(8,128)(2,1)S(1)}, bf16[32,512]{1,0:T(8,128)(2,1)}, u32[]{:S(2)}) copy-start(bf16[32,512]{1,0:T(8,128)(2,1)} %copy-done.10) | copy-start | bytes 98308
  90.8 21.8 %copy-start.21 = (pred[512]{0:T(512)(128)(4,1)S(1)}, pred[512]{0:T(512)(128)(4,1)}, u32[]{:S(2)}) copy-start(pred[512]{0:T(512)(128)(4,1)} %maximum_compare_fusion) | copy-start | bytes 1540
  92.4 90.3 %copy-start.3 = (bf16[128,512]{1,0:T(8,128)(2,1)S(1)}, bf16[128,512]{1,0:T(8,128)(2,1)}, u32[]{:S(2)}) copy-start(bf16[128,512]{1,0:T(8,128)(2,1)} %copy-done.2) | copy-start | bytes 393220
  116.7 66.1 %all-gather.8.cloned.1.call-start = ((), (), s32[]{:S(2)}) async-start(), calls=%async_computation.4 | async-start | bytes 1179648 | tf_op jit(solution)/shard_map/all_gather | solution.py:166
  187.1 7.5 %copy-start.13 = (f32[32,512]{1,0:T(8,128)S(1)}, f32[32,512]{1,0:T(8,128)}, u32[]{:S(2)}) copy-start(f32[32,512]{1,0:T(8,128)} %maximum_multiply_fusion) | copy-start | bytes 196612
  188.7 6.1 %copy-start.22 = (bf16[1024,512]{1,0:T(8,128)(2,1)S(1)}, bf16[1024,512]{1,0:T(8,128)(2,1)}, u32[]{:S(2)}) copy-start(bf16[1024,512]{1,0:T(8,128)(2,1)} %all-gather.8.cloned.1.call-done) | copy-start | bytes 3145732
  188.7 6.1 %copy-start.23 = (bf16[1024,512]{1,0:T(8,128)(2,1)S(1)}, bf16[1024,512]{1,0:T(8,128)(2,1)}, u32[]{:S(2)}) copy-start(bf16[1024,512]{1,0:T(8,128)(2,1)} %all-gather.6.cloned.1.call-done) | copy-start | bytes 3145732
  188.8 13.5 %collective-permute-start.14 = (bf16[4,128,512]{2,1,0:T(8,128)(2,1)S(1)}, bf16[4,128,512]{2,1,0:T(8,128)(2,1)S(1)}, u32[]{:S(2)}, u32[]{:S(2)}) collective-permute-start(bf16[4,128,512]{2,1,0:T(8,128)(2,1)S(1)} %select_bitcast_fusion), channel_id=1, source_target_pairs={{0,8},{8,0},{16,24},{24,16},{32,40},{40,32},{48,56},{56,48},{64,72... | collective-permute-start | bytes 1572872 | tf_op jit(solution)/shard_map/ppermute | solution.py:57
  194.8 5.5 %copy-start.12 = (f32[32,512]{1,0:T(8,128)S(1)}, f32[32,512]{1,0:T(8,128)}, u32[]{:S(2)}) copy-start(f32[32,512]{1,0:T(8,128)} %maximum_multiply_fusion.1) | copy-start | bytes 196612
  196.0 7.5 %collective-permute-start.18 = (bf16[128,512]{1,0:T(8,128)(2,1)S(1)}, bf16[128,512]{1,0:T(8,128)(2,1)S(1)}, u32[]{:S(2)}, u32[]{:S(2)}) collective-permute-start(bf16[128,512]{1,0:T(8,128)(2,1)S(1)} %get-tuple-element.38), channel_id=1, source_target_pairs={{0,192},{8,200},{16,208},{24,216},{32,224},{40,232},{48,240},{56,2... | collective-permute-start | bytes 393224 | tf_op jit(solution)/shard_map/ppermute | solution.py:51
  198.5 7.2 %collective-permute-start.20 = (bf16[128,512]{1,0:T(8,128)(2,1)S(1)}, bf16[128,512]{1,0:T(8,128)(2,1)S(1)}, u32[]{:S(2)}, u32[]{:S(2)}) collective-permute-start(bf16[128,512]{1,0:T(8,128)(2,1)S(1)} %get-tuple-element.39), channel_id=1, source_target_pairs={{0,64},{8,72},{16,80},{24,88},{32,96},{40,104},{48,112},{56,120},{... | collective-permute-start | bytes 393224 | tf_op jit(solution)/shard_map/ppermute | solution.py:51
  198.5 9.6 %collective-permute-start.19 = (bf16[128,512]{1,0:T(8,128)(2,1)S(1)}, bf16[128,512]{1,0:T(8,128)(2,1)S(1)}, u32[]{:S(2)}, u32[]{:S(2)}) collective-permute-start(bf16[128,512]{1,0:T(8,128)(2,1)S(1)} %get-tuple-element.40), channel_id=1, source_target_pairs={{0,128},{8,136},{16,144},{24,152},{32,160},{40,168},{48,176},{56,1... | collective-permute-start | bytes 393224 | tf_op jit(solution)/shard_map/ppermute | solution.py:51
  201.2 13.3 %copy-start.5 = (pred[16,8,4,128]{3,1,2,0:T(8,128)(4,1)S(1)}, pred[16,8,4,128]{3,1,2,0:T(8,128)(4,1)}, u32[]{:S(2)}) copy-start(pred[16,8,4,128]{3,1,2,0:T(8,128)(4,1)} %copy-done.4) | copy-start | bytes 196612
  201.3 6.8 %collective-permute-start.21 = (bf16[128,512]{1,0:T(8,128)(2,1)S(1)}, bf16[128,512]{1,0:T(8,128)(2,1)S(1)}, u32[]{:S(2)}, u32[]{:S(2)}) collective-permute-start(bf16[128,512]{1,0:T(8,128)(2,1)S(1)} %get-tuple-element.35), channel_id=1, source_target_pairs={{0,192},{8,200},{16,208},{24,216},{32,224},{40,232},{48,240},{56,2... | collective-permute-start | bytes 393224 | tf_op jit(solution)/shard_map/ppermute | solution.py:51
  202.3 10.6 %collective-permute-start.23 = (bf16[128,512]{1,0:T(8,128)(2,1)S(1)}, bf16[128,512]{1,0:T(8,128)(2,1)S(1)}, u32[]{:S(2)}, u32[]{:S(2)}) collective-permute-start(bf16[128,512]{1,0:T(8,128)(2,1)S(1)} %get-tuple-element.36), channel_id=1, source_target_pairs={{0,64},{8,72},{16,80},{24,88},{32,96},{40,104},{48,112},{56,120},{... | collective-permute-start | bytes 393224 | tf_op jit(solution)/shard_map/ppermute | solution.py:51
  203.4 9.5 %collective-permute-start.22 = (bf16[128,512]{1,0:T(8,128)(2,1)S(1)}, bf16[128,512]{1,0:T(8,128)(2,1)S(1)}, u32[]{:S(2)}, u32[]{:S(2)}) collective-permute-start(bf16[128,512]{1,0:T(8,128)(2,1)S(1)} %get-tuple-element.37), channel_id=1, source_target_pairs={{0,128},{8,136},{16,144},{24,152},{32,160},{40,168},{48,176},{56,1... | collective-permute-start | bytes 393224 | tf_op jit(solution)/shard_map/ppermute | solution.py:51
  205.7 7.2 %collective-permute-start.15 = (bf16[128,512]{1,0:T(8,128)(2,1)S(1)}, bf16[128,512]{1,0:T(8,128)(2,1)S(1)}, u32[]{:S(2)}, u32[]{:S(2)}) collective-permute-start(bf16[128,512]{1,0:T(8,128)(2,1)S(1)} %get-tuple-element.41), channel_id=1, source_target_pairs={{0,48},{8,56},{16,0},{24,8},{32,16},{40,24},{48,32},{56,40},{64,11... | collective-permute-start | bytes 393224 | tf_op jit(solution)/shard_map/ppermute | solution.py:54
  208.1 6.4 %collective-permute-start.17 = (bf16[128,512]{1,0:T(8,128)(2,1)S(1)}, bf16[128,512]{1,0:T(8,128)(2,1)S(1)}, u32[]{:S(2)}, u32[]{:S(2)}) collective-permute-start(bf16[128,512]{1,0:T(8,128)(2,1)S(1)} %get-tuple-element.42), channel_id=1, source_target_pairs={{0,16},{8,24},{16,32},{24,40},{32,48},{40,56},{48,0},{56,8},{64,80... | collective-permute-start | bytes 393224 | tf_op jit(solution)/shard_map/ppermute | solution.py:54
  208.1 6.4 %collective-permute-start.16 = (bf16[128,512]{1,0:T(8,128)(2,1)S(1)}, bf16[128,512]{1,0:T(8,128)(2,1)S(1)}, u32[]{:S(2)}, u32[]{:S(2)}) collective-permute-start(bf16[128,512]{1,0:T(8,128)(2,1)S(1)} %get-tuple-element.43), channel_id=1, source_target_pairs={{0,32},{8,40},{16,48},{24,56},{32,0},{40,8},{48,16},{56,24},{64,96... | collective-permute-start | bytes 393224 | tf_op jit(solution)/shard_map/ppermute | solution.py:54
Sparse Core Ops, SparseCore 0:
  37.9 37.5 reduce-scatter.1
  116.8 26.4 all-gather.5
  145.6 37.0 all-gather.7

commit v3 on v2

--- a/solution.py
+++ b/solution.py
@@ -56,6 +56,13 @@
     def swap_core(table):
         return lax.ppermute(table, "row", [(at(y, x, c), at(y, x, 1 - c)) for y, x, c in cells])
 
+    def share(table, axis, groups=None):
+        count = lax.axis_size(axis) if groups is None else len(groups[0])
+        copies = jnp.broadcast_to(table[None], (count,) + table.shape)
+        return lax.all_to_all(
+            copies, axis, split_axis=0, concat_axis=0, tiled=True, axis_index_groups=groups
+        )
+
     def by_core(own, other):
         first = jnp.where(own_core == 0, own, other)
         second = jnp.where(own_core == 0, other, own)
@@ -86,7 +93,7 @@
     logit_scale = 1.0 / math.sqrt(total_cols * feature)
     inv_root = 1.0 / math.sqrt(feature)
 
-    q_flat, k_flat = masked(queries), masked(keys)
+    q_flat, k_flat = lax.optimization_barrier((masked(queries), masked(keys)))
     k_blk = jnp.concatenate(key_block(k_flat), axis=0)
     q_blk = query_block(q_flat)
     logit_piece = dot_f32(q_blk, k_blk, ROW_PAIR)
@@ -104,6 +111,7 @@
     dprob_piece = dot_f32(g_blk, v_blk, ROW_PAIR).astype(jnp.bfloat16)
     dprob_parts = lax.all_to_all(dprob_piece, "col", split_axis=0, concat_axis=0, tiled=True)
 
+    k_tok, _ = lax.optimization_barrier((k_blk, dprob_piece))
     tokens = block_keys // group_rows
 
     def pooled(blk):
@@ -112,7 +120,7 @@
         )
         return (summed / group_rows).astype(jnp.bfloat16)
 
-    sum_k, sum_v = pooled(k_blk), pooled(v_blk)
+    sum_k, sum_v = pooled(k_tok), pooled(v_blk)
     cross_exp, cross_dp, cross_stats = [], [], []
     for c in range(cols_dev):
         lanes = slice(c * feature, (c + 1) * feature)
@@ -126,8 +134,49 @@
             jnp.stack([peak, jnp.sum(lifted, axis=0), jnp.sum(lifted * dp, axis=0)])
         )
     own_stats = jnp.stack(cross_stats, axis=1)
-    all_stats = lax.all_gather(own_stats, "row", axis=0, tiled=False, axis_index_groups=near)
-    c_peak, c_total, c_delta = merge_stats(all_stats)
+    logit_sum, own_stats, cross_exp, cross_dp = lax.optimization_barrier(
+        (logit_sum, own_stats, cross_exp, cross_dp)
+    )
+
+    def spread(wide):
+        return jnp.broadcast_to(wide[:, None, :], (tokens, group_rows, flat_width)).reshape(
+            block_keys, flat_width
+        )
+
+    dprob_sum = jnp.sum(
+        dprob_parts.reshape(-1, block_rows // lax.axis_size("col"), block_keys),
+        axis=0,
+        dtype=jnp.float32,
+    )
+    logits = jnp.where(key_flags[None, :] > 0, logit_sum * logit_scale, -1e30)
+    peak = jnp.max(logits, axis=1)
+    lifted = jnp.exp(logits - peak[:, None])
+    total = jnp.sum(lifted, axis=1)
+    weighted = jnp.sum(lifted * dprob_sum, axis=1)
+    delta = weighted / total
+    lift_bf = lifted.astype(jnp.bfloat16)
+    tilt_bf = (lifted * (dprob_sum - delta[:, None])).astype(jnp.bfloat16)
+    both = jnp.concatenate([lift_bf, tilt_bf], axis=1)
+    peak, total, weighted, both_sent = lax.optimization_barrier((peak, total, weighted, both))
+    both = lax.all_gather(both_sent, "col", axis=0, tiled=True)
+    row_stats = jnp.stack([peak, total, weighted]).reshape(1, 3 * rows_dev)
+    packed = jnp.concatenate(
+        [
+            own_stats.reshape(3 * cols_dev, block_rows),
+            jnp.pad(row_stats, ((0, 0), (0, block_rows - 3 * rows_dev))),
+        ],
+        axis=0,
+    )
+    packed = share(packed, "row", near)
+    m_peak, m_total, m_delta = merge_stats(
+        packed[:, -1, : 3 * rows_dev].reshape(near_size, 3, rows_dev)
+    )
+    scaling = jnp.stack([jnp.exp(peak - m_peak) / m_total, m_delta - delta])
+    scaling = share(scaling, "col")
+    scaling = jnp.swapaxes(scaling, 0, 1).reshape(2, block_rows)
+    c_peak, c_total, c_delta = merge_stats(
+        packed[:, :-1].reshape(near_size, 3, cols_dev, block_rows)
+    )
     dq_cross, dk_sum, dv_sum = [], [], []
     for c in range(cols_dev):
         lanes = slice(c * feature, (c + 1) * feature)
@@ -141,41 +190,11 @@
     dq_cross = jnp.concatenate(dq_cross, axis=1)
     dk_sum = jnp.concatenate(dk_sum, axis=1) / group_rows
     dv_sum = jnp.concatenate(dv_sum, axis=1) / group_rows
-    logit_sum, dq_cross, dk_sum, dv_sum = lax.optimization_barrier(
-        (logit_sum, dq_cross, dk_sum, dv_sum)
-    )
-
-    def spread(wide):
-        return jnp.broadcast_to(wide[:, None, :], (tokens, group_rows, flat_width)).reshape(
-            block_keys, flat_width
-        )
-
-    dprob_sum = jnp.sum(
-        dprob_parts.reshape(-1, block_rows // lax.axis_size("col"), block_keys),
-        axis=0,
-        dtype=jnp.float32,
-    )
-    logits = jnp.where(key_flags[None, :] > 0, logit_sum * logit_scale, -1e30)
-    peak = jnp.max(logits, axis=1)
-    lifted = jnp.exp(logits - peak[:, None])
-    total = jnp.sum(lifted, axis=1)
-    weighted = jnp.sum(lifted * dprob_sum, axis=1)
-    delta = weighted / total
-    lift_bf = lifted.astype(jnp.bfloat16)
-    tilt_bf = (lifted * (dprob_sum - delta[:, None])).astype(jnp.bfloat16)
-    lift_blk = lax.all_gather(lift_bf, "col", axis=0, tiled=True).astype(jnp.float32)
-    tilt_blk = lax.all_gather(tilt_bf, "col", axis=0, tiled=True).astype(jnp.float32)
-    m_peak, m_total, m_delta = merge_stats(
-        lax.all_gather(
-            jnp.stack([peak, total, weighted]),
-            "row",
-            axis=0,
-            tiled=False,
-            axis_index_groups=near,
-        )
-    )
-    scaling = jnp.stack([jnp.exp(peak - m_peak) / m_total, m_delta - delta])
-    scaling = lax.all_gather(scaling, "col", axis=1, tiled=True)
+    both, scaling, dq_cross, dk_sum, dv_sum = lax.optimization_barrier(
+        (both, scaling, dq_cross, dk_sum, dv_sum)
+    )
+    lift_blk = both[:, :block_keys].astype(jnp.float32)
+    tilt_blk = both[:, block_keys:].astype(jnp.float32)
     weight, offset = scaling[0][:, None], scaling[1][:, None]
     prob_blk = (lift_blk * weight).astype(jnp.bfloat16)
     dlogit_blk = (logit_scale * weight * (tilt_blk - lift_blk * offset)).astype(jnp.bfloat16)

time: 227 us -> 192 us (0.85)
  blocking collectives: 37 us -> 0 us
  starting transfers between devices: 44.5 us -> 60.7 us
  waiting for transfers between devices: 88.3 us -> 72.2 us
  matrix products: 17.5 us -> 20.8 us
    all_gather x3 -> x0, blocking collectives: 37 us -> none  [the longest x1 14.8 us: shards(): lax.all_gather(own_stats, 'row', axis=0, tiled=False, axis_index_groups=n...]
    all_gather x2 -> x1, waiting for transfers between devices: 43 us -> 12.6 us  [shards(): both = lax.all_gather(both_sent, 'col', axis=0, tiled=True)]
    all_to_all x1, waiting for transfers between devices: 20 us -> 36 us  [shards(): lax.all_to_all(dprob_piece, 'col', split_axis=0, concat_axis=0, tiled=True)]
    all_to_all x0 -> x2, starting transfers between devices: none -> 11.7 us  [share(): lax.all_to_all(copies, axis, split_axis=0, concat_axis=0, tiled=True, axi...]
    ppermute x12, waiting for transfers between devices: 15.1 us -> 3.8 us  [shift_y(): lax.ppermute(table, 'row', [(at(y, x, c), at(y + step, x, c)) for y, x, c...]
    all_to_all x0 -> x2, waiting for transfers between devices: none -> 8.73 us  [share(): lax.all_to_all(copies, axis, split_axis=0, concat_axis=0, tiled=True, axi...]
    dot_general x25, matrix products: 17.5 us -> 20.8 us  [dot_f32(): lax.dot_general(left, right, dims, preferred_element_type=jnp.float32)]
    ppermute x12, starting transfers between devices: 12.3 us -> 15.3 us  [shift_y(): lax.ppermute(table, 'row', [(at(y, x, c), at(y + step, x, c)) for y, x, c...]
  transfers between devices with their start and end apart: 28 -> 29, of which waited for: 13 -> 13; matrix products, arithmetic and copies ran while one was open for 9% -> 12% of each run, Pallas kernels for 0% -> 0%
where the time goes in v3:
time: 192 us; the launch traced here: 190 us
  waiting for transfers between devices  72.2 us (38%)
  starting transfers between devices  60.7 us (32%)
  matrix products  20.8 us (11%)
  between operations  15 us (8%)
  other arithmetic  14.4 us (8%)
  local copies, waits for them, and re-layouts  7.06 us (4%)
    all_to_all x1, waiting for transfers between devices, shards(): lax.all_to_all(dprob_piece, 'col', split_axis=0, concat_axis=0, tiled=True)  36 us
    dot_general x25, matrix products, dot_f32(): lax.dot_general(left, right, dims, preferred_element_type=jnp.float32)  20.8 us
    ppermute x12, starting transfers between devices, shift_y(): lax.ppermute(table, 'row', [(at(y, x, c), at(y + step, x, c)) for y, x, c...  15.3 us
    ppermute x9, starting transfers between devices, shift_x(): lax.ppermute(table, 'row', [(at(y, x, c), at(y, x + step, c)) for y, x, c...  14.8 us
    all_gather x1, waiting for transfers between devices, shards(): both = lax.all_gather(both_sent, 'col', axis=0, tiled=True)  12.6 us
    all_to_all x2, starting transfers between devices, share(): lax.all_to_all(copies, axis, split_axis=0, concat_axis=0, tiled=True, axi...  11.7 us
    ppermute x3, starting transfers between devices, swap_core(): lax.ppermute(table, 'row', [(at(y, x, c), at(y, x, 1 - c)) for y, x, c in...  10.7 us
    ppermute x9, waiting for transfers between devices, shift_x(): lax.ppermute(table, 'row', [(at(y, x, c), at(y, x + step, c)) for y, x, c...  9.13 us
  transfers between devices with their start and end apart: 29, of which 13 were waited for; matrix products, arithmetic and copies ran while one was open for 12% of the time, Pallas kernels for 0%

profile of v3, /device:TPU:1, one launch (start us, length us, event | category | flops | bytes accessed | tf_op | source)
XLA Modules:
  0.0 190.2 jit_solution(2181432823429840240)
XLA Ops:
  7.9 0.7 compare_and_fusion
  9.0 1.0 bitcast_select_fusion.2
  10.0 2.1 %collective-permute-start = (bf16[128,512]{1,0:T(8,128)(2,1)S(1)}, bf16[128,512]{1,0:T(8,128)(2,1)S(1)}, u32[]{:S(2)}, u32[]{:S(2)}) collective-permute-start(bf16[128,512]{1,0:T(8,128)(2,1)S(1)} %get-tuple-element.26), channel_id=1, source_target_pairs={{0,16},{8,24},{16,32},{24,40},{32,48},{40,56},{48,0},{56,8},{64,80... | collective-permute-start | bytes 393224 | tf_op jit(solution)/shard_map/ppermute | solution.py:54
  12.1 2.5 %collective-permute-start.1 = (bf16[128,512]{1,0:T(8,128)(2,1)S(1)}, bf16[128,512]{1,0:T(8,128)(2,1)S(1)}, u32[]{:S(2)}, u32[]{:S(2)}) collective-permute-start(bf16[128,512]{1,0:T(8,128)(2,1)S(1)} %get-tuple-element.26), channel_id=1, source_target_pairs={{0,32},{8,40},{16,48},{24,56},{32,0},{40,8},{48,16},{56,24},{64,96... | collective-permute-start | bytes 393224 | tf_op jit(solution)/shard_map/ppermute | solution.py:54
  14.6 1.2 collective-permute-start.2
  15.7 1.3 collective-permute-start.4
  17.0 2.6 %collective-permute-start.5 = (bf16[128,512]{1,0:T(8,128)(2,1)S(1)}, bf16[128,512]{1,0:T(8,128)(2,1)S(1)}, u32[]{:S(2)}, u32[]{:S(2)}) collective-permute-start(bf16[128,512]{1,0:T(8,128)(2,1)S(1)} %get-tuple-element.27), channel_id=1, source_target_pairs={{0,128},{8,136},{16,144},{24,152},{32,160},{40,168},{48,176},{56,1... | collective-permute-start | bytes 393224 | tf_op jit(solution)/shard_map/ppermute | solution.py:51
  19.7 1.1 collective-permute-start.6
  21.0 2.4 %collective-permute-start.3 = (bf16[4,128,512]{2,1,0:T(8,128)(2,1)S(1)}, bf16[4,128,512]{2,1,0:T(8,128)(2,1)S(1)}, u32[]{:S(2)}, u32[]{:S(2)}) collective-permute-start(bf16[4,128,512]{2,1,0:T(8,128)(2,1)S(1)} %bitcast_dynamic-update-slice_fusion.4), channel_id=1, source_target_pairs={{0,8},{8,0},{16,24},{24,16},{32,40},{40,32},{48,56},{56,48},{64,72... | collective-permute-start | bytes 1572872 | tf_op jit(solution)/shard_map/ppermute | solution.py:57
  24.2 1.1 collective-permute-done.6
  26.1 2.1 %fusion.97 = f32[1024,512]{1,0:T(8,128)} fusion(bf16[1024,512]{1,0:T(8,128)(2,1)S(1)} %bitcast.198, bf16[512,512]{1,0:T(8,128)(2,1)S(1)} %constant_dynamic-update-slice_fusion), kind=kOutput, calls=%fused_computation.206 | convolution fusion | flops 536870912 | bytes 3670016 | tf_op jit(solution)/shard_map/dot_general | solution.py:18
  28.8 2.4 %collective-permute-start.9 = (bf16[144,512]{1,0:T(8,128)(2,1)S(1)}, bf16[144,512]{1,0:T(8,128)(2,1)S(1)}, u32[]{:S(2)}, u32[]{:S(2)}) collective-permute-start(bf16[144,512]{1,0:T(8,128)(2,1)S(1)} %fusion.44), channel_id=1, source_target_pairs={{0,192},{8,200},{16,208},{24,216},{32,224},{40,232},{48,240},{56,2... | collective-permute-start | bytes 442376 | tf_op jit(solution)/shard_map/ppermute | solution.py:51
  31.2 0.7 collective-permute-start.7
  31.8 1.2 collective-permute-start.11
  33.4 1.0 collective-permute-start.12
  34.4 2.7 %collective-permute-done.11 = bf16[128,512]{1,0:T(8,128)(2,1)S(1)} collective-permute-done((bf16[128,512]{1,0:T(8,128)(2,1)S(1)}, bf16[128,512]{1,0:T(8,128)(2,1)S(1)}, u32[]{:S(2)}, u32[]{:S(2)}) %collective-permute-start.11) | collective-permute-done | bytes 131104 | tf_op jit(solution)/shard_map/ppermute | solution.py:54
  37.2 1.7 collective-permute-done.12
  38.9 4.0 %collective-permute-start.13 = (bf16[4,128,512]{2,1,0:T(8,128)(2,1)S(1)}, bf16[4,128,512]{2,1,0:T(8,128)(2,1)S(1)}, u32[]{:S(2)}, u32[]{:S(2)}) collective-permute-start(bf16[4,128,512]{2,1,0:T(8,128)(2,1)S(1)} %bitcast_dynamic-update-slice_fusion), channel_id=1, source_target_pairs={{0,8},{8,0},{16,24},{24,16},{32,40},{40,32},{48,56},{56,48},{64,72... | collective-permute-start | bytes 1572872 | tf_op jit(solution)/shard_map/ppermute | solution.py:57
  43.2 1.2 collective-permute-done.13
  44.7 1.7 convolution_convert_fusion
  46.9 0.9 fusion.84
  47.8 8.2 %all-to-all-start = ((bf16[8,128,512]{2,1,0:T(8,128)(2,1)}), bf16[8,128,512]{2,1,0:T(8,128)(2,1)S(1)}, u32[]{:S(2)}, u32[]{:S(2)}) async-start(bf16[8,128,512]{2,1,0:T(8,128)(2,1)} %bitcast.226), calls=%async_computation.1 | async-start | bytes 2097152 | tf_op jit(solution)/shard_map/all_to_all | solution.py:112
  56.2 0.9 fusion.85
  57.3 0.9 fusion.86
  58.4 0.9 fusion.87
  59.3 0.7 pad_maximum_fusion.5
  60.0 36.0 %all-to-all-done = bf16[8,128,512]{2,1,0:T(8,128)(2,1)S(1)} async-done(((bf16[8,128,512]{2,1,0:T(8,128)(2,1)}), bf16[8,128,512]{2,1,0:T(8,128)(2,1)S(1)}, u32[]{:S(2)}, u32[]{:S(2)}) %all-to-all-start) | async-done | bytes 1048608 | tf_op jit(solution)/shard_map/all_to_all | solution.py:112
  96.2 1.1 fusion.15
  97.2 1.2 multiply_reduce_fusion
  98.4 1.1 fusion.80
  99.5 0.7 pad_maximum_fusion.4
  100.3 0.9 broadcast_in_dim.108
  101.2 6.4 %all-to-all-start.1 = ((f32[8,13,1024]{2,1,0:T(8,128)}), f32[8,13,1024]{2,1,0:T(8,128)S(1)}, u32[]{:S(2)}, u32[]{:S(2)}) async-start(f32[8,13,1024]{2,1,0:T(8,128)} %broadcast_in_dim.108), calls=%async_computation.2 | async-start | bytes 1048576 | tf_op jit(solution)/shard_map/all_to_all | solution.py:62
  107.7 0.7 all-gather.2.cloned.1.call-update
  108.4 8.7 %all-to-all-done.1 = f32[8,13,1024]{2,1,0:T(8,128)S(1)} async-done(((f32[8,13,1024]{2,1,0:T(8,128)}), f32[8,13,1024]{2,1,0:T(8,128)S(1)}, u32[]{:S(2)}, u32[]{:S(2)}) %all-to-all-start.1) | async-done | bytes 426016 | tf_op jit(solution)/shard_map/all_to_all | solution.py:62
  117.5 1.5 slice_divide_fusion.3
  119.1 0.7 fusion.79
  120.4 5.2 %all-to-all-start.2 = ((f32[8,2,128]{2,1,0:T(2,128)}), f32[8,2,128]{2,1,0:T(2,128)S(1)}, u32[]{:S(2)}, u32[]{:S(2)}) async-start(f32[8,2,128]{2,1,0:T(2,128)} %broadcast_in_dim.109), calls=%async_computation.3 | async-start | bytes 16384 | tf_op jit(solution)/shard_map/all_to_all | solution.py:62
  125.6 0.8 fusion.37
  126.5 0.8 fusion.30
  127.4 0.8 fusion.23
  128.2 0.8 fusion.16
  129.1 0.7 multiply_convert_fusion.3
  129.9 1.0 fusion.67
  130.8 1.0 fusion.64
  131.8 1.0 multiply_convert_fusion.1
  133.3 1.6 pad_maximum_fusion
  135.6 12.6 %all-gather.2.cloned.1.call-done = bf16[1024,1024]{1,0:T(8,128)(2,1)} async-done(((bf16[128,1024]{1,0:T(8,128)(2,1)}), bf16[1024,1024]{1,0:T(8,128)(2,1)}) %all-gather.2.cloned.1.call-update) | async-done | bytes 2097168 | tf_op jit(solution)/shard_map/all_gather | solution.py:161
  148.3 4.3 %add_convert_fusion = bf16[1024,512]{0,1:T(8,128)(2,1)} fusion(f32[1024,512]{0,1:T(8,128)} %pad_maximum_fusion, bf16[512,512]{1,0:T(8,128)(2,1)S(1)} %copy-done.2, f32[1024]{0:T(1024)S(1)} %bitcast.266, bf16[1024,1024]{1,0:T(8,128)(2,1)} %all-gather.2.cloned.1.call-done, f32[1024]{0:T(1024)S(1)} %broadcast_multiply_fusion), kind=kOutput, calls=%fused_computation.7 | convolution fusion | flops 541065216 | bytes 5775360 | tf_op jit(solution)/shard_map/dot_general | solution.py:18
  152.6 1.5 copy.40
  154.1 4.3 %collective-permute-start.14 = (bf16[4,128,512]{2,1,0:T(8,128)(2,1)S(1)}, bf16[4,128,512]{2,1,0:T(8,128)(2,1)S(1)}, u32[]{:S(2)}, u32[]{:S(2)}) collective-permute-start(bf16[4,128,512]{2,1,0:T(8,128)(2,1)S(1)} %select_bitcast_fusion), channel_id=1, source_target_pairs={{0,8},{8,0},{16,24},{24,16},{32,40},{40,32},{48,56},{56,48},{64,72... | collective-permute-start | bytes 1572872 | tf_op jit(solution)/shard_map/ppermute | solution.py:57
  158.6 1.2 fusion.4
  159.8 2.6 %collective-permute-start.18 = (bf16[128,512]{1,0:T(8,128)(2,1)S(1)}, bf16[128,512]{1,0:T(8,128)(2,1)S(1)}, u32[]{:S(2)}, u32[]{:S(2)}) collective-permute-start(bf16[128,512]{1,0:T(8,128)(2,1)S(1)} %get-tuple-element.76), channel_id=1, source_target_pairs={{0,192},{8,200},{16,208},{24,216},{32,224},{40,232},{48,240},{56,2... | collective-permute-start | bytes 393224 | tf_op jit(solution)/shard_map/ppermute | solution.py:51
  162.3 0.7 collective-permute-start.19
  163.6 0.8 fusion.5
  164.5 2.3 %collective-permute-start.21 = (bf16[128,512]{1,0:T(8,128)(2,1)S(1)}, bf16[128,512]{1,0:T(8,128)(2,1)S(1)}, u32[]{:S(2)}, u32[]{:S(2)}) collective-permute-start(bf16[128,512]{1,0:T(8,128)(2,1)S(1)} %get-tuple-element.73), channel_id=1, source_target_pairs={{0,192},{8,200},{16,208},{24,216},{32,224},{40,232},{48,240},{56,2... | collective-permute-start | bytes 393224 | tf_op jit(solution)/shard_map/ppermute | solution.py:51
  166.8 1.0 collective-permute-start.22
  168.2 2.7 %collective-permute-start.15 = (bf16[128,512]{1,0:T(8,128)(2,1)S(1)}, bf16[128,512]{1,0:T(8,128)(2,1)S(1)}, u32[]{:S(2)}, u32[]{:S(2)}) collective-permute-start(bf16[128,512]{1,0:T(8,128)(2,1)S(1)} %get-tuple-element.79), channel_id=1, source_target_pairs={{0,48},{8,56},{16,0},{24,8},{32,16},{40,24},{48,32},{56,40},{64,11... | collective-permute-start | bytes 393224 | tf_op jit(solution)/shard_map/ppermute | solution.py:54
  171.1 3.5 %collective-permute-start.16 = (bf16[128,512]{1,0:T(8,128)(2,1)S(1)}, bf16[128,512]{1,0:T(8,128)(2,1)S(1)}, u32[]{:S(2)}, u32[]{:S(2)}) collective-permute-start(bf16[128,512]{1,0:T(8,128)(2,1)S(1)} %get-tuple-element.81), channel_id=1, source_target_pairs={{0,32},{8,40},{16,48},{24,56},{32,0},{40,8},{48,16},{56,24},{64,96... | collective-permute-start | bytes 393224 | tf_op jit(solution)/shard_map/ppermute | solution.py:54
  174.8 1.9 collective-permute-done.23
  177.0 4.1 %collective-permute-done.17 = bf16[128,512]{1,0:T(8,128)(2,1)S(1)} collective-permute-done((bf16[128,512]{1,0:T(8,128)(2,1)S(1)}, bf16[128,512]{1,0:T(8,128)(2,1)S(1)}, u32[]{:S(2)}, u32[]{:S(2)}) %collective-permute-start.17) | collective-permute-done | bytes 131104 | tf_op jit(solution)/shard_map/ppermute | solution.py:54
  181.3 0.7 reshape.242
  182.0 0.7 reshape.244
  182.7 0.7 reshape.246
  (157 shorter events, 9.8 us)
Async XLA Ops:
  7.2 16.2 %copy-start.21 = (s32[128]{0:T(128)S(1)}, s32[128]{0:T(128)}, u32[]{:S(2)}) copy-start(s32[128]{0:T(128)} %param.10) | copy-start | bytes 1540
  7.2 89.0 %reduce-scatter.2.cloned.1.call-start = ((), (), s32[]{:S(2)}) async-start(), calls=%async_computation.4 | async-start | bytes 2359296 | tf_op jit(solution)/shard_map/reduce_scatter | solution.py:101
  10.0 9.7 %collective-permute-start = (bf16[128,512]{1,0:T(8,128)(2,1)S(1)}, bf16[128,512]{1,0:T(8,128)(2,1)S(1)}, u32[]{:S(2)}, u32[]{:S(2)}) collective-permute-start(bf16[128,512]{1,0:T(8,128)(2,1)S(1)} %get-tuple-element.26), channel_id=1, source_target_pairs={{0,16},{8,24},{16,32},{24,40},{32,48},{40,56},{48,0},{56,8},{64,80... | collective-permute-start | bytes 393224 | tf_op jit(solution)/shard_map/ppermute | solution.py:54
  12.1 8.8 %collective-permute-start.1 = (bf16[128,512]{1,0:T(8,128)(2,1)S(1)}, bf16[128,512]{1,0:T(8,128)(2,1)S(1)}, u32[]{:S(2)}, u32[]{:S(2)}) collective-permute-start(bf16[128,512]{1,0:T(8,128)(2,1)S(1)} %get-tuple-element.26), channel_id=1, source_target_pairs={{0,32},{8,40},{16,48},{24,56},{32,0},{40,8},{48,16},{56,24},{64,96... | collective-permute-start | bytes 393224 | tf_op jit(solution)/shard_map/ppermute | solution.py:54
  14.6 6.3 %collective-permute-start.2 = (bf16[128,512]{1,0:T(8,128)(2,1)S(1)}, bf16[128,512]{1,0:T(8,128)(2,1)S(1)}, u32[]{:S(2)}, u32[]{:S(2)}) collective-permute-start(bf16[128,512]{1,0:T(8,128)(2,1)S(1)} %get-tuple-element.26), channel_id=1, source_target_pairs={{0,48},{8,56},{16,0},{24,8},{32,16},{40,24},{48,32},{56,40},{64,11... | collective-permute-start | bytes 393224 | tf_op jit(solution)/shard_map/ppermute | solution.py:54
  15.7 7.8 %collective-permute-start.4 = (bf16[128,512]{1,0:T(8,128)(2,1)S(1)}, bf16[128,512]{1,0:T(8,128)(2,1)S(1)}, u32[]{:S(2)}, u32[]{:S(2)}) collective-permute-start(bf16[128,512]{1,0:T(8,128)(2,1)S(1)} %get-tuple-element.27), channel_id=1, source_target_pairs={{0,64},{8,72},{16,80},{24,88},{32,96},{40,104},{48,112},{56,120},{... | collective-permute-start | bytes 393224 | tf_op jit(solution)/shard_map/ppermute | solution.py:51
  17.0 7.1 %collective-permute-start.5 = (bf16[128,512]{1,0:T(8,128)(2,1)S(1)}, bf16[128,512]{1,0:T(8,128)(2,1)S(1)}, u32[]{:S(2)}, u32[]{:S(2)}) collective-permute-start(bf16[128,512]{1,0:T(8,128)(2,1)S(1)} %get-tuple-element.27), channel_id=1, source_target_pairs={{0,128},{8,136},{16,144},{24,152},{32,160},{40,168},{48,176},{56,1... | collective-permute-start | bytes 393224 | tf_op jit(solution)/shard_map/ppermute | solution.py:51
  19.7 5.6 %collective-permute-start.6 = (bf16[128,512]{1,0:T(8,128)(2,1)S(1)}, bf16[128,512]{1,0:T(8,128)(2,1)S(1)}, u32[]{:S(2)}, u32[]{:S(2)}) collective-permute-start(bf16[128,512]{1,0:T(8,128)(2,1)S(1)} %get-tuple-element.27), channel_id=1, source_target_pairs={{0,192},{8,200},{16,208},{24,216},{32,224},{40,232},{48,240},{56,2... | collective-permute-start | bytes 393224 | tf_op jit(solution)/shard_map/ppermute | solution.py:51
  21.0 4.4 %collective-permute-start.3 = (bf16[4,128,512]{2,1,0:T(8,128)(2,1)S(1)}, bf16[4,128,512]{2,1,0:T(8,128)(2,1)S(1)}, u32[]{:S(2)}, u32[]{:S(2)}) collective-permute-start(bf16[4,128,512]{2,1,0:T(8,128)(2,1)S(1)} %bitcast_dynamic-update-slice_fusion.4), channel_id=1, source_target_pairs={{0,8},{8,0},{16,24},{24,16},{32,40},{40,32},{48,56},{56,48},{64,72... | collective-permute-start | bytes 1572872 | tf_op jit(solution)/shard_map/ppermute | solution.py:57
  23.5 5.2 %copy-start.6 = (pred[16,8,4,128]{3,1,2,0:T(8,128)(4,1)}, pred[16,8,4,128]{3,1,2,0:T(8,128)(4,1)S(1)}, u32[]{:S(2)}) copy-start(pred[16,8,4,128]{3,1,2,0:T(8,128)(4,1)S(1)} %copy.70) | copy-start | bytes 196612
  25.3 0.8 copy-start
  26.1 2.1 %copy-start.15 = (bf16[128,4,128]{2,1,0:T(4,128)(2,1)S(1)}, bf16[128,4,128]{2,1,0:T(4,128)(2,1)}, u32[]{:S(2)}) copy-start(bf16[128,4,128]{2,1,0:T(4,128)(2,1)} %param.9) | copy-start | bytes 393220
  26.1 2.6 %copy-start.14 = (bf16[128,4,128]{2,1,0:T(4,128)(2,1)S(1)}, bf16[128,4,128]{2,1,0:T(4,128)(2,1)}, u32[]{:S(2)}) copy-start(bf16[128,4,128]{2,1,0:T(4,128)(2,1)} %param.8) | copy-start | bytes 393220
  28.3 5.1 %collective-permute-start.10 = (bf16[128,512]{1,0:T(8,128)(2,1)S(1)}, bf16[128,512]{1,0:T(8,128)(2,1)S(1)}, u32[]{:S(2)}, u32[]{:S(2)}) collective-permute-start(bf16[128,512]{1,0:T(8,128)(2,1)S(1)} %get-tuple-element.68), channel_id=1, source_target_pairs={{0,16},{8,24},{16,32},{24,40},{32,48},{40,56},{48,0},{56,8},{64,80... | collective-permute-start | bytes 393224 | tf_op jit(solution)/shard_map/ppermute | solution.py:54
  28.8 14.2 %collective-permute-start.9 = (bf16[144,512]{1,0:T(8,128)(2,1)S(1)}, bf16[144,512]{1,0:T(8,128)(2,1)S(1)}, u32[]{:S(2)}, u32[]{:S(2)}) collective-permute-start(bf16[144,512]{1,0:T(8,128)(2,1)S(1)} %fusion.44), channel_id=1, source_target_pairs={{0,192},{8,200},{16,208},{24,216},{32,224},{40,232},{48,240},{56,2... | collective-permute-start | bytes 442376 | tf_op jit(solution)/shard_map/ppermute | solution.py:51
  31.2 11.8 %collective-permute-start.8 = (bf16[144,512]{1,0:T(8,128)(2,1)S(1)}, bf16[144,512]{1,0:T(8,128)(2,1)S(1)}, u32[]{:S(2)}, u32[]{:S(2)}) collective-permute-start(bf16[144,512]{1,0:T(8,128)(2,1)S(1)} %fusion.44), channel_id=1, source_target_pairs={{0,128},{8,136},{16,144},{24,152},{32,160},{40,168},{48,176},{56,1... | collective-permute-start | bytes 442376 | tf_op jit(solution)/shard_map/ppermute | solution.py:51
  31.2 11.7 %collective-permute-start.7 = (bf16[144,512]{1,0:T(8,128)(2,1)S(1)}, bf16[144,512]{1,0:T(8,128)(2,1)S(1)}, u32[]{:S(2)}, u32[]{:S(2)}) collective-permute-start(bf16[144,512]{1,0:T(8,128)(2,1)S(1)} %fusion.44), channel_id=1, source_target_pairs={{0,64},{8,72},{16,80},{24,88},{32,96},{40,104},{48,112},{56,120},{... | collective-permute-start | bytes 442376 | tf_op jit(solution)/shard_map/ppermute | solution.py:51
  31.8 5.3 %collective-permute-start.11 = (bf16[128,512]{1,0:T(8,128)(2,1)S(1)}, bf16[128,512]{1,0:T(8,128)(2,1)S(1)}, u32[]{:S(2)}, u32[]{:S(2)}) collective-permute-start(bf16[128,512]{1,0:T(8,128)(2,1)S(1)} %get-tuple-element.68), channel_id=1, source_target_pairs={{0,32},{8,40},{16,48},{24,56},{32,0},{40,8},{48,16},{56,24},{64,96... | collective-permute-start | bytes 393224 | tf_op jit(solution)/shard_map/ppermute | solution.py:54
  33.4 5.5 %collective-permute-start.12 = (bf16[128,512]{1,0:T(8,128)(2,1)S(1)}, bf16[128,512]{1,0:T(8,128)(2,1)S(1)}, u32[]{:S(2)}, u32[]{:S(2)}) collective-permute-start(bf16[128,512]{1,0:T(8,128)(2,1)S(1)} %get-tuple-element.68), channel_id=1, source_target_pairs={{0,48},{8,56},{16,0},{24,8},{32,16},{40,24},{48,32},{56,40},{64,11... | collective-permute-start | bytes 393224 | tf_op jit(solution)/shard_map/ppermute | solution.py:54
  38.9 5.5 %collective-permute-start.13 = (bf16[4,128,512]{2,1,0:T(8,128)(2,1)S(1)}, bf16[4,128,512]{2,1,0:T(8,128)(2,1)S(1)}, u32[]{:S(2)}, u32[]{:S(2)}) collective-permute-start(bf16[4,128,512]{2,1,0:T(8,128)(2,1)S(1)} %bitcast_dynamic-update-slice_fusion), channel_id=1, source_target_pairs={{0,8},{8,0},{16,24},{24,16},{32,40},{40,32},{48,56},{56,48},{64,72... | collective-permute-start | bytes 1572872 | tf_op jit(solution)/shard_map/ppermute | solution.py:57
  44.7 1.8 copy-start.1
  46.7 11.5 %copy-start.11 = (bf16[32,512]{1,0:T(8,128)(2,1)}, bf16[32,512]{1,0:T(8,128)(2,1)S(1)}, u32[]{:S(2)}) copy-start(bf16[32,512]{1,0:T(8,128)(2,1)S(1)} %multiply_convert_fusion.14) | copy-start | bytes 98308
  47.8 48.2 %all-to-all-start = ((bf16[8,128,512]{2,1,0:T(8,128)(2,1)}), bf16[8,128,512]{2,1,0:T(8,128)(2,1)S(1)}, u32[]{:S(2)}, u32[]{:S(2)}) async-start(bf16[8,128,512]{2,1,0:T(8,128)(2,1)} %bitcast.226), calls=%async_computation.1 | async-start | bytes 2097152 | tf_op jit(solution)/shard_map/all_to_all | solution.py:112
  96.1 4.1 %copy-start.13 = (f32[3,4,1024]{2,1,0:T(4,128)S(1)}, f32[3,4,1024]{2,1,0:T(4,128)}, u32[]{:S(2)}) copy-start(f32[3,4,1024]{2,1,0:T(4,128)} %pad_maximum_fusion.5) | copy-start | bytes 147460
  97.2 3.0 %copy-start.18 = (f32[128]{0:T(128)}, f32[128]{0:T(128)S(1)}, u32[]{:S(2)}) copy-start(f32[128]{0:T(128)S(1)} %fusion.15) | copy-start | bytes 1540
  98.4 1.9 copy-start.19
  100.3 26.2 %copy-start.3 = (f32[32,1024]{1,0:T(8,128)S(1)}, f32[32,1024]{1,0:T(8,128)}, u32[]{:S(2)}) copy-start(f32[32,1024]{1,0:T(8,128)} %get-tuple-element.38) | copy-start | bytes 393220
  100.3 27.0 %copy-start.4 = (f32[32,1024]{1,0:T(8,128)S(1)}, f32[32,1024]{1,0:T(8,128)}, u32[]{:S(2)}) copy-start(f32[32,1024]{1,0:T(8,128)} %get-tuple-element.40) | copy-start | bytes 393220
  101.2 27.0 %copy-start.5 = (f32[32,1024]{1,0:T(8,128)S(1)}, f32[32,1024]{1,0:T(8,128)}, u32[]{:S(2)}) copy-start(f32[32,1024]{1,0:T(8,128)} %get-tuple-element.42) | copy-start | bytes 393220
  101.2 15.9 %all-to-all-start.1 = ((f32[8,13,1024]{2,1,0:T(8,128)}), f32[8,13,1024]{2,1,0:T(8,128)S(1)}, u32[]{:S(2)}, u32[]{:S(2)}) async-start(f32[8,13,1024]{2,1,0:T(8,128)} %broadcast_in_dim.108), calls=%async_computation.2 | async-start | bytes 1048576 | tf_op jit(solution)/shard_map/all_to_all | solution.py:62
  107.6 21.5 %copy-start.8 = (f32[32,1024]{1,0:T(8,128)S(1)}, f32[32,1024]{1,0:T(8,128)}, u32[]{:S(2)}) copy-start(f32[32,1024]{1,0:T(8,128)} %get-tuple-element.37) | copy-start | bytes 393220
  107.6 21.5 %copy-start.9 = (f32[32,1024]{1,0:T(8,128)S(1)}, f32[32,1024]{1,0:T(8,128)}, u32[]{:S(2)}) copy-start(f32[32,1024]{1,0:T(8,128)} %get-tuple-element.39) | copy-start | bytes 393220
  107.6 40.6 %all-gather.2.cloned.1.call-start = ((), (), s32[]{:S(2)}) async-start(), calls=%async_computation.5 | async-start | bytes 2359296 | tf_op jit(solution)/shard_map/all_gather | solution.py:161
  117.4 14.4 %copy-start.10 = (f32[32,1024]{1,0:T(8,128)S(1)}, f32[32,1024]{1,0:T(8,128)}, u32[]{:S(2)}) copy-start(f32[32,1024]{1,0:T(8,128)} %get-tuple-element.41) | copy-start | bytes 393220
  119.1 12.7 %copy-start.16 = (f32[1,1024]{1,0:T(1,128)S(1)}, f32[1,1024]{1,0:T(1,128)}, u32[]{:S(2)}) copy-start(f32[1,1024]{1,0:T(1,128)} %get-tuple-element.85) | copy-start | bytes 12292
  119.1 12.7 %copy-start.17 = (f32[1,1024]{1,0:T(1,128)S(1)}, f32[1,1024]{1,0:T(1,128)}, u32[]{:S(2)}) copy-start(f32[1,1024]{1,0:T(1,128)} %get-tuple-element.86) | copy-start | bytes 12292
  120.4 15.2 %all-to-all-start.2 = ((f32[8,2,128]{2,1,0:T(2,128)}), f32[8,2,128]{2,1,0:T(2,128)S(1)}, u32[]{:S(2)}, u32[]{:S(2)}) async-start(f32[8,2,128]{2,1,0:T(2,128)} %broadcast_in_dim.109), calls=%async_computation.3 | async-start | bytes 16384 | tf_op jit(solution)/shard_map/all_to_all | solution.py:62
  125.6 7.1 %copy-start.12 = (bf16[32,512]{1,0:T(8,128)(2,1)S(1)}, bf16[32,512]{1,0:T(8,128)(2,1)}, u32[]{:S(2)}) copy-start(bf16[32,512]{1,0:T(8,128)(2,1)} %copy-done.11) | copy-start | bytes 98308
  133.3 14.9 %copy-start.2 = (bf16[512,512]{1,0:T(8,128)(2,1)S(1)}, bf16[512,512]{1,0:T(8,128)(2,1)}, u32[]{:S(2)}) copy-start(bf16[512,512]{1,0:T(8,128)(2,1)} %copy-done) | copy-start | bytes 1572868
  154.1 4.5 %copy-start.20 = (bf16[1024,1024]{1,0:T(8,128)(2,1)S(1)}, bf16[1024,1024]{1,0:T(8,128)(2,1)}, u32[]{:S(2)}) copy-start(bf16[1024,1024]{1,0:T(8,128)(2,1)} %all-gather.2.cloned.1.call-done) | copy-start | bytes 6291460
  154.1 12.7 %collective-permute-start.14 = (bf16[4,128,512]{2,1,0:T(8,128)(2,1)S(1)}, bf16[4,128,512]{2,1,0:T(8,128)(2,1)S(1)}, u32[]{:S(2)}, u32[]{:S(2)}) collective-permute-start(bf16[4,128,512]{2,1,0:T(8,128)(2,1)S(1)} %select_bitcast_fusion), channel_id=1, source_target_pairs={{0,8},{8,0},{16,24},{24,16},{32,40},{40,32},{48,56},{56,48},{64,72... | collective-permute-start | bytes 1572872 | tf_op jit(solution)/shard_map/ppermute | solution.py:57
  159.8 8.4 %collective-permute-start.18 = (bf16[128,512]{1,0:T(8,128)(2,1)S(1)}, bf16[128,512]{1,0:T(8,128)(2,1)S(1)}, u32[]{:S(2)}, u32[]{:S(2)}) collective-permute-start(bf16[128,512]{1,0:T(8,128)(2,1)S(1)} %get-tuple-element.76), channel_id=1, source_target_pairs={{0,192},{8,200},{16,208},{24,216},{32,224},{40,232},{48,240},{56,2... | collective-permute-start | bytes 393224 | tf_op jit(solution)/shard_map/ppermute | solution.py:51
  162.3 5.9 %collective-permute-start.19 = (bf16[128,512]{1,0:T(8,128)(2,1)S(1)}, bf16[128,512]{1,0:T(8,128)(2,1)S(1)}, u32[]{:S(2)}, u32[]{:S(2)}) collective-permute-start(bf16[128,512]{1,0:T(8,128)(2,1)S(1)} %get-tuple-element.78), channel_id=1, source_target_pairs={{0,128},{8,136},{16,144},{24,152},{32,160},{40,168},{48,176},{56,1... | collective-permute-start | bytes 393224 | tf_op jit(solution)/shard_map/ppermute | solution.py:51
  163.1 8.0 %collective-permute-start.20 = (bf16[128,512]{1,0:T(8,128)(2,1)S(1)}, bf16[128,512]{1,0:T(8,128)(2,1)S(1)}, u32[]{:S(2)}, u32[]{:S(2)}) collective-permute-start(bf16[128,512]{1,0:T(8,128)(2,1)S(1)} %get-tuple-element.77), channel_id=1, source_target_pairs={{0,64},{8,72},{16,80},{24,88},{32,96},{40,104},{48,112},{56,120},{... | collective-permute-start | bytes 393224 | tf_op jit(solution)/shard_map/ppermute | solution.py:51
  164.5 16.6 %copy-start.7 = (pred[16,8,4,128]{3,1,2,0:T(8,128)(4,1)S(1)}, pred[16,8,4,128]{3,1,2,0:T(8,128)(4,1)}, u32[]{:S(2)}) copy-start(pred[16,8,4,128]{3,1,2,0:T(8,128)(4,1)} %copy-done.6) | copy-start | bytes 196612
  164.5 10.1 %collective-permute-start.21 = (bf16[128,512]{1,0:T(8,128)(2,1)S(1)}, bf16[128,512]{1,0:T(8,128)(2,1)S(1)}, u32[]{:S(2)}, u32[]{:S(2)}) collective-permute-start(bf16[128,512]{1,0:T(8,128)(2,1)S(1)} %get-tuple-element.73), channel_id=1, source_target_pairs={{0,192},{8,200},{16,208},{24,216},{32,224},{40,232},{48,240},{56,2... | collective-permute-start | bytes 393224 | tf_op jit(solution)/shard_map/ppermute | solution.py:51
  166.8 7.9 %collective-permute-start.22 = (bf16[128,512]{1,0:T(8,128)(2,1)S(1)}, bf16[128,512]{1,0:T(8,128)(2,1)S(1)}, u32[]{:S(2)}, u32[]{:S(2)}) collective-permute-start(bf16[128,512]{1,0:T(8,128)(2,1)S(1)} %get-tuple-element.75), channel_id=1, source_target_pairs={{0,128},{8,136},{16,144},{24,152},{32,160},{40,168},{48,176},{56,1... | collective-permute-start | bytes 393224 | tf_op jit(solution)/shard_map/ppermute | solution.py:51
  168.1 8.5 %collective-permute-start.23 = (bf16[128,512]{1,0:T(8,128)(2,1)S(1)}, bf16[128,512]{1,0:T(8,128)(2,1)S(1)}, u32[]{:S(2)}, u32[]{:S(2)}) collective-permute-start(bf16[128,512]{1,0:T(8,128)(2,1)S(1)} %get-tuple-element.74), channel_id=1, source_target_pairs={{0,64},{8,72},{16,80},{24,88},{32,96},{40,104},{48,112},{56,120},{... | collective-permute-start | bytes 393224 | tf_op jit(solution)/shard_map/ppermute | solution.py:51
  168.2 8.4 %collective-permute-start.15 = (bf16[128,512]{1,0:T(8,128)(2,1)S(1)}, bf16[128,512]{1,0:T(8,128)(2,1)S(1)}, u32[]{:S(2)}, u32[]{:S(2)}) collective-permute-start(bf16[128,512]{1,0:T(8,128)(2,1)S(1)} %get-tuple-element.79), channel_id=1, source_target_pairs={{0,48},{8,56},{16,0},{24,8},{32,16},{40,24},{48,32},{56,40},{64,11... | collective-permute-start | bytes 393224 | tf_op jit(solution)/shard_map/ppermute | solution.py:54
  171.1 5.9 %collective-permute-start.16 = (bf16[128,512]{1,0:T(8,128)(2,1)S(1)}, bf16[128,512]{1,0:T(8,128)(2,1)S(1)}, u32[]{:S(2)}, u32[]{:S(2)}) collective-permute-start(bf16[128,512]{1,0:T(8,128)(2,1)S(1)} %get-tuple-element.81), channel_id=1, source_target_pairs={{0,32},{8,40},{16,48},{24,56},{32,0},{40,8},{48,16},{56,24},{64,96... | collective-permute-start | bytes 393224 | tf_op jit(solution)/shard_map/ppermute | solution.py:54
  174.6 6.4 %collective-permute-start.17 = (bf16[128,512]{1,0:T(8,128)(2,1)S(1)}, bf16[128,512]{1,0:T(8,128)(2,1)S(1)}, u32[]{:S(2)}, u32[]{:S(2)}) collective-permute-start(bf16[128,512]{1,0:T(8,128)(2,1)S(1)} %get-tuple-element.80), channel_id=1, source_target_pairs={{0,16},{8,24},{16,32},{24,40},{32,48},{40,56},{48,0},{56,8},{64,80... | collective-permute-start | bytes 393224 | tf_op jit(solution)/shard_map/ppermute | solution.py:54
Sparse Core Ops, SparseCore 0:
  33.2 62.4 reduce-scatter.1
  110.3 37.9 all-gather.1

commit v4 on v3

--- a/solution.py
+++ b/solution.py
@@ -3,6 +3,8 @@
 import jax
 import jax.numpy as jnp
 from jax import lax
+from jax.experimental import pallas as pl
+from jax.experimental.pallas import tpu as pltpu
 from jax.experimental.layout import Layout, with_layout_constraint
 from jax.sharding import PartitionSpec as P
 
@@ -16,6 +18,127 @@
 
 def dot_f32(left, right, dims=PLAIN):
     return lax.dot_general(left, right, dims, preferred_element_type=jnp.float32)
+
+
+def across(column):
+    n = column.shape[0]
+    eye = lax.broadcasted_iota(jnp.int32, (n, n), 0) == lax.broadcasted_iota(jnp.int32, (n, n), 1)
+    return jnp.sum(jnp.where(eye, column, 0.0), axis=0, keepdims=True)
+
+
+def upright(row):
+    n = row.shape[1]
+    eye = lax.broadcasted_iota(jnp.int32, (n, n), 0) == lax.broadcasted_iota(jnp.int32, (n, n), 1)
+    return jnp.sum(jnp.where(eye, row, 0.0), axis=1, keepdims=True)
+
+
+def block_softmax(logit_scale, logit_sum, own, forward, back, key_flags):
+    rows, width = logit_sum.shape
+
+    def kernel(logit_ref, own_ref, forward_ref, back_ref, flag_ref, both_ref, stat_ref):
+        dprob = (
+            own_ref[...].astype(jnp.float32)
+            + forward_ref[...].astype(jnp.float32)
+            + back_ref[...].astype(jnp.float32)
+        )
+        logits = jnp.where(flag_ref[...] > 0, logit_ref[...] * logit_scale, -1e30)
+        peak = jnp.max(logits, axis=1, keepdims=True)
+        lifted = jnp.exp(logits - peak)
+        total = jnp.sum(lifted, axis=1, keepdims=True)
+        weighted = jnp.sum(lifted * dprob, axis=1, keepdims=True)
+        delta = weighted / total
+        both_ref[:, :width] = lifted.astype(jnp.bfloat16)
+        both_ref[:, width:] = (lifted * (dprob - delta)).astype(jnp.bfloat16)
+        for i, column in enumerate((peak, total, weighted, delta)):
+            stat_ref[i : i + 1, :] = across(column)
+        stat_ref[4:8, :] = jnp.zeros((4, rows), jnp.float32)
+
+    return pl.pallas_call(
+        kernel,
+        out_shape=(
+            jax.ShapeDtypeStruct((rows, 2 * width), jnp.bfloat16),
+            jax.ShapeDtypeStruct((8, rows), jnp.float32),
+        ),
+        name="block_softmax",
+    )(logit_sum, own, forward, back, key_flags)
+
+
+def query_grads(logit_scale, core, both, scaling, k_blk, cross_dl, sum_k, rows_dev):
+    block_rows, width = both.shape[0], both.shape[1] // 2
+    flat_width = k_blk.shape[1]
+    chunks = block_rows // rows_dev
+    tokens = sum_k.shape[0]
+    columns = cross_dl.shape[0] // tokens
+    feature = flat_width // columns
+
+    def kernel(core_ref, both_ref, scale_ref, k_ref, dl_ref, sk_ref, p_ref, ds_ref, own_ref, other_ref, dq_ref):
+        for i in range(chunks):
+            rows = slice(i * rows_dev, (i + 1) * rows_dev)
+            weight = upright(scale_ref[i, 0:1, :])
+            offset = upright(scale_ref[i, 1:2, :])
+            lifted = both_ref[rows, :width].astype(jnp.float32)
+            tilted = both_ref[rows, width:].astype(jnp.float32)
+            p_ref[rows, :] = (lifted * weight).astype(jnp.bfloat16)
+            ds_ref[rows, :] = ((tilted - lifted * offset) * (weight * logit_scale)).astype(
+                jnp.bfloat16
+            )
+        dq_ref[...] = dot_f32(ds_ref[...], k_ref[...])
+        for c in range(columns):
+            lanes = slice(c * feature, (c + 1) * feature)
+            dq_ref[:, lanes] += dot_f32(
+                dl_ref[c * tokens : (c + 1) * tokens, :], sk_ref[:, lanes], LEAD_PAIR
+            )
+        core = core_ref[0]
+        for x in range(chunks // 2):
+            rows = slice(x * rows_dev, (x + 1) * rows_dev)
+            mine = pl.multiple_of((2 * x + core) * rows_dev, rows_dev)
+            theirs = pl.multiple_of((2 * x + 1 - core) * rows_dev, rows_dev)
+            own_ref[rows, :] = dq_ref[pl.ds(mine, rows_dev), :]
+            other_ref[rows, :] = dq_ref[pl.ds(theirs, rows_dev), :].astype(jnp.bfloat16)
+
+    vmem = pl.BlockSpec(memory_space=pltpu.VMEM)
+    return pl.pallas_call(
+        kernel,
+        in_specs=[pl.BlockSpec(memory_space=pltpu.SMEM)] + [vmem] * 5,
+        out_shape=(
+            jax.ShapeDtypeStruct((block_rows, width), jnp.bfloat16),
+            jax.ShapeDtypeStruct((block_rows, width), jnp.bfloat16),
+            jax.ShapeDtypeStruct((block_rows // 2, flat_width), jnp.float32),
+            jax.ShapeDtypeStruct((block_rows // 2, flat_width), jnp.bfloat16),
+        ),
+        scratch_shapes=[pltpu.VMEM((block_rows, flat_width), jnp.float32)],
+        compiler_params=pltpu.CompilerParams(vmem_limit_bytes=40 * 1024 * 1024),
+        name="query_grads",
+    )(core, both, scaling, k_blk, cross_dl, sum_k)
+
+
+def key_grads(prob, dlogit, q_blk, g_blk, dk_sum, dv_sum, pieces):
+    width, flat_width = prob.shape[1], q_blk.shape[1]
+    tokens = dk_sum.shape[0]
+    group = width // tokens
+    piece = width // pieces
+
+    def kernel(p_ref, ds_ref, q_ref, g_ref, dk_ref, dv_ref, *out_refs):
+        for half, (w_ref, t_ref, s_ref) in enumerate(
+            ((ds_ref, q_ref, dk_ref), (p_ref, g_ref, dv_ref))
+        ):
+            grads = dot_f32(w_ref[...], t_ref[...], LEAD_PAIR)
+            grads = (
+                grads.reshape(tokens, group, flat_width) + s_ref[...][:, None, :]
+            ).reshape(width, flat_width)
+            for s, out_ref in enumerate(out_refs):
+                out_ref[:, half * flat_width : (half + 1) * flat_width] = grads[
+                    s * piece : (s + 1) * piece
+                ].astype(jnp.bfloat16)
+
+    return pl.pallas_call(
+        kernel,
+        out_shape=tuple(
+            jax.ShapeDtypeStruct((piece, 2 * flat_width), jnp.bfloat16) for _ in range(pieces)
+        ),
+        compiler_params=pltpu.CompilerParams(vmem_limit_bytes=40 * 1024 * 1024),
+        name="key_grads",
+    )(prob, dlogit, q_blk, g_blk, dk_sum, dv_sum)
 
 
 def merge_stats(stats):
@@ -109,7 +232,28 @@
     key_flags = jnp.concatenate([p[rows_dev, :rows_dev] for p in v_pieces])
     g_blk = query_block(g_flat)
     dprob_piece = dot_f32(g_blk, v_blk, ROW_PAIR).astype(jnp.bfloat16)
-    dprob_parts = lax.all_to_all(dprob_piece, "col", split_axis=0, concat_axis=0, tiled=True)
+    zs = lax.axis_size("col")
+    own_z = lax.axis_index("col")
+    dprob_chunks = dprob_piece.reshape(zs, block_rows // zs, block_keys)
+
+    def part(step):
+        return lax.dynamic_index_in_dim(dprob_chunks, (own_z + step) % zs, axis=0, keepdims=False)
+
+    def shift_z(table, step):
+        return lax.ppermute(table, "col", [(z, (z + step) % zs) for z in range(zs)])
+
+    def passed(step, count):
+        moving = part(step * count)
+        for left in range(count - 1, -1, -1):
+            moving = shift_z(moving, step)
+            if left > 0:
+                moving = (
+                    moving.astype(jnp.float32) + part(step * left).astype(jnp.float32)
+                ).astype(jnp.bfloat16)
+        return moving
+
+    dprob_forward = passed(1, zs // 2)
+    dprob_back = passed(-1, zs - 1 - zs // 2)
 
     k_tok, _ = lax.optimization_barrier((k_blk, dprob_piece))
     tokens = block_keys // group_rows
@@ -143,23 +287,12 @@
             block_keys, flat_width
         )
 
-    dprob_sum = jnp.sum(
-        dprob_parts.reshape(-1, block_rows // lax.axis_size("col"), block_keys),
-        axis=0,
-        dtype=jnp.float32,
-    )
-    logits = jnp.where(key_flags[None, :] > 0, logit_sum * logit_scale, -1e30)
-    peak = jnp.max(logits, axis=1)
-    lifted = jnp.exp(logits - peak[:, None])
-    total = jnp.sum(lifted, axis=1)
-    weighted = jnp.sum(lifted * dprob_sum, axis=1)
-    delta = weighted / total
-    lift_bf = lifted.astype(jnp.bfloat16)
-    tilt_bf = (lifted * (dprob_sum - delta[:, None])).astype(jnp.bfloat16)
-    both = jnp.concatenate([lift_bf, tilt_bf], axis=1)
-    peak, total, weighted, both_sent = lax.optimization_barrier((peak, total, weighted, both))
-    both = lax.all_gather(both_sent, "col", axis=0, tiled=True)
-    row_stats = jnp.stack([peak, total, weighted]).reshape(1, 3 * rows_dev)
+    both, stats = block_softmax(
+        logit_scale, logit_sum, part(0), dprob_forward, dprob_back, key_flags[None, :]
+    )
+    peak, total, weighted, delta = stats[0], stats[1], stats[2], stats[3]
+    both = lax.all_gather(both, "col", axis=0, tiled=True)
+    row_stats = stats[:3].reshape(1, 3 * rows_dev)
     packed = jnp.concatenate(
         [
             own_stats.reshape(3 * cols_dev, block_rows),
@@ -173,49 +306,43 @@
     )
     scaling = jnp.stack([jnp.exp(peak - m_peak) / m_total, m_delta - delta])
     scaling = share(scaling, "col")
-    scaling = jnp.swapaxes(scaling, 0, 1).reshape(2, block_rows)
     c_peak, c_total, c_delta = merge_stats(
         packed[:, :-1].reshape(near_size, 3, cols_dev, block_rows)
     )
-    dq_cross, dk_sum, dv_sum = [], [], []
+    cross_dl, dk_sum, dv_sum = [], [], []
     for c in range(cols_dev):
         lanes = slice(c * feature, (c + 1) * feature)
         weight = jnp.exp(own_stats[0, c] - c_peak[c]) / c_total[c]
         probs = cross_exp[c] * weight[None, :]
         prob_bf = probs.astype(jnp.bfloat16)
         dl_bf = (inv_root * probs * (cross_dp[c] - c_delta[c][None, :])).astype(jnp.bfloat16)
-        dq_cross.append(dot_f32(dl_bf, sum_k[:, lanes], LEAD_PAIR))
+        cross_dl.append(dl_bf)
         dk_sum.append(dot_f32(dl_bf, q_blk[:, lanes]))
         dv_sum.append(dot_f32(prob_bf, g_blk[:, lanes]))
-    dq_cross = jnp.concatenate(dq_cross, axis=1)
+    cross_dl = jnp.concatenate(cross_dl, axis=0)
     dk_sum = jnp.concatenate(dk_sum, axis=1) / group_rows
     dv_sum = jnp.concatenate(dv_sum, axis=1) / group_rows
-    both, scaling, dq_cross, dk_sum, dv_sum = lax.optimization_barrier(
-        (both, scaling, dq_cross, dk_sum, dv_sum)
-    )
-    lift_blk = both[:, :block_keys].astype(jnp.float32)
-    tilt_blk = both[:, block_keys:].astype(jnp.float32)
-    weight, offset = scaling[0][:, None], scaling[1][:, None]
-    prob_blk = (lift_blk * weight).astype(jnp.bfloat16)
-    dlogit_blk = (logit_scale * weight * (tilt_blk - lift_blk * offset)).astype(jnp.bfloat16)
-
-    def reduce_keys(part):
-        part = part.astype(jnp.bfloat16).reshape(ys, rows_dev, flat_width)
-        moved = [part[0]] + [shift_y(part[s], -s) for s in range(1, ys)]
-        return sum(m.astype(jnp.float32) for m in moved)
-
-    def reduce_queries(part):
-        part = part.astype(jnp.bfloat16).reshape(XS, 2, rows_dev, flat_width)
-        own, other = by_core(part[:, 0], part[:, 1])
-        line = (own.astype(jnp.float32) + swap_core(other).astype(jnp.float32)).astype(
-            jnp.bfloat16
-        )
-
-        def piece(s):
-            return lax.dynamic_index_in_dim(line, (own_x - s) % XS, axis=0, keepdims=False)
-
-        moved = [piece(0)] + [shift_x(piece(s), -s) for s in range(1, XS)]
-        return sum(m.astype(jnp.float32) for m in moved)
+    both, scaling, cross_dl, dk_sum, dv_sum = lax.optimization_barrier(
+        (both, scaling, cross_dl, dk_sum, dv_sum)
+    )
+    core = jnp.reshape(own_core, (1,)).astype(jnp.int32)
+    prob, dlogit, dq_own, dq_other = query_grads(
+        logit_scale, core, both, scaling, k_blk, cross_dl, sum_k, rows_dev
+    )
+    dq_swapped = swap_core(dq_other)
+    pieces = key_grads(prob, dlogit, q_blk, g_blk, dk_sum, dv_sum, ys)
+    line = (dq_own + dq_swapped.astype(jnp.float32)).astype(jnp.bfloat16)
+    line = line.reshape(XS, rows_dev, flat_width)
+    line, pieces = lax.optimization_barrier((line, pieces))
+
+    def line_piece(s):
+        return lax.dynamic_index_in_dim(line, (own_x - s) % XS, axis=0, keepdims=False)
+
+    def added(parts):
+        return sum(p.astype(jnp.float32) for p in parts)
+
+    grad_q = added([line_piece(0)] + [shift_x(line_piece(s), -s) for s in range(1, XS)])
+    grad_kv = added([pieces[0]] + [shift_y(pieces[s], -s) for s in range(1, ys)])
 
     def finished(rows):
         return (
@@ -224,10 +351,11 @@
             .reshape(rows_dev, cols_dev, feature)
         )
 
-    grad_v = finished(reduce_keys(dot_f32(prob_blk, g_blk, LEAD_PAIR) + spread(dv_sum)))
-    grad_q = finished(reduce_queries(dot_f32(dlogit_blk, k_blk) + dq_cross))
-    grad_k = finished(reduce_keys(dot_f32(dlogit_blk, q_blk, LEAD_PAIR) + spread(dk_sum)))
-    return (grad_q, grad_k, grad_v)
+    return (
+        finished(grad_q),
+        finished(grad_kv[:, :flat_width]),
+        finished(grad_kv[:, flat_width:]),
+    )
 
 
 def solution(mesh):

time: 192 us -> 172 us (0.90)
  matrix products: 20.8 us -> 8.36 us
  starting transfers between devices: 60.7 us -> 50.2 us
  other arithmetic: 14.4 us -> 6.76 us
  Pallas kernels: 0 us -> 4.77 us
  waiting for transfers between devices: 72.2 us -> 76.5 us
  local copies, waits for them, and re-layouts: 7.06 us -> 9.68 us
    all_to_all x1 -> x0, waiting for transfers between devices: 36 us -> none  [shards(): lax.all_to_all(dprob_piece, 'col', split_axis=0, concat_axis=0, tiled=True)]
    ppermute x0 -> x7, waiting for transfers between devices: none -> 19.1 us  [shift_z(): return lax.ppermute(table, 'col', [(z, (z + step) % zs) for z in range(zs)])]
    ppermute x12 -> x9, waiting for transfers between devices: 3.8 us -> 17.2 us  [shift_y(): lax.ppermute(table, 'row', [(at(y, x, c), at(y + step, x, c)) for y, x, c...]
    dot_general x25 -> x18, matrix products: 20.8 us -> 8.36 us  [dot_f32(): lax.dot_general(left, right, dims, preferred_element_type=jnp.float32)]
    ppermute x0 -> x7, starting transfers between devices: none -> 8.66 us  [shift_z(): return lax.ppermute(table, 'col', [(z, (z + step) % zs) for z in range(zs)])]
    all_to_all x1 -> x0, starting transfers between devices: 8.2 us -> none  [shards(): lax.all_to_all(dprob_piece, 'col', split_axis=0, concat_axis=0, tiled=True)]
    ppermute x12 -> x9, starting transfers between devices: 15.3 us -> 9.23 us  [shift_y(): lax.ppermute(table, 'row', [(at(y, x, c), at(y + step, x, c)) for y, x, c...]
    pallas_call x0 -> x3, Pallas kernels: none -> 4.77 us  [the longest x1 2.08 us: block_softmax(): pl.pallas_call(kernel, out_shape=(jax.ShapeDtypeStruct((rows, 2 * width),...]
  transfers between devices with their start and end apart: 29 -> 32, of which waited for: 13 -> 20; matrix products, arithmetic and copies ran while one was open for 12% -> 8% of each run, Pallas kernels for 0% -> 1%
where the time goes in v4:
time: 172 us; the launch traced here: 171 us
  waiting for transfers between devices  76.5 us (44%)
  starting transfers between devices  50.2 us (29%)
  between operations  15 us (9%)
  local copies, waits for them, and re-layouts  9.68 us (6%)
  matrix products  8.36 us (5%)
  other arithmetic  6.76 us (4%)
  Pallas kernels  4.77 us (3%)
    ppermute x7, waiting for transfers between devices, shift_z(): return lax.ppermute(table, 'col', [(z, (z + step) % zs) for z in range(zs)])  19.1 us
    ppermute x9, waiting for transfers between devices, shift_y(): lax.ppermute(table, 'row', [(at(y, x, c), at(y + step, x, c)) for y, x, c...  17.2 us
    all_gather x1, waiting for transfers between devices, shards(): both = lax.all_gather(both, 'col', axis=0, tiled=True)  15.5 us
    all_to_all x2, waiting for transfers between devices, share(): lax.all_to_all(copies, axis, split_axis=0, concat_axis=0, tiled=True, axi...  12.3 us
    all_to_all x2, starting transfers between devices, share(): lax.all_to_all(copies, axis, split_axis=0, concat_axis=0, tiled=True, axi...  12.1 us
    ppermute x9, starting transfers between devices, shift_x(): lax.ppermute(table, 'row', [(at(y, x, c), at(y, x + step, c)) for y, x, c...  11.3 us
    ppermute x9, waiting for transfers between devices, shift_x(): lax.ppermute(table, 'row', [(at(y, x, c), at(y, x + step, c)) for y, x, c...  11.3 us
    ppermute x9, starting transfers between devices, shift_y(): lax.ppermute(table, 'row', [(at(y, x, c), at(y + step, x, c)) for y, x, c...  9.23 us
  transfers between devices with their start and end apart: 32, of which 20 were waited for; matrix products, arithmetic and copies ran while one was open for 8% of the time, Pallas kernels for 1%

profile of v4, /device:TPU:1, one launch (start us, length us, event | category | flops | bytes accessed | tf_op | source)
XLA Modules:
  0.0 171.2 jit_solution(14282524963828957046)
XLA Ops:
  7.2 0.7 broadcast_compare_fusion
  7.9 0.7 compare_and_fusion
  9.0 1.0 bitcast_select_fusion.2
  10.0 3.4 %collective-permute-start.2 = (bf16[128,512]{1,0:T(8,128)(2,1)S(1)}, bf16[128,512]{1,0:T(8,128)(2,1)S(1)}, u32[]{:S(2)}, u32[]{:S(2)}) collective-permute-start(bf16[128,512]{1,0:T(8,128)(2,1)S(1)} %get-tuple-element.37), channel_id=1, source_target_pairs={{0,48},{8,56},{16,0},{24,8},{32,16},{40,24},{48,32},{56,40},{64,11... | collective-permute-start | bytes 393224 | tf_op jit(solution)/shard_map/ppermute | solution.py:177
  13.9 0.6 collective-permute-start
  14.5 2.7 %collective-permute-start.6 = (bf16[128,512]{1,0:T(8,128)(2,1)S(1)}, bf16[128,512]{1,0:T(8,128)(2,1)S(1)}, u32[]{:S(2)}, u32[]{:S(2)}) collective-permute-start(bf16[128,512]{1,0:T(8,128)(2,1)S(1)} %get-tuple-element.38), channel_id=1, source_target_pairs={{0,192},{8,200},{16,208},{24,216},{32,224},{40,232},{48,240},{56,2... | collective-permute-start | bytes 393224 | tf_op jit(solution)/shard_map/ppermute | solution.py:174
  17.7 5.3 %collective-permute-done = bf16[128,512]{1,0:T(8,128)(2,1)S(1)} collective-permute-done((bf16[128,512]{1,0:T(8,128)(2,1)S(1)}, bf16[128,512]{1,0:T(8,128)(2,1)S(1)}, u32[]{:S(2)}, u32[]{:S(2)}) %collective-permute-start) | collective-permute-done | bytes 131104 | tf_op jit(solution)/shard_map/ppermute | solution.py:177
  22.9 1.3 collective-permute-start.4
  24.3 1.1 collective-permute-start.3
  25.6 3.0 %collective-permute-done.4 = bf16[128,512]{1,0:T(8,128)(2,1)S(1)} collective-permute-done((bf16[128,512]{1,0:T(8,128)(2,1)S(1)}, bf16[128,512]{1,0:T(8,128)(2,1)S(1)}, u32[]{:S(2)}, u32[]{:S(2)}) %collective-permute-start.4) | collective-permute-done | bytes 131104 | tf_op jit(solution)/shard_map/ppermute | solution.py:174
  29.0 2.1 %fusion.79 = f32[1024,512]{1,0:T(8,128)} fusion(bf16[1024,512]{1,0:T(8,128)(2,1)S(1)} %bitcast.195, bf16[512,512]{1,0:T(8,128)(2,1)S(1)} %constant_dynamic-update-slice_fusion.k_ref), kind=kOutput, calls=%fused_computation.186 | convolution fusion | flops 536870912 | bytes 3670016 | tf_op jit(solution)/shard_map/dot_general | solution.py:20
  31.1 0.8 copy-done.11
  32.1 1.4 collective-permute-start.8
  33.5 1.3 collective-permute-start.9
  34.8 1.5 collective-permute-start.13
  36.6 2.5 %collective-permute-done.7 = bf16[128,512]{1,0:T(8,128)(2,1)S(1)} collective-permute-done((bf16[128,512]{1,0:T(8,128)(2,1)S(1)}, bf16[128,512]{1,0:T(8,128)(2,1)S(1)}, u32[]{:S(2)}, u32[]{:S(2)}) %collective-permute-start.7) | collective-permute-done | bytes 131104 | tf_op jit(solution)/shard_map/ppermute | solution.py:177
  39.2 0.8 collective-permute-done.9
  40.0 2.9 %collective-permute-start.10 = (bf16[4,128,512]{2,1,0:T(8,128)(2,1)S(1)}, bf16[4,128,512]{2,1,0:T(8,128)(2,1)S(1)}, u32[]{:S(2)}, u32[]{:S(2)}) collective-permute-start(bf16[4,128,512]{2,1,0:T(8,128)(2,1)S(1)} %bitcast_dynamic-update-slice_fusion), channel_id=1, source_target_pairs={{0,8},{8,0},{16,24},{24,16},{32,40},{40,32},{48,56},{56,48},{64,72... | collective-permute-start | bytes 1572872 | tf_op jit(solution)/shard_map/ppermute | solution.py:180
  42.9 3.0 %collective-permute-done.11 = bf16[144,512]{1,0:T(8,128)(2,1)S(1)} collective-permute-done((bf16[144,512]{1,0:T(8,128)(2,1)S(1)}, bf16[144,512]{1,0:T(8,128)(2,1)S(1)}, u32[]{:S(2)}, u32[]{:S(2)}) %collective-permute-start.11) | collective-permute-done | bytes 147488 | tf_op jit(solution)/shard_map/ppermute | solution.py:174
  47.0 0.7 convolution_convert_fusion
  47.8 0.7 dynamic-slice_bitcast_fusion.3
  48.5 5.6 %collective-permute-start.18 = (bf16[128,512]{1,0:T(8,128)(2,1)S(1)}, bf16[128,512]{1,0:T(8,128)(2,1)S(1)}, u32[]{:S(2)}, u32[]{:S(2)}) collective-permute-start(bf16[128,512]{1,0:T(8,128)(2,1)S(1)} %get-tuple-element.93), channel_id=1, source_target_pairs={{0,7},{1,0},{2,1},{3,2},{4,3},{5,4},{6,5},{7,6},{8,15},{9,8},{10,9... | collective-permute-start | bytes 393224 | tf_op jit(solution)/shard_map/ppermute | solution.py:243
  54.9 0.9 fusion.69
  55.7 0.9 fusion.70
  56.6 0.8 fusion.71
  57.7 4.1 %collective-permute-done.14 = bf16[128,512]{1,0:T(8,128)(2,1)S(1)} collective-permute-done((bf16[128,512]{1,0:T(8,128)(2,1)S(1)}, bf16[128,512]{1,0:T(8,128)(2,1)S(1)}, u32[]{:S(2)}, u32[]{:S(2)}) %collective-permute-start.14) | collective-permute-done | bytes 131104 | tf_op jit(solution)/shard_map/ppermute | solution.py:243
  61.9 0.9 fusion.72
  62.8 7.0 %collective-permute-done.15 = bf16[128,512]{1,0:T(8,128)(2,1)S(1)} collective-permute-done((bf16[128,512]{1,0:T(8,128)(2,1)S(1)}, bf16[128,512]{1,0:T(8,128)(2,1)S(1)}, u32[]{:S(2)}, u32[]{:S(2)}) %collective-permute-start.15) | collective-permute-done | bytes 131104 | tf_op jit(solution)/shard_map/ppermute | solution.py:243
  70.0 1.5 collective-permute-start.16
  71.5 3.3 %collective-permute-done.19 = bf16[128,512]{1,0:T(8,128)(2,1)S(1)} collective-permute-done((bf16[128,512]{1,0:T(8,128)(2,1)S(1)}, bf16[128,512]{1,0:T(8,128)(2,1)S(1)}, u32[]{:S(2)}, u32[]{:S(2)}) %collective-permute-start.19) | collective-permute-done | bytes 131104 | tf_op jit(solution)/shard_map/ppermute | solution.py:243
  74.7 0.7 collective-permute-done.16
  75.4 0.7 fusion.7
  76.1 0.6 collective-permute-start.20
  76.8 0.8 collective-permute-start.17
  77.8 2.3 %collective-permute-done.20.back_ref = bf16[128,512]{1,0:T(8,128)(2,1)S(1)} collective-permute-done((bf16[128,512]{1,0:T(8,128)(2,1)}, bf16[128,512]{1,0:T(8,128)(2,1)S(1)}, u32[]{:S(2)}, u32[]{:S(2)}) %collective-permute-start.20) | collective-permute-done | bytes 131104 | tf_op jit(solution)/shard_map/ppermute | solution.py:243
  80.2 1.6 collective-permute-done.17.forward_ref
  81.8 0.7 copy-done.9
  82.5 2.1 %block_softmax.1 = (bf16[128,1024]{1,0:T(8,128)(2,1)}, f32[8,128]{1,0:T(8,128)}) custom-call(f32[128,512]{1,0:T(8,128)} %reduce-scatter.2.cloned.1.call-done.logit_ref, bf16[128,512]{1,0:T(8,128)(2,1)} %get-tuple-element.95.own_ref, bf16[128,512]{1,0:T(8,128)(2,1)} %copy-done.9, bf16[128,512]{1,0:T(8,128)(2,1)} %copy-done.8, ...), custom_call_target="tpu_custom_call" | custom-call | tf_op jit(solution)/shard_map/block_softmax/pallas_call | solution.py:56
  84.6 0.7 slice_bitcast_fusion.4
  85.3 0.9 broadcast_in_dim.86
  86.1 8.7 %all-to-all-start = ((f32[8,13,1024]{2,1,0:T(8,128)}), f32[8,13,1024]{2,1,0:T(8,128)S(1)}, u32[]{:S(2)}, u32[]{:S(2)}) async-start(f32[8,13,1024]{2,1,0:T(8,128)} %broadcast_in_dim.86), calls=%async_computation.1 | async-start | bytes 1048576 | tf_op jit(solution)/shard_map/all_to_all | solution.py:185
  94.9 0.7 all-gather.2.cloned.1.call-update
  95.6 8.8 %all-to-all-done = f32[8,13,1024]{2,1,0:T(8,128)S(1)} async-done(((f32[8,13,1024]{2,1,0:T(8,128)}), f32[8,13,1024]{2,1,0:T(8,128)S(1)}, u32[]{:S(2)}, u32[]{:S(2)}) %all-to-all-start) | async-done | bytes 426016 | tf_op jit(solution)/shard_map/all_to_all | solution.py:185
  104.4 0.8 bitcast_divide_fusion.1
  105.2 0.6 broadcast_in_dim.87
  105.8 3.3 %all-to-all-start.1 = ((f32[8,2,128]{2,1,0:T(2,128)}), f32[8,2,128]{2,1,0:T(2,128)S(1)}, u32[]{:S(2)}, u32[]{:S(2)}) async-start(f32[8,2,128]{2,1,0:T(2,128)} %broadcast_in_dim.87), calls=%async_computation.2 | async-start | bytes 16384 | tf_op jit(solution)/shard_map/all_to_all | solution.py:185
  109.6 0.9 slice_divide_fusion.3
  112.2 3.6 %all-to-all-done.1.scale_ref = f32[8,2,128]{2,1,0:T(2,128)S(1)} async-done(((f32[8,2,128]{2,1,0:T(2,128)}), f32[8,2,128]{2,1,0:T(2,128)S(1)}, u32[]{:S(2)}, u32[]{:S(2)}) %all-to-all-start.1) | async-done | bytes 8224 | tf_op jit(solution)/shard_map/all_to_all | solution.py:185
  115.7 15.5 %all-gather.2.cloned.1.call-done.both_ref = bf16[1024,1024]{1,0:T(8,128)(2,1)} async-done(((bf16[128,1024]{1,0:T(8,128)(2,1)}), bf16[1024,1024]{1,0:T(8,128)(2,1)}) %all-gather.2.cloned.1.call-update) | async-done | bytes 2097168 | tf_op jit(solution)/shard_map/all_gather | solution.py:294
  131.3 1.6 copy-done
  132.9 1.4 query_grads.1
  134.3 4.9 %collective-permute-start.21 = (bf16[512,512]{1,0:T(8,128)(2,1)S(1)}, bf16[512,512]{1,0:T(8,128)(2,1)S(1)}, u32[]{:S(2)}, u32[]{:S(2)}) collective-permute-start(bf16[512,512]{1,0:T(8,128)(2,1)S(1)} %get-tuple-element.57), channel_id=1, source_target_pairs={{0,8},{8,0},{16,24},{24,16},{32,40},{40,32},{48,56},{56,48},{64,72... | collective-permute-start | bytes 1572872 | tf_op jit(solution)/shard_map/ppermute | solution.py:180
  139.2 1.3 key_grads.1
  140.9 1.8 %collective-permute-start.22 = (bf16[128,512]{1,0:T(8,128)(2,1)S(1)}, bf16[128,512]{1,0:T(8,128)(2,1)S(1)}, u32[]{:S(2)}, u32[]{:S(2)}) collective-permute-start(bf16[128,512]{1,0:T(8,128)(2,1)S(1)} %get-tuple-element.100), channel_id=1, source_target_pairs={{0,48},{8,56},{16,0},{24,8},{32,16},{40,24},{48,32},{56,40},{64,11... | collective-permute-start | bytes 393224 | tf_op jit(solution)/shard_map/ppermute | solution.py:177
  142.7 2.2 %collective-permute-start.23 = (bf16[128,512]{1,0:T(8,128)(2,1)S(1)}, bf16[128,512]{1,0:T(8,128)(2,1)S(1)}, u32[]{:S(2)}, u32[]{:S(2)}) collective-permute-start(bf16[128,512]{1,0:T(8,128)(2,1)S(1)} %get-tuple-element.102), channel_id=1, source_target_pairs={{0,32},{8,40},{16,48},{24,56},{32,0},{40,8},{48,16},{56,24},{64,96... | collective-permute-start | bytes 393224 | tf_op jit(solution)/shard_map/ppermute | solution.py:177
  145.0 2.4 %collective-permute-start.25 = (bf16[128,1024]{1,0:T(8,128)(2,1)S(1)}, bf16[128,1024]{1,0:T(8,128)(2,1)S(1)}, u32[]{:S(2)}, u32[]{:S(2)}) collective-permute-start(bf16[128,1024]{1,0:T(8,128)(2,1)S(1)} %get-tuple-element.68), channel_id=1, source_target_pairs={{0,192},{8,200},{16,208},{24,216},{32,224},{40,232},{48,240},{56,2... | collective-permute-start | bytes 786440 | tf_op jit(solution)/shard_map/ppermute | solution.py:174
  148.0 0.7 collective-permute-done.24
  148.7 2.0 %collective-permute-done.23 = bf16[128,512]{1,0:T(8,128)(2,1)S(1)} collective-permute-done((bf16[128,512]{1,0:T(8,128)(2,1)S(1)}, bf16[128,512]{1,0:T(8,128)(2,1)S(1)}, u32[]{:S(2)}, u32[]{:S(2)}) %collective-permute-start.23) | collective-permute-done | bytes 131104 | tf_op jit(solution)/shard_map/ppermute | solution.py:177
  150.8 0.7 reshape.160
  151.5 1.1 collective-permute-done.25
  152.6 2.8 %collective-permute-done.26 = bf16[128,1024]{1,0:T(8,128)(2,1)S(1)} collective-permute-done((bf16[128,1024]{1,0:T(8,128)(2,1)S(1)}, bf16[128,1024]{1,0:T(8,128)(2,1)S(1)}, u32[]{:S(2)}, u32[]{:S(2)}) %collective-permute-start.26) | collective-permute-done | bytes 262176 | tf_op jit(solution)/shard_map/ppermute | solution.py:174
  155.3 7.4 %collective-permute-done.27 = bf16[128,1024]{1,0:T(8,128)(2,1)S(1)} collective-permute-done((bf16[128,1024]{1,0:T(8,128)(2,1)S(1)}, bf16[128,1024]{1,0:T(8,128)(2,1)S(1)}, u32[]{:S(2)}, u32[]{:S(2)}) %collective-permute-start.27) | collective-permute-done | bytes 262176 | tf_op jit(solution)/shard_map/ppermute | solution.py:174
  162.9 0.7 reshape.162
  163.6 0.7 reshape.161
  (134 shorter events, 8.2 us)
Async XLA Ops:
  7.2 18.2 %copy-start.12 = (s32[128]{0:T(128)S(1)}, s32[128]{0:T(128)}, u32[]{:S(2)}) copy-start(s32[128]{0:T(128)} %param.10) | copy-start | bytes 1540
  7.2 70.6 %reduce-scatter.2.cloned.1.call-start = ((), (), s32[]{:S(2)}) async-start(), calls=%async_computation.3 | async-start | bytes 2359296 | tf_op jit(solution)/shard_map/reduce_scatter | solution.py:224
  10.0 14.3 %collective-permute-start.2 = (bf16[128,512]{1,0:T(8,128)(2,1)S(1)}, bf16[128,512]{1,0:T(8,128)(2,1)S(1)}, u32[]{:S(2)}, u32[]{:S(2)}) collective-permute-start(bf16[128,512]{1,0:T(8,128)(2,1)S(1)} %get-tuple-element.37), channel_id=1, source_target_pairs={{0,48},{8,56},{16,0},{24,8},{32,16},{40,24},{48,32},{56,40},{64,11... | collective-permute-start | bytes 393224 | tf_op jit(solution)/shard_map/ppermute | solution.py:177
  13.4 10.9 %collective-permute-start.1 = (bf16[128,512]{1,0:T(8,128)(2,1)S(1)}, bf16[128,512]{1,0:T(8,128)(2,1)S(1)}, u32[]{:S(2)}, u32[]{:S(2)}) collective-permute-start(bf16[128,512]{1,0:T(8,128)(2,1)S(1)} %get-tuple-element.37), channel_id=1, source_target_pairs={{0,32},{8,40},{16,48},{24,56},{32,0},{40,8},{48,16},{56,24},{64,96... | collective-permute-start | bytes 393224 | tf_op jit(solution)/shard_map/ppermute | solution.py:177
  13.9 9.0 %collective-permute-start = (bf16[128,512]{1,0:T(8,128)(2,1)S(1)}, bf16[128,512]{1,0:T(8,128)(2,1)S(1)}, u32[]{:S(2)}, u32[]{:S(2)}) collective-permute-start(bf16[128,512]{1,0:T(8,128)(2,1)S(1)} %get-tuple-element.37), channel_id=1, source_target_pairs={{0,16},{8,24},{16,32},{24,40},{32,48},{40,56},{48,0},{56,8},{64,80... | collective-permute-start | bytes 393224 | tf_op jit(solution)/shard_map/ppermute | solution.py:177
  14.5 14.2 %collective-permute-start.6 = (bf16[128,512]{1,0:T(8,128)(2,1)S(1)}, bf16[128,512]{1,0:T(8,128)(2,1)S(1)}, u32[]{:S(2)}, u32[]{:S(2)}) collective-permute-start(bf16[128,512]{1,0:T(8,128)(2,1)S(1)} %get-tuple-element.38), channel_id=1, source_target_pairs={{0,192},{8,200},{16,208},{24,216},{32,224},{40,232},{48,240},{56,2... | collective-permute-start | bytes 393224 | tf_op jit(solution)/shard_map/ppermute | solution.py:174
  17.3 11.4 %collective-permute-start.5 = (bf16[128,512]{1,0:T(8,128)(2,1)S(1)}, bf16[128,512]{1,0:T(8,128)(2,1)S(1)}, u32[]{:S(2)}, u32[]{:S(2)}) collective-permute-start(bf16[128,512]{1,0:T(8,128)(2,1)S(1)} %get-tuple-element.38), channel_id=1, source_target_pairs={{0,128},{8,136},{16,144},{24,152},{32,160},{40,168},{48,176},{56,1... | collective-permute-start | bytes 393224 | tf_op jit(solution)/shard_map/ppermute | solution.py:174
  22.9 5.7 %collective-permute-start.4 = (bf16[128,512]{1,0:T(8,128)(2,1)S(1)}, bf16[128,512]{1,0:T(8,128)(2,1)S(1)}, u32[]{:S(2)}, u32[]{:S(2)}) collective-permute-start(bf16[128,512]{1,0:T(8,128)(2,1)S(1)} %get-tuple-element.38), channel_id=1, source_target_pairs={{0,64},{8,72},{16,80},{24,88},{32,96},{40,104},{48,112},{56,120},{... | collective-permute-start | bytes 393224 | tf_op jit(solution)/shard_map/ppermute | solution.py:174
  24.3 4.4 %collective-permute-start.3 = (bf16[4,128,512]{2,1,0:T(8,128)(2,1)S(1)}, bf16[4,128,512]{2,1,0:T(8,128)(2,1)S(1)}, u32[]{:S(2)}, u32[]{:S(2)}) collective-permute-start(bf16[4,128,512]{2,1,0:T(8,128)(2,1)S(1)} %bitcast_dynamic-update-slice_fusion.4), channel_id=1, source_target_pairs={{0,8},{8,0},{16,24},{24,16},{32,40},{40,32},{48,56},{56,48},{64,72... | collective-permute-start | bytes 1572872 | tf_op jit(solution)/shard_map/ppermute | solution.py:180
  31.1 0.9 copy-start.11
  31.1 3.7 %copy-start.10 = (bf16[128,4,128]{2,1,0:T(4,128)(2,1)S(1)}, bf16[128,4,128]{2,1,0:T(4,128)(2,1)}, u32[]{:S(2)}) copy-start(bf16[128,4,128]{2,1,0:T(4,128)(2,1)} %param.8) | copy-start | bytes 393220
  32.0 7.1 %collective-permute-start.7 = (bf16[128,512]{1,0:T(8,128)(2,1)S(1)}, bf16[128,512]{1,0:T(8,128)(2,1)S(1)}, u32[]{:S(2)}, u32[]{:S(2)}) collective-permute-start(bf16[128,512]{1,0:T(8,128)(2,1)S(1)} %get-tuple-element.88), channel_id=1, source_target_pairs={{0,16},{8,24},{16,32},{24,40},{32,48},{40,56},{48,0},{56,8},{64,80... | collective-permute-start | bytes 393224 | tf_op jit(solution)/shard_map/ppermute | solution.py:177
  32.1 7.0 %collective-permute-start.8 = (bf16[128,512]{1,0:T(8,128)(2,1)S(1)}, bf16[128,512]{1,0:T(8,128)(2,1)S(1)}, u32[]{:S(2)}, u32[]{:S(2)}) collective-permute-start(bf16[128,512]{1,0:T(8,128)(2,1)S(1)} %get-tuple-element.88), channel_id=1, source_target_pairs={{0,32},{8,40},{16,48},{24,56},{32,0},{40,8},{48,16},{56,24},{64,96... | collective-permute-start | bytes 393224 | tf_op jit(solution)/shard_map/ppermute | solution.py:177
  33.5 6.5 %collective-permute-start.9 = (bf16[128,512]{1,0:T(8,128)(2,1)S(1)}, bf16[128,512]{1,0:T(8,128)(2,1)S(1)}, u32[]{:S(2)}, u32[]{:S(2)}) collective-permute-start(bf16[128,512]{1,0:T(8,128)(2,1)S(1)} %get-tuple-element.88), channel_id=1, source_target_pairs={{0,48},{8,56},{16,0},{24,8},{32,16},{40,24},{48,32},{56,40},{64,11... | collective-permute-start | bytes 393224 | tf_op jit(solution)/shard_map/ppermute | solution.py:177
  34.8 8.1 %collective-permute-start.13 = (bf16[144,512]{1,0:T(8,128)(2,1)S(1)}, bf16[144,512]{1,0:T(8,128)(2,1)S(1)}, u32[]{:S(2)}, u32[]{:S(2)}) collective-permute-start(bf16[144,512]{1,0:T(8,128)(2,1)S(1)} %fusion.40), channel_id=1, source_target_pairs={{0,192},{8,200},{16,208},{24,216},{32,224},{40,232},{48,240},{56,2... | collective-permute-start | bytes 442376 | tf_op jit(solution)/shard_map/ppermute | solution.py:174
  36.3 6.6 %collective-permute-start.12 = (bf16[144,512]{1,0:T(8,128)(2,1)S(1)}, bf16[144,512]{1,0:T(8,128)(2,1)S(1)}, u32[]{:S(2)}, u32[]{:S(2)}) collective-permute-start(bf16[144,512]{1,0:T(8,128)(2,1)S(1)} %fusion.40), channel_id=1, source_target_pairs={{0,128},{8,136},{16,144},{24,152},{32,160},{40,168},{48,176},{56,1... | collective-permute-start | bytes 442376 | tf_op jit(solution)/shard_map/ppermute | solution.py:174
  39.1 6.9 %collective-permute-start.11 = (bf16[144,512]{1,0:T(8,128)(2,1)S(1)}, bf16[144,512]{1,0:T(8,128)(2,1)S(1)}, u32[]{:S(2)}, u32[]{:S(2)}) collective-permute-start(bf16[144,512]{1,0:T(8,128)(2,1)S(1)} %fusion.40), channel_id=1, source_target_pairs={{0,64},{8,72},{16,80},{24,88},{32,96},{40,104},{48,112},{56,120},{... | collective-permute-start | bytes 442376 | tf_op jit(solution)/shard_map/ppermute | solution.py:174
  40.0 6.8 %collective-permute-start.10 = (bf16[4,128,512]{2,1,0:T(8,128)(2,1)S(1)}, bf16[4,128,512]{2,1,0:T(8,128)(2,1)S(1)}, u32[]{:S(2)}, u32[]{:S(2)}) collective-permute-start(bf16[4,128,512]{2,1,0:T(8,128)(2,1)S(1)} %bitcast_dynamic-update-slice_fusion), channel_id=1, source_target_pairs={{0,8},{8,0},{16,24},{24,16},{32,40},{40,32},{48,56},{56,48},{64,72... | collective-permute-start | bytes 1572872 | tf_op jit(solution)/shard_map/ppermute | solution.py:180
  48.5 14.3 %collective-permute-start.18 = (bf16[128,512]{1,0:T(8,128)(2,1)S(1)}, bf16[128,512]{1,0:T(8,128)(2,1)S(1)}, u32[]{:S(2)}, u32[]{:S(2)}) collective-permute-start(bf16[128,512]{1,0:T(8,128)(2,1)S(1)} %get-tuple-element.93), channel_id=1, source_target_pairs={{0,7},{1,0},{2,1},{3,2},{4,3},{5,4},{6,5},{7,6},{8,15},{9,8},{10,9... | collective-permute-start | bytes 393224 | tf_op jit(solution)/shard_map/ppermute | solution.py:243
  54.0 7.7 %collective-permute-start.14 = (bf16[128,512]{1,0:T(8,128)(2,1)S(1)}, bf16[128,512]{1,0:T(8,128)(2,1)S(1)}, u32[]{:S(2)}, u32[]{:S(2)}) collective-permute-start(bf16[128,512]{1,0:T(8,128)(2,1)S(1)} %get-tuple-element.94), channel_id=1, source_target_pairs={{0,1},{1,2},{2,3},{3,4},{4,5},{5,6},{6,7},{7,0},{8,9},{9,10},{10,1... | collective-permute-start | bytes 393224 | tf_op jit(solution)/shard_map/ppermute | solution.py:243
  61.8 8.0 %collective-permute-start.15 = (bf16[128,512]{1,0:T(8,128)(2,1)S(1)}, bf16[128,512]{1,0:T(8,128)(2,1)S(1)}, u32[]{:S(2)}, u32[]{:S(2)}) collective-permute-start(bf16[128,512]{1,0:T(8,128)(2,1)S(1)} %fusion.11), channel_id=1, source_target_pairs={{0,1},{1,2},{2,3},{3,4},{4,5},{5,6},{6,7},{7,0},{8,9},{9,10},{10,1... | collective-permute-start | bytes 393224 | tf_op jit(solution)/shard_map/ppermute | solution.py:243
  69.9 4.8 %collective-permute-start.19 = (bf16[128,512]{1,0:T(8,128)(2,1)S(1)}, bf16[128,512]{1,0:T(8,128)(2,1)S(1)}, u32[]{:S(2)}, u32[]{:S(2)}) collective-permute-start(bf16[128,512]{1,0:T(8,128)(2,1)S(1)} %get-tuple-element.91), channel_id=1, source_target_pairs={{0,7},{1,0},{2,1},{3,2},{4,3},{5,4},{6,5},{7,6},{8,15},{9,8},{10,9... | collective-permute-start | bytes 393224 | tf_op jit(solution)/shard_map/ppermute | solution.py:243
  70.0 5.5 %collective-permute-start.16 = (bf16[128,512]{1,0:T(8,128)(2,1)S(1)}, bf16[128,512]{1,0:T(8,128)(2,1)S(1)}, u32[]{:S(2)}, u32[]{:S(2)}) collective-permute-start(bf16[128,512]{1,0:T(8,128)(2,1)S(1)} %get-tuple-element.92), channel_id=1, source_target_pairs={{0,1},{1,2},{2,3},{3,4},{4,5},{5,6},{6,7},{7,0},{8,9},{9,10},{10,1... | collective-permute-start | bytes 393224 | tf_op jit(solution)/shard_map/ppermute | solution.py:243
  76.1 4.0 %collective-permute-start.20 = (bf16[128,512]{1,0:T(8,128)(2,1)}, bf16[128,512]{1,0:T(8,128)(2,1)S(1)}, u32[]{:S(2)}, u32[]{:S(2)}) collective-permute-start(bf16[128,512]{1,0:T(8,128)(2,1)} %get-tuple-element.89), channel_id=1, source_target_pairs={{0,7},{1,0},{2,1},{3,2},{4,3},{5,4},{6,5},{7,6},{8,15},{9,8},{10,9... | collective-permute-start | bytes 393224 | tf_op jit(solution)/shard_map/ppermute | solution.py:243
  76.8 5.0 %collective-permute-start.17 = (bf16[128,512]{1,0:T(8,128)(2,1)S(1)}, bf16[128,512]{1,0:T(8,128)(2,1)S(1)}, u32[]{:S(2)}, u32[]{:S(2)}) collective-permute-start(bf16[128,512]{1,0:T(8,128)(2,1)S(1)} %get-tuple-element.90), channel_id=1, source_target_pairs={{0,1},{1,2},{2,3},{3,4},{4,5},{5,6},{6,7},{7,0},{8,9},{9,10},{10,1... | collective-permute-start | bytes 393224 | tf_op jit(solution)/shard_map/ppermute | solution.py:243
  77.8 8.4 %copy-start.7 = (f32[3,4,1024]{2,1,0:T(4,128)}, f32[3,4,1024]{2,1,0:T(4,128)S(1)}, u32[]{:S(2)}) copy-start(f32[3,4,1024]{2,1,0:T(4,128)S(1)} %pad_maximum_fusion.4) | copy-start | bytes 147460
  80.2 1.7 copy-start.8
  81.8 0.7 copy-start.9
  86.1 18.2 %all-to-all-start = ((f32[8,13,1024]{2,1,0:T(8,128)}), f32[8,13,1024]{2,1,0:T(8,128)S(1)}, u32[]{:S(2)}, u32[]{:S(2)}) async-start(f32[8,13,1024]{2,1,0:T(8,128)} %broadcast_in_dim.86), calls=%async_computation.1 | async-start | bytes 1048576 | tf_op jit(solution)/shard_map/all_to_all | solution.py:185
  94.9 36.4 %all-gather.2.cloned.1.call-start = ((), (), s32[]{:S(2)}) async-start(), calls=%async_computation.4 | async-start | bytes 2359296 | tf_op jit(solution)/shard_map/all_gather | solution.py:294
  105.8 9.9 %all-to-all-start.1 = ((f32[8,2,128]{2,1,0:T(2,128)}), f32[8,2,128]{2,1,0:T(2,128)S(1)}, u32[]{:S(2)}, u32[]{:S(2)}) async-start(f32[8,2,128]{2,1,0:T(2,128)} %broadcast_in_dim.87), calls=%async_computation.2 | async-start | bytes 16384 | tf_op jit(solution)/shard_map/all_to_all | solution.py:185
  109.1 1.6 copy-start.1
  109.2 1.9 %copy-start.2 = (f32[32,1024]{1,0:T(8,128)S(1)}, f32[32,1024]{1,0:T(8,128)}, u32[]{:S(2)}) copy-start(f32[32,1024]{1,0:T(8,128)} %get-tuple-element.51) | copy-start | bytes 393220
  109.2 2.1 %copy-start.3 = (f32[32,1024]{1,0:T(8,128)S(1)}, f32[32,1024]{1,0:T(8,128)}, u32[]{:S(2)}) copy-start(f32[32,1024]{1,0:T(8,128)} %get-tuple-element.46) | copy-start | bytes 393220
  109.2 2.1 %copy-start.5 = (f32[32,1024]{1,0:T(8,128)S(1)}, f32[32,1024]{1,0:T(8,128)}, u32[]{:S(2)}) copy-start(f32[32,1024]{1,0:T(8,128)} %get-tuple-element.48) | copy-start | bytes 393220
  109.2 2.2 %copy-start.4 = (f32[32,1024]{1,0:T(8,128)S(1)}, f32[32,1024]{1,0:T(8,128)}, u32[]{:S(2)}) copy-start(f32[32,1024]{1,0:T(8,128)} %get-tuple-element.50) | copy-start | bytes 393220
  109.2 2.2 %copy-start.6 = (f32[32,1024]{1,0:T(8,128)S(1)}, f32[32,1024]{1,0:T(8,128)}, u32[]{:S(2)}) copy-start(f32[32,1024]{1,0:T(8,128)} %get-tuple-element.52) | copy-start | bytes 393220
  131.3 1.6 copy-start
  134.3 6.4 %collective-permute-start.21 = (bf16[512,512]{1,0:T(8,128)(2,1)S(1)}, bf16[512,512]{1,0:T(8,128)(2,1)S(1)}, u32[]{:S(2)}, u32[]{:S(2)}) collective-permute-start(bf16[512,512]{1,0:T(8,128)(2,1)S(1)} %get-tuple-element.57), channel_id=1, source_target_pairs={{0,8},{8,0},{16,24},{24,16},{32,40},{40,32},{48,56},{56,48},{64,72... | collective-permute-start | bytes 1572872 | tf_op jit(solution)/shard_map/ppermute | solution.py:180
  140.9 6.8 %collective-permute-start.22 = (bf16[128,512]{1,0:T(8,128)(2,1)S(1)}, bf16[128,512]{1,0:T(8,128)(2,1)S(1)}, u32[]{:S(2)}, u32[]{:S(2)}) collective-permute-start(bf16[128,512]{1,0:T(8,128)(2,1)S(1)} %get-tuple-element.100), channel_id=1, source_target_pairs={{0,48},{8,56},{16,0},{24,8},{32,16},{40,24},{48,32},{56,40},{64,11... | collective-permute-start | bytes 393224 | tf_op jit(solution)/shard_map/ppermute | solution.py:177
  142.7 6.0 %collective-permute-start.24 = (bf16[128,512]{1,0:T(8,128)(2,1)S(1)}, bf16[128,512]{1,0:T(8,128)(2,1)S(1)}, u32[]{:S(2)}, u32[]{:S(2)}) collective-permute-start(bf16[128,512]{1,0:T(8,128)(2,1)S(1)} %get-tuple-element.101), channel_id=1, source_target_pairs={{0,16},{8,24},{16,32},{24,40},{32,48},{40,56},{48,0},{56,8},{64,80... | collective-permute-start | bytes 393224 | tf_op jit(solution)/shard_map/ppermute | solution.py:177
  142.7 8.0 %collective-permute-start.23 = (bf16[128,512]{1,0:T(8,128)(2,1)S(1)}, bf16[128,512]{1,0:T(8,128)(2,1)S(1)}, u32[]{:S(2)}, u32[]{:S(2)}) collective-permute-start(bf16[128,512]{1,0:T(8,128)(2,1)S(1)} %get-tuple-element.102), channel_id=1, source_target_pairs={{0,32},{8,40},{16,48},{24,56},{32,0},{40,8},{48,16},{56,24},{64,96... | collective-permute-start | bytes 393224 | tf_op jit(solution)/shard_map/ppermute | solution.py:177
  145.0 7.6 %collective-permute-start.25 = (bf16[128,1024]{1,0:T(8,128)(2,1)S(1)}, bf16[128,1024]{1,0:T(8,128)(2,1)S(1)}, u32[]{:S(2)}, u32[]{:S(2)}) collective-permute-start(bf16[128,1024]{1,0:T(8,128)(2,1)S(1)} %get-tuple-element.68), channel_id=1, source_target_pairs={{0,192},{8,200},{16,208},{24,216},{32,224},{40,232},{48,240},{56,2... | collective-permute-start | bytes 786440 | tf_op jit(solution)/shard_map/ppermute | solution.py:174
  147.4 7.9 %collective-permute-start.26 = (bf16[128,1024]{1,0:T(8,128)(2,1)S(1)}, bf16[128,1024]{1,0:T(8,128)(2,1)S(1)}, u32[]{:S(2)}, u32[]{:S(2)}) collective-permute-start(bf16[128,1024]{1,0:T(8,128)(2,1)S(1)} %get-tuple-element.69), channel_id=1, source_target_pairs={{0,128},{8,136},{16,144},{24,152},{32,160},{40,168},{48,176},{56,1... | collective-permute-start | bytes 786440 | tf_op jit(solution)/shard_map/ppermute | solution.py:174
  147.7 15.0 %collective-permute-start.27 = (bf16[128,1024]{1,0:T(8,128)(2,1)S(1)}, bf16[128,1024]{1,0:T(8,128)(2,1)S(1)}, u32[]{:S(2)}, u32[]{:S(2)}) collective-permute-start(bf16[128,1024]{1,0:T(8,128)(2,1)S(1)} %get-tuple-element.70), channel_id=1, source_target_pairs={{0,64},{8,72},{16,80},{24,88},{32,96},{40,104},{48,112},{56,120},{... | collective-permute-start | bytes 786440 | tf_op jit(solution)/shard_map/ppermute | solution.py:174
Sparse Core Ops, SparseCore 0:
  31.2 41.1 reduce-scatter.1
  97.5 33.7 all-gather.1

commit v5 on v4

v5 whole, which is shorter than its diff:
```python
import math

import jax
import jax.numpy as jnp
from jax import lax
from jax.experimental import pallas as pl
from jax.experimental.layout import Layout, with_layout_constraint
from jax.experimental.pallas import tpu as pltpu
from jax.sharding import PartitionSpec as P

SUMMARIES = 256
XS = 4
FLAG_ROWS = 16

ROW_PAIR = (((1,), (1,)), ((), ()))
LEAD_PAIR = (((0,), (0,)), ((), ()))
PLAIN = (((1,), (0,)), ((), ()))

VMEM = pl.BlockSpec(memory_space=pltpu.VMEM)
SMEM = pl.BlockSpec(memory_space=pltpu.SMEM)
ROOM = pltpu.CompilerParams(vmem_limit_bytes=40 * 1024 * 1024)


def dot_f32(left, right, dims=PLAIN):
    return lax.dot_general(left, right, dims, preferred_element_type=jnp.float32)


def diagonal(n):
    return lax.broadcasted_iota(jnp.int32, (n, n), 0) == lax.broadcasted_iota(jnp.int32, (n, n), 1)


def across(column):
    return jnp.sum(jnp.where(diagonal(column.shape[0]), column, 0.0), axis=0, keepdims=True)


def upright(row):
    return jnp.sum(jnp.where(diagonal(row.shape[1]), row, 0.0), axis=1, keepdims=True)


def block_products(place, line, other_line, key_pieces, rows_dev, flat_width):
    lines = line.shape[0]
    block_rows, block_keys = 2 * lines * rows_dev, len(key_pieces) * rows_dev

    def kernel(place_ref, line_ref, other_ref, *refs):
        piece_refs, (qg_ref, kv_ref, logit_ref, dprob_ref) = refs[:-4], refs[-4:]
        core = place_ref[0]
        for s, piece_ref in enumerate(piece_refs):
            kv_ref[s * rows_dev : (s + 1) * rows_dev, :] = piece_ref[:rows_dev, :]
        for x in range(lines):
            mine = pl.multiple_of((2 * x + core) * rows_dev, rows_dev)
            theirs = pl.multiple_of((2 * x + 1 - core) * rows_dev, rows_dev)
            qg_ref[pl.ds(mine, rows_dev), :] = line_ref[x]
            qg_ref[pl.ds(theirs, rows_dev), :] = other_ref[x]
        logit_ref[...] = dot_f32(qg_ref[:, :flat_width], kv_ref[:, :flat_width], ROW_PAIR)
        dprob_ref[...] = dot_f32(qg_ref[:, flat_width:], kv_ref[:, flat_width:], ROW_PAIR).astype(
            jnp.bfloat16
        )

    return pl.pallas_call(
        kernel,
        in_specs=[SMEM] + [VMEM] * (2 + len(key_pieces)),
        out_shape=(
            jax.ShapeDtypeStruct((block_rows, 2 * flat_width), jnp.bfloat16),
            jax.ShapeDtypeStruct((block_keys, 2 * flat_width), jnp.bfloat16),
            jax.ShapeDtypeStruct((block_rows, block_keys), jnp.float32),
            jax.ShapeDtypeStruct((block_rows, block_keys), jnp.bfloat16),
        ),
        compiler_params=ROOM,
        name="block_products",
    )(place, line, other_line, *key_pieces)


def cross_scores(sums_ref, qg_ref, column, feature, inv_root):
    flat_width = qg_ref.shape[1] // 2
    lanes = slice(column * feature, (column + 1) * feature)
    other = slice(flat_width + column * feature, flat_width + (column + 1) * feature)
    scores = dot_f32(sums_ref[:, lanes], qg_ref[:, lanes], ROW_PAIR) * inv_root
    dprob = dot_f32(sums_ref[:, other], qg_ref[:, other], ROW_PAIR)
    return scores, dprob, lanes, other


def cross_statistics(qg_blk, kv_blk, tokens, feature, inv_root):
    block_keys, both_width = kv_blk.shape
    block_rows = qg_blk.shape[0]
    group = block_keys // tokens
    columns = both_width // (2 * feature)
    stat_rows = -(-3 * columns // 8) * 8

    def kernel(qg_ref, kv_ref, sums_ref, stat_ref):
        pooled = jnp.sum(
            kv_ref[...].astype(jnp.float32).reshape(tokens, group, both_width), axis=1
        )
        sums_ref[...] = (pooled / group).astype(jnp.bfloat16)
        for c in range(columns):
            scores, dprob, _, _ = cross_scores(sums_ref, qg_ref, c, feature, inv_root)
            peak = jnp.max(scores, axis=0, keepdims=True)
            lifted = jnp.exp(scores - peak)
            stat_ref[c : c + 1, :] = peak
            stat_ref[columns + c : columns + c + 1, :] = jnp.sum(lifted, axis=0, keepdims=True)
            stat_ref[2 * columns + c : 2 * columns + c + 1, :] = jnp.sum(
                lifted * dprob, axis=0, keepdims=True
            )
        if stat_rows > 3 * columns:
            stat_ref[3 * columns :, :] = jnp.zeros(
                (stat_rows - 3 * columns, block_rows), jnp.float32
            )

    return pl.pallas_call(
        kernel,
        in_specs=[VMEM] * 2,
        out_shape=(
            jax.ShapeDtypeStruct((tokens, both_width), jnp.bfloat16),
            jax.ShapeDtypeStruct((stat_rows, block_rows), jnp.float32),
        ),
        compiler_params=ROOM,
        name="cross_statistics",
    )(qg_blk, kv_blk)


def cross_grads(qg_blk, sums, all_stats, feature, inv_root):
    tokens, both_width = sums.shape
    block_rows = qg_blk.shape[0]
    columns = both_width // (2 * feature)

    def kernel(qg_ref, sums_ref, stat_ref, dl_ref, dsum_ref):
        peaks = stat_ref[:, :columns, :]
        peak = jnp.max(peaks, axis=0)
        weight = jnp.exp(peaks - peak[None])
        total = jnp.sum(weight * stat_ref[:, columns : 2 * columns, :], axis=0)
        delta = jnp.sum(weight * stat_ref[:, 2 * columns : 3 * columns, :], axis=0) / total
        for c in range(columns):
            scores, dprob, lanes, other = cross_scores(sums_ref, qg_ref, c, feature, inv_root)
            probs = jnp.exp(scores - peak[c : c + 1, :]) / total[c : c + 1, :]
            dl = (inv_root * probs * (dprob - delta[c : c + 1, :])).astype(jnp.bfloat16)
            dl_ref[c * tokens : (c + 1) * tokens, :] = dl
            dsum_ref[:, lanes] = dot_f32(dl, qg_ref[:, lanes])
            dsum_ref[:, other] = dot_f32(probs.astype(jnp.bfloat16), qg_ref[:, other])

    return pl.pallas_call(
        kernel,
        in_specs=[VMEM] * 3,
        out_shape=(
            jax.ShapeDtypeStruct((columns * tokens, block_rows), jnp.bfloat16),
            jax.ShapeDtypeStruct((tokens, both_width), jnp.float32),
        ),
        compiler_params=ROOM,
        name="cross_grads",
    )(qg_blk, sums, all_stats)


def block_softmax(logit_scale, logit_sum, own, forward, back, key_flags):
    rows, width = logit_sum.shape

    def kernel(logit_ref, own_ref, forward_ref, back_ref, flag_ref, both_ref, stat_ref):
        dprob = (
            own_ref[...].astype(jnp.float32)
            + forward_ref[...].astype(jnp.float32)
            + back_ref[...].astype(jnp.float32)
        )
        logits = jnp.where(flag_ref[...] > 0, logit_ref[...] * logit_scale, -1e30)
        peak = jnp.max(logits, axis=1, keepdims=True)
        lifted = jnp.exp(logits - peak)
        total = jnp.sum(lifted, axis=1, keepdims=True)
        weighted = jnp.sum(lifted * dprob, axis=1, keepdims=True)
        delta = weighted / total
        both_ref[:, :width] = lifted.astype(jnp.bfloat16)
        both_ref[:, width:] = (lifted * (dprob - delta)).astype(jnp.bfloat16)
        for i, column in enumerate((peak, total, weighted, delta)):
            stat_ref[i : i + 1, :] = across(column)
        stat_ref[4:8, :] = jnp.zeros((4, rows), jnp.float32)

    return pl.pallas_call(
        kernel,
        in_specs=[VMEM] * 5,
        out_shape=(
            jax.ShapeDtypeStruct((rows, 2 * width), jnp.bfloat16),
            jax.ShapeDtypeStruct((8, rows), jnp.float32),
        ),
        compiler_params=ROOM,
        name="block_softmax",
    )(logit_sum, own, forward, back, key_flags)


def query_grads(logit_scale, place, pieces, steps, scaling, kv_blk, cross_dl, sums):
    rows, width = pieces[0].shape[0], pieces[0].shape[1] // 2
    chunks = len(pieces)
    block_rows = chunks * rows
    flat_width = kv_blk.shape[1] // 2
    tokens = sums.shape[0]
    columns = cross_dl.shape[0] // tokens
    feature = flat_width // columns

    def kernel(place_ref, scale_ref, kv_ref, dl_ref, sums_ref, *refs):
        piece_refs = refs[:chunks]
        p_ref, ds_ref, own_ref, other_ref, dq_ref = refs[chunks:]
        core, own_z = place_ref[0], place_ref[1]
        for piece_ref, step in zip(piece_refs, steps):
            source = lax.rem(own_z + (2 * chunks - step), chunks)
            scale = scale_ref[source]
            weight, offset = upright(scale[0:1, :]), upright(scale[1:2, :])
            lifted = piece_ref[:, :width].astype(jnp.float32)
            tilted = piece_ref[:, width:].astype(jnp.float32)
            at = pl.ds(pl.multiple_of(source * rows, rows), rows)
            p_ref[at, :] = (lifted * weight).astype(jnp.bfloat16)
            ds_ref[at, :] = ((tilted - lifted * offset) * (weight * logit_scale)).astype(
                jnp.bfloat16
            )
        dq_ref[...] = dot_f32(ds_ref[...], kv_ref[:, :flat_width])
        for c in range(columns):
            lanes = slice(c * feature, (c + 1) * feature)
            dq_ref[:, lanes] += dot_f32(
                dl_ref[c * tokens : (c + 1) * tokens, :], sums_ref[:, lanes], LEAD_PAIR
            )
        for x in range(chunks // 2):
            to = slice(x * rows, (x + 1) * rows)
            mine = pl.multiple_of((2 * x + core) * rows, rows)
            theirs = pl.multiple_of((2 * x + 1 - core) * rows, rows)
            own_ref[to, :] = dq_ref[pl.ds(mine, rows), :]
            other_ref[to, :] = dq_ref[pl.ds(theirs, rows), :].astype(jnp.bfloat16)

    return pl.pallas_call(
        kernel,
        in_specs=[SMEM] + [VMEM] * (4 + chunks),
        out_shape=(
            jax.ShapeDtypeStruct((block_rows, width), jnp.bfloat16),
            jax.ShapeDtypeStruct((block_rows, width), jnp.bfloat16),
            jax.ShapeDtypeStruct((block_rows // 2, flat_width), jnp.float32),
            jax.ShapeDtypeStruct((block_rows // 2, flat_width), jnp.bfloat16),
        ),
        scratch_shapes=[pltpu.VMEM((block_rows, flat_width), jnp.float32)],
        compiler_params=ROOM,
        name="query_grads",
    )(place, scaling, kv_blk, cross_dl, sums, *pieces)


def key_grads(prob, dlogit, qg_blk, dsum, pieces):
    width, flat_width = prob.shape[1], qg_blk.shape[1] // 2
    tokens = dsum.shape[0]
    group = width // tokens
    piece = width // pieces

    def kernel(p_ref, ds_ref, qg_ref, dsum_ref, *out_refs):
        for half, w_ref in enumerate((ds_ref, p_ref)):
            lanes = slice(half * flat_width, (half + 1) * flat_width)
            grads = dot_f32(w_ref[...], qg_ref[:, lanes], LEAD_PAIR)
            shared = dsum_ref[:, lanes] / group
            grads = grads.reshape(tokens, group, flat_width) + shared[:, None, :]
            grads = grads.reshape(width, flat_width).astype(jnp.bfloat16)
            for s, out_ref in enumerate(out_refs):
                out_ref[:, lanes] = grads[s * piece : (s + 1) * piece]

    return pl.pallas_call(
        kernel,
        in_specs=[VMEM] * 4,
        out_shape=tuple(
            jax.ShapeDtypeStruct((piece, 2 * flat_width), jnp.bfloat16) for _ in range(pieces)
        ),
        compiler_params=ROOM,
        name="key_grads",
    )(prob, dlogit, qg_blk, dsum)


def shards(queries, keys, values, out_grad, row_keep, row_lengths):
    rows_dev, cols_dev, feature = queries.shape
    row_axis, zs = lax.axis_size("row"), lax.axis_size("col")
    ys = row_axis // (2 * XS)
    near_size = 2 * XS
    total_rows = rows_dev * row_axis
    total_cols = cols_dev * zs
    group_rows = total_rows // SUMMARIES
    flat_width = cols_dev * feature
    block_rows = near_size * rows_dev
    block_keys = ys * rows_dev
    tokens = block_keys // group_rows
    near = [[y * near_size + i for i in range(near_size)] for y in range(ys)]
    own_x = (lax.axis_index("row") // 2) % XS
    own_core = lax.axis_index("row") % 2
    own_z = lax.axis_index("col")
    place = jnp.stack([own_core, own_z]).astype(jnp.int32)
    logit_scale = 1.0 / math.sqrt(total_cols * feature)
    inv_root = 1.0 / math.sqrt(feature)

    def at(y, x, core):
        return ((y % ys) * XS + x % XS) * 2 + core

    cells = [(y, x, c) for y in range(ys) for x in range(XS) for c in range(2)]

    def shift_y(table, step):
        return lax.ppermute(table, "row", [(at(y, x, c), at(y + step, x, c)) for y, x, c in cells])

    def shift_x(table, step):
        return lax.ppermute(table, "row", [(at(y, x, c), at(y, x + step, c)) for y, x, c in cells])

    def swap_core(table):
        return lax.ppermute(table, "row", [(at(y, x, c), at(y, x, 1 - c)) for y, x, c in cells])

    def shift_z(table, step):
        return lax.ppermute(table, "col", [(z, (z + step) % zs) for z in range(zs)])

    def share(table, axis, groups=None):
        count = lax.axis_size(axis) if groups is None else len(groups[0])
        copies = jnp.broadcast_to(table[None], (count,) + table.shape)
        return lax.all_to_all(
            copies, axis, split_axis=0, concat_axis=0, tiled=True, axis_index_groups=groups
        )

    column_ids = own_z * cols_dev + jnp.arange(cols_dev, dtype=jnp.int32)
    cell_keep = (row_keep[:, None] == 1) & (column_ids[None, :] < row_lengths[:, None])
    keep_flat = jnp.broadcast_to(cell_keep[:, :, None], queries.shape).reshape(
        rows_dev, flat_width
    )
    zero = jnp.zeros((), queries.dtype)

    def masked(first, second):
        tables = (t.reshape(rows_dev, flat_width) for t in (first, second))
        flat = jnp.concatenate([jnp.where(keep_flat, t, zero) for t in tables], axis=1)
        return with_layout_constraint(flat, Layout((0, 1)))

    qg_flat = masked(queries, out_grad)
    flag_rows = jnp.pad(
        row_keep.astype(jnp.bfloat16)[None, :],
        ((0, FLAG_ROWS - 1), (0, 2 * flat_width - rows_dev)),
    )
    kv_flat = jnp.concatenate([masked(keys, values), flag_rows], axis=0)
    qg_flat, kv_flat = lax.optimization_barrier((qg_flat, kv_flat))
    order = (1, XS - 1, 2)
    query_pieces = {0: qg_flat} | {s: shift_x(qg_flat, s) for s in order}
    key_pieces = [kv_flat] + [shift_y(kv_flat, s) for s in range(1, ys)]
    query_pieces, key_pieces = lax.optimization_barrier((query_pieces, key_pieces))
    line = jnp.zeros((XS, rows_dev, 2 * flat_width), queries.dtype)
    for s, piece in query_pieces.items():
        line = lax.dynamic_update_slice(line, piece[None], ((own_x - s) % XS, 0, 0))
    qg_blk, kv_blk, logit_piece, dprob_piece = block_products(
        place, line, swap_core(line), key_pieces, rows_dev, flat_width
    )
    key_flags = jnp.concatenate([p[rows_dev, :rows_dev] for p in key_pieces])[None, :]
    logit_sum = lax.psum_scatter(logit_piece, "col", scatter_dimension=0, tiled=True)

    dprob_chunks = dprob_piece.reshape(zs, block_rows // zs, block_keys)

    def part(step):
        return lax.dynamic_index_in_dim(dprob_chunks, (own_z + step) % zs, axis=0, keepdims=False)

    def passed(step, count):
        moving = part(step * count)
        for left in range(count - 1, -1, -1):
            moving = shift_z(moving, step)
            if left > 0:
                moving = (
                    moving.astype(jnp.float32) + part(step * left).astype(jnp.float32)
                ).astype(jnp.bfloat16)
        return moving

    dprob_forward = passed(1, zs // 2)
    dprob_back = passed(-1, zs - 1 - zs // 2)

    sums, own_stats = cross_statistics(qg_blk, kv_blk, tokens, feature, inv_root)
    cross_dl, dsum = cross_grads(
        qg_blk, sums, share(own_stats, "row", near), feature, inv_root
    )

    both, stats = block_softmax(
        logit_scale, logit_sum, part(0), dprob_forward, dprob_back, key_flags
    )
    both, stats, cross_dl, dsum = lax.optimization_barrier((both, stats, cross_dl, dsum))
    forward, back = [both], []
    for _ in range(zs // 2):
        forward.append(shift_z(forward[-1], 1))
    for _ in range(zs - 1 - zs // 2):
        back.append(shift_z(back[-1] if back else both, -1))
    pieces = forward + back
    steps = list(range(zs // 2 + 1)) + [-s for s in range(1, zs - zs // 2)]

    all_stats = share(stats, "row", near)
    weight = jnp.exp(all_stats[:, 0] - jnp.max(all_stats[:, 0], axis=0))
    total = jnp.sum(weight * all_stats[:, 1], axis=0)
    delta = jnp.sum(weight * all_stats[:, 2], axis=0) / total
    own_weight = jnp.exp(stats[0] - jnp.max(all_stats[:, 0], axis=0)) / total
    scaling = share(jnp.stack([own_weight, delta - stats[3]]), "col")

    prob, dlogit, dq_own, dq_other = query_grads(
        logit_scale, place, pieces, steps, scaling, kv_blk, cross_dl, sums
    )
    dq_swapped = swap_core(dq_other)
    key_parts = key_grads(prob, dlogit, qg_blk, dsum, ys)
    key_moved = [shift_y(key_parts[s], -s) for s in range(1, ys)]
    line = (dq_own + dq_swapped.astype(jnp.float32)).astype(jnp.bfloat16)
    line = line.reshape(XS, rows_dev, flat_width)
    line, key_moved[0] = lax.optimization_barrier((line, key_moved[0]))

    def line_piece(s):
        return lax.dynamic_index_in_dim(line, (own_x - s) % XS, axis=0, keepdims=False)

    def added(parts):
        return sum(p.astype(jnp.float32) for p in parts)

    grad_q = added([line_piece(0)] + [shift_x(line_piece(s), -s) for s in range(1, XS)])
    grad_kv = added([key_parts[0]] + key_moved)

    def finished(rows):
        return (
            jnp.where(keep_flat, rows, 0.0)
            .astype(jnp.bfloat16)
            .reshape(rows_dev, cols_dev, feature)
        )

    return (
        finished(grad_q),
        finished(grad_kv[:, :flat_width]),
        finished(grad_kv[:, flat_width:]),
    )


def solution(mesh):
    return jax.shard_map(
        shards,
        mesh=mesh,
        in_specs=(
            P("row", "col", None),
            P("row", "col", None),
            P("row", "col", None),
            P("row", "col", None),
            P("row"),
            P("row"),
        ),
        out_specs=(P("row", "col", None), P("row", "col", None), P("row", "col", None)),
        check_vma=False,
    )
```

time: 172 us -> 181 us (1.052)
  the two profiles are of different devices: /device:TPU:1 before, /device:TPU:8 now
where the time goes in v5:
time: 181 us; the launch traced here: 180 us
  waiting for transfers between devices  55.5 us (31%)
  starting transfers between devices  49.8 us (28%)
  local copies, waits for them, and re-layouts  26.7 us (15%)
  between operations  14.4 us (8%)
  blocking collectives  12.5 us (7%)
  Pallas kernels  12 us (7%)
  other arithmetic  9.37 us (5%)
    ppermute x14, waiting for transfers between devices, shift_z(): return lax.ppermute(table, 'col', [(z, (z + step) % zs) for z in range(zs)])  24.8 us
    ppermute x14, starting transfers between devices, shift_z(): return lax.ppermute(table, 'col', [(z, (z + step) % zs) for z in range(zs)])  21.4 us
    unnamed x48, local copies, waits for them, and re-layouts  19.4 us
    all_to_all x1, blocking collectives, share(): lax.all_to_all(copies, axis, split_axis=0, concat_axis=0, tiled=True, axi...  12.5 us
    ppermute x6, waiting for transfers between devices, shift_x(): lax.ppermute(table, 'row', [(at(y, x, c), at(y, x + step, c)) for y, x, c...  12.4 us
    ppermute x6, starting transfers between devices, shift_x(): lax.ppermute(table, 'row', [(at(y, x, c), at(y, x + step, c)) for y, x, c...  11.5 us
    ppermute x6, waiting for transfers between devices, shift_y(): lax.ppermute(table, 'row', [(at(y, x, c), at(y + step, x, c)) for y, x, c...  10.3 us
    ppermute x6, starting transfers between devices, shift_y(): lax.ppermute(table, 'row', [(at(y, x, c), at(y + step, x, c)) for y, x, c...  8.83 us
  transfers between devices with their start and end apart: 31, of which 14 were waited for; matrix products, arithmetic and copies ran while one was open for 7% of the time, Pallas kernels for 3%

profile of v5, /device:TPU:8, one launch (start us, length us, event | category | flops | bytes accessed | tf_op | source)
XLA Modules:
  0.0 180.3 jit_solution(3985100757287433317)
XLA Ops:
  8.5 0.7 compare_and_fusion
  9.6 1.2 bitcast_select_fusion.1
  10.9 1.6 collective-permute-start
  12.5 1.6 collective-permute-start.3
  14.1 1.3 collective-permute-start.4
  15.3 2.1 %collective-permute-start.5 = (bf16[144,1024]{1,0:T(8,128)(2,1)S(1)}, bf16[144,1024]{1,0:T(8,128)(2,1)S(1)}, u32[]{:S(2)}, u32[]{:S(2)}) collective-permute-start(bf16[144,1024]{1,0:T(8,128)(2,1)S(1)} %fusion.1.refs_0_), channel_id=1, source_target_pairs={{0,192},{8,200},{16,208},{24,216},{32,224},{40,232},{48,240},{56,2... | collective-permute-start | bytes 884744 | tf_op jit(solution)/shard_map/ppermute | solution.py:289
  17.4 2.7 %collective-permute-start.1 = (bf16[128,1024]{1,0:T(8,128)(2,1)S(1)}, bf16[128,1024]{1,0:T(8,128)(2,1)S(1)}, u32[]{:S(2)}, u32[]{:S(2)}) collective-permute-start(bf16[128,1024]{1,0:T(8,128)(2,1)S(1)} %pad_maximum_fusion), channel_id=1, source_target_pairs={{0,32},{8,40},{16,48},{24,56},{32,0},{40,8},{48,16},{56,24},{64,96... | collective-permute-start | bytes 786440 | tf_op jit(solution)/shard_map/ppermute | solution.py:292
  20.2 2.5 %collective-permute-start.2 = (bf16[128,1024]{1,0:T(8,128)(2,1)S(1)}, bf16[128,1024]{1,0:T(8,128)(2,1)S(1)}, u32[]{:S(2)}, u32[]{:S(2)}) collective-permute-start(bf16[128,1024]{1,0:T(8,128)(2,1)S(1)} %pad_maximum_fusion), channel_id=1, source_target_pairs={{0,48},{8,56},{16,0},{24,8},{32,16},{40,24},{48,32},{56,40},{64,11... | collective-permute-start | bytes 786440 | tf_op jit(solution)/shard_map/ppermute | solution.py:292
  22.7 4.1 %collective-permute-done.1 = bf16[128,1024]{1,0:T(8,128)(2,1)S(1)} collective-permute-done((bf16[128,1024]{1,0:T(8,128)(2,1)S(1)}, bf16[128,1024]{1,0:T(8,128)(2,1)S(1)}, u32[]{:S(2)}, u32[]{:S(2)}) %collective-permute-start.1) | collective-permute-done | bytes 262176 | tf_op jit(solution)/shard_map/ppermute | solution.py:292
  26.8 3.7 %collective-permute-done.2 = bf16[128,1024]{1,0:T(8,128)(2,1)S(1)} collective-permute-done((bf16[128,1024]{1,0:T(8,128)(2,1)S(1)}, bf16[128,1024]{1,0:T(8,128)(2,1)S(1)}, u32[]{:S(2)}, u32[]{:S(2)}) %collective-permute-start.2) | collective-permute-done | bytes 262176 | tf_op jit(solution)/shard_map/ppermute | solution.py:292
  32.0 0.7 copy-done.11
  33.1 1.0 copy-done
  34.2 1.5 collective-permute-done.6.other_ref
  35.7 1.0 copy-done.3
  36.7 1.2 copy-done.1
  37.9 1.2 copy-done.4
  39.2 1.0 copy-done.8
  40.1 1.0 copy-done.10
  41.1 1.0 copy-done.12
  42.0 1.9 %block_products.1 = (bf16[1024,1024]{1,0:T(8,128)(2,1)S(1)}, bf16[512,1024]{1,0:T(8,128)(2,1)S(1)}, f32[1024,512]{1,0:T(8,128)S(1)}, bf16[1024,512]{1,0:T(8,128)(2,1)S(1)}) custom-call(s32[2]{0:T(128)S(1)} %pad_add_fusion.place_ref, bf16[4,128,1024]{2,1,0:T(8,128)(2,1)S(1)} %copy-done.1, bf16[4,128,1024]{2,1,0:T(8,128)(2,1)S(1)} %copy-done.4, ...), custom_call_target="tpu_custom_call" | custom-call | tf_op jit(solution)/shard_map/block_products/pallas_call | solution.py:59
  44.0 1.3 copy-done.2
  45.3 1.0 copy-done.5
  46.4 1.8 dynamic-slice_bitcast_fusion.3
  48.2 1.9 %collective-permute-start.7 = (bf16[128,512]{1,0:T(8,128)(2,1)}, bf16[128,512]{1,0:T(8,128)(2,1)}, u32[]{:S(2)}, u32[]{:S(2)}) collective-permute-start(bf16[128,512]{1,0:T(8,128)(2,1)} %get-tuple-element.78), channel_id=1, source_target_pairs={{0,1},{1,2},{2,3},{3,4},{4,5},{5,6},{6,7},{7,0},{8,9},{9,10},{10,1... | collective-permute-start | bytes 393224 | tf_op jit(solution)/shard_map/ppermute | solution.py:298
  50.1 3.9 %collective-permute-start.11 = (bf16[128,512]{1,0:T(8,128)(2,1)}, bf16[128,512]{1,0:T(8,128)(2,1)}, u32[]{:S(2)}, u32[]{:S(2)}) collective-permute-start(bf16[128,512]{1,0:T(8,128)(2,1)} %get-tuple-element.77), channel_id=1, source_target_pairs={{0,7},{1,0},{2,1},{3,2},{4,3},{5,4},{6,5},{7,6},{8,15},{9,8},{10,9... | collective-permute-start | bytes 393224 | tf_op jit(solution)/shard_map/ppermute | solution.py:298
  54.0 4.1 %collective-permute-done.7 = bf16[128,512]{1,0:T(8,128)(2,1)} collective-permute-done((bf16[128,512]{1,0:T(8,128)(2,1)}, bf16[128,512]{1,0:T(8,128)(2,1)}, u32[]{:S(2)}, u32[]{:S(2)}) %collective-permute-start.7) | collective-permute-done | bytes 131104 | tf_op jit(solution)/shard_map/ppermute | solution.py:298
  58.1 1.7 fusion.12
  59.8 10.1 %collective-permute-done.8 = bf16[128,512]{1,0:T(8,128)(2,1)} collective-permute-done((bf16[128,512]{1,0:T(8,128)(2,1)}, bf16[128,512]{1,0:T(8,128)(2,1)}, u32[]{:S(2)}, u32[]{:S(2)}) %collective-permute-start.8) | collective-permute-done | bytes 131104 | tf_op jit(solution)/shard_map/ppermute | solution.py:298
  69.9 1.9 %fusion.9 = (bf16[128,512]{1,0:T(8,128)(2,1)}, bf16[128,512]{1,0:T(8,128)(2,1)}) fusion(bf16[128,512]{1,0:T(8,128)(2,1)} %collective-permute-done.11, bf16[8,128,512]{2,1,0:T(8,128)(2,1)} %bitcast.95, s32[]{:T(128)S(6)} %select_n.164, s32[]{:T(128)S(6)} %select_n.158, bf16[128,512]{1,0:T(8,128)(2,1)} %collective-permute-done.8), kind=kLoop, calls=%fused_computation.18 | loop fusion | flops 524288 | bytes 786440 | tf_op jit(solution)/shard_map/convert_element_type | solution.py:351
  71.9 1.9 %collective-permute-start.9 = (bf16[128,512]{1,0:T(8,128)(2,1)}, bf16[128,512]{1,0:T(8,128)(2,1)}, u32[]{:S(2)}, u32[]{:S(2)}) collective-permute-start(bf16[128,512]{1,0:T(8,128)(2,1)} %get-tuple-element.76), channel_id=1, source_target_pairs={{0,1},{1,2},{2,3},{3,4},{4,5},{5,6},{6,7},{7,0},{8,9},{9,10},{10,1... | collective-permute-start | bytes 393224 | tf_op jit(solution)/shard_map/ppermute | solution.py:298
  74.5 1.3 cross_statistics.1
  75.8 0.9 broadcast_in_dim.71
  76.6 4.3 %all-to-all-start = ((f32[8,16,1024]{2,1,0:T(8,128)}), f32[8,16,1024]{2,1,0:T(8,128)}, u32[]{:S(2)}, u32[]{:S(2)}) async-start(f32[8,16,1024]{2,1,0:T(8,128)} %broadcast_in_dim.71), calls=%async_computation.1 | async-start | bytes 1048576 | tf_op jit(solution)/shard_map/all_to_all | solution.py:303
  81.0 1.9 %fusion.8 = (bf16[128,512]{1,0:T(8,128)(2,1)}, bf16[128,512]{1,0:T(8,128)(2,1)}) fusion(bf16[128,512]{1,0:T(8,128)(2,1)} %collective-permute-done.12, bf16[8,128,512]{2,1,0:T(8,128)(2,1)} %bitcast.96, s32[]{:T(128)S(6)} %select_n.166, s32[]{:T(128)S(6)} %select_n.160, bf16[128,512]{1,0:T(8,128)(2,1)} %collective-permute-done.9), kind=kLoop, calls=%fused_computation.16 | loop fusion | flops 524288 | bytes 786440 | tf_op jit(solution)/shard_map/convert_element_type | solution.py:351
  82.9 1.2 collective-permute-start.10
  84.1 2.0 %collective-permute-start.13 = (bf16[128,512]{1,0:T(8,128)(2,1)}, bf16[128,512]{1,0:T(8,128)(2,1)}, u32[]{:S(2)}, u32[]{:S(2)}) collective-permute-start(bf16[128,512]{1,0:T(8,128)(2,1)} %get-tuple-element.73), channel_id=1, source_target_pairs={{0,7},{1,0},{2,1},{3,2},{4,3},{5,4},{6,5},{7,6},{8,15},{9,8},{10,9... | collective-permute-start | bytes 393224 | tf_op jit(solution)/shard_map/ppermute | solution.py:298
  86.8 4.6 %all-to-all-done.stat_ref = f32[8,16,1024]{2,1,0:T(8,128)} async-done(((f32[8,16,1024]{2,1,0:T(8,128)}), f32[8,16,1024]{2,1,0:T(8,128)}, u32[]{:S(2)}, u32[]{:S(2)}) %all-to-all-start) | async-done | bytes 524320 | tf_op jit(solution)/shard_map/all_to_all | solution.py:303
  91.4 2.6 %cross_grads.1 = (bf16[128,1024]{1,0:T(8,128)(2,1)S(1)}, f32[32,1024]{1,0:T(8,128)S(1)}) custom-call(bf16[1024,1024]{1,0:T(8,128)(2,1)S(1)} %get-tuple-element.51.qg_ref, bf16[32,1024]{1,0:T(8,128)(2,1)S(1)} %get-tuple-element.53.sums_ref, f32[8,16,1024]{2,1,0:T(8,128)} %all-to-all-done.stat_ref), custom_call_target="tpu_custom_call" | custom-call | tf_op jit(solution)/shard_map/cross_grads/pallas_call | solution.py:139
  95.5 0.9 copy-done.6
  96.4 0.9 copy-done.19
  97.3 1.9 %block_softmax.1 = (bf16[128,1024]{1,0:T(8,128)(2,1)}, f32[8,128]{1,0:T(8,128)S(1)}) custom-call(f32[128,512]{1,0:T(8,128)S(1)} %copy-done.19, bf16[128,512]{1,0:T(8,128)(2,1)S(1)} %copy-done.6, bf16[128,512]{1,0:T(8,128)(2,1)} %collective-permute-done.10.forward_ref, bf16[128,512]{1,0:T(8,128)(2,1)} %collective-permute-done.13.back_ref, ...), custom_call_target="tpu_custom_call" | custom-call | tf_op jit(solution)/shard_map/block_softmax/pallas_call | solution.py:172
  99.2 3.2 %collective-permute-start.18 = (bf16[128,1024]{1,0:T(8,128)(2,1)}, bf16[128,1024]{1,0:T(8,128)(2,1)}, u32[]{:S(2)}, u32[]{:S(2)}) collective-permute-start(bf16[128,1024]{1,0:T(8,128)(2,1)} %get-tuple-element.59.refs_0_), channel_id=1, source_target_pairs={{0,7},{1,0},{2,1},{3,2},{4,3},{5,4},{6,5},{7,6},{8,15},{9,8},{10,9... | collective-permute-start | bytes 786440 | tf_op jit(solution)/shard_map/ppermute | solution.py:298
  102.5 6.0 %collective-permute-done.14.refs_1_ = bf16[128,1024]{1,0:T(8,128)(2,1)S(1)} collective-permute-done((bf16[128,1024]{1,0:T(8,128)(2,1)}, bf16[128,1024]{1,0:T(8,128)(2,1)S(1)}, u32[]{:S(2)}, u32[]{:S(2)}) %collective-permute-start.14) | collective-permute-done | bytes 262176 | tf_op jit(solution)/shard_map/ppermute | solution.py:298
  108.5 0.7 copy-done.15
  109.9 3.3 %all-to-all-start.1 = ((f32[8,8,128]{2,1,0:T(8,128)}), f32[8,8,128]{2,1,0:T(8,128)S(1)}, u32[]{:S(2)}, u32[]{:S(2)}) async-start(f32[8,8,128]{2,1,0:T(8,128)} %broadcast_in_dim.72), calls=%async_computation.2 | async-start | bytes 65536 | tf_op jit(solution)/shard_map/all_to_all | solution.py:303
  113.2 3.3 %collective-permute-start.19 = (bf16[128,1024]{1,0:T(8,128)(2,1)}, bf16[128,1024]{1,0:T(8,128)(2,1)}, u32[]{:S(2)}, u32[]{:S(2)}) collective-permute-start(bf16[128,1024]{1,0:T(8,128)(2,1)} %collective-permute-done.18.refs_5_), channel_id=1, source_target_pairs={{0,7},{1,0},{2,1},{3,2},{4,3},{5,4},{6,5},{7,6},{8,15},{9,8},{10,9... | collective-permute-start | bytes 786440 | tf_op jit(solution)/shard_map/ppermute | solution.py:298
  116.8 1.8 %all-to-all-done.1 = f32[8,8,128]{2,1,0:T(8,128)S(1)} async-done(((f32[8,8,128]{2,1,0:T(8,128)}), f32[8,8,128]{2,1,0:T(8,128)S(1)}, u32[]{:S(2)}, u32[]{:S(2)}) %all-to-all-start.1) | async-done | bytes 32800 | tf_op jit(solution)/shard_map/all_to_all | solution.py:303
  118.6 4.3 %collective-permute-done.19.refs_6_ = bf16[128,1024]{1,0:T(8,128)(2,1)} collective-permute-done((bf16[128,1024]{1,0:T(8,128)(2,1)}, bf16[128,1024]{1,0:T(8,128)(2,1)}, u32[]{:S(2)}, u32[]{:S(2)}) %collective-permute-start.19) | collective-permute-done | bytes 262176 | tf_op jit(solution)/shard_map/ppermute | solution.py:298
  122.9 3.7 %collective-permute-start.20 = (bf16[128,1024]{1,0:T(8,128)(2,1)}, bf16[128,1024]{1,0:T(8,128)(2,1)S(1)}, u32[]{:S(2)}, u32[]{:S(2)}) collective-permute-start(bf16[128,1024]{1,0:T(8,128)(2,1)} %collective-permute-done.19.refs_6_), channel_id=1, source_target_pairs={{0,7},{1,0},{2,1},{3,2},{4,3},{5,4},{6,5},{7,6},{8,15},{9,8},{10,9... | collective-permute-start | bytes 786440 | tf_op jit(solution)/shard_map/ppermute | solution.py:298
  127.4 12.5 %all_to_all.15.scale_ref = f32[8,2,128]{2,1,0:T(2,128)S(1)} all-to-all(f32[8,2,128]{2,1,0:T(2,128)S(1)} %broadcast_in_dim.73), channel_id=1, replica_groups=mesh['row'=32,'col'=8] {'col'}, dimensions={0} | all-to-all | bytes 16384 | tf_op jit(solution)/shard_map/all_to_all | solution.py:303
  139.9 0.9 copy-done.14
  140.8 0.9 copy-done.16
  141.8 0.9 copy-done.18
  142.7 3.0 %query_grads.1 = (bf16[1024,512]{1,0:T(8,128)(2,1)S(1)}, bf16[1024,512]{1,0:T(8,128)(2,1)S(1)}, f32[512,512]{1,0:T(8,128)S(1)}, bf16[512,512]{1,0:T(8,128)(2,1)S(1)}) custom-call(s32[2]{0:T(128)S(1)} %pad_add_fusion.place_ref, f32[8,2,128]{2,1,0:T(2,128)S(1)} %all_to_all.15.scale_ref, bf16[512,1024]{1,0:T(8,128)(2,1)S(1)} %get-tuple-element.52.kv_ref, ...), custom_call_target="tpu_custom_call" | custom-call | tf_op jit(solution)/shard_map/query_grads/pallas_call | solution.py:221
  146.1 1.3 key_grads.1
  147.4 0.9 collective-permute-start.22
  148.2 1.1 collective-permute-start.26
  149.3 1.9 %collective-permute-start.27 = (bf16[128,1024]{1,0:T(8,128)(2,1)S(1)}, bf16[128,1024]{1,0:T(8,128)(2,1)S(1)}, u32[]{:S(2)}, u32[]{:S(2)}) collective-permute-start(bf16[128,1024]{1,0:T(8,128)(2,1)S(1)} %get-tuple-element.70), channel_id=1, source_target_pairs={{0,64},{8,72},{16,80},{24,88},{32,96},{40,104},{48,112},{56,120},{... | collective-permute-start | bytes 786440 | tf_op jit(solution)/shard_map/ppermute | solution.py:289
  151.4 10.3 %collective-permute-done.22 = bf16[128,1024]{1,0:T(8,128)(2,1)S(1)} collective-permute-done((bf16[128,1024]{1,0:T(8,128)(2,1)S(1)}, bf16[128,1024]{1,0:T(8,128)(2,1)S(1)}, u32[]{:S(2)}, u32[]{:S(2)}) %collective-permute-start.22) | collective-permute-done | bytes 262176 | tf_op jit(solution)/shard_map/ppermute | solution.py:289
  161.8 3.0 %collective-permute-start.23 = (bf16[128,512]{1,0:T(8,128)(2,1)S(1)}, bf16[128,512]{1,0:T(8,128)(2,1)S(1)}, u32[]{:S(2)}, u32[]{:S(2)}) collective-permute-start(bf16[128,512]{1,0:T(8,128)(2,1)S(1)} %get-tuple-element.80), channel_id=1, source_target_pairs={{0,48},{8,56},{16,0},{24,8},{32,16},{40,24},{48,32},{56,40},{64,11... | collective-permute-start | bytes 393224 | tf_op jit(solution)/shard_map/ppermute | solution.py:292
  164.8 0.8 collective-permute-start.24
  165.6 0.9 collective-permute-start.25
  168.1 3.2 %collective-permute-done.24 = bf16[128,512]{1,0:T(8,128)(2,1)S(1)} collective-permute-done((bf16[128,512]{1,0:T(8,128)(2,1)S(1)}, bf16[128,512]{1,0:T(8,128)(2,1)S(1)}, u32[]{:S(2)}, u32[]{:S(2)}) %collective-permute-start.24) | collective-permute-done | bytes 131104 | tf_op jit(solution)/shard_map/ppermute | solution.py:292
  171.3 1.3 collective-permute-done.25
  (93 shorter events, 11.2 us)
Async XLA Ops:
  7.2 88.3 %reduce-scatter.2.cloned.1.call-start = ((), (), s32[]{:S(2)}) async-start(), calls=%async_computation.4 | async-start | bytes 2359296 | tf_op jit(solution)/shard_map/reduce_scatter | solution.py:337
  9.6 1.3 copy-start.22
  10.9 9.3 %collective-permute-start = (bf16[128,1024]{1,0:T(8,128)(2,1)S(1)}, bf16[128,1024]{1,0:T(8,128)(2,1)S(1)}, u32[]{:S(2)}, u32[]{:S(2)}) collective-permute-start(bf16[128,1024]{1,0:T(8,128)(2,1)S(1)} %pad_maximum_fusion), channel_id=1, source_target_pairs={{0,16},{8,24},{16,32},{24,40},{32,48},{40,56},{48,0},{56,8},{64,80... | collective-permute-start | bytes 786440 | tf_op jit(solution)/shard_map/ppermute | solution.py:292
  12.5 18.1 %collective-permute-start.3 = (bf16[144,1024]{1,0:T(8,128)(2,1)S(1)}, bf16[144,1024]{1,0:T(8,128)(2,1)S(1)}, u32[]{:S(2)}, u32[]{:S(2)}) collective-permute-start(bf16[144,1024]{1,0:T(8,128)(2,1)S(1)} %fusion.1.refs_0_), channel_id=1, source_target_pairs={{0,64},{8,72},{16,80},{24,88},{32,96},{40,104},{48,112},{56,120},{... | collective-permute-start | bytes 884744 | tf_op jit(solution)/shard_map/ppermute | solution.py:289
  14.1 17.2 %collective-permute-start.4 = (bf16[144,1024]{1,0:T(8,128)(2,1)S(1)}, bf16[144,1024]{1,0:T(8,128)(2,1)S(1)}, u32[]{:S(2)}, u32[]{:S(2)}) collective-permute-start(bf16[144,1024]{1,0:T(8,128)(2,1)S(1)} %fusion.1.refs_0_), channel_id=1, source_target_pairs={{0,128},{8,136},{16,144},{24,152},{32,160},{40,168},{48,176},{56,1... | collective-permute-start | bytes 884744 | tf_op jit(solution)/shard_map/ppermute | solution.py:289
  15.3 16.6 %collective-permute-start.5 = (bf16[144,1024]{1,0:T(8,128)(2,1)S(1)}, bf16[144,1024]{1,0:T(8,128)(2,1)S(1)}, u32[]{:S(2)}, u32[]{:S(2)}) collective-permute-start(bf16[144,1024]{1,0:T(8,128)(2,1)S(1)} %fusion.1.refs_0_), channel_id=1, source_target_pairs={{0,192},{8,200},{16,208},{24,216},{32,224},{40,232},{48,240},{56,2... | collective-permute-start | bytes 884744 | tf_op jit(solution)/shard_map/ppermute | solution.py:289
  17.4 9.4 %collective-permute-start.1 = (bf16[128,1024]{1,0:T(8,128)(2,1)S(1)}, bf16[128,1024]{1,0:T(8,128)(2,1)S(1)}, u32[]{:S(2)}, u32[]{:S(2)}) collective-permute-start(bf16[128,1024]{1,0:T(8,128)(2,1)S(1)} %pad_maximum_fusion), channel_id=1, source_target_pairs={{0,32},{8,40},{16,48},{24,56},{32,0},{40,8},{48,16},{56,24},{64,96... | collective-permute-start | bytes 786440 | tf_op jit(solution)/shard_map/ppermute | solution.py:292
  20.2 10.3 %collective-permute-start.2 = (bf16[128,1024]{1,0:T(8,128)(2,1)S(1)}, bf16[128,1024]{1,0:T(8,128)(2,1)S(1)}, u32[]{:S(2)}, u32[]{:S(2)}) collective-permute-start(bf16[128,1024]{1,0:T(8,128)(2,1)S(1)} %pad_maximum_fusion), channel_id=1, source_target_pairs={{0,48},{8,56},{16,0},{24,8},{32,16},{40,24},{48,32},{56,40},{64,11... | collective-permute-start | bytes 786440 | tf_op jit(solution)/shard_map/ppermute | solution.py:292
  30.5 0.7 copy-start.7
  31.3 0.7 copy-start.9
  32.0 0.7 copy-start.11
  33.0 2.7 %collective-permute-start.6 = (bf16[4,128,1024]{2,1,0:T(8,128)(2,1)S(1)}, bf16[4,128,1024]{2,1,0:T(8,128)(2,1)S(1)}, u32[]{:S(2)}, u32[]{:S(2)}) collective-permute-start(bf16[4,128,1024]{2,1,0:T(8,128)(2,1)S(1)} %bitcast_dynamic-update-slice_fusion.line_ref), channel_id=1, source_target_pairs={{0,8},{8,0},{16,24},{24,16},{32,40},{40,32},{48,56},{56,48},{64,72... | collective-permute-start | bytes 3145736 | tf_op jit(solution)/shard_map/ppermute | solution.py:295
  33.1 1.0 copy-start
  35.7 1.0 copy-start.3
  36.7 1.2 copy-start.1
  37.9 1.2 copy-start.4
  39.2 1.0 copy-start.8
  40.1 1.0 copy-start.10
  41.1 1.0 copy-start.12
  44.0 1.3 copy-start.2
  45.3 1.0 copy-start.5
  48.2 10.0 %collective-permute-start.7 = (bf16[128,512]{1,0:T(8,128)(2,1)}, bf16[128,512]{1,0:T(8,128)(2,1)}, u32[]{:S(2)}, u32[]{:S(2)}) collective-permute-start(bf16[128,512]{1,0:T(8,128)(2,1)} %get-tuple-element.78), channel_id=1, source_target_pairs={{0,1},{1,2},{2,3},{3,4},{4,5},{5,6},{6,7},{7,0},{8,9},{9,10},{10,1... | collective-permute-start | bytes 393224 | tf_op jit(solution)/shard_map/ppermute | solution.py:298
  50.1 9.7 %collective-permute-start.11 = (bf16[128,512]{1,0:T(8,128)(2,1)}, bf16[128,512]{1,0:T(8,128)(2,1)}, u32[]{:S(2)}, u32[]{:S(2)}) collective-permute-start(bf16[128,512]{1,0:T(8,128)(2,1)} %get-tuple-element.77), channel_id=1, source_target_pairs={{0,7},{1,0},{2,1},{3,2},{4,3},{5,4},{6,5},{7,6},{8,15},{9,8},{10,9... | collective-permute-start | bytes 393224 | tf_op jit(solution)/shard_map/ppermute | solution.py:298
  59.8 10.1 %collective-permute-start.8 = (bf16[128,512]{1,0:T(8,128)(2,1)}, bf16[128,512]{1,0:T(8,128)(2,1)}, u32[]{:S(2)}, u32[]{:S(2)}) collective-permute-start(bf16[128,512]{1,0:T(8,128)(2,1)} %fusion.12), channel_id=1, source_target_pairs={{0,1},{1,2},{2,3},{3,4},{4,5},{5,6},{6,7},{7,0},{8,9},{9,10},{10,1... | collective-permute-start | bytes 393224 | tf_op jit(solution)/shard_map/ppermute | solution.py:298
  71.8 9.2 %collective-permute-start.12 = (bf16[128,512]{1,0:T(8,128)(2,1)}, bf16[128,512]{1,0:T(8,128)(2,1)}, u32[]{:S(2)}, u32[]{:S(2)}) collective-permute-start(bf16[128,512]{1,0:T(8,128)(2,1)} %get-tuple-element.75), channel_id=1, source_target_pairs={{0,7},{1,0},{2,1},{3,2},{4,3},{5,4},{6,5},{7,6},{8,15},{9,8},{10,9... | collective-permute-start | bytes 393224 | tf_op jit(solution)/shard_map/ppermute | solution.py:298
  71.9 9.1 %collective-permute-start.9 = (bf16[128,512]{1,0:T(8,128)(2,1)}, bf16[128,512]{1,0:T(8,128)(2,1)}, u32[]{:S(2)}, u32[]{:S(2)}) collective-permute-start(bf16[128,512]{1,0:T(8,128)(2,1)} %get-tuple-element.76), channel_id=1, source_target_pairs={{0,1},{1,2},{2,3},{3,4},{4,5},{5,6},{6,7},{7,0},{8,9},{9,10},{10,1... | collective-permute-start | bytes 393224 | tf_op jit(solution)/shard_map/ppermute | solution.py:298
  76.6 14.8 %all-to-all-start = ((f32[8,16,1024]{2,1,0:T(8,128)}), f32[8,16,1024]{2,1,0:T(8,128)}, u32[]{:S(2)}, u32[]{:S(2)}) async-start(f32[8,16,1024]{2,1,0:T(8,128)} %broadcast_in_dim.71), calls=%async_computation.1 | async-start | bytes 1048576 | tf_op jit(solution)/shard_map/all_to_all | solution.py:303
  82.9 12.6 %collective-permute-start.10 = (bf16[128,512]{1,0:T(8,128)(2,1)}, bf16[128,512]{1,0:T(8,128)(2,1)}, u32[]{:S(2)}, u32[]{:S(2)}) collective-permute-start(bf16[128,512]{1,0:T(8,128)(2,1)} %get-tuple-element.74), channel_id=1, source_target_pairs={{0,1},{1,2},{2,3},{3,4},{4,5},{5,6},{6,7},{7,0},{8,9},{9,10},{10,1... | collective-permute-start | bytes 393224 | tf_op jit(solution)/shard_map/ppermute | solution.py:298
  84.1 11.4 %collective-permute-start.13 = (bf16[128,512]{1,0:T(8,128)(2,1)}, bf16[128,512]{1,0:T(8,128)(2,1)}, u32[]{:S(2)}, u32[]{:S(2)}) collective-permute-start(bf16[128,512]{1,0:T(8,128)(2,1)} %get-tuple-element.73), channel_id=1, source_target_pairs={{0,7},{1,0},{2,1},{3,2},{4,3},{5,4},{6,5},{7,6},{8,15},{9,8},{10,9... | collective-permute-start | bytes 393224 | tf_op jit(solution)/shard_map/ppermute | solution.py:298
  94.1 0.7 copy-start.13
  94.8 0.7 copy-start.20
  95.5 0.9 copy-start.6
  96.4 0.9 copy-start.19
  99.2 9.3 %collective-permute-start.14 = (bf16[128,1024]{1,0:T(8,128)(2,1)}, bf16[128,1024]{1,0:T(8,128)(2,1)S(1)}, u32[]{:S(2)}, u32[]{:S(2)}) collective-permute-start(bf16[128,1024]{1,0:T(8,128)(2,1)} %get-tuple-element.59.refs_0_), channel_id=1, source_target_pairs={{0,1},{1,2},{2,3},{3,4},{4,5},{5,6},{6,7},{7,0},{8,9},{9,10},{10,1... | collective-permute-start | bytes 786440 | tf_op jit(solution)/shard_map/ppermute | solution.py:298
  99.2 14.0 %collective-permute-start.18 = (bf16[128,1024]{1,0:T(8,128)(2,1)}, bf16[128,1024]{1,0:T(8,128)(2,1)}, u32[]{:S(2)}, u32[]{:S(2)}) collective-permute-start(bf16[128,1024]{1,0:T(8,128)(2,1)} %get-tuple-element.59.refs_0_), channel_id=1, source_target_pairs={{0,7},{1,0},{2,1},{3,2},{4,3},{5,4},{6,5},{7,6},{8,15},{9,8},{10,9... | collective-permute-start | bytes 786440 | tf_op jit(solution)/shard_map/ppermute | solution.py:298
  108.5 8.3 %collective-permute-start.15 = (bf16[128,1024]{1,0:T(8,128)(2,1)S(1)}, bf16[128,1024]{1,0:T(8,128)(2,1)}, u32[]{:S(2)}, u32[]{:S(2)}) collective-permute-start(bf16[128,1024]{1,0:T(8,128)(2,1)S(1)} %collective-permute-done.14.refs_1_), channel_id=1, source_target_pairs={{0,1},{1,2},{2,3},{3,4},{4,5},{5,6},{6,7},{7,0},{8,9},{9,10},{10,1... | collective-permute-start | bytes 786440 | tf_op jit(solution)/shard_map/ppermute | solution.py:298
  108.5 0.7 copy-start.15
  109.9 8.7 %all-to-all-start.1 = ((f32[8,8,128]{2,1,0:T(8,128)}), f32[8,8,128]{2,1,0:T(8,128)S(1)}, u32[]{:S(2)}, u32[]{:S(2)}) async-start(f32[8,8,128]{2,1,0:T(8,128)} %broadcast_in_dim.72), calls=%async_computation.2 | async-start | bytes 65536 | tf_op jit(solution)/shard_map/all_to_all | solution.py:303
  113.2 9.7 %collective-permute-start.19 = (bf16[128,1024]{1,0:T(8,128)(2,1)}, bf16[128,1024]{1,0:T(8,128)(2,1)}, u32[]{:S(2)}, u32[]{:S(2)}) collective-permute-start(bf16[128,1024]{1,0:T(8,128)(2,1)} %collective-permute-done.18.refs_5_), channel_id=1, source_target_pairs={{0,7},{1,0},{2,1},{3,2},{4,3},{5,4},{6,5},{7,6},{8,15},{9,8},{10,9... | collective-permute-start | bytes 786440 | tf_op jit(solution)/shard_map/ppermute | solution.py:298
  116.8 9.8 %collective-permute-start.16 = (bf16[128,1024]{1,0:T(8,128)(2,1)}, bf16[128,1024]{1,0:T(8,128)(2,1)S(1)}, u32[]{:S(2)}, u32[]{:S(2)}) collective-permute-start(bf16[128,1024]{1,0:T(8,128)(2,1)} %collective-permute-done.15.refs_2_), channel_id=1, source_target_pairs={{0,1},{1,2},{2,3},{3,4},{4,5},{5,6},{6,7},{7,0},{8,9},{9,10},{10,1... | collective-permute-start | bytes 786440 | tf_op jit(solution)/shard_map/ppermute | solution.py:298
  122.9 17.0 %collective-permute-start.20 = (bf16[128,1024]{1,0:T(8,128)(2,1)}, bf16[128,1024]{1,0:T(8,128)(2,1)S(1)}, u32[]{:S(2)}, u32[]{:S(2)}) collective-permute-start(bf16[128,1024]{1,0:T(8,128)(2,1)} %collective-permute-done.19.refs_6_), channel_id=1, source_target_pairs={{0,7},{1,0},{2,1},{3,2},{4,3},{5,4},{6,5},{7,6},{8,15},{9,8},{10,9... | collective-permute-start | bytes 786440 | tf_op jit(solution)/shard_map/ppermute | solution.py:298
  126.6 13.3 %collective-permute-start.17 = (bf16[128,1024]{1,0:T(8,128)(2,1)S(1)}, bf16[128,1024]{1,0:T(8,128)(2,1)S(1)}, u32[]{:S(2)}, u32[]{:S(2)}) collective-permute-start(bf16[128,1024]{1,0:T(8,128)(2,1)S(1)} %collective-permute-done.16.refs_3_), channel_id=1, source_target_pairs={{0,1},{1,2},{2,3},{3,4},{4,5},{5,6},{6,7},{7,0},{8,9},{9,10},{10,1... | collective-permute-start | bytes 786440 | tf_op jit(solution)/shard_map/ppermute | solution.py:298
  126.6 0.7 copy-start.17
  139.9 1.0 copy-start.14
  140.8 0.9 copy-start.16
  141.8 0.9 copy-start.18
  142.7 3.3 %copy-start.21 = (f32[32,1024]{1,0:T(8,128)S(1)}, f32[32,1024]{1,0:T(8,128)}, u32[]{:S(2)}) copy-start(f32[32,1024]{1,0:T(8,128)} %copy-done.20) | copy-start | bytes 393220
  145.7 5.5 %collective-permute-start.21 = (bf16[512,512]{1,0:T(8,128)(2,1)S(1)}, bf16[512,512]{1,0:T(8,128)(2,1)S(1)}, u32[]{:S(2)}, u32[]{:S(2)}) collective-permute-start(bf16[512,512]{1,0:T(8,128)(2,1)S(1)} %get-tuple-element.61), channel_id=1, source_target_pairs={{0,8},{8,0},{16,24},{24,16},{32,40},{40,32},{48,56},{56,48},{64,72... | collective-permute-start | bytes 1572872 | tf_op jit(solution)/shard_map/ppermute | solution.py:295
  147.4 14.4 %collective-permute-start.22 = (bf16[128,1024]{1,0:T(8,128)(2,1)S(1)}, bf16[128,1024]{1,0:T(8,128)(2,1)S(1)}, u32[]{:S(2)}, u32[]{:S(2)}) collective-permute-start(bf16[128,1024]{1,0:T(8,128)(2,1)S(1)} %get-tuple-element.65), channel_id=1, source_target_pairs={{0,192},{8,200},{16,208},{24,216},{32,224},{40,232},{48,240},{56,2... | collective-permute-start | bytes 786440 | tf_op jit(solution)/shard_map/ppermute | solution.py:289
  148.2 18.2 %collective-permute-start.26 = (bf16[128,1024]{1,0:T(8,128)(2,1)S(1)}, bf16[128,1024]{1,0:T(8,128)(2,1)S(1)}, u32[]{:S(2)}, u32[]{:S(2)}) collective-permute-start(bf16[128,1024]{1,0:T(8,128)(2,1)S(1)} %get-tuple-element.69), channel_id=1, source_target_pairs={{0,128},{8,136},{16,144},{24,152},{32,160},{40,168},{48,176},{56,1... | collective-permute-start | bytes 786440 | tf_op jit(solution)/shard_map/ppermute | solution.py:289
  149.3 17.2 %collective-permute-start.27 = (bf16[128,1024]{1,0:T(8,128)(2,1)S(1)}, bf16[128,1024]{1,0:T(8,128)(2,1)S(1)}, u32[]{:S(2)}, u32[]{:S(2)}) collective-permute-start(bf16[128,1024]{1,0:T(8,128)(2,1)S(1)} %get-tuple-element.70), channel_id=1, source_target_pairs={{0,64},{8,72},{16,80},{24,88},{32,96},{40,104},{48,112},{56,120},{... | collective-permute-start | bytes 786440 | tf_op jit(solution)/shard_map/ppermute | solution.py:289
  151.3 15.4 %copy-start.23 = (pred[128,4,128]{2,1,0:T(4,128)(4,1)S(1)}, pred[128,4,128]{2,1,0:T(4,128)(4,1)}, u32[]{:S(2)}) copy-start(pred[128,4,128]{2,1,0:T(4,128)(4,1)} %copy-done.22) | copy-start | bytes 196612
  161.8 6.3 %collective-permute-start.23 = (bf16[128,512]{1,0:T(8,128)(2,1)S(1)}, bf16[128,512]{1,0:T(8,128)(2,1)S(1)}, u32[]{:S(2)}, u32[]{:S(2)}) collective-permute-start(bf16[128,512]{1,0:T(8,128)(2,1)S(1)} %get-tuple-element.80), channel_id=1, source_target_pairs={{0,48},{8,56},{16,0},{24,8},{32,16},{40,24},{48,32},{56,40},{64,11... | collective-permute-start | bytes 393224 | tf_op jit(solution)/shard_map/ppermute | solution.py:292
  164.8 6.6 %collective-permute-start.24 = (bf16[128,512]{1,0:T(8,128)(2,1)S(1)}, bf16[128,512]{1,0:T(8,128)(2,1)S(1)}, u32[]{:S(2)}, u32[]{:S(2)}) collective-permute-start(bf16[128,512]{1,0:T(8,128)(2,1)S(1)} %get-tuple-element.82), channel_id=1, source_target_pairs={{0,32},{8,40},{16,48},{24,56},{32,0},{40,8},{48,16},{56,24},{64,96... | collective-permute-start | bytes 393224 | tf_op jit(solution)/shard_map/ppermute | solution.py:292
  165.6 7.0 %collective-permute-start.25 = (bf16[128,512]{1,0:T(8,128)(2,1)S(1)}, bf16[128,512]{1,0:T(8,128)(2,1)S(1)}, u32[]{:S(2)}, u32[]{:S(2)}) collective-permute-start(bf16[128,512]{1,0:T(8,128)(2,1)S(1)} %get-tuple-element.81), channel_id=1, source_target_pairs={{0,16},{8,24},{16,32},{24,40},{32,48},{40,56},{48,0},{56,8},{64,80... | collective-permute-start | bytes 393224 | tf_op jit(solution)/shard_map/ppermute | solution.py:292
Sparse Core Ops, SparseCore 0:
  46.4 47.0 reduce-scatter.1

commit v6 on v5

--- a/solution.py
+++ b/solution.py
@@ -16,9 +16,9 @@
 LEAD_PAIR = (((0,), (0,)), ((), ()))
 PLAIN = (((1,), (0,)), ((), ()))
 
-VMEM = pl.BlockSpec(memory_space=pltpu.VMEM)
+WHOLE = pl.BlockSpec()
 SMEM = pl.BlockSpec(memory_space=pltpu.SMEM)
-ROOM = pltpu.CompilerParams(vmem_limit_bytes=40 * 1024 * 1024)
+ROOM = pltpu.CompilerParams(vmem_limit_bytes=24 * 1024 * 1024)
 
 
 def dot_f32(left, right, dims=PLAIN):
@@ -37,62 +37,33 @@
     return jnp.sum(jnp.where(diagonal(row.shape[1]), row, 0.0), axis=1, keepdims=True)
 
 
-def block_products(place, line, other_line, key_pieces, rows_dev, flat_width):
-    lines = line.shape[0]
-    block_rows, block_keys = 2 * lines * rows_dev, len(key_pieces) * rows_dev
-
-    def kernel(place_ref, line_ref, other_ref, *refs):
-        piece_refs, (qg_ref, kv_ref, logit_ref, dprob_ref) = refs[:-4], refs[-4:]
-        core = place_ref[0]
-        for s, piece_ref in enumerate(piece_refs):
-            kv_ref[s * rows_dev : (s + 1) * rows_dev, :] = piece_ref[:rows_dev, :]
-        for x in range(lines):
-            mine = pl.multiple_of((2 * x + core) * rows_dev, rows_dev)
-            theirs = pl.multiple_of((2 * x + 1 - core) * rows_dev, rows_dev)
-            qg_ref[pl.ds(mine, rows_dev), :] = line_ref[x]
-            qg_ref[pl.ds(theirs, rows_dev), :] = other_ref[x]
-        logit_ref[...] = dot_f32(qg_ref[:, :flat_width], kv_ref[:, :flat_width], ROW_PAIR)
-        dprob_ref[...] = dot_f32(qg_ref[:, flat_width:], kv_ref[:, flat_width:], ROW_PAIR).astype(
-            jnp.bfloat16
-        )
-
-    return pl.pallas_call(
-        kernel,
-        in_specs=[SMEM] + [VMEM] * (2 + len(key_pieces)),
-        out_shape=(
-            jax.ShapeDtypeStruct((block_rows, 2 * flat_width), jnp.bfloat16),
-            jax.ShapeDtypeStruct((block_keys, 2 * flat_width), jnp.bfloat16),
-            jax.ShapeDtypeStruct((block_rows, block_keys), jnp.float32),
-            jax.ShapeDtypeStruct((block_rows, block_keys), jnp.bfloat16),
-        ),
-        compiler_params=ROOM,
-        name="block_products",
-    )(place, line, other_line, *key_pieces)
-
-
-def cross_scores(sums_ref, qg_ref, column, feature, inv_root):
-    flat_width = qg_ref.shape[1] // 2
+def cross_scores(sums_ref, q_ref, g_ref, column, feature, inv_root):
+    flat_width = q_ref.shape[1]
     lanes = slice(column * feature, (column + 1) * feature)
     other = slice(flat_width + column * feature, flat_width + (column + 1) * feature)
-    scores = dot_f32(sums_ref[:, lanes], qg_ref[:, lanes], ROW_PAIR) * inv_root
-    dprob = dot_f32(sums_ref[:, other], qg_ref[:, other], ROW_PAIR)
+    scores = dot_f32(sums_ref[:, lanes], q_ref[:, lanes], ROW_PAIR) * inv_root
+    dprob = dot_f32(sums_ref[:, other], g_ref[:, lanes], ROW_PAIR)
     return scores, dprob, lanes, other
 
 
-def cross_statistics(qg_blk, kv_blk, tokens, feature, inv_root):
-    block_keys, both_width = kv_blk.shape
-    block_rows = qg_blk.shape[0]
+def cross_statistics(q_blk, g_blk, k_blk, v_blk, tokens, feature, inv_root):
+    block_keys, flat_width = k_blk.shape
+    both_width = 2 * flat_width
+    block_rows = q_blk.shape[0]
     group = block_keys // tokens
     columns = both_width // (2 * feature)
     stat_rows = -(-3 * columns // 8) * 8
 
-    def kernel(qg_ref, kv_ref, sums_ref, stat_ref):
-        pooled = jnp.sum(
-            kv_ref[...].astype(jnp.float32).reshape(tokens, group, both_width), axis=1
-        )
-        sums_ref[...] = (pooled / group).astype(jnp.bfloat16)
+    def kernel(q_ref, g_ref, k_ref, v_ref, sums_ref, stat_ref):
+        for half, table_ref in enumerate((k_ref, v_ref)):
+            pooled = jnp.sum(
+                table_ref[...].astype(jnp.float32).reshape(tokens, group, flat_width), axis=1
+            )
+            sums_ref[:, half * flat_width : (half + 1) * flat_width] = (pooled / group).astype(
+                jnp.bfloat16
+            )
         for c in range(columns):
-            scores, dprob, _, _ = cross_scores(sums_ref, qg_ref, c, feature, inv_root)
+            scores, dprob, _, _ = cross_scores(sums_ref, q_ref, g_ref, c, feature, inv_root)
             peak = jnp.max(scores, axis=0, keepdims=True)
             lifted = jnp.exp(scores - peak)
             stat_ref[c : c + 1, :] = peak
@@ -107,45 +78,43 @@
 
     return pl.pallas_call(
         kernel,
-        in_specs=[VMEM] * 2,
         out_shape=(
             jax.ShapeDtypeStruct((tokens, both_width), jnp.bfloat16),
             jax.ShapeDtypeStruct((stat_rows, block_rows), jnp.float32),
         ),
         compiler_params=ROOM,
         name="cross_statistics",
-    )(qg_blk, kv_blk)
-
-
-def cross_grads(qg_blk, sums, all_stats, feature, inv_root):
+    )(q_blk, g_blk, k_blk, v_blk)
+
+
+def cross_grads(q_blk, g_blk, sums, all_stats, feature, inv_root):
     tokens, both_width = sums.shape
-    block_rows = qg_blk.shape[0]
+    block_rows = q_blk.shape[0]
     columns = both_width // (2 * feature)
 
-    def kernel(qg_ref, sums_ref, stat_ref, dl_ref, dsum_ref):
+    def kernel(q_ref, g_ref, sums_ref, stat_ref, dl_ref, dsum_ref):
         peaks = stat_ref[:, :columns, :]
         peak = jnp.max(peaks, axis=0)
         weight = jnp.exp(peaks - peak[None])
         total = jnp.sum(weight * stat_ref[:, columns : 2 * columns, :], axis=0)
         delta = jnp.sum(weight * stat_ref[:, 2 * columns : 3 * columns, :], axis=0) / total
         for c in range(columns):
-            scores, dprob, lanes, other = cross_scores(sums_ref, qg_ref, c, feature, inv_root)
+            scores, dprob, lanes, other = cross_scores(sums_ref, q_ref, g_ref, c, feature, inv_root)
             probs = jnp.exp(scores - peak[c : c + 1, :]) / total[c : c + 1, :]
             dl = (inv_root * probs * (dprob - delta[c : c + 1, :])).astype(jnp.bfloat16)
             dl_ref[c * tokens : (c + 1) * tokens, :] = dl
-            dsum_ref[:, lanes] = dot_f32(dl, qg_ref[:, lanes])
-            dsum_ref[:, other] = dot_f32(probs.astype(jnp.bfloat16), qg_ref[:, other])
-
-    return pl.pallas_call(
-        kernel,
-        in_specs=[VMEM] * 3,
+            dsum_ref[:, lanes] = dot_f32(dl, q_ref[:, lanes])
+            dsum_ref[:, other] = dot_f32(probs.astype(jnp.bfloat16), g_ref[:, lanes])
+
+    return pl.pallas_call(
+        kernel,
         out_shape=(
             jax.ShapeDtypeStruct((columns * tokens, block_rows), jnp.bfloat16),
             jax.ShapeDtypeStruct((tokens, both_width), jnp.float32),
         ),
         compiler_params=ROOM,
         name="cross_grads",
-    )(qg_blk, sums, all_stats)
+    )(q_blk, g_blk, sums, all_stats)
 
 
 def block_softmax(logit_scale, logit_sum, own, forward, back, key_flags):
@@ -171,7 +140,6 @@
 
     return pl.pallas_call(
         kernel,
-        in_specs=[VMEM] * 5,
         out_shape=(
             jax.ShapeDtypeStruct((rows, 2 * width), jnp.bfloat16),
             jax.ShapeDtypeStruct((8, rows), jnp.float32),
@@ -181,31 +149,26 @@
     )(logit_sum, own, forward, back, key_flags)
 
 
-def query_grads(logit_scale, place, pieces, steps, scaling, kv_blk, cross_dl, sums):
-    rows, width = pieces[0].shape[0], pieces[0].shape[1] // 2
-    chunks = len(pieces)
-    block_rows = chunks * rows
-    flat_width = kv_blk.shape[1] // 2
+def query_grads(logit_scale, place, both, scaling, k_blk, cross_dl, sums, chunks):
+    block_rows, width = both.shape[0], both.shape[1] // 2
+    rows = block_rows // chunks
+    flat_width = k_blk.shape[1]
     tokens = sums.shape[0]
     columns = cross_dl.shape[0] // tokens
     feature = flat_width // columns
 
-    def kernel(place_ref, scale_ref, kv_ref, dl_ref, sums_ref, *refs):
-        piece_refs = refs[:chunks]
-        p_ref, ds_ref, own_ref, other_ref, dq_ref = refs[chunks:]
-        core, own_z = place_ref[0], place_ref[1]
-        for piece_ref, step in zip(piece_refs, steps):
-            source = lax.rem(own_z + (2 * chunks - step), chunks)
-            scale = scale_ref[source]
-            weight, offset = upright(scale[0:1, :]), upright(scale[1:2, :])
-            lifted = piece_ref[:, :width].astype(jnp.float32)
-            tilted = piece_ref[:, width:].astype(jnp.float32)
-            at = pl.ds(pl.multiple_of(source * rows, rows), rows)
+    def kernel(place_ref, both_ref, scale_ref, k_ref, dl_ref, sums_ref, p_ref, ds_ref, own_ref, other_ref, dq_ref):
+        core = place_ref[0]
+        for i in range(chunks):
+            at = slice(i * rows, (i + 1) * rows)
+            weight, offset = upright(scale_ref[i, 0:1, :]), upright(scale_ref[i, 1:2, :])
+            lifted = both_ref[at, :width].astype(jnp.float32)
+            tilted = both_ref[at, width:].astype(jnp.float32)
             p_ref[at, :] = (lifted * weight).astype(jnp.bfloat16)
             ds_ref[at, :] = ((tilted - lifted * offset) * (weight * logit_scale)).astype(
                 jnp.bfloat16
             )
-        dq_ref[...] = dot_f32(ds_ref[...], kv_ref[:, :flat_width])
+        dq_ref[...] = dot_f32(ds_ref[...], k_ref[...])
         for c in range(columns):
             lanes = slice(c * feature, (c + 1) * feature)
             dq_ref[:, lanes] += dot_f32(
@@ -220,7 +183,7 @@
 
     return pl.pallas_call(
         kernel,
-        in_specs=[SMEM] + [VMEM] * (4 + chunks),
+        in_specs=[SMEM] + [WHOLE] * 5,
         out_shape=(
             jax.ShapeDtypeStruct((block_rows, width), jnp.bfloat16),
             jax.ShapeDtypeStruct((block_rows, width), jnp.bfloat16),
@@ -230,19 +193,19 @@
         scratch_shapes=[pltpu.VMEM((block_rows, flat_width), jnp.float32)],
         compiler_params=ROOM,
         name="query_grads",
-    )(place, scaling, kv_blk, cross_dl, sums, *pieces)
-
-
-def key_grads(prob, dlogit, qg_blk, dsum, pieces):
-    width, flat_width = prob.shape[1], qg_blk.shape[1] // 2
+    )(place, both, scaling, k_blk, cross_dl, sums)
+
+
+def key_grads(prob, dlogit, q_blk, g_blk, dsum, pieces):
+    width, flat_width = prob.shape[1], q_blk.shape[1]
     tokens = dsum.shape[0]
     group = width // tokens
     piece = width // pieces
 
-    def kernel(p_ref, ds_ref, qg_ref, dsum_ref, *out_refs):
-        for half, w_ref in enumerate((ds_ref, p_ref)):
+    def kernel(p_ref, ds_ref, q_ref, g_ref, dsum_ref, *out_refs):
+        for half, (w_ref, t_ref) in enumerate(((ds_ref, q_ref), (p_ref, g_ref))):
             lanes = slice(half * flat_width, (half + 1) * flat_width)
-            grads = dot_f32(w_ref[...], qg_ref[:, lanes], LEAD_PAIR)
+            grads = dot_f32(w_ref[...], t_ref[...], LEAD_PAIR)
             shared = dsum_ref[:, lanes] / group
             grads = grads.reshape(tokens, group, flat_width) + shared[:, None, :]
             grads = grads.reshape(width, flat_width).astype(jnp.bfloat16)
@@ -251,13 +214,12 @@
 
     return pl.pallas_call(
         kernel,
-        in_specs=[VMEM] * 4,
         out_shape=tuple(
             jax.ShapeDtypeStruct((piece, 2 * flat_width), jnp.bfloat16) for _ in range(pieces)
         ),
         compiler_params=ROOM,
         name="key_grads",
-    )(prob, dlogit, qg_blk, dsum)
+    )(prob, dlogit, q_blk, g_blk, dsum)
 
 
 def shards(queries, keys, values, out_grad, row_keep, row_lengths):
@@ -327,12 +289,25 @@
     query_pieces = {0: qg_flat} | {s: shift_x(qg_flat, s) for s in order}
     key_pieces = [kv_flat] + [shift_y(kv_flat, s) for s in range(1, ys)]
     query_pieces, key_pieces = lax.optimization_barrier((query_pieces, key_pieces))
-    line = jnp.zeros((XS, rows_dev, 2 * flat_width), queries.dtype)
-    for s, piece in query_pieces.items():
-        line = lax.dynamic_update_slice(line, piece[None], ((own_x - s) % XS, 0, 0))
-    qg_blk, kv_blk, logit_piece, dprob_piece = block_products(
-        place, line, swap_core(line), key_pieces, rows_dev, flat_width
-    )
+    halves = (slice(0, flat_width), slice(flat_width, 2 * flat_width))
+
+    def query_block(half):
+        line = jnp.zeros((XS, rows_dev, flat_width), queries.dtype)
+        for s, piece in query_pieces.items():
+            line = lax.dynamic_update_slice(line, piece[None, :, half], ((own_x - s) % XS, 0, 0))
+        other = swap_core(line)
+        first = jnp.where(own_core == 0, line, other)
+        second = jnp.where(own_core == 0, other, line)
+        return jnp.stack([first, second], axis=1).reshape(block_rows, flat_width)
+
+    def key_block(half):
+        return jnp.concatenate([p[:rows_dev, half] for p in key_pieces], axis=0)
+
+    q_blk, g_blk = query_block(halves[0]), query_block(halves[1])
+    k_blk, v_blk = key_block(halves[0]), key_block(halves[1])
+    logit_piece = dot_f32(q_blk, k_blk, ROW_PAIR)
+    g_blk, _ = lax.optimization_barrier((g_blk, logit_piece))
+    dprob_piece = dot_f32(g_blk, v_blk, ROW_PAIR).astype(jnp.bfloat16)
     key_flags = jnp.concatenate([p[rows_dev, :rows_dev] for p in key_pieces])[None, :]
     logit_sum = lax.psum_scatter(logit_piece, "col", scatter_dimension=0, tiled=True)
 
@@ -354,23 +329,16 @@
     dprob_forward = passed(1, zs // 2)
     dprob_back = passed(-1, zs - 1 - zs // 2)
 
-    sums, own_stats = cross_statistics(qg_blk, kv_blk, tokens, feature, inv_root)
+    sums, own_stats = cross_statistics(q_blk, g_blk, k_blk, v_blk, tokens, feature, inv_root)
     cross_dl, dsum = cross_grads(
-        qg_blk, sums, share(own_stats, "row", near), feature, inv_root
+        q_blk, g_blk, sums, share(own_stats, "row", near), feature, inv_root
     )
 
     both, stats = block_softmax(
         logit_scale, logit_sum, part(0), dprob_forward, dprob_back, key_flags
     )
     both, stats, cross_dl, dsum = lax.optimization_barrier((both, stats, cross_dl, dsum))
-    forward, back = [both], []
-    for _ in range(zs // 2):
-        forward.append(shift_z(forward[-1], 1))
-    for _ in range(zs - 1 - zs // 2):
-        back.append(shift_z(back[-1] if back else both, -1))
-    pieces = forward + back
-    steps = list(range(zs // 2 + 1)) + [-s for s in range(1, zs - zs // 2)]
-
+    both = lax.all_gather(both, "col", axis=0, tiled=True)
     all_stats = share(stats, "row", near)
     weight = jnp.exp(all_stats[:, 0] - jnp.max(all_stats[:, 0], axis=0))
     total = jnp.sum(weight * all_stats[:, 1], axis=0)
@@ -379,10 +347,10 @@
     scaling = share(jnp.stack([own_weight, delta - stats[3]]), "col")
 
     prob, dlogit, dq_own, dq_other = query_grads(
-        logit_scale, place, pieces, steps, scaling, kv_blk, cross_dl, sums
+        logit_scale, place, both, scaling, k_blk, cross_dl, sums, zs
     )
     dq_swapped = swap_core(dq_other)
-    key_parts = key_grads(prob, dlogit, qg_blk, dsum, ys)
+    key_parts = key_grads(prob, dlogit, q_blk, g_blk, dsum, ys)
     key_moved = [shift_y(key_parts[s], -s) for s in range(1, ys)]
     line = (dq_own + dq_swapped.astype(jnp.float32)).astype(jnp.bfloat16)
     line = line.reshape(XS, rows_dev, flat_width)

time: 181 us -> 173 us (0.956)
  the two profiles are of different devices: /device:TPU:8 before, /device:TPU:1 now
where the time goes in v6:
time: 173 us; the launch traced here: 172 us
  waiting for transfers between devices  72.3 us (42%)
  starting transfers between devices  40.4 us (23%)
  between operations  14.5 us (8%)
  local copies, waits for them, and re-layouts  14.4 us (8%)
  blocking collectives  10.1 us (6%)
  other arithmetic  8.92 us (5%)
  Pallas kernels  7.75 us (4%)
  matrix products  3.81 us (2%)
    all_gather x1, waiting for transfers between devices, shards(): both = lax.all_gather(both, 'col', axis=0, tiled=True)  16.7 us
    ppermute x6, waiting for transfers between devices, shift_x(): lax.ppermute(table, 'row', [(at(y, x, c), at(y, x + step, c)) for y, x, c...  16.7 us
    ppermute x6, waiting for transfers between devices, shift_y(): lax.ppermute(table, 'row', [(at(y, x, c), at(y + step, x, c)) for y, x, c...  13.4 us
    all_to_all x2, waiting for transfers between devices, share(): lax.all_to_all(copies, axis, split_axis=0, concat_axis=0, tiled=True, axi...  12 us
    ppermute x7, waiting for transfers between devices, shift_z(): return lax.ppermute(table, 'col', [(z, (z + step) % zs) for z in range(zs)])  11.6 us
    all_to_all x1, blocking collectives, share(): lax.all_to_all(copies, axis, split_axis=0, concat_axis=0, tiled=True, axi...  10.1 us
    all_to_all x2, starting transfers between devices, share(): lax.all_to_all(copies, axis, split_axis=0, concat_axis=0, tiled=True, axi...  9.57 us
    ppermute x6, starting transfers between devices, shift_x(): lax.ppermute(table, 'row', [(at(y, x, c), at(y, x + step, c)) for y, x, c...  8.9 us
  transfers between devices with their start and end apart: 26, of which 12 were waited for; matrix products, arithmetic and copies ran while one was open for 9% of the time, Pallas kernels for 2%

profile of v6, /device:TPU:1, one launch (start us, length us, event | category | flops | bytes accessed | tf_op | source)
XLA Modules:
  0.0 172.2 jit_solution(17792075202539970721)
XLA Ops:
  7.2 0.7 convert_bitcast_fusion
  7.9 0.7 broadcast_compare_fusion
  8.5 0.7 compare_and_fusion
  9.4 0.2 broadcast_in_dim.71
  9.6 1.2 bitcast_select_fusion.1
  10.9 3.4 %collective-permute-start.2 = (bf16[128,1024]{1,0:T(8,128)(2,1)S(1)}, bf16[128,1024]{1,0:T(8,128)(2,1)S(1)}, u32[]{:S(2)}, u32[]{:S(2)}) collective-permute-start(bf16[128,1024]{1,0:T(8,128)(2,1)S(1)} %pad_maximum_fusion.4), channel_id=1, source_target_pairs={{0,48},{8,56},{16,0},{24,8},{32,16},{40,24},{48,32},{56,40},{64,11... | collective-permute-start | bytes 786440 | tf_op jit(solution)/shard_map/ppermute | solution.py:254
  14.3 2.7 %collective-permute-start.5 = (bf16[144,1024]{1,0:T(8,128)(2,1)S(1)}, bf16[144,1024]{1,0:T(8,128)(2,1)S(1)}, u32[]{:S(2)}, u32[]{:S(2)}) collective-permute-start(bf16[144,1024]{1,0:T(8,128)(2,1)S(1)} %fusion.1), channel_id=1, source_target_pairs={{0,192},{8,200},{16,208},{24,216},{32,224},{40,232},{48,240},{56,2... | collective-permute-start | bytes 884744 | tf_op jit(solution)/shard_map/ppermute | solution.py:251
  17.0 0.3 collective-permute-start.4
  17.4 0.7 collective-permute-start.3
  18.1 0.5 collective-permute-start.1
  18.6 0.7 collective-permute-done.2
  19.3 0.9 collective-permute-start
  20.2 5.5 %collective-permute-done.1 = bf16[128,1024]{1,0:T(8,128)(2,1)S(1)} collective-permute-done((bf16[128,1024]{1,0:T(8,128)(2,1)S(1)}, bf16[128,1024]{1,0:T(8,128)(2,1)S(1)}, u32[]{:S(2)}, u32[]{:S(2)}) %collective-permute-start.1) | collective-permute-done | bytes 262176 | tf_op jit(solution)/shard_map/ppermute | solution.py:254
  25.7 5.1 %collective-permute-done = bf16[128,1024]{1,0:T(8,128)(2,1)S(1)} collective-permute-done((bf16[128,1024]{1,0:T(8,128)(2,1)S(1)}, bf16[128,1024]{1,0:T(8,128)(2,1)S(1)}, u32[]{:S(2)}, u32[]{:S(2)}) %collective-permute-start) | collective-permute-done | bytes 262176 | tf_op jit(solution)/shard_map/ppermute | solution.py:254
  30.8 3.1 %collective-permute-done.3 = bf16[144,1024]{1,0:T(8,128)(2,1)} collective-permute-done((bf16[144,1024]{1,0:T(8,128)(2,1)S(1)}, bf16[144,1024]{1,0:T(8,128)(2,1)}, u32[]{:S(2)}, u32[]{:S(2)}) %collective-permute-start.3) | collective-permute-done | bytes 294944 | tf_op jit(solution)/shard_map/ppermute | solution.py:251
  34.1 1.3 collective-permute-start.6
  35.5 1.0 fusion.16
  36.5 1.1 fusion.18
  37.9 2.1 %fusion.15 = f32[1024,512]{1,0:T(8,128)} fusion(bf16[1024,512]{1,0:T(8,128)(2,1)S(1)} %bitcast.115, bf16[128,512]{1,0:T(8,128)(2,1)S(1)} %get-tuple-element.112, bf16[128,512]{1,0:T(8,128)(2,1)S(1)} %get-tuple-element.88, bf16[128,512]{1,0:T(8,128)(2,1)S(1)} %get-tuple-element.110, bf16[128,512]{1,0:T(8,128)(2,1)S(1)} %get-tuple-element.84), kind=kOutput, calls=%fused_computation.71 | convolution fusion | flops 538968064 | bytes 3670016 | tf_op jit(solution)/shard_map/dot_general | solution.py:25
  40.2 1.8 %collective-permute-done.7 = bf16[4,128,512]{2,1,0:T(8,128)(2,1)S(1)} collective-permute-done((bf16[4,128,512]{2,1,0:T(8,128)(2,1)S(1)}, bf16[4,128,512]{2,1,0:T(8,128)(2,1)S(1)}, u32[]{:S(2)}, u32[]{:S(2)}) %collective-permute-start.7) | collective-permute-done | bytes 524320 | tf_op jit(solution)/shard_map/ppermute | solution.py:257
  42.3 1.7 %convolution_convert_fusion = bf16[1024,512]{1,0:T(8,128)(2,1)} fusion(bf16[1024,512]{1,0:T(8,128)(2,1)S(1)} %bitcast.119, bf16[128,512]{1,0:T(8,128)(2,1)S(1)} %get-tuple-element.113, bf16[128,512]{1,0:T(8,128)(2,1)S(1)} %get-tuple-element.87, bf16[128,512]{1,0:T(8,128)(2,1)S(1)} %get-tuple-element.111, bf16[128,512]{1,0:T(8,128)(2,1)S(1)} %get-tuple-element.83), kind=kOutput, calls=%fused_computation | convolution fusion | flops 539492352 | bytes 2621440 | tf_op jit(solution)/shard_map/dot_general | solution.py:25
  44.0 1.8 %dynamic-slice_bitcast_fusion.3 = (bf16[128,512]{1,0:T(8,128)(2,1)}, bf16[128,512]{1,0:T(8,128)(2,1)}, bf16[128,512]{1,0:T(8,128)(2,1)S(1)}) fusion(bf16[8,128,512]{2,1,0:T(8,128)(2,1)} %bitcast.18, s32[]{:T(128)S(6)} %select_n.199, s32[]{:T(128)S(6)} %select_n.191, s32[]{:T(128)S(6)} %select_n.189), kind=kLoop, calls=%fused_computation.49 | loop fusion | bytes 786444 | tf_op jit(solution)/shard_map/jit(dynamic_index_in_dim)/squeeze | solution.py:317
  45.7 1.6 collective-permute-start.8
  47.4 4.0 %collective-permute-start.12 = (bf16[128,512]{1,0:T(8,128)(2,1)}, bf16[128,512]{1,0:T(8,128)(2,1)S(1)}, u32[]{:S(2)}, u32[]{:S(2)}) collective-permute-start(bf16[128,512]{1,0:T(8,128)(2,1)} %get-tuple-element.71), channel_id=1, source_target_pairs={{0,7},{1,0},{2,1},{3,2},{4,3},{5,4},{6,5},{7,6},{8,15},{9,8},{10,9... | collective-permute-start | bytes 393224 | tf_op jit(solution)/shard_map/ppermute | solution.py:260
  51.4 3.9 %collective-permute-done.8 = bf16[128,512]{1,0:T(8,128)(2,1)S(1)} collective-permute-done((bf16[128,512]{1,0:T(8,128)(2,1)}, bf16[128,512]{1,0:T(8,128)(2,1)S(1)}, u32[]{:S(2)}, u32[]{:S(2)}) %collective-permute-start.8) | collective-permute-done | bytes 131104 | tf_op jit(solution)/shard_map/ppermute | solution.py:260
  55.3 0.9 fusion.12
  56.3 0.7 slice_bitcast_fusion.2
  57.0 7.7 %collective-permute-done.9 = bf16[128,512]{1,0:T(8,128)(2,1)S(1)} collective-permute-done((bf16[128,512]{1,0:T(8,128)(2,1)S(1)}, bf16[128,512]{1,0:T(8,128)(2,1)S(1)}, u32[]{:S(2)}, u32[]{:S(2)}) %collective-permute-start.9) | collective-permute-done | bytes 131104 | tf_op jit(solution)/shard_map/ppermute | solution.py:260
  64.7 1.7 %fusion.9 = (bf16[128,512]{1,0:T(8,128)(2,1)}, bf16[128,512]{1,0:T(8,128)(2,1)}) fusion(bf16[128,512]{1,0:T(8,128)(2,1)S(1)} %collective-permute-done.12, bf16[8,128,512]{2,1,0:T(8,128)(2,1)} %bitcast.18, s32[]{:T(128)S(6)} %select_n.201, s32[]{:T(128)S(6)} %select_n.195, bf16[128,512]{1,0:T(8,128)(2,1)S(1)} %collective-permute-done.9), kind=kLoop, calls=%fused_computation.27 | loop fusion | flops 524288 | bytes 786440 | tf_op jit(solution)/shard_map/convert_element_type | solution.py:326
  66.5 0.6 collective-permute-start.13
  67.0 0.9 collective-permute-start.10
  68.0 1.1 cross_statistics.1
  69.1 0.8 broadcast_in_dim.83
  70.0 6.0 %all-to-all-start = ((f32[8,16,1024]{2,1,0:T(8,128)}), f32[8,16,1024]{2,1,0:T(8,128)S(1)}, u32[]{:S(2)}, u32[]{:S(2)}) async-start(f32[8,16,1024]{2,1,0:T(8,128)} %broadcast_in_dim.83), calls=%async_computation.1 | async-start | bytes 1048576 | tf_op jit(solution)/shard_map/all_to_all | solution.py:265
  76.0 1.9 %fusion.8 = (bf16[128,512]{1,0:T(8,128)(2,1)}, bf16[128,512]{1,0:T(8,128)(2,1)}) fusion(bf16[128,512]{1,0:T(8,128)(2,1)} %collective-permute-done.13, bf16[8,128,512]{2,1,0:T(8,128)(2,1)} %bitcast.18, s32[]{:T(128)S(6)} %select_n.203, s32[]{:T(128)S(6)} %select_n.197, bf16[128,512]{1,0:T(8,128)(2,1)} %collective-permute-done.10), kind=kLoop, calls=%fused_computation.25 | loop fusion | flops 524288 | bytes 786440 | tf_op jit(solution)/shard_map/convert_element_type | solution.py:326
  77.9 1.5 collective-permute-start.14
  79.4 0.7 slice_bitcast_fusion
  80.1 5.4 %all-to-all-done.stat_ref = f32[8,16,1024]{2,1,0:T(8,128)S(1)} async-done(((f32[8,16,1024]{2,1,0:T(8,128)}), f32[8,16,1024]{2,1,0:T(8,128)S(1)}, u32[]{:S(2)}, u32[]{:S(2)}) %all-to-all-start) | async-done | bytes 524320 | tf_op jit(solution)/shard_map/all_to_all | solution.py:265
  85.5 0.8 copy-done.3
  86.3 1.5 cross_grads.1
  87.8 0.7 copy-done.5
  88.5 0.9 copy-done.1
  89.4 2.0 %block_softmax.1 = (bf16[128,1024]{1,0:T(8,128)(2,1)}, f32[8,128]{1,0:T(8,128)S(1)}) custom-call(f32[128,512]{1,0:T(8,128)S(1)} %copy-done.1, bf16[128,512]{1,0:T(8,128)(2,1)S(1)} %get-tuple-element.73.own_ref, bf16[128,512]{1,0:T(8,128)(2,1)} %collective-permute-done.11.forward_ref, bf16[128,512]{1,0:T(8,128)(2,1)} %collective-permute-done.14.back_ref, ...), custom_call_target="tpu_custom_call" | custom-call | tf_op jit(solution)/shard_map/block_softmax/pallas_call | solution.py:141
  91.4 10.1 %all_to_all.15 = f32[8,8,128]{2,1,0:T(8,128)S(1)} all-to-all(f32[8,8,128]{2,1,0:T(8,128)S(1)} %broadcast_in_dim.84), channel_id=1, replica_groups={{0,8,16,24,32,40,48,56},{64,72,80,88,96,104,112,120},{128,136,144,152,1..., dimensions={0} | all-to-all | bytes 65536 | tf_op jit(solution)/shard_map/all_to_all | solution.py:265
  101.7 0.6 broadcast_in_dim.85
  102.3 3.6 %all-to-all-start.2 = ((f32[8,2,128]{2,1,0:T(2,128)}), f32[8,2,128]{2,1,0:T(2,128)S(1)}, u32[]{:S(2)}, u32[]{:S(2)}) async-start(f32[8,2,128]{2,1,0:T(2,128)} %broadcast_in_dim.85), calls=%async_computation.3 | async-start | bytes 16384 | tf_op jit(solution)/shard_map/all_to_all | solution.py:265
  105.9 6.6 %all-to-all-done.2.scale_ref = f32[8,2,128]{2,1,0:T(2,128)S(1)} async-done(((f32[8,2,128]{2,1,0:T(2,128)}), f32[8,2,128]{2,1,0:T(2,128)S(1)}, u32[]{:S(2)}, u32[]{:S(2)}) %all-to-all-start.2) | async-done | bytes 8224 | tf_op jit(solution)/shard_map/all_to_all | solution.py:265
  112.5 16.7 %all-gather.2.cloned.1.call-done.both_ref = bf16[1024,1024]{1,0:T(8,128)(2,1)} async-done(((bf16[128,1024]{1,0:T(8,128)(2,1)}), bf16[1024,1024]{1,0:T(8,128)(2,1)}) %all-gather.2.cloned.1.call-update) | async-done | bytes 2097168 | tf_op jit(solution)/shard_map/all_gather | solution.py:341
  129.2 1.6 copy-done
  130.8 0.8 copy-done.4
  131.7 2.0 %query_grads.1 = (bf16[1024,512]{1,0:T(8,128)(2,1)S(1)}, bf16[1024,512]{1,0:T(8,128)(2,1)S(1)}, f32[512,512]{1,0:T(8,128)S(1)}, bf16[512,512]{1,0:T(8,128)(2,1)S(1)}) custom-call(s32[2]{0:T(128)S(1)} %pad_add_fusion.place_ref, bf16[1024,1024]{1,0:T(8,128)(2,1)S(1)} %copy-done, f32[8,2,128]{2,1,0:T(2,128)S(1)} %all-to-all-done.2.scale_ref, ...), custom_call_target="tpu_custom_call" | custom-call | tf_op jit(solution)/shard_map/query_grads/pallas_call | solution.py:184
  133.6 4.8 %collective-permute-start.15 = (bf16[512,512]{1,0:T(8,128)(2,1)S(1)}, bf16[512,512]{1,0:T(8,128)(2,1)S(1)}, u32[]{:S(2)}, u32[]{:S(2)}) collective-permute-start(bf16[512,512]{1,0:T(8,128)(2,1)S(1)} %get-tuple-element.55), channel_id=1, source_target_pairs={{0,8},{8,0},{16,24},{24,16},{32,40},{40,32},{48,56},{56,48},{64,72... | collective-permute-start | bytes 1572872 | tf_op jit(solution)/shard_map/ppermute | solution.py:257
  138.4 1.3 key_grads.1
  139.7 2.5 %collective-permute-start.16 = (bf16[128,1024]{1,0:T(8,128)(2,1)S(1)}, bf16[128,1024]{1,0:T(8,128)(2,1)S(1)}, u32[]{:S(2)}, u32[]{:S(2)}) collective-permute-start(bf16[128,1024]{1,0:T(8,128)(2,1)S(1)} %get-tuple-element.59), channel_id=1, source_target_pairs={{0,192},{8,200},{16,208},{24,216},{32,224},{40,232},{48,240},{56,2... | collective-permute-start | bytes 786440 | tf_op jit(solution)/shard_map/ppermute | solution.py:251
  142.2 0.6 collective-permute-start.21
  142.9 0.2 add_convert_fusion
  143.0 10.3 %collective-permute-done.16 = bf16[128,1024]{1,0:T(8,128)(2,1)S(1)} collective-permute-done((bf16[128,1024]{1,0:T(8,128)(2,1)S(1)}, bf16[128,1024]{1,0:T(8,128)(2,1)S(1)}, u32[]{:S(2)}, u32[]{:S(2)}) %collective-permute-start.16) | collective-permute-done | bytes 262176 | tf_op jit(solution)/shard_map/ppermute | solution.py:251
  153.4 2.5 %collective-permute-start.17 = (bf16[128,512]{1,0:T(8,128)(2,1)S(1)}, bf16[128,512]{1,0:T(8,128)(2,1)S(1)}, u32[]{:S(2)}, u32[]{:S(2)}) collective-permute-start(bf16[128,512]{1,0:T(8,128)(2,1)S(1)} %get-tuple-element.78), channel_id=1, source_target_pairs={{0,48},{8,56},{16,0},{24,8},{32,16},{40,24},{48,32},{56,40},{64,11... | collective-permute-start | bytes 393224 | tf_op jit(solution)/shard_map/ppermute | solution.py:254
  155.9 1.5 collective-permute-start.18
  157.5 0.2 convert_add_fusion
  157.7 0.7 reshape.131
  158.4 0.7 reshape.130
  159.1 5.4 %collective-permute-done.19 = bf16[128,512]{1,0:T(8,128)(2,1)S(1)} collective-permute-done((bf16[128,512]{1,0:T(8,128)(2,1)S(1)}, bf16[128,512]{1,0:T(8,128)(2,1)S(1)}, u32[]{:S(2)}, u32[]{:S(2)}) %collective-permute-start.19) | collective-permute-done | bytes 131104 | tf_op jit(solution)/shard_map/ppermute | solution.py:254
  164.6 0.7 reshape.129
  (76 shorter events, 1.6 us)
Async XLA Ops:
  7.2 81.3 %reduce-scatter.2.cloned.1.call-start = ((), (), s32[]{:S(2)}) async-start(), calls=%async_computation.4 | async-start | bytes 2359296 | tf_op jit(solution)/shard_map/reduce_scatter | solution.py:312
  9.6 24.3 %copy-start.7 = (pred[128,4,128]{2,1,0:T(4,128)(4,1)}, pred[128,4,128]{2,1,0:T(4,128)(4,1)S(1)}, u32[]{:S(2)}) copy-start(pred[128,4,128]{2,1,0:T(4,128)(4,1)S(1)} %broadcast_in_dim.71) | copy-start | bytes 196612
  10.9 8.4 %collective-permute-start.2 = (bf16[128,1024]{1,0:T(8,128)(2,1)S(1)}, bf16[128,1024]{1,0:T(8,128)(2,1)S(1)}, u32[]{:S(2)}, u32[]{:S(2)}) collective-permute-start(bf16[128,1024]{1,0:T(8,128)(2,1)S(1)} %pad_maximum_fusion.4), channel_id=1, source_target_pairs={{0,48},{8,56},{16,0},{24,8},{32,16},{40,24},{48,32},{56,40},{64,11... | collective-permute-start | bytes 786440 | tf_op jit(solution)/shard_map/ppermute | solution.py:254
  14.3 16.5 %collective-permute-start.5 = (bf16[144,1024]{1,0:T(8,128)(2,1)S(1)}, bf16[144,1024]{1,0:T(8,128)(2,1)S(1)}, u32[]{:S(2)}, u32[]{:S(2)}) collective-permute-start(bf16[144,1024]{1,0:T(8,128)(2,1)S(1)} %fusion.1), channel_id=1, source_target_pairs={{0,192},{8,200},{16,208},{24,216},{32,224},{40,232},{48,240},{56,2... | collective-permute-start | bytes 884744 | tf_op jit(solution)/shard_map/ppermute | solution.py:251
  17.0 13.8 %collective-permute-start.4 = (bf16[144,1024]{1,0:T(8,128)(2,1)S(1)}, bf16[144,1024]{1,0:T(8,128)(2,1)}, u32[]{:S(2)}, u32[]{:S(2)}) collective-permute-start(bf16[144,1024]{1,0:T(8,128)(2,1)S(1)} %fusion.1), channel_id=1, source_target_pairs={{0,128},{8,136},{16,144},{24,152},{32,160},{40,168},{48,176},{56,1... | collective-permute-start | bytes 884744 | tf_op jit(solution)/shard_map/ppermute | solution.py:251
  17.4 16.5 %collective-permute-start.3 = (bf16[144,1024]{1,0:T(8,128)(2,1)S(1)}, bf16[144,1024]{1,0:T(8,128)(2,1)}, u32[]{:S(2)}, u32[]{:S(2)}) collective-permute-start(bf16[144,1024]{1,0:T(8,128)(2,1)S(1)} %fusion.1), channel_id=1, source_target_pairs={{0,64},{8,72},{16,80},{24,88},{32,96},{40,104},{48,112},{56,120},{... | collective-permute-start | bytes 884744 | tf_op jit(solution)/shard_map/ppermute | solution.py:251
  18.1 7.6 %collective-permute-start.1 = (bf16[128,1024]{1,0:T(8,128)(2,1)S(1)}, bf16[128,1024]{1,0:T(8,128)(2,1)S(1)}, u32[]{:S(2)}, u32[]{:S(2)}) collective-permute-start(bf16[128,1024]{1,0:T(8,128)(2,1)S(1)} %pad_maximum_fusion.4), channel_id=1, source_target_pairs={{0,32},{8,40},{16,48},{24,56},{32,0},{40,8},{48,16},{56,24},{64,96... | collective-permute-start | bytes 786440 | tf_op jit(solution)/shard_map/ppermute | solution.py:254
  19.3 11.5 %collective-permute-start = (bf16[128,1024]{1,0:T(8,128)(2,1)S(1)}, bf16[128,1024]{1,0:T(8,128)(2,1)S(1)}, u32[]{:S(2)}, u32[]{:S(2)}) collective-permute-start(bf16[128,1024]{1,0:T(8,128)(2,1)S(1)} %pad_maximum_fusion.4), channel_id=1, source_target_pairs={{0,16},{8,24},{16,32},{24,40},{32,48},{40,56},{48,0},{56,8},{64,80... | collective-permute-start | bytes 786440 | tf_op jit(solution)/shard_map/ppermute | solution.py:254
  30.8 3.1 %copy-start.13 = (bf16[144,1024]{1,0:T(8,128)(2,1)}, bf16[144,1024]{1,0:T(8,128)(2,1)S(1)}, u32[]{:S(2)}) copy-start(bf16[144,1024]{1,0:T(8,128)(2,1)S(1)} %collective-permute-done.5) | copy-start | bytes 884740
  34.1 3.5 %collective-permute-start.6 = (bf16[4,128,512]{2,1,0:T(8,128)(2,1)S(1)}, bf16[4,128,512]{2,1,0:T(8,128)(2,1)S(1)}, u32[]{:S(2)}, u32[]{:S(2)}) collective-permute-start(bf16[4,128,512]{2,1,0:T(8,128)(2,1)S(1)} %get-tuple-element.92), channel_id=1, source_target_pairs={{0,8},{8,0},{16,24},{24,16},{32,40},{40,32},{48,56},{56,48},{64,72... | collective-permute-start | bytes 1572872 | tf_op jit(solution)/shard_map/ppermute | solution.py:257
  37.6 4.6 %copy-start.9 = (bf16[128,512]{1,0:T(8,128)(2,1)}, bf16[128,512]{1,0:T(8,128)(2,1)S(1)}, u32[]{:S(2)}) copy-start(bf16[128,512]{1,0:T(8,128)(2,1)S(1)} %get-tuple-element.87) | copy-start | bytes 393220
  37.6 4.6 %copy-start.11 = (bf16[128,512]{1,0:T(8,128)(2,1)}, bf16[128,512]{1,0:T(8,128)(2,1)S(1)}, u32[]{:S(2)}) copy-start(bf16[128,512]{1,0:T(8,128)(2,1)S(1)} %get-tuple-element.113) | copy-start | bytes 393220
  40.1 2.0 %collective-permute-start.7 = (bf16[4,128,512]{2,1,0:T(8,128)(2,1)S(1)}, bf16[4,128,512]{2,1,0:T(8,128)(2,1)S(1)}, u32[]{:S(2)}, u32[]{:S(2)}) collective-permute-start(bf16[4,128,512]{2,1,0:T(8,128)(2,1)S(1)} %get-tuple-element.91), channel_id=1, source_target_pairs={{0,8},{8,0},{16,24},{24,16},{32,40},{40,32},{48,56},{56,48},{64,72... | collective-permute-start | bytes 1572872 | tf_op jit(solution)/shard_map/ppermute | solution.py:257
  45.7 9.5 %collective-permute-start.8 = (bf16[128,512]{1,0:T(8,128)(2,1)}, bf16[128,512]{1,0:T(8,128)(2,1)S(1)}, u32[]{:S(2)}, u32[]{:S(2)}) collective-permute-start(bf16[128,512]{1,0:T(8,128)(2,1)} %get-tuple-element.72), channel_id=1, source_target_pairs={{0,1},{1,2},{2,3},{3,4},{4,5},{5,6},{6,7},{7,0},{8,9},{9,10},{10,1... | collective-permute-start | bytes 393224 | tf_op jit(solution)/shard_map/ppermute | solution.py:260
  47.4 20.6 %copy-start.10 = (bf16[128,512]{1,0:T(8,128)(2,1)S(1)}, bf16[128,512]{1,0:T(8,128)(2,1)}, u32[]{:S(2)}) copy-start(bf16[128,512]{1,0:T(8,128)(2,1)} %copy-done.9) | copy-start | bytes 393220
  47.4 20.6 %copy-start.12 = (bf16[128,512]{1,0:T(8,128)(2,1)S(1)}, bf16[128,512]{1,0:T(8,128)(2,1)}, u32[]{:S(2)}) copy-start(bf16[128,512]{1,0:T(8,128)(2,1)} %copy-done.11) | copy-start | bytes 393220
  47.4 9.6 %collective-permute-start.12 = (bf16[128,512]{1,0:T(8,128)(2,1)}, bf16[128,512]{1,0:T(8,128)(2,1)S(1)}, u32[]{:S(2)}, u32[]{:S(2)}) collective-permute-start(bf16[128,512]{1,0:T(8,128)(2,1)} %get-tuple-element.71), channel_id=1, source_target_pairs={{0,7},{1,0},{2,1},{3,2},{4,3},{5,4},{6,5},{7,6},{8,15},{9,8},{10,9... | collective-permute-start | bytes 393224 | tf_op jit(solution)/shard_map/ppermute | solution.py:260
  56.2 8.5 %collective-permute-start.9 = (bf16[128,512]{1,0:T(8,128)(2,1)S(1)}, bf16[128,512]{1,0:T(8,128)(2,1)S(1)}, u32[]{:S(2)}, u32[]{:S(2)}) collective-permute-start(bf16[128,512]{1,0:T(8,128)(2,1)S(1)} %fusion.12), channel_id=1, source_target_pairs={{0,1},{1,2},{2,3},{3,4},{4,5},{5,6},{6,7},{7,0},{8,9},{9,10},{10,1... | collective-permute-start | bytes 393224 | tf_op jit(solution)/shard_map/ppermute | solution.py:260
  66.5 9.5 %collective-permute-start.13 = (bf16[128,512]{1,0:T(8,128)(2,1)}, bf16[128,512]{1,0:T(8,128)(2,1)}, u32[]{:S(2)}, u32[]{:S(2)}) collective-permute-start(bf16[128,512]{1,0:T(8,128)(2,1)} %get-tuple-element.69), channel_id=1, source_target_pairs={{0,7},{1,0},{2,1},{3,2},{4,3},{5,4},{6,5},{7,6},{8,15},{9,8},{10,9... | collective-permute-start | bytes 393224 | tf_op jit(solution)/shard_map/ppermute | solution.py:260
  67.0 9.0 %collective-permute-start.10 = (bf16[128,512]{1,0:T(8,128)(2,1)}, bf16[128,512]{1,0:T(8,128)(2,1)}, u32[]{:S(2)}, u32[]{:S(2)}) collective-permute-start(bf16[128,512]{1,0:T(8,128)(2,1)} %get-tuple-element.70), channel_id=1, source_target_pairs={{0,1},{1,2},{2,3},{3,4},{4,5},{5,6},{6,7},{7,0},{8,9},{9,10},{10,1... | collective-permute-start | bytes 393224 | tf_op jit(solution)/shard_map/ppermute | solution.py:260
  69.1 0.8 copy-start.2
  70.0 15.5 %all-to-all-start = ((f32[8,16,1024]{2,1,0:T(8,128)}), f32[8,16,1024]{2,1,0:T(8,128)S(1)}, u32[]{:S(2)}, u32[]{:S(2)}) async-start(f32[8,16,1024]{2,1,0:T(8,128)} %broadcast_in_dim.83), calls=%async_computation.1 | async-start | bytes 1048576 | tf_op jit(solution)/shard_map/all_to_all | solution.py:265
  76.0 53.3 %all-gather.2.cloned.1.call-start = ((), (), s32[]{:S(2)}) async-start(), calls=%async_computation.5 | async-start | bytes 2359296 | tf_op jit(solution)/shard_map/all_gather | solution.py:341
  77.9 10.6 %collective-permute-start.14 = (bf16[128,512]{1,0:T(8,128)(2,1)}, bf16[128,512]{1,0:T(8,128)(2,1)}, u32[]{:S(2)}, u32[]{:S(2)}) collective-permute-start(bf16[128,512]{1,0:T(8,128)(2,1)} %get-tuple-element.67), channel_id=1, source_target_pairs={{0,7},{1,0},{2,1},{3,2},{4,3},{5,4},{6,5},{7,6},{8,15},{9,8},{10,9... | collective-permute-start | bytes 393224 | tf_op jit(solution)/shard_map/ppermute | solution.py:260
  79.4 9.1 %collective-permute-start.11 = (bf16[128,512]{1,0:T(8,128)(2,1)}, bf16[128,512]{1,0:T(8,128)(2,1)}, u32[]{:S(2)}, u32[]{:S(2)}) collective-permute-start(bf16[128,512]{1,0:T(8,128)(2,1)} %get-tuple-element.68), channel_id=1, source_target_pairs={{0,1},{1,2},{2,3},{3,4},{4,5},{5,6},{6,7},{7,0},{8,9},{9,10},{10,1... | collective-permute-start | bytes 393224 | tf_op jit(solution)/shard_map/ppermute | solution.py:260
  85.5 0.8 copy-start.3
  87.8 0.7 copy-start.5
  88.5 1.0 copy-start.1
  89.4 49.0 %copy-start.6 = (f32[32,1024]{1,0:T(8,128)S(1)}, f32[32,1024]{1,0:T(8,128)}, u32[]{:S(2)}) copy-start(f32[32,1024]{1,0:T(8,128)} %copy-done.5) | copy-start | bytes 393220
  102.3 10.2 %all-to-all-start.2 = ((f32[8,2,128]{2,1,0:T(2,128)}), f32[8,2,128]{2,1,0:T(2,128)S(1)}, u32[]{:S(2)}, u32[]{:S(2)}) async-start(f32[8,2,128]{2,1,0:T(2,128)} %broadcast_in_dim.85), calls=%async_computation.3 | async-start | bytes 16384 | tf_op jit(solution)/shard_map/all_to_all | solution.py:265
  129.2 1.6 copy-start
  130.8 0.8 copy-start.4
  133.6 9.3 %collective-permute-start.15 = (bf16[512,512]{1,0:T(8,128)(2,1)S(1)}, bf16[512,512]{1,0:T(8,128)(2,1)S(1)}, u32[]{:S(2)}, u32[]{:S(2)}) collective-permute-start(bf16[512,512]{1,0:T(8,128)(2,1)S(1)} %get-tuple-element.55), channel_id=1, source_target_pairs={{0,8},{8,0},{16,24},{24,16},{32,40},{40,32},{48,56},{56,48},{64,72... | collective-permute-start | bytes 1572872 | tf_op jit(solution)/shard_map/ppermute | solution.py:257
  139.7 13.7 %collective-permute-start.16 = (bf16[128,1024]{1,0:T(8,128)(2,1)S(1)}, bf16[128,1024]{1,0:T(8,128)(2,1)S(1)}, u32[]{:S(2)}, u32[]{:S(2)}) collective-permute-start(bf16[128,1024]{1,0:T(8,128)(2,1)S(1)} %get-tuple-element.59), channel_id=1, source_target_pairs={{0,192},{8,200},{16,208},{24,216},{32,224},{40,232},{48,240},{56,2... | collective-permute-start | bytes 786440 | tf_op jit(solution)/shard_map/ppermute | solution.py:251
  142.2 15.3 %collective-permute-start.20 = (bf16[128,1024]{1,0:T(8,128)(2,1)S(1)}, bf16[128,1024]{1,0:T(8,128)(2,1)S(1)}, u32[]{:S(2)}, u32[]{:S(2)}) collective-permute-start(bf16[128,1024]{1,0:T(8,128)(2,1)S(1)} %get-tuple-element.63), channel_id=1, source_target_pairs={{0,128},{8,136},{16,144},{24,152},{32,160},{40,168},{48,176},{56,1... | collective-permute-start | bytes 786440 | tf_op jit(solution)/shard_map/ppermute | solution.py:251
  142.2 15.3 %collective-permute-start.21 = (bf16[128,1024]{1,0:T(8,128)(2,1)S(1)}, bf16[128,1024]{1,0:T(8,128)(2,1)S(1)}, u32[]{:S(2)}, u32[]{:S(2)}) collective-permute-start(bf16[128,1024]{1,0:T(8,128)(2,1)S(1)} %get-tuple-element.64), channel_id=1, source_target_pairs={{0,64},{8,72},{16,80},{24,88},{32,96},{40,104},{48,112},{56,120},{... | collective-permute-start | bytes 786440 | tf_op jit(solution)/shard_map/ppermute | solution.py:251
  142.9 14.8 %copy-start.8 = (pred[128,4,128]{2,1,0:T(4,128)(4,1)S(1)}, pred[128,4,128]{2,1,0:T(4,128)(4,1)}, u32[]{:S(2)}) copy-start(pred[128,4,128]{2,1,0:T(4,128)(4,1)} %copy-done.7) | copy-start | bytes 196612
  153.4 5.7 %collective-permute-start.17 = (bf16[128,512]{1,0:T(8,128)(2,1)S(1)}, bf16[128,512]{1,0:T(8,128)(2,1)S(1)}, u32[]{:S(2)}, u32[]{:S(2)}) collective-permute-start(bf16[128,512]{1,0:T(8,128)(2,1)S(1)} %get-tuple-element.78), channel_id=1, source_target_pairs={{0,48},{8,56},{16,0},{24,8},{32,16},{40,24},{48,32},{56,40},{64,11... | collective-permute-start | bytes 393224 | tf_op jit(solution)/shard_map/ppermute | solution.py:254
  155.9 8.6 %collective-permute-start.19 = (bf16[128,512]{1,0:T(8,128)(2,1)S(1)}, bf16[128,512]{1,0:T(8,128)(2,1)S(1)}, u32[]{:S(2)}, u32[]{:S(2)}) collective-permute-start(bf16[128,512]{1,0:T(8,128)(2,1)S(1)} %get-tuple-element.79), channel_id=1, source_target_pairs={{0,16},{8,24},{16,32},{24,40},{32,48},{40,56},{48,0},{56,8},{64,80... | collective-permute-start | bytes 393224 | tf_op jit(solution)/shard_map/ppermute | solution.py:254
  155.9 8.6 %collective-permute-start.18 = (bf16[128,512]{1,0:T(8,128)(2,1)S(1)}, bf16[128,512]{1,0:T(8,128)(2,1)S(1)}, u32[]{:S(2)}, u32[]{:S(2)}) collective-permute-start(bf16[128,512]{1,0:T(8,128)(2,1)S(1)} %get-tuple-element.80), channel_id=1, source_target_pairs={{0,32},{8,40},{16,48},{24,56},{32,0},{40,8},{48,16},{56,24},{64,96... | collective-permute-start | bytes 393224 | tf_op jit(solution)/shard_map/ppermute | solution.py:254
Sparse Core Ops, SparseCore 0:
  40.2 44.0 reduce-scatter.1
  91.5 37.6 all-gather.1

commit v7 on v6

--- a/solution.py
+++ b/solution.py
@@ -273,39 +273,51 @@
     )
     zero = jnp.zeros((), queries.dtype)
 
-    def masked(first, second):
-        tables = (t.reshape(rows_dev, flat_width) for t in (first, second))
-        flat = jnp.concatenate([jnp.where(keep_flat, t, zero) for t in tables], axis=1)
+    def masked(table):
+        flat = jnp.where(keep_flat, table.reshape(rows_dev, flat_width), zero)
         return with_layout_constraint(flat, Layout((0, 1)))
 
-    qg_flat = masked(queries, out_grad)
-    flag_rows = jnp.pad(
-        row_keep.astype(jnp.bfloat16)[None, :],
-        ((0, FLAG_ROWS - 1), (0, 2 * flat_width - rows_dev)),
-    )
-    kv_flat = jnp.concatenate([masked(keys, values), flag_rows], axis=0)
-    qg_flat, kv_flat = lax.optimization_barrier((qg_flat, kv_flat))
-    order = (1, XS - 1, 2)
-    query_pieces = {0: qg_flat} | {s: shift_x(qg_flat, s) for s in order}
-    key_pieces = [kv_flat] + [shift_y(kv_flat, s) for s in range(1, ys)]
-    query_pieces, key_pieces = lax.optimization_barrier((query_pieces, key_pieces))
-    halves = (slice(0, flat_width), slice(flat_width, 2 * flat_width))
-
-    def query_block(half):
+    def in_line(table, moved):
         line = jnp.zeros((XS, rows_dev, flat_width), queries.dtype)
-        for s, piece in query_pieces.items():
-            line = lax.dynamic_update_slice(line, piece[None, :, half], ((own_x - s) % XS, 0, 0))
-        other = swap_core(line)
+        for s, piece in ({0: table} | moved).items():
+            line = lax.dynamic_update_slice(line, piece[None], ((own_x - s) % XS, 0, 0))
+        return line
+
+    def both_lines(line, other):
         first = jnp.where(own_core == 0, line, other)
         second = jnp.where(own_core == 0, other, line)
         return jnp.stack([first, second], axis=1).reshape(block_rows, flat_width)
 
-    def key_block(half):
-        return jnp.concatenate([p[:rows_dev, half] for p in key_pieces], axis=0)
-
-    q_blk, g_blk = query_block(halves[0]), query_block(halves[1])
-    k_blk, v_blk = key_block(halves[0]), key_block(halves[1])
+    flag_rows = jnp.pad(
+        row_keep.astype(jnp.bfloat16)[None, :], ((0, FLAG_ROWS - 1), (0, flat_width - rows_dev))
+    )
+    q_flat, k_flat = lax.optimization_barrier((masked(queries), masked(keys)))
+    g_flat, v_flat = masked(out_grad), masked(values)
+    v_flat = jnp.concatenate([v_flat, flag_rows], axis=0)
+    q_moved = {s: shift_x(q_flat, s) for s in (2, 1, XS - 1)}
+    k_moved = {s: shift_y(k_flat, s) for s in range(1, ys)}
+    g_flat, v_flat, q_moved[1], k_moved[1] = lax.optimization_barrier(
+        (g_flat, v_flat, q_moved[1], k_moved[1])
+    )
+    q_moved, k_moved = lax.optimization_barrier((q_moved, k_moved))
+    k_blk = jnp.concatenate([k_flat] + [k_moved[s] for s in range(1, ys)], axis=0)
+    q_line = in_line(q_flat, q_moved)
+    q_other = swap_core(q_line)
+    g_moved = {s: shift_x(g_flat, s) for s in (1, XS - 1)}
+    v_moved = {s: shift_y(v_flat, s) for s in (1, ys - 1)}
+    g_late, v_late, q_other, g_moved, v_moved = lax.optimization_barrier(
+        (g_flat, v_flat, q_other, g_moved, v_moved)
+    )
+    q_blk = both_lines(q_line, q_other)
     logit_piece = dot_f32(q_blk, k_blk, ROW_PAIR)
+    for s in range(2, XS - 1):
+        g_moved[s] = shift_x(g_late, s)
+    for s in range(2, ys - 1):
+        v_moved[s] = shift_y(v_late, s)
+    key_pieces = [v_flat] + [v_moved[s] for s in range(1, ys)]
+    v_blk = jnp.concatenate([p[:rows_dev] for p in key_pieces], axis=0)
+    g_line = in_line(g_flat, g_moved)
+    g_blk = both_lines(g_line, swap_core(g_line))
     g_blk, _ = lax.optimization_barrier((g_blk, logit_piece))
     dprob_piece = dot_f32(g_blk, v_blk, ROW_PAIR).astype(jnp.bfloat16)
     key_flags = jnp.concatenate([p[rows_dev, :rows_dev] for p in key_pieces])[None, :]
@@ -354,15 +366,15 @@
     key_moved = [shift_y(key_parts[s], -s) for s in range(1, ys)]
     line = (dq_own + dq_swapped.astype(jnp.float32)).astype(jnp.bfloat16)
     line = line.reshape(XS, rows_dev, flat_width)
-    line, key_moved[0] = lax.optimization_barrier((line, key_moved[0]))
-
-    def line_piece(s):
-        return lax.dynamic_index_in_dim(line, (own_x - s) % XS, axis=0, keepdims=False)
+    lines = [[at(y, x, c) for x in range(XS)] for y in range(ys) for c in range(2)]
+    line = lax.all_to_all(
+        line, "row", split_axis=0, concat_axis=0, tiled=True, axis_index_groups=lines
+    )
 
     def added(parts):
         return sum(p.astype(jnp.float32) for p in parts)
 
-    grad_q = added([line_piece(0)] + [shift_x(line_piece(s), -s) for s in range(1, XS)])
+    grad_q = added([line[x] for x in range(XS)])
     grad_kv = added([key_parts[0]] + key_moved)
 
     def finished(rows):

time: 173 us -> 182 us (1.052)
  starting transfers between devices: 40.4 us -> 47.8 us
  waiting for transfers between devices: 72.3 us -> 76.7 us
  blocking collectives: 10.1 us -> 7.95 us
    ppermute x6 -> x9, waiting for transfers between devices: 13.4 us -> 21.5 us  [shift_y(): lax.ppermute(table, 'row', [(at(y, x, c), at(y + step, x, c)) for y, x, c...]
    all_to_all x0 -> x1, starting transfers between devices: none -> 4.43 us  [shards(): lax.all_to_all(line, 'row', split_axis=0, concat_axis=0, tiled=True, axis...]
    ppermute x7, waiting for transfers between devices: 11.6 us -> 15.3 us  [shift_z(): return lax.ppermute(table, 'col', [(z, (z + step) % zs) for z in range(zs)])]
    ppermute x6, waiting for transfers between devices: 16.7 us -> 13.6 us  [shift_x(): lax.ppermute(table, 'row', [(at(y, x, c), at(y, x + step, c)) for y, x, c...]
    ppermute x3, starting transfers between devices: 6.21 us -> 8.83 us  [swap_core(): lax.ppermute(table, 'row', [(at(y, x, c), at(y, x, 1 - c)) for y, x, c in...]
    ppermute x6 -> x9, starting transfers between devices: 6.97 us -> 9.51 us  [shift_y(): lax.ppermute(table, 'row', [(at(y, x, c), at(y + step, x, c)) for y, x, c...]
    ppermute x6, starting transfers between devices: 8.9 us -> 6.4 us  [shift_x(): lax.ppermute(table, 'row', [(at(y, x, c), at(y, x + step, c)) for y, x, c...]
    all_gather x1, waiting for transfers between devices: 16.7 us -> 14.2 us  [shards(): both = lax.all_gather(both, 'col', axis=0, tiled=True)]
  transfers between devices with their start and end apart: 26 -> 30, of which waited for: 12 -> 14; matrix products, arithmetic and copies ran while one was open for 9% -> 8% of each run, Pallas kernels for 2% -> 2%
where the time goes in v7:
time: 182 us; the launch traced here: 181 us
  waiting for transfers between devices  76.7 us (42%)
  starting transfers between devices  47.8 us (26%)
  between operations  14.5 us (8%)
  local copies, waits for them, and re-layouts  13.9 us (8%)
  other arithmetic  9.84 us (5%)
  blocking collectives  7.95 us (4%)
  Pallas kernels  7.75 us (4%)
  matrix products  2.83 us (2%)
    ppermute x9, waiting for transfers between devices, shift_y(): lax.ppermute(table, 'row', [(at(y, x, c), at(y + step, x, c)) for y, x, c...  21.5 us
    ppermute x7, waiting for transfers between devices, shift_z(): return lax.ppermute(table, 'col', [(z, (z + step) % zs) for z in range(zs)])  15.3 us
    all_gather x1, waiting for transfers between devices, shards(): both = lax.all_gather(both, 'col', axis=0, tiled=True)  14.2 us
    ppermute x6, waiting for transfers between devices, shift_x(): lax.ppermute(table, 'row', [(at(y, x, c), at(y, x + step, c)) for y, x, c...  13.6 us
    all_to_all x2, waiting for transfers between devices, share(): lax.all_to_all(copies, axis, split_axis=0, concat_axis=0, tiled=True, axi...  12 us
    all_to_all x2, starting transfers between devices, share(): lax.all_to_all(copies, axis, split_axis=0, concat_axis=0, tiled=True, axi...  9.95 us
    ppermute x9, starting transfers between devices, shift_y(): lax.ppermute(table, 'row', [(at(y, x, c), at(y + step, x, c)) for y, x, c...  9.51 us
    ppermute x3, starting transfers between devices, swap_core(): lax.ppermute(table, 'row', [(at(y, x, c), at(y, x, 1 - c)) for y, x, c in...  8.83 us
  transfers between devices with their start and end apart: 30, of which 14 were waited for; matrix products, arithmetic and copies ran while one was open for 8% of the time, Pallas kernels for 2%

profile of v7, /device:TPU:1, one launch (start us, length us, event | category | flops | bytes accessed | tf_op | source)
XLA Modules:
  0.0 181.1 jit_solution(13496688385758107218)
XLA Ops:
  7.2 0.7 broadcast_compare_fusion
  7.9 0.7 compare_and_fusion
  9.0 1.2 bitcast_select_fusion.2
  10.2 3.4 %collective-permute-start.3 = (bf16[128,512]{1,0:T(8,128)(2,1)S(1)}, bf16[128,512]{1,0:T(8,128)(2,1)S(1)}, u32[]{:S(2)}, u32[]{:S(2)}) collective-permute-start(bf16[128,512]{1,0:T(8,128)(2,1)S(1)} %get-tuple-element.41), channel_id=1, source_target_pairs={{0,48},{8,56},{16,0},{24,8},{32,16},{40,24},{48,32},{56,40},{64,11... | collective-permute-start | bytes 393224 | tf_op jit(solution)/shard_map/ppermute | solution.py:254
  13.6 0.5 collective-permute-start.2
  14.1 0.6 collective-permute-start
  14.7 2.7 %collective-permute-start.5 = (bf16[128,512]{1,0:T(8,128)(2,1)S(1)}, bf16[128,512]{1,0:T(8,128)(2,1)S(1)}, u32[]{:S(2)}, u32[]{:S(2)}) collective-permute-start(bf16[128,512]{1,0:T(8,128)(2,1)S(1)} %get-tuple-element.42), channel_id=1, source_target_pairs={{0,192},{8,200},{16,208},{24,216},{32,224},{40,232},{48,240},{56,2... | collective-permute-start | bytes 393224 | tf_op jit(solution)/shard_map/ppermute | solution.py:251
  17.9 5.3 %collective-permute-done = bf16[128,512]{1,0:T(8,128)(2,1)S(1)} collective-permute-done((bf16[128,512]{1,0:T(8,128)(2,1)S(1)}, bf16[128,512]{1,0:T(8,128)(2,1)S(1)}, u32[]{:S(2)}, u32[]{:S(2)}) %collective-permute-start) | collective-permute-done | bytes 131104 | tf_op jit(solution)/shard_map/ppermute | solution.py:254
  23.1 1.3 collective-permute-start.1
  24.5 4.4 %collective-permute-done.1 = bf16[128,512]{1,0:T(8,128)(2,1)S(1)} collective-permute-done((bf16[128,512]{1,0:T(8,128)(2,1)S(1)}, bf16[128,512]{1,0:T(8,128)(2,1)S(1)}, u32[]{:S(2)}, u32[]{:S(2)}) %collective-permute-start.1) | collective-permute-done | bytes 131104 | tf_op jit(solution)/shard_map/ppermute | solution.py:251
  28.9 1.6 collective-permute-start.6
  30.9 1.2 collective-permute-start.7
  32.1 1.5 collective-permute-start.10
  33.6 2.1 %collective-permute-done.8 = bf16[128,512]{1,0:T(8,128)(2,1)S(1)} collective-permute-done((bf16[128,512]{1,0:T(8,128)(2,1)S(1)}, bf16[128,512]{1,0:T(8,128)(2,1)S(1)}, u32[]{:S(2)}, u32[]{:S(2)}) %collective-permute-start.8) | collective-permute-done | bytes 131104 | tf_op jit(solution)/shard_map/ppermute | solution.py:254
  35.7 1.2 collective-permute-done.7
  36.9 2.4 %collective-permute-done.9 = bf16[144,512]{1,0:T(8,128)(2,1)S(1)} collective-permute-done((bf16[144,512]{1,0:T(8,128)(2,1)S(1)}, bf16[144,512]{1,0:T(8,128)(2,1)S(1)}, u32[]{:S(2)}, u32[]{:S(2)}) %collective-permute-start.9) | collective-permute-done | bytes 147488 | tf_op jit(solution)/shard_map/ppermute | solution.py:251
  40.0 2.1 %fusion.12 = f32[1024,512]{1,0:T(8,128)} fusion(bf16[1024,512]{1,0:T(8,128)(2,1)S(1)} %bitcast.106, bf16[512,512]{1,0:T(8,128)(2,1)S(1)} %constant_dynamic-update-slice_fusion.k_ref), kind=kOutput, calls=%fused_computation.68 | convolution fusion | flops 536870912 | bytes 3670016 | tf_op jit(solution)/shard_map/dot_general | solution.py:25
  42.6 5.0 %collective-permute-done.11 = bf16[128,512]{1,0:T(8,128)(2,1)S(1)} collective-permute-done((bf16[128,512]{1,0:T(8,128)(2,1)S(1)}, bf16[128,512]{1,0:T(8,128)(2,1)S(1)}, u32[]{:S(2)}, u32[]{:S(2)}) %collective-permute-start.11) | collective-permute-done | bytes 131104 | tf_op jit(solution)/shard_map/ppermute | solution.py:254
  47.6 3.0 %collective-permute-start.12 = (bf16[4,128,512]{2,1,0:T(8,128)(2,1)S(1)}, bf16[4,128,512]{2,1,0:T(8,128)(2,1)S(1)}, u32[]{:S(2)}, u32[]{:S(2)}) collective-permute-start(bf16[4,128,512]{2,1,0:T(8,128)(2,1)S(1)} %bitcast_dynamic-update-slice_fusion), channel_id=1, source_target_pairs={{0,8},{8,0},{16,24},{24,16},{32,40},{40,32},{48,56},{56,48},{64,72... | collective-permute-start | bytes 1572872 | tf_op jit(solution)/shard_map/ppermute | solution.py:257
  50.6 0.9 slice.60
  51.6 6.1 %collective-permute-done.13 = bf16[144,512]{1,0:T(8,128)(2,1)} collective-permute-done((bf16[144,512]{1,0:T(8,128)(2,1)S(1)}, bf16[144,512]{1,0:T(8,128)(2,1)}, u32[]{:S(2)}, u32[]{:S(2)}) %collective-permute-start.13) | collective-permute-done | bytes 147488 | tf_op jit(solution)/shard_map/ppermute | solution.py:251
  57.6 0.9 slice.78
  58.8 0.7 convolution_convert_fusion
  59.5 1.0 copy-done.7
  60.5 0.7 dynamic-slice_bitcast_fusion
  61.2 1.6 collective-permute-start.14
  62.9 3.9 %collective-permute-start.18 = (bf16[128,512]{1,0:T(8,128)(2,1)}, bf16[128,512]{1,0:T(8,128)(2,1)S(1)}, u32[]{:S(2)}, u32[]{:S(2)}) collective-permute-start(bf16[128,512]{1,0:T(8,128)(2,1)} %get-tuple-element.85), channel_id=1, source_target_pairs={{0,7},{1,0},{2,1},{3,2},{4,3},{5,4},{6,5},{7,6},{8,15},{9,8},{10,9... | collective-permute-start | bytes 393224 | tf_op jit(solution)/shard_map/ppermute | solution.py:260
  66.8 6.6 %collective-permute-done.14 = bf16[128,512]{1,0:T(8,128)(2,1)S(1)} collective-permute-done((bf16[128,512]{1,0:T(8,128)(2,1)}, bf16[128,512]{1,0:T(8,128)(2,1)S(1)}, u32[]{:S(2)}, u32[]{:S(2)}) %collective-permute-start.14) | collective-permute-done | bytes 131104 | tf_op jit(solution)/shard_map/ppermute | solution.py:260
  73.4 0.9 fusion.7
  74.5 8.7 %collective-permute-done.15 = bf16[128,512]{1,0:T(8,128)(2,1)S(1)} collective-permute-done((bf16[128,512]{1,0:T(8,128)(2,1)S(1)}, bf16[128,512]{1,0:T(8,128)(2,1)S(1)}, u32[]{:S(2)}, u32[]{:S(2)}) %collective-permute-start.15) | collective-permute-done | bytes 131104 | tf_op jit(solution)/shard_map/ppermute | solution.py:260
  83.2 1.7 fusion.4
  84.9 1.5 collective-permute-start.16
  86.4 0.7 slice_bitcast_fusion.1
  87.1 1.1 cross_statistics.1
  88.2 0.8 broadcast_in_dim.85
  89.0 5.7 %all-to-all-start = ((f32[8,16,1024]{2,1,0:T(8,128)}), f32[8,16,1024]{2,1,0:T(8,128)S(1)}, u32[]{:S(2)}, u32[]{:S(2)}) async-start(f32[8,16,1024]{2,1,0:T(8,128)} %broadcast_in_dim.85), calls=%async_computation.1 | async-start | bytes 1048576 | tf_op jit(solution)/shard_map/all_to_all | solution.py:265
  94.7 1.9 %fusion.3 = (bf16[128,512]{1,0:T(8,128)(2,1)}, bf16[128,512]{1,0:T(8,128)(2,1)}) fusion(bf16[128,512]{1,0:T(8,128)(2,1)} %collective-permute-done.19, bf16[8,128,512]{2,1,0:T(8,128)(2,1)} %bitcast.117, s32[]{:T(128)S(6)} %select_n.191, s32[]{:T(128)S(6)} %select_n.185, bf16[128,512]{1,0:T(8,128)(2,1)} %collective-permute-done.16), kind=kLoop, calls=%fused_computation.17 | loop fusion | flops 524288 | bytes 786440 | tf_op jit(solution)/shard_map/convert_element_type | solution.py:338
  96.5 1.3 collective-permute-start.20
  98.0 0.7 slice_bitcast_fusion
  98.7 5.4 %all-to-all-done.stat_ref = f32[8,16,1024]{2,1,0:T(8,128)S(1)} async-done(((f32[8,16,1024]{2,1,0:T(8,128)}), f32[8,16,1024]{2,1,0:T(8,128)S(1)}, u32[]{:S(2)}, u32[]{:S(2)}) %all-to-all-start) | async-done | bytes 524320 | tf_op jit(solution)/shard_map/all_to_all | solution.py:265
  104.1 0.8 copy-done.3
  105.0 1.5 cross_grads.1
  106.5 0.7 copy-done.5
  107.2 0.9 copy-done.1
  108.1 2.0 %block_softmax.1 = (bf16[128,1024]{1,0:T(8,128)(2,1)}, f32[8,128]{1,0:T(8,128)S(1)}) custom-call(f32[128,512]{1,0:T(8,128)S(1)} %copy-done.1, bf16[128,512]{1,0:T(8,128)(2,1)S(1)} %get-tuple-element.87.own_ref, bf16[128,512]{1,0:T(8,128)(2,1)} %collective-permute-done.17.forward_ref, bf16[128,512]{1,0:T(8,128)(2,1)} %collective-permute-done.20.back_ref, ...), custom_call_target="tpu_custom_call" | custom-call | tf_op jit(solution)/shard_map/block_softmax/pallas_call | solution.py:141
  110.1 8.0 %all_to_all.20 = f32[8,8,128]{2,1,0:T(8,128)S(1)} all-to-all(f32[8,8,128]{2,1,0:T(8,128)S(1)} %broadcast_in_dim.86), channel_id=1, replica_groups={{0,8,16,24,32,40,48,56},{64,72,80,88,96,104,112,120},{128,136,144,152,1..., dimensions={0} | all-to-all | bytes 65536 | tf_op jit(solution)/shard_map/all_to_all | solution.py:265
  118.1 0.6 broadcast_in_dim.87
  118.8 4.3 %all-to-all-start.2 = ((f32[8,2,128]{2,1,0:T(2,128)}), f32[8,2,128]{2,1,0:T(2,128)S(1)}, u32[]{:S(2)}, u32[]{:S(2)}) async-start(f32[8,2,128]{2,1,0:T(2,128)} %broadcast_in_dim.87), calls=%async_computation.3 | async-start | bytes 16384 | tf_op jit(solution)/shard_map/all_to_all | solution.py:265
  123.1 6.6 %all-to-all-done.2.scale_ref = f32[8,2,128]{2,1,0:T(2,128)S(1)} async-done(((f32[8,2,128]{2,1,0:T(2,128)}), f32[8,2,128]{2,1,0:T(2,128)S(1)}, u32[]{:S(2)}, u32[]{:S(2)}) %all-to-all-start.2) | async-done | bytes 8224 | tf_op jit(solution)/shard_map/all_to_all | solution.py:265
  129.7 14.2 %all-gather.2.cloned.1.call-done.both_ref = bf16[1024,1024]{1,0:T(8,128)(2,1)} async-done(((bf16[128,1024]{1,0:T(8,128)(2,1)}), bf16[1024,1024]{1,0:T(8,128)(2,1)}) %all-gather.2.cloned.1.call-update) | async-done | bytes 2097168 | tf_op jit(solution)/shard_map/all_gather | solution.py:353
  144.0 1.6 copy-done
  145.5 0.8 copy-done.4
  146.4 2.0 %query_grads.1 = (bf16[1024,512]{1,0:T(8,128)(2,1)S(1)}, bf16[1024,512]{1,0:T(8,128)(2,1)S(1)}, f32[512,512]{1,0:T(8,128)S(1)}, bf16[512,512]{1,0:T(8,128)(2,1)S(1)}) custom-call(s32[2]{0:T(128)S(1)} %pad_add_fusion.place_ref, bf16[1024,1024]{1,0:T(8,128)(2,1)S(1)} %copy-done, f32[8,2,128]{2,1,0:T(2,128)S(1)} %all-to-all-done.2.scale_ref, ...), custom_call_target="tpu_custom_call" | custom-call | tf_op jit(solution)/shard_map/query_grads/pallas_call | solution.py:184
  148.3 4.2 %collective-permute-start.21 = (bf16[512,512]{1,0:T(8,128)(2,1)S(1)}, bf16[512,512]{1,0:T(8,128)(2,1)S(1)}, u32[]{:S(2)}, u32[]{:S(2)}) collective-permute-start(bf16[512,512]{1,0:T(8,128)(2,1)S(1)} %get-tuple-element.71), channel_id=1, source_target_pairs={{0,8},{8,0},{16,24},{24,16},{32,40},{40,32},{48,56},{56,48},{64,72... | collective-permute-start | bytes 1572872 | tf_op jit(solution)/shard_map/ppermute | solution.py:257
  152.6 1.3 key_grads.1
  153.9 3.0 %collective-permute-start.22 = (bf16[128,1024]{1,0:T(8,128)(2,1)S(1)}, bf16[128,1024]{1,0:T(8,128)(2,1)S(1)}, u32[]{:S(2)}, u32[]{:S(2)}) collective-permute-start(bf16[128,1024]{1,0:T(8,128)(2,1)S(1)} %get-tuple-element.76), channel_id=1, source_target_pairs={{0,192},{8,200},{16,208},{24,216},{32,224},{40,232},{48,240},{56,2... | collective-permute-start | bytes 786440 | tf_op jit(solution)/shard_map/ppermute | solution.py:251
  156.8 0.7 collective-permute-start.24
  157.5 1.0 add_convert_fusion
  158.5 4.4 %all-to-all-start.3 = ((bf16[4,128,512]{2,1,0:T(8,128)(2,1)}), bf16[4,128,512]{2,1,0:T(8,128)(2,1)S(1)}, u32[]{:S(2)}, u32[]{:S(2)}) async-start(bf16[4,128,512]{2,1,0:T(8,128)(2,1)} %bitcast.37), calls=%async_computation.4 | async-start | bytes 1048576 | tf_op jit(solution)/shard_map/all_to_all | solution.py:370
  162.9 5.1 %collective-permute-done.22 = bf16[128,1024]{1,0:T(8,128)(2,1)S(1)} collective-permute-done((bf16[128,1024]{1,0:T(8,128)(2,1)S(1)}, bf16[128,1024]{1,0:T(8,128)(2,1)S(1)}, u32[]{:S(2)}, u32[]{:S(2)}) %collective-permute-start.22) | collective-permute-done | bytes 262176 | tf_op jit(solution)/shard_map/ppermute | solution.py:251
  168.0 3.6 %collective-permute-done.24 = bf16[128,1024]{1,0:T(8,128)(2,1)S(1)} collective-permute-done((bf16[128,1024]{1,0:T(8,128)(2,1)S(1)}, bf16[128,1024]{1,0:T(8,128)(2,1)S(1)}, u32[]{:S(2)}, u32[]{:S(2)}) %collective-permute-start.24) | collective-permute-done | bytes 262176 | tf_op jit(solution)/shard_map/ppermute | solution.py:251
  171.9 0.7 reshape.137
  172.6 0.7 reshape.136
  173.4 0.9 select_convert_fusion
  (94 shorter events, 3.5 us)
Async XLA Ops:
  7.2 17.3 %copy-start.14 = (s32[128]{0:T(128)S(1)}, s32[128]{0:T(128)}, u32[]{:S(2)}) copy-start(s32[128]{0:T(128)} %param.10) | copy-start | bytes 1540
  7.2 100.0 %reduce-scatter.2.cloned.1.call-start = ((), (), s32[]{:S(2)}) async-start(), calls=%async_computation.5 | async-start | bytes 2359296 | tf_op jit(solution)/shard_map/reduce_scatter | solution.py:324
  8.8 21.7 %copy-start.10 = (pred[128,4]{1,0:T(8,128)(4,1)}, pred[128,4]{1,0:T(8,128)(4,1)S(1)}, u32[]{:S(2)}) copy-start(pred[128,4]{1,0:T(8,128)(4,1)S(1)} %copy.19) | copy-start | bytes 1540
  9.0 21.5 %copy-start.8 = (pred[128,4,128]{2,1,0:T(4,128)(4,1)}, pred[128,4,128]{2,1,0:T(4,128)(4,1)S(1)}, u32[]{:S(2)}) copy-start(pred[128,4,128]{2,1,0:T(4,128)(4,1)S(1)} %broadcast_in_dim.73) | copy-start | bytes 196612
  10.2 18.6 %collective-permute-start.3 = (bf16[128,512]{1,0:T(8,128)(2,1)S(1)}, bf16[128,512]{1,0:T(8,128)(2,1)S(1)}, u32[]{:S(2)}, u32[]{:S(2)}) collective-permute-start(bf16[128,512]{1,0:T(8,128)(2,1)S(1)} %get-tuple-element.41), channel_id=1, source_target_pairs={{0,48},{8,56},{16,0},{24,8},{32,16},{40,24},{48,32},{56,40},{64,11... | collective-permute-start | bytes 393224 | tf_op jit(solution)/shard_map/ppermute | solution.py:254
  13.6 15.2 %collective-permute-start.2 = (bf16[128,512]{1,0:T(8,128)(2,1)S(1)}, bf16[128,512]{1,0:T(8,128)(2,1)S(1)}, u32[]{:S(2)}, u32[]{:S(2)}) collective-permute-start(bf16[128,512]{1,0:T(8,128)(2,1)S(1)} %get-tuple-element.41), channel_id=1, source_target_pairs={{0,32},{8,40},{16,48},{24,56},{32,0},{40,8},{48,16},{56,24},{64,96... | collective-permute-start | bytes 393224 | tf_op jit(solution)/shard_map/ppermute | solution.py:254
  14.1 9.0 %collective-permute-start = (bf16[128,512]{1,0:T(8,128)(2,1)S(1)}, bf16[128,512]{1,0:T(8,128)(2,1)S(1)}, u32[]{:S(2)}, u32[]{:S(2)}) collective-permute-start(bf16[128,512]{1,0:T(8,128)(2,1)S(1)} %get-tuple-element.41), channel_id=1, source_target_pairs={{0,16},{8,24},{16,32},{24,40},{32,48},{40,56},{48,0},{56,8},{64,80... | collective-permute-start | bytes 393224 | tf_op jit(solution)/shard_map/ppermute | solution.py:254
  14.7 14.1 %collective-permute-start.5 = (bf16[128,512]{1,0:T(8,128)(2,1)S(1)}, bf16[128,512]{1,0:T(8,128)(2,1)S(1)}, u32[]{:S(2)}, u32[]{:S(2)}) collective-permute-start(bf16[128,512]{1,0:T(8,128)(2,1)S(1)} %get-tuple-element.42), channel_id=1, source_target_pairs={{0,192},{8,200},{16,208},{24,216},{32,224},{40,232},{48,240},{56,2... | collective-permute-start | bytes 393224 | tf_op jit(solution)/shard_map/ppermute | solution.py:251
  17.5 11.4 %collective-permute-start.4 = (bf16[128,512]{1,0:T(8,128)(2,1)S(1)}, bf16[128,512]{1,0:T(8,128)(2,1)S(1)}, u32[]{:S(2)}, u32[]{:S(2)}) collective-permute-start(bf16[128,512]{1,0:T(8,128)(2,1)S(1)} %get-tuple-element.42), channel_id=1, source_target_pairs={{0,128},{8,136},{16,144},{24,152},{32,160},{40,168},{48,176},{56,1... | collective-permute-start | bytes 393224 | tf_op jit(solution)/shard_map/ppermute | solution.py:251
  23.1 5.7 %collective-permute-start.1 = (bf16[128,512]{1,0:T(8,128)(2,1)S(1)}, bf16[128,512]{1,0:T(8,128)(2,1)S(1)}, u32[]{:S(2)}, u32[]{:S(2)}) collective-permute-start(bf16[128,512]{1,0:T(8,128)(2,1)S(1)} %get-tuple-element.42), channel_id=1, source_target_pairs={{0,64},{8,72},{16,80},{24,88},{32,96},{40,104},{48,112},{56,120},{... | collective-permute-start | bytes 393224 | tf_op jit(solution)/shard_map/ppermute | solution.py:251
  28.9 10.3 %collective-permute-start.6 = (bf16[4,128,512]{2,1,0:T(8,128)(2,1)S(1)}, bf16[4,128,512]{2,1,0:T(8,128)(2,1)S(1)}, u32[]{:S(2)}, u32[]{:S(2)}) collective-permute-start(bf16[4,128,512]{2,1,0:T(8,128)(2,1)S(1)} %bitcast_dynamic-update-slice_fusion.4), channel_id=1, source_target_pairs={{0,8},{8,0},{16,24},{24,16},{32,40},{40,32},{48,56},{56,48},{64,72... | collective-permute-start | bytes 1572872 | tf_op jit(solution)/shard_map/ppermute | solution.py:257
  30.5 5.2 %collective-permute-start.8 = (bf16[128,512]{1,0:T(8,128)(2,1)S(1)}, bf16[128,512]{1,0:T(8,128)(2,1)S(1)}, u32[]{:S(2)}, u32[]{:S(2)}) collective-permute-start(bf16[128,512]{1,0:T(8,128)(2,1)S(1)} %get-tuple-element.56), channel_id=1, source_target_pairs={{0,48},{8,56},{16,0},{24,8},{32,16},{40,24},{48,32},{56,40},{64,11... | collective-permute-start | bytes 393224 | tf_op jit(solution)/shard_map/ppermute | solution.py:254
  30.9 6.0 %collective-permute-start.7 = (bf16[128,512]{1,0:T(8,128)(2,1)S(1)}, bf16[128,512]{1,0:T(8,128)(2,1)S(1)}, u32[]{:S(2)}, u32[]{:S(2)}) collective-permute-start(bf16[128,512]{1,0:T(8,128)(2,1)S(1)} %get-tuple-element.56), channel_id=1, source_target_pairs={{0,16},{8,24},{16,32},{24,40},{32,48},{40,56},{48,0},{56,8},{64,80... | collective-permute-start | bytes 393224 | tf_op jit(solution)/shard_map/ppermute | solution.py:254
  32.1 4.8 %collective-permute-start.10 = (bf16[144,512]{1,0:T(8,128)(2,1)S(1)}, bf16[144,512]{1,0:T(8,128)(2,1)S(1)}, u32[]{:S(2)}, u32[]{:S(2)}) collective-permute-start(bf16[144,512]{1,0:T(8,128)(2,1)S(1)} %fusion.8), channel_id=1, source_target_pairs={{0,192},{8,200},{16,208},{24,216},{32,224},{40,232},{48,240},{56,2... | collective-permute-start | bytes 442376 | tf_op jit(solution)/shard_map/ppermute | solution.py:251
  33.5 5.7 %collective-permute-start.9 = (bf16[144,512]{1,0:T(8,128)(2,1)S(1)}, bf16[144,512]{1,0:T(8,128)(2,1)S(1)}, u32[]{:S(2)}, u32[]{:S(2)}) collective-permute-start(bf16[144,512]{1,0:T(8,128)(2,1)S(1)} %fusion.8), channel_id=1, source_target_pairs={{0,64},{8,72},{16,80},{24,88},{32,96},{40,104},{48,112},{56,120},{... | collective-permute-start | bytes 442376 | tf_op jit(solution)/shard_map/ppermute | solution.py:251
  36.9 14.7 %copy-start.12 = (bf16[144,512]{1,0:T(8,128)(2,1)}, bf16[144,512]{1,0:T(8,128)(2,1)S(1)}, u32[]{:S(2)}) copy-start(bf16[144,512]{1,0:T(8,128)(2,1)S(1)} %collective-permute-done.10) | copy-start | bytes 442372
  39.2 0.7 copy-start.13
  42.2 5.4 %collective-permute-start.11 = (bf16[128,512]{1,0:T(8,128)(2,1)S(1)}, bf16[128,512]{1,0:T(8,128)(2,1)S(1)}, u32[]{:S(2)}, u32[]{:S(2)}) collective-permute-start(bf16[128,512]{1,0:T(8,128)(2,1)S(1)} %get-tuple-element.56), channel_id=1, source_target_pairs={{0,32},{8,40},{16,48},{24,56},{32,0},{40,8},{48,16},{56,24},{64,96... | collective-permute-start | bytes 393224 | tf_op jit(solution)/shard_map/ppermute | solution.py:254
  47.6 11.0 %collective-permute-start.12 = (bf16[4,128,512]{2,1,0:T(8,128)(2,1)S(1)}, bf16[4,128,512]{2,1,0:T(8,128)(2,1)S(1)}, u32[]{:S(2)}, u32[]{:S(2)}) collective-permute-start(bf16[4,128,512]{2,1,0:T(8,128)(2,1)S(1)} %bitcast_dynamic-update-slice_fusion), channel_id=1, source_target_pairs={{0,8},{8,0},{16,24},{24,16},{32,40},{40,32},{48,56},{56,48},{64,72... | collective-permute-start | bytes 1572872 | tf_op jit(solution)/shard_map/ppermute | solution.py:257
  50.6 7.0 %collective-permute-start.13 = (bf16[144,512]{1,0:T(8,128)(2,1)S(1)}, bf16[144,512]{1,0:T(8,128)(2,1)}, u32[]{:S(2)}, u32[]{:S(2)}) collective-permute-start(bf16[144,512]{1,0:T(8,128)(2,1)S(1)} %fusion.8), channel_id=1, source_target_pairs={{0,128},{8,136},{16,144},{24,152},{32,160},{40,168},{48,176},{56,1... | collective-permute-start | bytes 442376 | tf_op jit(solution)/shard_map/ppermute | solution.py:251
  59.5 1.0 copy-start.7
  61.2 12.2 %collective-permute-start.14 = (bf16[128,512]{1,0:T(8,128)(2,1)}, bf16[128,512]{1,0:T(8,128)(2,1)S(1)}, u32[]{:S(2)}, u32[]{:S(2)}) collective-permute-start(bf16[128,512]{1,0:T(8,128)(2,1)} %get-tuple-element.86), channel_id=1, source_target_pairs={{0,1},{1,2},{2,3},{3,4},{4,5},{5,6},{6,7},{7,0},{8,9},{9,10},{10,1... | collective-permute-start | bytes 393224 | tf_op jit(solution)/shard_map/ppermute | solution.py:260
  62.9 11.6 %collective-permute-start.18 = (bf16[128,512]{1,0:T(8,128)(2,1)}, bf16[128,512]{1,0:T(8,128)(2,1)S(1)}, u32[]{:S(2)}, u32[]{:S(2)}) collective-permute-start(bf16[128,512]{1,0:T(8,128)(2,1)} %get-tuple-element.85), channel_id=1, source_target_pairs={{0,7},{1,0},{2,1},{3,2},{4,3},{5,4},{6,5},{7,6},{8,15},{9,8},{10,9... | collective-permute-start | bytes 393224 | tf_op jit(solution)/shard_map/ppermute | solution.py:260
  74.3 8.8 %collective-permute-start.15 = (bf16[128,512]{1,0:T(8,128)(2,1)S(1)}, bf16[128,512]{1,0:T(8,128)(2,1)S(1)}, u32[]{:S(2)}, u32[]{:S(2)}) collective-permute-start(bf16[128,512]{1,0:T(8,128)(2,1)S(1)} %fusion.7), channel_id=1, source_target_pairs={{0,1},{1,2},{2,3},{3,4},{4,5},{5,6},{6,7},{7,0},{8,9},{9,10},{10,1... | collective-permute-start | bytes 393224 | tf_op jit(solution)/shard_map/ppermute | solution.py:260
  84.9 9.8 %collective-permute-start.19 = (bf16[128,512]{1,0:T(8,128)(2,1)}, bf16[128,512]{1,0:T(8,128)(2,1)}, u32[]{:S(2)}, u32[]{:S(2)}) collective-permute-start(bf16[128,512]{1,0:T(8,128)(2,1)} %get-tuple-element.83), channel_id=1, source_target_pairs={{0,7},{1,0},{2,1},{3,2},{4,3},{5,4},{6,5},{7,6},{8,15},{9,8},{10,9... | collective-permute-start | bytes 393224 | tf_op jit(solution)/shard_map/ppermute | solution.py:260
  84.9 9.8 %collective-permute-start.16 = (bf16[128,512]{1,0:T(8,128)(2,1)}, bf16[128,512]{1,0:T(8,128)(2,1)}, u32[]{:S(2)}, u32[]{:S(2)}) collective-permute-start(bf16[128,512]{1,0:T(8,128)(2,1)} %get-tuple-element.84), channel_id=1, source_target_pairs={{0,1},{1,2},{2,3},{3,4},{4,5},{5,6},{6,7},{7,0},{8,9},{9,10},{10,1... | collective-permute-start | bytes 393224 | tf_op jit(solution)/shard_map/ppermute | solution.py:260
  88.2 0.9 copy-start.2
  89.0 15.1 %all-to-all-start = ((f32[8,16,1024]{2,1,0:T(8,128)}), f32[8,16,1024]{2,1,0:T(8,128)S(1)}, u32[]{:S(2)}, u32[]{:S(2)}) async-start(f32[8,16,1024]{2,1,0:T(8,128)} %broadcast_in_dim.85), calls=%async_computation.1 | async-start | bytes 1048576 | tf_op jit(solution)/shard_map/all_to_all | solution.py:265
  94.7 49.3 %all-gather.2.cloned.1.call-start = ((), (), s32[]{:S(2)}) async-start(), calls=%async_computation.6 | async-start | bytes 2359296 | tf_op jit(solution)/shard_map/all_gather | solution.py:353
  96.5 10.6 %collective-permute-start.20 = (bf16[128,512]{1,0:T(8,128)(2,1)}, bf16[128,512]{1,0:T(8,128)(2,1)}, u32[]{:S(2)}, u32[]{:S(2)}) collective-permute-start(bf16[128,512]{1,0:T(8,128)(2,1)} %get-tuple-element.81), channel_id=1, source_target_pairs={{0,7},{1,0},{2,1},{3,2},{4,3},{5,4},{6,5},{7,6},{8,15},{9,8},{10,9... | collective-permute-start | bytes 393224 | tf_op jit(solution)/shard_map/ppermute | solution.py:260
  97.9 9.3 %collective-permute-start.17 = (bf16[128,512]{1,0:T(8,128)(2,1)}, bf16[128,512]{1,0:T(8,128)(2,1)}, u32[]{:S(2)}, u32[]{:S(2)}) collective-permute-start(bf16[128,512]{1,0:T(8,128)(2,1)} %get-tuple-element.82), channel_id=1, source_target_pairs={{0,1},{1,2},{2,3},{3,4},{4,5},{5,6},{6,7},{7,0},{8,9},{9,10},{10,1... | collective-permute-start | bytes 393224 | tf_op jit(solution)/shard_map/ppermute | solution.py:260
  104.1 0.8 copy-start.3
  106.5 0.7 copy-start.5
  107.2 1.0 copy-start.1
  108.1 44.5 %copy-start.6 = (f32[32,1024]{1,0:T(8,128)S(1)}, f32[32,1024]{1,0:T(8,128)}, u32[]{:S(2)}) copy-start(f32[32,1024]{1,0:T(8,128)} %copy-done.5) | copy-start | bytes 393220
  118.8 11.0 %all-to-all-start.2 = ((f32[8,2,128]{2,1,0:T(2,128)}), f32[8,2,128]{2,1,0:T(2,128)S(1)}, u32[]{:S(2)}, u32[]{:S(2)}) async-start(f32[8,2,128]{2,1,0:T(2,128)} %broadcast_in_dim.87), calls=%async_computation.3 | async-start | bytes 16384 | tf_op jit(solution)/shard_map/all_to_all | solution.py:265
  144.0 1.6 copy-start
  145.5 0.8 copy-start.4
  148.3 9.2 %collective-permute-start.21 = (bf16[512,512]{1,0:T(8,128)(2,1)S(1)}, bf16[512,512]{1,0:T(8,128)(2,1)S(1)}, u32[]{:S(2)}, u32[]{:S(2)}) collective-permute-start(bf16[512,512]{1,0:T(8,128)(2,1)S(1)} %get-tuple-element.71), channel_id=1, source_target_pairs={{0,8},{8,0},{16,24},{24,16},{32,40},{40,32},{48,56},{56,48},{64,72... | collective-permute-start | bytes 1572872 | tf_op jit(solution)/shard_map/ppermute | solution.py:257
  153.9 14.2 %collective-permute-start.22 = (bf16[128,1024]{1,0:T(8,128)(2,1)S(1)}, bf16[128,1024]{1,0:T(8,128)(2,1)S(1)}, u32[]{:S(2)}, u32[]{:S(2)}) collective-permute-start(bf16[128,1024]{1,0:T(8,128)(2,1)S(1)} %get-tuple-element.76), channel_id=1, source_target_pairs={{0,192},{8,200},{16,208},{24,216},{32,224},{40,232},{48,240},{56,2... | collective-permute-start | bytes 786440 | tf_op jit(solution)/shard_map/ppermute | solution.py:251
  156.8 11.2 %collective-permute-start.23 = (bf16[128,1024]{1,0:T(8,128)(2,1)S(1)}, bf16[128,1024]{1,0:T(8,128)(2,1)S(1)}, u32[]{:S(2)}, u32[]{:S(2)}) collective-permute-start(bf16[128,1024]{1,0:T(8,128)(2,1)S(1)} %get-tuple-element.77), channel_id=1, source_target_pairs={{0,128},{8,136},{16,144},{24,152},{32,160},{40,168},{48,176},{56,1... | collective-permute-start | bytes 786440 | tf_op jit(solution)/shard_map/ppermute | solution.py:251
  156.8 14.8 %collective-permute-start.24 = (bf16[128,1024]{1,0:T(8,128)(2,1)S(1)}, bf16[128,1024]{1,0:T(8,128)(2,1)S(1)}, u32[]{:S(2)}, u32[]{:S(2)}) collective-permute-start(bf16[128,1024]{1,0:T(8,128)(2,1)S(1)} %get-tuple-element.78), channel_id=1, source_target_pairs={{0,64},{8,72},{16,80},{24,88},{32,96},{40,104},{48,112},{56,120},{... | collective-permute-start | bytes 786440 | tf_op jit(solution)/shard_map/ppermute | solution.py:251
  157.5 14.3 %copy-start.9 = (pred[128,4,128]{2,1,0:T(4,128)(4,1)S(1)}, pred[128,4,128]{2,1,0:T(4,128)(4,1)}, u32[]{:S(2)}) copy-start(pred[128,4,128]{2,1,0:T(4,128)(4,1)} %copy-done.8) | copy-start | bytes 196612
  158.5 14.9 %copy-start.11 = (pred[128,4]{1,0:T(8,128)(4,1)S(1)}, pred[128,4]{1,0:T(8,128)(4,1)}, u32[]{:S(2)}) copy-start(pred[128,4]{1,0:T(8,128)(4,1)} %copy-done.10) | copy-start | bytes 1540
  158.5 14.8 %all-to-all-start.3 = ((bf16[4,128,512]{2,1,0:T(8,128)(2,1)}), bf16[4,128,512]{2,1,0:T(8,128)(2,1)S(1)}, u32[]{:S(2)}, u32[]{:S(2)}) async-start(bf16[4,128,512]{2,1,0:T(8,128)(2,1)} %bitcast.37), calls=%async_computation.4 | async-start | bytes 1048576 | tf_op jit(solution)/shard_map/all_to_all | solution.py:370
Sparse Core Ops, SparseCore 0:
  42.2 41.8 reduce-scatter.1
  110.2 33.6 all-gather.1

commit v8 on v6

--- a/solution.py
+++ b/solution.py
@@ -46,15 +46,16 @@
     return scores, dprob, lanes, other
 
 
-def cross_statistics(q_blk, g_blk, k_blk, v_blk, tokens, feature, inv_root):
+def cross_statistics(q_blk, g_blk, k_blk, v_blk, row_stats, tokens, feature, inv_root):
     block_keys, flat_width = k_blk.shape
     both_width = 2 * flat_width
     block_rows = q_blk.shape[0]
     group = block_keys // tokens
     columns = both_width // (2 * feature)
-    stat_rows = -(-3 * columns // 8) * 8
-
-    def kernel(q_ref, g_ref, k_ref, v_ref, sums_ref, stat_ref):
+    stat_rows = -(-(3 * columns + 1) // 8) * 8
+    kinds, rows = 3, row_stats.shape[1]
+
+    def kernel(q_ref, g_ref, k_ref, v_ref, row_ref, sums_ref, stat_ref):
         for half, table_ref in enumerate((k_ref, v_ref)):
             pooled = jnp.sum(
                 table_ref[...].astype(jnp.float32).reshape(tokens, group, flat_width), axis=1
@@ -71,10 +72,11 @@
             stat_ref[2 * columns + c : 2 * columns + c + 1, :] = jnp.sum(
                 lifted * dprob, axis=0, keepdims=True
             )
-        if stat_rows > 3 * columns:
-            stat_ref[3 * columns :, :] = jnp.zeros(
-                (stat_rows - 3 * columns, block_rows), jnp.float32
-            )
+        stat_ref[3 * columns :, :] = jnp.zeros((stat_rows - 3 * columns, block_rows), jnp.float32)
+        for i in range(kinds):
+            stat_ref[3 * columns : 3 * columns + 1, i * rows : (i + 1) * rows] = row_ref[
+                i : i + 1, :
+            ]
 
     return pl.pallas_call(
         kernel,
@@ -84,7 +86,7 @@
         ),
         compiler_params=ROOM,
         name="cross_statistics",
-    )(q_blk, g_blk, k_blk, v_blk)
+    )(q_blk, g_blk, k_blk, v_blk, row_stats)
 
 
 def cross_grads(q_blk, g_blk, sums, all_stats, feature, inv_root):
@@ -157,13 +159,19 @@
     columns = cross_dl.shape[0] // tokens
     feature = flat_width // columns
 
-    def kernel(place_ref, both_ref, scale_ref, k_ref, dl_ref, sums_ref, p_ref, ds_ref, own_ref, other_ref, dq_ref):
+    def kernel(place_ref, both_ref, scale_ref, k_ref, dl_ref, sums_ref, p_ref, ds_ref, own_ref, other_ref, dq_ref, held_ref, sems):
         core = place_ref[0]
+        copies = []
+        for i in range(chunks):
+            at = pl.ds(i * rows, rows)
+            copies.append(pltpu.make_async_copy(both_ref.at[at], held_ref.at[at], sems.at[i]))
+            copies[i].start()
         for i in range(chunks):
             at = slice(i * rows, (i + 1) * rows)
+            copies[i].wait()
             weight, offset = upright(scale_ref[i, 0:1, :]), upright(scale_ref[i, 1:2, :])
-            lifted = both_ref[at, :width].astype(jnp.float32)
-            tilted = both_ref[at, width:].astype(jnp.float32)
+            lifted = held_ref[at, :width].astype(jnp.float32)
+            tilted = held_ref[at, width:].astype(jnp.float32)
             p_ref[at, :] = (lifted * weight).astype(jnp.bfloat16)
             ds_ref[at, :] = ((tilted - lifted * offset) * (weight * logit_scale)).astype(
                 jnp.bfloat16
@@ -183,14 +191,18 @@
 
     return pl.pallas_call(
         kernel,
-        in_specs=[SMEM] + [WHOLE] * 5,
+        in_specs=[SMEM, pl.BlockSpec(memory_space=pltpu.HBM)] + [WHOLE] * 4,
         out_shape=(
             jax.ShapeDtypeStruct((block_rows, width), jnp.bfloat16),
             jax.ShapeDtypeStruct((block_rows, width), jnp.bfloat16),
             jax.ShapeDtypeStruct((block_rows // 2, flat_width), jnp.float32),
             jax.ShapeDtypeStruct((block_rows // 2, flat_width), jnp.bfloat16),
         ),
-        scratch_shapes=[pltpu.VMEM((block_rows, flat_width), jnp.float32)],
+        scratch_shapes=[
+            pltpu.VMEM((block_rows, flat_width), jnp.float32),
+            pltpu.VMEM((block_rows, 2 * width), jnp.bfloat16),
+            pltpu.SemaphoreType.DMA((chunks,)),
+        ],
         compiler_params=ROOM,
         name="query_grads",
     )(place, both, scaling, k_blk, cross_dl, sums)
@@ -329,22 +341,23 @@
     dprob_forward = passed(1, zs // 2)
     dprob_back = passed(-1, zs - 1 - zs // 2)
 
-    sums, own_stats = cross_statistics(q_blk, g_blk, k_blk, v_blk, tokens, feature, inv_root)
-    cross_dl, dsum = cross_grads(
-        q_blk, g_blk, sums, share(own_stats, "row", near), feature, inv_root
-    )
-
     both, stats = block_softmax(
         logit_scale, logit_sum, part(0), dprob_forward, dprob_back, key_flags
     )
-    both, stats, cross_dl, dsum = lax.optimization_barrier((both, stats, cross_dl, dsum))
     both = lax.all_gather(both, "col", axis=0, tiled=True)
-    all_stats = share(stats, "row", near)
-    weight = jnp.exp(all_stats[:, 0] - jnp.max(all_stats[:, 0], axis=0))
-    total = jnp.sum(weight * all_stats[:, 1], axis=0)
-    delta = jnp.sum(weight * all_stats[:, 2], axis=0) / total
-    own_weight = jnp.exp(stats[0] - jnp.max(all_stats[:, 0], axis=0)) / total
-    scaling = share(jnp.stack([own_weight, delta - stats[3]]), "col")
+
+    sums, own_stats = cross_statistics(
+        q_blk, g_blk, k_blk, v_blk, stats, tokens, feature, inv_root
+    )
+    all_stats = share(own_stats, "row", near)
+    row_stats = all_stats[:, 3 * cols_dev, : 3 * rows_dev].reshape(near_size, 3, rows_dev)
+    peak = jnp.max(row_stats[:, 0], axis=0)
+    weight = jnp.exp(row_stats[:, 0] - peak)
+    total = jnp.sum(weight * row_stats[:, 1], axis=0)
+    delta = jnp.sum(weight * row_stats[:, 2], axis=0) / total
+    scaling = share(jnp.stack([jnp.exp(stats[0] - peak) / total, delta - stats[3]]), "col")
+    cross_dl, dsum = cross_grads(q_blk, g_blk, sums, all_stats, feature, inv_root)
+    both, scaling, cross_dl, dsum = lax.optimization_barrier((both, scaling, cross_dl, dsum))
 
     prob, dlogit, dq_own, dq_other = query_grads(
         logit_scale, place, both, scaling, k_blk, cross_dl, sums, zs
@@ -354,15 +367,15 @@
     key_moved = [shift_y(key_parts[s], -s) for s in range(1, ys)]
     line = (dq_own + dq_swapped.astype(jnp.float32)).astype(jnp.bfloat16)
     line = line.reshape(XS, rows_dev, flat_width)
-    line, key_moved[0] = lax.optimization_barrier((line, key_moved[0]))
-
-    def line_piece(s):
-        return lax.dynamic_index_in_dim(line, (own_x - s) % XS, axis=0, keepdims=False)
+    lines = [[at(y, x, c) for x in range(XS)] for y in range(ys) for c in range(2)]
+    line = lax.all_to_all(
+        line, "row", split_axis=0, concat_axis=0, tiled=True, axis_index_groups=lines
+    )
 
     def added(parts):
         return sum(p.astype(jnp.float32) for p in parts)
 
-    grad_q = added([line_piece(0)] + [shift_x(line_piece(s), -s) for s in range(1, XS)])
+    grad_q = added([line[x] for x in range(XS)])
     grad_kv = added([key_parts[0]] + key_moved)
 
     def finished(rows):

time: 173 us -> 166 us (0.960)
  waiting for transfers between devices: 72.3 us -> 63.2 us
  blocking collectives: 10.1 us -> 17.4 us
  starting transfers between devices: 40.4 us -> 35.7 us
  local copies, waits for them, and re-layouts: 14.4 us -> 12.5 us
  other arithmetic: 8.92 us -> 10.8 us
    ppermute x7, waiting for transfers between devices: 11.6 us -> 24.4 us  [shift_z(): return lax.ppermute(table, 'col', [(z, (z + step) % zs) for z in range(zs)])]
    all_gather x1, waiting for transfers between devices: 16.7 us -> 8.76 us  [shards(): both = lax.all_gather(both, 'col', axis=0, tiled=True)]
    all_to_all x2 -> x1, waiting for transfers between devices: 12 us -> 4.41 us  [share(): lax.all_to_all(copies, axis, split_axis=0, concat_axis=0, tiled=True, axi...]
    all_to_all x1, blocking collectives: 10.1 us -> 17.4 us  [share(): lax.all_to_all(copies, axis, split_axis=0, concat_axis=0, tiled=True, axi...]
    all_to_all x2 -> x1, starting transfers between devices: 9.57 us -> 3.71 us  [share(): lax.all_to_all(copies, axis, split_axis=0, concat_axis=0, tiled=True, axi...]
    ppermute x6 -> x3, waiting for transfers between devices: 16.7 us -> 11.2 us  [shift_x(): lax.ppermute(table, 'row', [(at(y, x, c), at(y, x + step, c)) for y, x, c...]
    all_to_all x0 -> x1, starting transfers between devices: none -> 4.1 us  [shards(): lax.all_to_all(line, 'row', split_axis=0, concat_axis=0, tiled=True, axis...]
    ppermute x6 -> x3, starting transfers between devices: 8.9 us -> 4.84 us  [shift_x(): lax.ppermute(table, 'row', [(at(y, x, c), at(y, x + step, c)) for y, x, c...]
  transfers between devices with their start and end apart: 26 -> 23, of which waited for: 12 -> 16; matrix products, arithmetic and copies ran while one was open for 9% -> 10% of each run, Pallas kernels for 2% -> 2%
where the time goes in v8:
time: 166 us; the launch traced here: 165 us
  waiting for transfers between devices  63.2 us (38%)
  starting transfers between devices  35.7 us (22%)
  blocking collectives  17.4 us (10%)
  between operations  14.3 us (9%)
  local copies, waits for them, and re-layouts  12.5 us (8%)
  other arithmetic  10.8 us (7%)
  Pallas kernels  7.62 us (5%)
  matrix products  3.8 us (2%)
    ppermute x7, waiting for transfers between devices, shift_z(): return lax.ppermute(table, 'col', [(z, (z + step) % zs) for z in range(zs)])  24.4 us
    all_to_all x1, blocking collectives, share(): lax.all_to_all(copies, axis, split_axis=0, concat_axis=0, tiled=True, axi...  17.4 us
    ppermute x6, waiting for transfers between devices, shift_y(): lax.ppermute(table, 'row', [(at(y, x, c), at(y + step, x, c)) for y, x, c...  11.5 us
    ppermute x3, waiting for transfers between devices, shift_x(): lax.ppermute(table, 'row', [(at(y, x, c), at(y, x + step, c)) for y, x, c...  11.2 us
    ppermute x7, starting transfers between devices, shift_z(): return lax.ppermute(table, 'col', [(z, (z + step) % zs) for z in range(zs)])  8.85 us
    all_gather x1, waiting for transfers between devices, shards(): both = lax.all_gather(both, 'col', axis=0, tiled=True)  8.76 us
    ppermute x6, starting transfers between devices, shift_y(): lax.ppermute(table, 'row', [(at(y, x, c), at(y + step, x, c)) for y, x, c...  7.58 us
    ppermute x3, starting transfers between devices, swap_core(): lax.ppermute(table, 'row', [(at(y, x, c), at(y, x, 1 - c)) for y, x, c in...  6.5 us
  transfers between devices with their start and end apart: 23, of which 16 were waited for; matrix products, arithmetic and copies ran while one was open for 10% of the time, Pallas kernels for 2%

profile of v8, /device:TPU:1, one launch (start us, length us, event | category | flops | bytes accessed | tf_op | source)
XLA Modules:
  0.0 165.3 jit_solution(16762389451589882613)
XLA Ops:
  7.2 0.7 convert_bitcast_fusion
  7.9 0.7 broadcast_compare_fusion
  8.5 0.7 compare_and_fusion
  9.6 1.2 bitcast_select_fusion.1
  10.9 3.4 %collective-permute-start.2 = (bf16[128,1024]{1,0:T(8,128)(2,1)S(1)}, bf16[128,1024]{1,0:T(8,128)(2,1)S(1)}, u32[]{:S(2)}, u32[]{:S(2)}) collective-permute-start(bf16[128,1024]{1,0:T(8,128)(2,1)S(1)} %pad_maximum_fusion.4), channel_id=1, source_target_pairs={{0,48},{8,56},{16,0},{24,8},{32,16},{40,24},{48,32},{56,40},{64,11... | collective-permute-start | bytes 786440 | tf_op jit(solution)/shard_map/ppermute | solution.py:266
  14.3 2.7 %collective-permute-start.5 = (bf16[144,1024]{1,0:T(8,128)(2,1)S(1)}, bf16[144,1024]{1,0:T(8,128)(2,1)S(1)}, u32[]{:S(2)}, u32[]{:S(2)}) collective-permute-start(bf16[144,1024]{1,0:T(8,128)(2,1)S(1)} %fusion.1), channel_id=1, source_target_pairs={{0,192},{8,200},{16,208},{24,216},{32,224},{40,232},{48,240},{56,2... | collective-permute-start | bytes 884744 | tf_op jit(solution)/shard_map/ppermute | solution.py:263
  17.4 0.7 collective-permute-start.3
  18.1 0.5 collective-permute-start.1
  18.6 0.7 collective-permute-done.2
  19.2 0.9 collective-permute-start
  20.2 5.4 %collective-permute-done.1 = bf16[128,1024]{1,0:T(8,128)(2,1)S(1)} collective-permute-done((bf16[128,1024]{1,0:T(8,128)(2,1)S(1)}, bf16[128,1024]{1,0:T(8,128)(2,1)S(1)}, u32[]{:S(2)}, u32[]{:S(2)}) %collective-permute-start.1) | collective-permute-done | bytes 262176 | tf_op jit(solution)/shard_map/ppermute | solution.py:266
  25.6 5.1 %collective-permute-done = bf16[128,1024]{1,0:T(8,128)(2,1)S(1)} collective-permute-done((bf16[128,1024]{1,0:T(8,128)(2,1)S(1)}, bf16[128,1024]{1,0:T(8,128)(2,1)S(1)}, u32[]{:S(2)}, u32[]{:S(2)}) %collective-permute-start) | collective-permute-done | bytes 262176 | tf_op jit(solution)/shard_map/ppermute | solution.py:266
  30.7 0.7 copy-done.7
  31.4 2.3 %collective-permute-done.3 = bf16[144,1024]{1,0:T(8,128)(2,1)S(1)} collective-permute-done((bf16[144,1024]{1,0:T(8,128)(2,1)S(1)}, bf16[144,1024]{1,0:T(8,128)(2,1)S(1)}, u32[]{:S(2)}, u32[]{:S(2)}) %collective-permute-start.3) | collective-permute-done | bytes 294944 | tf_op jit(solution)/shard_map/ppermute | solution.py:263
  34.0 1.5 collective-permute-start.6
  35.5 1.0 fusion.17
  36.6 1.8 %fusion.19 = (bf16[128,512]{1,0:T(8,128)(2,1)S(1)}, bf16[128,512]{1,0:T(8,128)(2,1)S(1)}, bf16[128,512]{1,0:T(8,128)(2,1)S(1)}, bf16[128,512]{1,0:T(8,128)(2,1)}) fusion(bf16[144,1024]{1,0:T(8,128)(2,1)} %copy-done.7, bf16[144,1024]{1,0:T(8,128)(2,1)} %copy-done.6), kind=kLoop, calls=%fused_computation.75 | loop fusion | bytes 1048576 | tf_op jit(solution)/shard_map/slice | solution.py:316
  38.6 2.1 %fusion.16 = f32[1024,512]{1,0:T(8,128)} fusion(bf16[1024,512]{1,0:T(8,128)(2,1)S(1)} %bitcast.121, bf16[128,512]{1,0:T(8,128)(2,1)S(1)} %get-tuple-element.102, bf16[128,512]{1,0:T(8,128)(2,1)S(1)} %get-tuple-element.81, bf16[128,512]{1,0:T(8,128)(2,1)S(1)} %get-tuple-element.100, bf16[128,512]{1,0:T(8,128)(2,1)S(1)} %get-tuple-element.77), kind=kOutput, calls=%fused_computation.72 | convolution fusion | flops 538968064 | bytes 3670016 | tf_op jit(solution)/shard_map/dot_general | solution.py:25
  40.8 0.5 collective-permute-start.7
  41.2 1.5 collective-permute-done.7
  43.0 1.7 %convolution_convert_fusion = bf16[1024,512]{1,0:T(8,128)(2,1)} fusion(bf16[1024,512]{1,0:T(8,128)(2,1)S(1)} %bitcast.125, bf16[128,512]{1,0:T(8,128)(2,1)S(1)} %copy-done.5, bf16[128,512]{1,0:T(8,128)(2,1)S(1)} %get-tuple-element.80, bf16[128,512]{1,0:T(8,128)(2,1)S(1)} %get-tuple-element.101, bf16[128,512]{1,0:T(8,128)(2,1)S(1)} %get-tuple-element.76), kind=kOutput, calls=%fused_computation | convolution fusion | flops 539492352 | bytes 2621440 | tf_op jit(solution)/shard_map/dot_general | solution.py:25
  44.7 1.8 %dynamic-slice_bitcast_fusion = (bf16[128,512]{1,0:T(8,128)(2,1)}, bf16[128,512]{1,0:T(8,128)(2,1)}, bf16[128,512]{1,0:T(8,128)(2,1)S(1)}) fusion(bf16[8,128,512]{2,1,0:T(8,128)(2,1)} %bitcast.18, s32[]{:T(128)S(6)} %select_n.187, s32[]{:T(128)S(6)} %select_n.179, s32[]{:T(128)S(6)} %select_n.177), kind=kLoop, calls=%fused_computation.43 | loop fusion | bytes 786444 | tf_op jit(solution)/shard_map/jit(dynamic_index_in_dim)/squeeze | solution.py:329
  46.5 1.6 collective-permute-start.8
  48.1 3.9 %collective-permute-start.12 = (bf16[128,512]{1,0:T(8,128)(2,1)}, bf16[128,512]{1,0:T(8,128)(2,1)}, u32[]{:S(2)}, u32[]{:S(2)}) collective-permute-start(bf16[128,512]{1,0:T(8,128)(2,1)} %get-tuple-element.67), channel_id=1, source_target_pairs={{0,7},{1,0},{2,1},{3,2},{4,3},{5,4},{6,5},{7,6},{8,15},{9,8},{10,9... | collective-permute-start | bytes 393224 | tf_op jit(solution)/shard_map/ppermute | solution.py:272
  52.0 3.9 %collective-permute-done.8 = bf16[128,512]{1,0:T(8,128)(2,1)} collective-permute-done((bf16[128,512]{1,0:T(8,128)(2,1)}, bf16[128,512]{1,0:T(8,128)(2,1)}, u32[]{:S(2)}, u32[]{:S(2)}) %collective-permute-start.8) | collective-permute-done | bytes 131104 | tf_op jit(solution)/shard_map/ppermute | solution.py:272
  55.9 1.7 %fusion.8 = bf16[128,512]{1,0:T(8,128)(2,1)} fusion(bf16[128,512]{1,0:T(8,128)(2,1)} %collective-permute-done.8, bf16[8,128,512]{2,1,0:T(8,128)(2,1)} %bitcast.18, s32[]{:T(128)S(6)} %select_n.181), kind=kLoop, calls=%fused_computation.28 | loop fusion | flops 262144 | bytes 393220 | tf_op jit(solution)/shard_map/convert_element_type | solution.py:338
  57.6 8.1 %collective-permute-done.9 = bf16[128,512]{1,0:T(8,128)(2,1)} collective-permute-done((bf16[128,512]{1,0:T(8,128)(2,1)}, bf16[128,512]{1,0:T(8,128)(2,1)}, u32[]{:S(2)}, u32[]{:S(2)}) %collective-permute-start.9) | collective-permute-done | bytes 131104 | tf_op jit(solution)/shard_map/ppermute | solution.py:272
  65.7 1.2 fusion.5
  66.8 0.9 collective-permute-start.13
  67.8 0.6 collective-permute-start.10
  68.4 0.7 slice_bitcast_fusion.4
  69.0 4.4 %collective-permute-done.13 = bf16[128,512]{1,0:T(8,128)(2,1)S(1)} collective-permute-done((bf16[128,512]{1,0:T(8,128)(2,1)S(1)}, bf16[128,512]{1,0:T(8,128)(2,1)S(1)}, u32[]{:S(2)}, u32[]{:S(2)}) %collective-permute-start.13) | collective-permute-done | bytes 131104 | tf_op jit(solution)/shard_map/ppermute | solution.py:272
  73.5 1.0 collective-permute-done.10
  74.5 1.0 fusion.4
  75.5 1.6 collective-permute-start.14
  77.2 0.7 slice_bitcast_fusion.2
  77.9 4.5 %collective-permute-done.14.back_ref = bf16[128,512]{1,0:T(8,128)(2,1)S(1)} collective-permute-done((bf16[128,512]{1,0:T(8,128)(2,1)S(1)}, bf16[128,512]{1,0:T(8,128)(2,1)S(1)}, u32[]{:S(2)}, u32[]{:S(2)}) %collective-permute-start.14) | collective-permute-done | bytes 131104 | tf_op jit(solution)/shard_map/ppermute | solution.py:272
  82.4 2.5 %collective-permute-done.11.forward_ref = bf16[128,512]{1,0:T(8,128)(2,1)S(1)} collective-permute-done((bf16[128,512]{1,0:T(8,128)(2,1)S(1)}, bf16[128,512]{1,0:T(8,128)(2,1)S(1)}, u32[]{:S(2)}, u32[]{:S(2)}) %collective-permute-start.11) | collective-permute-done | bytes 131104 | tf_op jit(solution)/shard_map/ppermute | solution.py:272
  84.9 1.4 reduce-scatter.2.cloned.1.call-done.logit_ref
  86.3 0.9 copy-done.1
  87.2 1.0 block_softmax.1
  88.3 1.0 pad_maximum_fusion.3.v_ref
  89.3 1.1 cross_statistics.1
  90.4 17.4 %all_to_all.15.stat_ref = f32[8,16,1024]{2,1,0:T(8,128)S(1)} all-to-all(f32[8,16,1024]{2,1,0:T(8,128)S(1)} %broadcast_in_dim.79), channel_id=1, replica_groups={{0,8,16,24,32,40,48,56},{64,72,80,88,96,104,112,120},{128,136,144,152,1..., dimensions={0} | all-to-all | bytes 1048576 | tf_op jit(solution)/shard_map/all_to_all | solution.py:277
  107.9 0.6 broadcast_in_dim.80
  108.5 3.7 %all-to-all-start.1 = ((f32[8,2,128]{2,1,0:T(2,128)}), f32[8,2,128]{2,1,0:T(2,128)S(1)}, u32[]{:S(2)}, u32[]{:S(2)}) async-start(f32[8,2,128]{2,1,0:T(2,128)} %broadcast_in_dim.80), calls=%async_computation.2 | async-start | bytes 16384 | tf_op jit(solution)/shard_map/all_to_all | solution.py:277
  112.3 1.5 cross_grads.1
  113.8 0.7 copy-done.2
  114.4 4.4 %all-to-all-done.1.scale_ref = f32[8,2,128]{2,1,0:T(2,128)S(1)} async-done(((f32[8,2,128]{2,1,0:T(2,128)}), f32[8,2,128]{2,1,0:T(2,128)S(1)}, u32[]{:S(2)}, u32[]{:S(2)}) %all-to-all-start.1) | async-done | bytes 8224 | tf_op jit(solution)/shard_map/all_to_all | solution.py:277
  118.8 8.8 %all-gather.2.cloned.1.call-done.both_ref = bf16[1024,1024]{1,0:T(8,128)(2,1)} async-done(((bf16[128,1024]{1,0:T(8,128)(2,1)}), bf16[1024,1024]{1,0:T(8,128)(2,1)}) %all-gather.2.cloned.1.call-update) | async-done | bytes 2097168 | tf_op jit(solution)/shard_map/all_gather | solution.py:347
  127.6 1.6 copy-done
  129.2 2.8 %query_grads.1 = (bf16[1024,512]{1,0:T(8,128)(2,1)S(1)}, bf16[1024,512]{1,0:T(8,128)(2,1)S(1)}, f32[512,512]{1,0:T(8,128)S(1)}, bf16[512,512]{1,0:T(8,128)(2,1)S(1)}) custom-call(s32[2]{0:T(128)S(1)} %pad_add_fusion.place_ref, bf16[1024,1024]{1,0:T(8,128)(2,1)S(1)} %copy-done, f32[8,2,128]{2,1,0:T(2,128)S(1)} %all-to-all-done.1.scale_ref, ...), custom_call_target="tpu_custom_call" | custom-call | tf_op jit(solution)/shard_map/query_grads/pallas_call | solution.py:192
  132.0 4.5 %collective-permute-start.15 = (bf16[512,512]{1,0:T(8,128)(2,1)S(1)}, bf16[512,512]{1,0:T(8,128)(2,1)S(1)}, u32[]{:S(2)}, u32[]{:S(2)}) collective-permute-start(bf16[512,512]{1,0:T(8,128)(2,1)S(1)} %get-tuple-element.53), channel_id=1, source_target_pairs={{0,8},{8,0},{16,24},{24,16},{32,40},{40,32},{48,56},{56,48},{64,72... | collective-permute-start | bytes 1572872 | tf_op jit(solution)/shard_map/ppermute | solution.py:269
  136.5 1.3 key_grads.1
  137.8 2.7 %collective-permute-start.16 = (bf16[128,1024]{1,0:T(8,128)(2,1)S(1)}, bf16[128,1024]{1,0:T(8,128)(2,1)S(1)}, u32[]{:S(2)}, u32[]{:S(2)}) collective-permute-start(bf16[128,1024]{1,0:T(8,128)(2,1)S(1)} %get-tuple-element.58), channel_id=1, source_target_pairs={{0,192},{8,200},{16,208},{24,216},{32,224},{40,232},{48,240},{56,2... | collective-permute-start | bytes 786440 | tf_op jit(solution)/shard_map/ppermute | solution.py:263
  140.5 0.4 collective-permute-start.17
  140.9 0.7 collective-permute-start.18
  141.6 1.0 add_convert_fusion
  142.6 4.1 %all-to-all-start.2 = ((bf16[4,128,512]{2,1,0:T(8,128)(2,1)}), bf16[4,128,512]{2,1,0:T(8,128)(2,1)S(1)}, u32[]{:S(2)}, u32[]{:S(2)}) async-start(bf16[4,128,512]{2,1,0:T(8,128)(2,1)} %bitcast.38), calls=%async_computation.3 | async-start | bytes 1048576 | tf_op jit(solution)/shard_map/all_to_all | solution.py:371
  146.7 5.0 %collective-permute-done.16 = bf16[128,1024]{1,0:T(8,128)(2,1)S(1)} collective-permute-done((bf16[128,1024]{1,0:T(8,128)(2,1)S(1)}, bf16[128,1024]{1,0:T(8,128)(2,1)S(1)}, u32[]{:S(2)}, u32[]{:S(2)}) %collective-permute-start.16) | collective-permute-done | bytes 262176 | tf_op jit(solution)/shard_map/ppermute | solution.py:263
  151.7 4.2 %collective-permute-done.18 = bf16[128,1024]{1,0:T(8,128)(2,1)S(1)} collective-permute-done((bf16[128,1024]{1,0:T(8,128)(2,1)S(1)}, bf16[128,1024]{1,0:T(8,128)(2,1)S(1)}, u32[]{:S(2)}, u32[]{:S(2)}) %collective-permute-start.18) | collective-permute-done | bytes 262176 | tf_op jit(solution)/shard_map/ppermute | solution.py:263
  156.1 0.7 reshape.136
  156.8 0.7 reshape.135
  157.6 0.9 select_convert_fusion
  (64 shorter events, 2.3 us)
Async XLA Ops:
  7.2 79.1 %reduce-scatter.2.cloned.1.call-start = ((), (), s32[]{:S(2)}) async-start(), calls=%async_computation.4 | async-start | bytes 2359296 | tf_op jit(solution)/shard_map/reduce_scatter | solution.py:324
  9.4 1.5 copy-start.9
  10.9 8.4 %collective-permute-start.2 = (bf16[128,1024]{1,0:T(8,128)(2,1)S(1)}, bf16[128,1024]{1,0:T(8,128)(2,1)S(1)}, u32[]{:S(2)}, u32[]{:S(2)}) collective-permute-start(bf16[128,1024]{1,0:T(8,128)(2,1)S(1)} %pad_maximum_fusion.4), channel_id=1, source_target_pairs={{0,48},{8,56},{16,0},{24,8},{32,16},{40,24},{48,32},{56,40},{64,11... | collective-permute-start | bytes 786440 | tf_op jit(solution)/shard_map/ppermute | solution.py:266
  14.3 16.4 %collective-permute-start.5 = (bf16[144,1024]{1,0:T(8,128)(2,1)S(1)}, bf16[144,1024]{1,0:T(8,128)(2,1)S(1)}, u32[]{:S(2)}, u32[]{:S(2)}) collective-permute-start(bf16[144,1024]{1,0:T(8,128)(2,1)S(1)} %fusion.1), channel_id=1, source_target_pairs={{0,192},{8,200},{16,208},{24,216},{32,224},{40,232},{48,240},{56,2... | collective-permute-start | bytes 884744 | tf_op jit(solution)/shard_map/ppermute | solution.py:263
  17.0 13.7 %collective-permute-start.4 = (bf16[144,1024]{1,0:T(8,128)(2,1)S(1)}, bf16[144,1024]{1,0:T(8,128)(2,1)S(1)}, u32[]{:S(2)}, u32[]{:S(2)}) collective-permute-start(bf16[144,1024]{1,0:T(8,128)(2,1)S(1)} %fusion.1), channel_id=1, source_target_pairs={{0,128},{8,136},{16,144},{24,152},{32,160},{40,168},{48,176},{56,1... | collective-permute-start | bytes 884744 | tf_op jit(solution)/shard_map/ppermute | solution.py:263
  17.4 16.4 %collective-permute-start.3 = (bf16[144,1024]{1,0:T(8,128)(2,1)S(1)}, bf16[144,1024]{1,0:T(8,128)(2,1)S(1)}, u32[]{:S(2)}, u32[]{:S(2)}) collective-permute-start(bf16[144,1024]{1,0:T(8,128)(2,1)S(1)} %fusion.1), channel_id=1, source_target_pairs={{0,64},{8,72},{16,80},{24,88},{32,96},{40,104},{48,112},{56,120},{... | collective-permute-start | bytes 884744 | tf_op jit(solution)/shard_map/ppermute | solution.py:263
  18.1 7.5 %collective-permute-start.1 = (bf16[128,1024]{1,0:T(8,128)(2,1)S(1)}, bf16[128,1024]{1,0:T(8,128)(2,1)S(1)}, u32[]{:S(2)}, u32[]{:S(2)}) collective-permute-start(bf16[128,1024]{1,0:T(8,128)(2,1)S(1)} %pad_maximum_fusion.4), channel_id=1, source_target_pairs={{0,32},{8,40},{16,48},{24,56},{32,0},{40,8},{48,16},{56,24},{64,96... | collective-permute-start | bytes 786440 | tf_op jit(solution)/shard_map/ppermute | solution.py:266
  19.2 11.4 %collective-permute-start = (bf16[128,1024]{1,0:T(8,128)(2,1)S(1)}, bf16[128,1024]{1,0:T(8,128)(2,1)S(1)}, u32[]{:S(2)}, u32[]{:S(2)}) collective-permute-start(bf16[128,1024]{1,0:T(8,128)(2,1)S(1)} %pad_maximum_fusion.4), channel_id=1, source_target_pairs={{0,16},{8,24},{16,32},{24,40},{32,48},{40,56},{48,0},{56,8},{64,80... | collective-permute-start | bytes 786440 | tf_op jit(solution)/shard_map/ppermute | solution.py:266
  30.7 3.1 %copy-start.6 = (bf16[144,1024]{1,0:T(8,128)(2,1)}, bf16[144,1024]{1,0:T(8,128)(2,1)S(1)}, u32[]{:S(2)}) copy-start(bf16[144,1024]{1,0:T(8,128)(2,1)S(1)} %collective-permute-done.5) | copy-start | bytes 884740
  30.7 0.7 copy-start.7
  33.8 1.8 %copy-start.8 = (bf16[144,1024]{1,0:T(8,128)(2,1)}, bf16[144,1024]{1,0:T(8,128)(2,1)S(1)}, u32[]{:S(2)}) copy-start(bf16[144,1024]{1,0:T(8,128)(2,1)S(1)} %collective-permute-done.3) | copy-start | bytes 884740
  34.0 4.3 %collective-permute-start.6 = (bf16[4,128,512]{2,1,0:T(8,128)(2,1)S(1)}, bf16[4,128,512]{2,1,0:T(8,128)(2,1)S(1)}, u32[]{:S(2)}, u32[]{:S(2)}) collective-permute-start(bf16[4,128,512]{2,1,0:T(8,128)(2,1)S(1)} %get-tuple-element.85), channel_id=1, source_target_pairs={{0,8},{8,0},{16,24},{24,16},{32,40},{40,32},{48,56},{56,48},{64,72... | collective-permute-start | bytes 1572872 | tf_op jit(solution)/shard_map/ppermute | solution.py:269
  38.3 4.6 %copy-start.4 = (bf16[128,512]{1,0:T(8,128)(2,1)}, bf16[128,512]{1,0:T(8,128)(2,1)S(1)}, u32[]{:S(2)}) copy-start(bf16[128,512]{1,0:T(8,128)(2,1)S(1)} %get-tuple-element.80) | copy-start | bytes 393220
  40.7 86.9 %all-gather.2.cloned.1.call-start = ((), (), s32[]{:S(2)}) async-start(), calls=%async_computation.5 | async-start | bytes 2359296 | tf_op jit(solution)/shard_map/all_gather | solution.py:347
  40.8 2.0 %collective-permute-start.7 = (bf16[4,128,512]{2,1,0:T(8,128)(2,1)S(1)}, bf16[4,128,512]{2,1,0:T(8,128)(2,1)S(1)}, u32[]{:S(2)}, u32[]{:S(2)}) collective-permute-start(bf16[4,128,512]{2,1,0:T(8,128)(2,1)S(1)} %get-tuple-element.84), channel_id=1, source_target_pairs={{0,8},{8,0},{16,24},{24,16},{32,40},{40,32},{48,56},{56,48},{64,72... | collective-permute-start | bytes 1572872 | tf_op jit(solution)/shard_map/ppermute | solution.py:269
  41.2 1.7 %copy-start.5 = (bf16[128,512]{1,0:T(8,128)(2,1)S(1)}, bf16[128,512]{1,0:T(8,128)(2,1)}, u32[]{:S(2)}) copy-start(bf16[128,512]{1,0:T(8,128)(2,1)} %get-tuple-element.103) | copy-start | bytes 393220
  46.5 9.5 %collective-permute-start.8 = (bf16[128,512]{1,0:T(8,128)(2,1)}, bf16[128,512]{1,0:T(8,128)(2,1)}, u32[]{:S(2)}, u32[]{:S(2)}) collective-permute-start(bf16[128,512]{1,0:T(8,128)(2,1)} %get-tuple-element.68), channel_id=1, source_target_pairs={{0,1},{1,2},{2,3},{3,4},{4,5},{5,6},{6,7},{7,0},{8,9},{9,10},{10,1... | collective-permute-start | bytes 393224 | tf_op jit(solution)/shard_map/ppermute | solution.py:272
  48.1 9.5 %collective-permute-start.12 = (bf16[128,512]{1,0:T(8,128)(2,1)}, bf16[128,512]{1,0:T(8,128)(2,1)}, u32[]{:S(2)}, u32[]{:S(2)}) collective-permute-start(bf16[128,512]{1,0:T(8,128)(2,1)} %get-tuple-element.67), channel_id=1, source_target_pairs={{0,7},{1,0},{2,1},{3,2},{4,3},{5,4},{6,5},{7,6},{8,15},{9,8},{10,9... | collective-permute-start | bytes 393224 | tf_op jit(solution)/shard_map/ppermute | solution.py:272
  57.6 8.1 %collective-permute-start.9 = (bf16[128,512]{1,0:T(8,128)(2,1)}, bf16[128,512]{1,0:T(8,128)(2,1)}, u32[]{:S(2)}, u32[]{:S(2)}) collective-permute-start(bf16[128,512]{1,0:T(8,128)(2,1)} %fusion.8), channel_id=1, source_target_pairs={{0,1},{1,2},{2,3},{3,4},{4,5},{5,6},{6,7},{7,0},{8,9},{9,10},{10,1... | collective-permute-start | bytes 393224 | tf_op jit(solution)/shard_map/ppermute | solution.py:272
  66.8 6.6 %collective-permute-start.13 = (bf16[128,512]{1,0:T(8,128)(2,1)S(1)}, bf16[128,512]{1,0:T(8,128)(2,1)S(1)}, u32[]{:S(2)}, u32[]{:S(2)}) collective-permute-start(bf16[128,512]{1,0:T(8,128)(2,1)S(1)} %get-tuple-element.65), channel_id=1, source_target_pairs={{0,7},{1,0},{2,1},{3,2},{4,3},{5,4},{6,5},{7,6},{8,15},{9,8},{10,9... | collective-permute-start | bytes 393224 | tf_op jit(solution)/shard_map/ppermute | solution.py:272
  67.8 6.7 %collective-permute-start.10 = (bf16[128,512]{1,0:T(8,128)(2,1)S(1)}, bf16[128,512]{1,0:T(8,128)(2,1)S(1)}, u32[]{:S(2)}, u32[]{:S(2)}) collective-permute-start(bf16[128,512]{1,0:T(8,128)(2,1)S(1)} %get-tuple-element.66), channel_id=1, source_target_pairs={{0,1},{1,2},{2,3},{3,4},{4,5},{5,6},{6,7},{7,0},{8,9},{9,10},{10,1... | collective-permute-start | bytes 393224 | tf_op jit(solution)/shard_map/ppermute | solution.py:272
  75.5 6.9 %collective-permute-start.14 = (bf16[128,512]{1,0:T(8,128)(2,1)S(1)}, bf16[128,512]{1,0:T(8,128)(2,1)S(1)}, u32[]{:S(2)}, u32[]{:S(2)}) collective-permute-start(bf16[128,512]{1,0:T(8,128)(2,1)S(1)} %get-tuple-element.63), channel_id=1, source_target_pairs={{0,7},{1,0},{2,1},{3,2},{4,3},{5,4},{6,5},{7,6},{8,15},{9,8},{10,9... | collective-permute-start | bytes 393224 | tf_op jit(solution)/shard_map/ppermute | solution.py:272
  77.1 7.9 %collective-permute-start.11 = (bf16[128,512]{1,0:T(8,128)(2,1)S(1)}, bf16[128,512]{1,0:T(8,128)(2,1)S(1)}, u32[]{:S(2)}, u32[]{:S(2)}) collective-permute-start(bf16[128,512]{1,0:T(8,128)(2,1)S(1)} %get-tuple-element.64), channel_id=1, source_target_pairs={{0,1},{1,2},{2,3},{3,4},{4,5},{5,6},{6,7},{7,0},{8,9},{9,10},{10,1... | collective-permute-start | bytes 393224 | tf_op jit(solution)/shard_map/ppermute | solution.py:272
  86.3 0.9 copy-start.1
  108.5 10.4 %all-to-all-start.1 = ((f32[8,2,128]{2,1,0:T(2,128)}), f32[8,2,128]{2,1,0:T(2,128)S(1)}, u32[]{:S(2)}, u32[]{:S(2)}) async-start(f32[8,2,128]{2,1,0:T(2,128)} %broadcast_in_dim.80), calls=%async_computation.2 | async-start | bytes 16384 | tf_op jit(solution)/shard_map/all_to_all | solution.py:277
  113.8 0.7 copy-start.2
  127.6 1.6 copy-start
  129.2 7.3 %copy-start.3 = (f32[32,1024]{1,0:T(8,128)S(1)}, f32[32,1024]{1,0:T(8,128)}, u32[]{:S(2)}) copy-start(f32[32,1024]{1,0:T(8,128)} %copy-done.2) | copy-start | bytes 393220
  132.0 9.6 %collective-permute-start.15 = (bf16[512,512]{1,0:T(8,128)(2,1)S(1)}, bf16[512,512]{1,0:T(8,128)(2,1)S(1)}, u32[]{:S(2)}, u32[]{:S(2)}) collective-permute-start(bf16[512,512]{1,0:T(8,128)(2,1)S(1)} %get-tuple-element.53), channel_id=1, source_target_pairs={{0,8},{8,0},{16,24},{24,16},{32,40},{40,32},{48,56},{56,48},{64,72... | collective-permute-start | bytes 1572872 | tf_op jit(solution)/shard_map/ppermute | solution.py:269
  137.8 13.9 %collective-permute-start.16 = (bf16[128,1024]{1,0:T(8,128)(2,1)S(1)}, bf16[128,1024]{1,0:T(8,128)(2,1)S(1)}, u32[]{:S(2)}, u32[]{:S(2)}) collective-permute-start(bf16[128,1024]{1,0:T(8,128)(2,1)S(1)} %get-tuple-element.58), channel_id=1, source_target_pairs={{0,192},{8,200},{16,208},{24,216},{32,224},{40,232},{48,240},{56,2... | collective-permute-start | bytes 786440 | tf_op jit(solution)/shard_map/ppermute | solution.py:263
  140.5 11.2 %collective-permute-start.17 = (bf16[128,1024]{1,0:T(8,128)(2,1)S(1)}, bf16[128,1024]{1,0:T(8,128)(2,1)S(1)}, u32[]{:S(2)}, u32[]{:S(2)}) collective-permute-start(bf16[128,1024]{1,0:T(8,128)(2,1)S(1)} %get-tuple-element.59), channel_id=1, source_target_pairs={{0,128},{8,136},{16,144},{24,152},{32,160},{40,168},{48,176},{56,1... | collective-permute-start | bytes 786440 | tf_op jit(solution)/shard_map/ppermute | solution.py:263
  140.9 14.9 %collective-permute-start.18 = (bf16[128,1024]{1,0:T(8,128)(2,1)S(1)}, bf16[128,1024]{1,0:T(8,128)(2,1)S(1)}, u32[]{:S(2)}, u32[]{:S(2)}) collective-permute-start(bf16[128,1024]{1,0:T(8,128)(2,1)S(1)} %get-tuple-element.60), channel_id=1, source_target_pairs={{0,64},{8,72},{16,80},{24,88},{32,96},{40,104},{48,112},{56,120},{... | collective-permute-start | bytes 786440 | tf_op jit(solution)/shard_map/ppermute | solution.py:263
  142.6 15.0 %copy-start.10 = (pred[128,4]{1,0:T(8,128)(4,1)S(1)}, pred[128,4]{1,0:T(8,128)(4,1)}, u32[]{:S(2)}) copy-start(pred[128,4]{1,0:T(8,128)(4,1)} %copy-done.9) | copy-start | bytes 1540
  142.6 14.9 %all-to-all-start.2 = ((bf16[4,128,512]{2,1,0:T(8,128)(2,1)}), bf16[4,128,512]{2,1,0:T(8,128)(2,1)S(1)}, u32[]{:S(2)}, u32[]{:S(2)}) async-start(bf16[4,128,512]{2,1,0:T(8,128)(2,1)} %bitcast.38), calls=%async_computation.3 | async-start | bytes 1048576 | tf_op jit(solution)/shard_map/all_to_all | solution.py:371
Sparse Core Ops, SparseCore 0:
  40.8 45.4 reduce-scatter.1
  88.3 39.2 all-gather.1

commit v9 on v8

--- a/solution.py
+++ b/solution.py
@@ -205,7 +205,7 @@
         ],
         compiler_params=ROOM,
         name="query_grads",
-    )(place, both, scaling, k_blk, cross_dl, sums)
+    )(place, pltpu.with_memory_space_constraint(both, pltpu.HBM), scaling, k_blk, cross_dl, sums)
 
 
 def key_grads(prob, dlogit, q_blk, g_blk, dsum, pieces):
@@ -285,40 +285,42 @@
     )
     zero = jnp.zeros((), queries.dtype)
 
-    def masked(first, second):
-        tables = (t.reshape(rows_dev, flat_width) for t in (first, second))
-        flat = jnp.concatenate([jnp.where(keep_flat, t, zero) for t in tables], axis=1)
+    def masked(table):
+        flat = jnp.where(keep_flat, table.reshape(rows_dev, flat_width), zero)
         return with_layout_constraint(flat, Layout((0, 1)))
 
-    qg_flat = masked(queries, out_grad)
-    flag_rows = jnp.pad(
-        row_keep.astype(jnp.bfloat16)[None, :],
-        ((0, FLAG_ROWS - 1), (0, 2 * flat_width - rows_dev)),
-    )
-    kv_flat = jnp.concatenate([masked(keys, values), flag_rows], axis=0)
-    qg_flat, kv_flat = lax.optimization_barrier((qg_flat, kv_flat))
-    order = (1, XS - 1, 2)
-    query_pieces = {0: qg_flat} | {s: shift_x(qg_flat, s) for s in order}
-    key_pieces = [kv_flat] + [shift_y(kv_flat, s) for s in range(1, ys)]
-    query_pieces, key_pieces = lax.optimization_barrier((query_pieces, key_pieces))
-    halves = (slice(0, flat_width), slice(flat_width, 2 * flat_width))
-
-    def query_block(half):
+    def key_pieces_of(table):
+        return [table] + [shift_y(table, s) for s in range(1, ys)]
+
+    def query_pieces_of(table):
+        return [table] + [shift_x(table, s) for s in range(1, XS)]
+
+    def query_block(pieces):
         line = jnp.zeros((XS, rows_dev, flat_width), queries.dtype)
-        for s, piece in query_pieces.items():
-            line = lax.dynamic_update_slice(line, piece[None, :, half], ((own_x - s) % XS, 0, 0))
+        for s, piece in enumerate(pieces):
+            line = lax.dynamic_update_slice(line, piece[None], ((own_x - s) % XS, 0, 0))
         other = swap_core(line)
         first = jnp.where(own_core == 0, line, other)
         second = jnp.where(own_core == 0, other, line)
         return jnp.stack([first, second], axis=1).reshape(block_rows, flat_width)
 
-    def key_block(half):
-        return jnp.concatenate([p[:rows_dev, half] for p in key_pieces], axis=0)
-
-    q_blk, g_blk = query_block(halves[0]), query_block(halves[1])
-    k_blk, v_blk = key_block(halves[0]), key_block(halves[1])
+    q_flat, k_flat = lax.optimization_barrier((masked(queries), masked(keys)))
+    k_pieces = key_pieces_of(k_flat)
+    q_blk = query_block(query_pieces_of(q_flat))
+    keep_flat, k_pieces = lax.optimization_barrier((keep_flat, k_pieces))
+    k_blk = jnp.concatenate(k_pieces, axis=0)
     logit_piece = dot_f32(q_blk, k_blk, ROW_PAIR)
-    g_blk, _ = lax.optimization_barrier((g_blk, logit_piece))
+    flag_rows = jnp.pad(
+        row_keep.astype(jnp.bfloat16)[None, :], ((0, FLAG_ROWS - 1), (0, flat_width - rows_dev))
+    )
+    g_pieces, key_pieces = lax.optimization_barrier(
+        (
+            query_pieces_of(masked(out_grad)),
+            key_pieces_of(jnp.concatenate([masked(values), flag_rows], axis=0)),
+        )
+    )
+    v_blk = jnp.concatenate([p[:rows_dev] for p in key_pieces], axis=0)
+    g_blk, _ = lax.optimization_barrier((query_block(g_pieces), logit_piece))
     dprob_piece = dot_f32(g_blk, v_blk, ROW_PAIR).astype(jnp.bfloat16)
     key_flags = jnp.concatenate([p[rows_dev, :rows_dev] for p in key_pieces])[None, :]
     logit_sum = lax.psum_scatter(logit_piece, "col", scatter_dimension=0, tiled=True)

time: 166 us -> 167 us (level)
  starting transfers between devices: 35.7 us -> 41.4 us
  other arithmetic: 10.8 us -> 8.17 us
  local copies, waits for them, and re-layouts: 12.5 us -> 10 us
  waiting for transfers between devices: 63.2 us -> 65.5 us
    ppermute x3 -> x6, waiting for transfers between devices: 11.2 us -> 19.6 us  [shift_x(): lax.ppermute(table, 'row', [(at(y, x, c), at(y, x + step, c)) for y, x, c...]
    ppermute x6 -> x9, starting transfers between devices: 7.58 us -> 11.8 us  [shift_y(): lax.ppermute(table, 'row', [(at(y, x, c), at(y + step, x, c)) for y, x, c...]
    ppermute x7, waiting for transfers between devices: 24.4 us -> 21.4 us  [shift_z(): return lax.ppermute(table, 'col', [(z, (z + step) % zs) for z in range(zs)])]
    ppermute x3, starting transfers between devices: 6.5 us -> 9.08 us  [swap_core(): lax.ppermute(table, 'row', [(at(y, x, c), at(y, x, 1 - c)) for y, x, c in...]
    ppermute x6 -> x9, waiting for transfers between devices: 11.5 us -> 9.26 us  [shift_y(): lax.ppermute(table, 'row', [(at(y, x, c), at(y + step, x, c)) for y, x, c...]
    ppermute x3 -> x6, starting transfers between devices: 4.84 us -> 3.08 us  [shift_x(): lax.ppermute(table, 'row', [(at(y, x, c), at(y, x + step, c)) for y, x, c...]
    unnamed x22 -> x24, local copies, waits for them, and re-layouts: 3.96 us -> 2.67 us
  transfers between devices with their start and end apart: 23 -> 29, of which waited for: 16 -> 16; matrix products, arithmetic and copies ran while one was open for 10% -> 7% of each run, Pallas kernels for 2% -> 2%
where the time goes in v9:
time: 167 us
  waiting for transfers between devices  65.5 us (39%)
  starting transfers between devices  41.4 us (25%)
  blocking collectives  15.8 us (9%)
  between operations  14.5 us (9%)
  local copies, waits for them, and re-layouts  10 us (6%)
  Pallas kernels  8.41 us (5%)
  other arithmetic  8.17 us (5%)
  matrix products  2.83 us (2%)
    ppermute x7, waiting for transfers between devices, shift_z(): return lax.ppermute(table, 'col', [(z, (z + step) % zs) for z in range(zs)])  21.4 us
    ppermute x6, waiting for transfers between devices, shift_x(): lax.ppermute(table, 'row', [(at(y, x, c), at(y, x + step, c)) for y, x, c...  19.6 us
    all_to_all x1, blocking collectives, share(): lax.all_to_all(copies, axis, split_axis=0, concat_axis=0, tiled=True, axi...  15.8 us
    ppermute x9, starting transfers between devices, shift_y(): lax.ppermute(table, 'row', [(at(y, x, c), at(y + step, x, c)) for y, x, c...  11.8 us
    all_gather x1, waiting for transfers between devices, shards(): both = lax.all_gather(both, 'col', axis=0, tiled=True)  9.44 us
    ppermute x9, waiting for transfers between devices, shift_y(): lax.ppermute(table, 'row', [(at(y, x, c), at(y + step, x, c)) for y, x, c...  9.26 us
    ppermute x3, starting transfers between devices, swap_core(): lax.ppermute(table, 'row', [(at(y, x, c), at(y, x, 1 - c)) for y, x, c in...  9.08 us
    ppermute x7, starting transfers between devices, shift_z(): return lax.ppermute(table, 'col', [(z, (z + step) % zs) for z in range(zs)])  8.66 us
  transfers between devices with their start and end apart: 29, of which 16 were waited for; matrix products, arithmetic and copies ran while one was open for 7% of the time, Pallas kernels for 2%

profile of v9, /device:TPU:1, one launch (start us, length us, event | category | flops | bytes accessed | tf_op | source)
XLA Modules:
  0.0 166.7 jit_solution(6778450143149646788)
XLA Ops:
  7.2 0.7 broadcast_compare_fusion
  7.9 0.7 compare_and_fusion
  9.0 1.0 bitcast_select_fusion.3
  10.0 3.6 %collective-permute-start.2 = (bf16[128,512]{1,0:T(8,128)(2,1)S(1)}, bf16[128,512]{1,0:T(8,128)(2,1)S(1)}, u32[]{:S(2)}, u32[]{:S(2)}) collective-permute-start(bf16[128,512]{1,0:T(8,128)(2,1)S(1)} %get-tuple-element.40), channel_id=1, source_target_pairs={{0,192},{8,200},{16,208},{24,216},{32,224},{40,232},{48,240},{56,2... | collective-permute-start | bytes 393224 | tf_op jit(solution)/shard_map/ppermute | solution.py:263
  13.7 0.3 collective-permute-start.1
  14.0 0.7 collective-permute-start
  14.7 2.5 %collective-permute-start.5 = (bf16[128,512]{1,0:T(8,128)(2,1)S(1)}, bf16[128,512]{1,0:T(8,128)(2,1)S(1)}, u32[]{:S(2)}, u32[]{:S(2)}) collective-permute-start(bf16[128,512]{1,0:T(8,128)(2,1)S(1)} %get-tuple-element.39), channel_id=1, source_target_pairs={{0,48},{8,56},{16,0},{24,8},{32,16},{40,24},{48,32},{56,40},{64,11... | collective-permute-start | bytes 393224 | tf_op jit(solution)/shard_map/ppermute | solution.py:266
  17.2 5.3 %collective-permute-done.3 = bf16[128,512]{1,0:T(8,128)(2,1)S(1)} collective-permute-done((bf16[128,512]{1,0:T(8,128)(2,1)S(1)}, bf16[128,512]{1,0:T(8,128)(2,1)S(1)}, u32[]{:S(2)}, u32[]{:S(2)}) %collective-permute-start.3) | collective-permute-done | bytes 131104 | tf_op jit(solution)/shard_map/ppermute | solution.py:266
  22.5 5.3 %collective-permute-done.4 = bf16[128,512]{1,0:T(8,128)(2,1)S(1)} collective-permute-done((bf16[128,512]{1,0:T(8,128)(2,1)S(1)}, bf16[128,512]{1,0:T(8,128)(2,1)S(1)}, u32[]{:S(2)}, u32[]{:S(2)}) %collective-permute-start.4) | collective-permute-done | bytes 131104 | tf_op jit(solution)/shard_map/ppermute | solution.py:266
  27.9 3.9 %collective-permute-start.6 = (bf16[4,128,512]{2,1,0:T(8,128)(2,1)S(1)}, bf16[4,128,512]{2,1,0:T(8,128)(2,1)S(1)}, u32[]{:S(2)}, u32[]{:S(2)}) collective-permute-start(bf16[4,128,512]{2,1,0:T(8,128)(2,1)S(1)} %bitcast_dynamic-update-slice_fusion.4), channel_id=1, source_target_pairs={{0,8},{8,0},{16,24},{24,16},{32,40},{40,32},{48,56},{56,48},{64,72... | collective-permute-start | bytes 1572872 | tf_op jit(solution)/shard_map/ppermute | solution.py:269
  31.9 1.4 collective-permute-done.6
  33.6 2.1 %fusion.17 = f32[1024,512]{1,0:T(8,128)} fusion(bf16[1024,512]{1,0:T(8,128)(2,1)S(1)} %bitcast.126, bf16[512,512]{1,0:T(8,128)(2,1)S(1)} %constant_dynamic-update-slice_fusion.k_ref), kind=kOutput, calls=%fused_computation.75 | convolution fusion | flops 536870912 | bytes 3670016 | tf_op jit(solution)/shard_map/dot_general | solution.py:25
  36.0 2.1 %collective-permute-start.12 = (bf16[144,512]{1,0:T(8,128)(2,1)S(1)}, bf16[144,512]{1,0:T(8,128)(2,1)}, u32[]{:S(2)}, u32[]{:S(2)}) collective-permute-start(bf16[144,512]{1,0:T(8,128)(2,1)S(1)} %fusion.9), channel_id=1, source_target_pairs={{0,192},{8,200},{16,208},{24,216},{32,224},{40,232},{48,240},{56,2... | collective-permute-start | bytes 442376 | tf_op jit(solution)/shard_map/ppermute | solution.py:263
  38.0 1.4 collective-permute-start.11
  39.4 0.3 collective-permute-start.8
  39.7 1.0 collective-permute-done.9
  40.8 0.2 collective-permute-start.7
  41.0 4.2 %collective-permute-done.8 = bf16[128,512]{1,0:T(8,128)(2,1)S(1)} collective-permute-done((bf16[128,512]{1,0:T(8,128)(2,1)S(1)}, bf16[128,512]{1,0:T(8,128)(2,1)S(1)}, u32[]{:S(2)}, u32[]{:S(2)}) %collective-permute-start.8) | collective-permute-done | bytes 131104 | tf_op jit(solution)/shard_map/ppermute | solution.py:266
  45.2 3.8 %collective-permute-done.7 = bf16[128,512]{1,0:T(8,128)(2,1)S(1)} collective-permute-done((bf16[128,512]{1,0:T(8,128)(2,1)S(1)}, bf16[128,512]{1,0:T(8,128)(2,1)S(1)}, u32[]{:S(2)}, u32[]{:S(2)}) %collective-permute-start.7) | collective-permute-done | bytes 131104 | tf_op jit(solution)/shard_map/ppermute | solution.py:266
  49.2 0.8 collective-permute-start.13
  50.0 0.9 slice.63
  50.9 0.9 slice.64
  52.0 0.7 convolution_convert_fusion
  52.8 1.0 copy-done.3
  53.7 0.7 dynamic-slice_bitcast_fusion
  54.4 1.6 collective-permute-start.14
  56.1 3.9 %collective-permute-start.18 = (bf16[128,512]{1,0:T(8,128)(2,1)}, bf16[128,512]{1,0:T(8,128)(2,1)}, u32[]{:S(2)}, u32[]{:S(2)}) collective-permute-start(bf16[128,512]{1,0:T(8,128)(2,1)} %get-tuple-element.77), channel_id=1, source_target_pairs={{0,7},{1,0},{2,1},{3,2},{4,3},{5,4},{6,5},{7,6},{8,15},{9,8},{10,9... | collective-permute-start | bytes 393224 | tf_op jit(solution)/shard_map/ppermute | solution.py:272
  60.0 6.3 %collective-permute-done.14 = bf16[128,512]{1,0:T(8,128)(2,1)} collective-permute-done((bf16[128,512]{1,0:T(8,128)(2,1)}, bf16[128,512]{1,0:T(8,128)(2,1)}, u32[]{:S(2)}, u32[]{:S(2)}) %collective-permute-start.14) | collective-permute-done | bytes 131104 | tf_op jit(solution)/shard_map/ppermute | solution.py:272
  66.4 1.7 fusion.7
  68.0 8.7 %collective-permute-done.15 = bf16[128,512]{1,0:T(8,128)(2,1)} collective-permute-done((bf16[128,512]{1,0:T(8,128)(2,1)}, bf16[128,512]{1,0:T(8,128)(2,1)}, u32[]{:S(2)}, u32[]{:S(2)}) %collective-permute-start.15) | collective-permute-done | bytes 131104 | tf_op jit(solution)/shard_map/ppermute | solution.py:272
  76.7 1.2 fusion.4
  77.9 0.6 collective-permute-start.19
  78.5 0.9 collective-permute-start.16
  79.4 0.7 slice_bitcast_fusion.4
  80.1 1.7 %collective-permute-done.19 = bf16[128,512]{1,0:T(8,128)(2,1)S(1)} collective-permute-done((bf16[128,512]{1,0:T(8,128)(2,1)S(1)}, bf16[128,512]{1,0:T(8,128)(2,1)S(1)}, u32[]{:S(2)}, u32[]{:S(2)}) %collective-permute-start.19) | collective-permute-done | bytes 131104 | tf_op jit(solution)/shard_map/ppermute | solution.py:272
  81.8 1.7 %collective-permute-done.16 = bf16[128,512]{1,0:T(8,128)(2,1)S(1)} collective-permute-done((bf16[128,512]{1,0:T(8,128)(2,1)S(1)}, bf16[128,512]{1,0:T(8,128)(2,1)S(1)}, u32[]{:S(2)}, u32[]{:S(2)}) %collective-permute-start.16) | collective-permute-done | bytes 131104 | tf_op jit(solution)/shard_map/ppermute | solution.py:272
  83.5 1.0 fusion.3
  84.6 1.5 collective-permute-start.17
  86.1 0.7 slice_bitcast_fusion.2
  86.8 1.6 collective-permute-done.20.back_ref
  88.5 1.3 collective-permute-done.17.forward_ref
  89.8 0.9 copy-done
  90.7 1.0 block_softmax.1
  91.7 1.1 cross_statistics.1
  92.9 15.8 %all_to_all.15.stat_ref = f32[8,16,1024]{2,1,0:T(8,128)S(1)} all-to-all(f32[8,16,1024]{2,1,0:T(8,128)S(1)} %broadcast_in_dim.77), channel_id=1, replica_groups={{0,8,16,24,32,40,48,56},{64,72,80,88,96,104,112,120},{128,136,144,152,1..., dimensions={0} | all-to-all | bytes 1048576 | tf_op jit(solution)/shard_map/all_to_all | solution.py:277
  108.8 0.6 broadcast_in_dim.78
  109.4 4.7 %all-to-all-start.1 = ((f32[8,2,128]{2,1,0:T(2,128)}), f32[8,2,128]{2,1,0:T(2,128)S(1)}, u32[]{:S(2)}, u32[]{:S(2)}) async-start(f32[8,2,128]{2,1,0:T(2,128)} %broadcast_in_dim.78), calls=%async_computation.2 | async-start | bytes 16384 | tf_op jit(solution)/shard_map/all_to_all | solution.py:277
  114.2 1.5 cross_grads.1
  115.7 0.7 copy-done.1
  116.4 4.4 %all-to-all-done.1.scale_ref = f32[8,2,128]{2,1,0:T(2,128)S(1)} async-done(((f32[8,2,128]{2,1,0:T(2,128)}), f32[8,2,128]{2,1,0:T(2,128)S(1)}, u32[]{:S(2)}, u32[]{:S(2)}) %all-to-all-start.1) | async-done | bytes 8224 | tf_op jit(solution)/shard_map/all_to_all | solution.py:277
  120.8 9.4 %all-gather.2.cloned.1.call-done.both_ref = bf16[1024,1024]{1,0:T(8,128)(2,1)} async-done(((bf16[128,1024]{1,0:T(8,128)(2,1)}), bf16[1024,1024]{1,0:T(8,128)(2,1)}) %all-gather.2.cloned.1.call-update) | async-done | bytes 2097168 | tf_op jit(solution)/shard_map/all_gather | solution.py:349
  130.2 3.6 %query_grads.1 = (bf16[1024,512]{1,0:T(8,128)(2,1)S(1)}, bf16[1024,512]{1,0:T(8,128)(2,1)S(1)}, f32[512,512]{1,0:T(8,128)S(1)}, bf16[512,512]{1,0:T(8,128)(2,1)S(1)}) custom-call(s32[2]{0:T(128)S(1)} %pad_add_fusion.place_ref, bf16[1024,1024]{1,0:T(8,128)(2,1)} %all-gather.2.cloned.1.call-done.both_ref, f32[8,2,128]{2,1,0:T(2,128)S(1)} %all-to-all-done.1.scale_ref, ...), custom_call_target="tpu_custom_call" | custom-call | tf_op jit(solution)/shard_map/query_grads/pallas_call | solution.py:192
  133.8 4.4 %collective-permute-start.21 = (bf16[512,512]{1,0:T(8,128)(2,1)S(1)}, bf16[512,512]{1,0:T(8,128)(2,1)S(1)}, u32[]{:S(2)}, u32[]{:S(2)}) collective-permute-start(bf16[512,512]{1,0:T(8,128)(2,1)S(1)} %get-tuple-element.63), channel_id=1, source_target_pairs={{0,8},{8,0},{16,24},{24,16},{32,40},{40,32},{48,56},{56,48},{64,72... | collective-permute-start | bytes 1572872 | tf_op jit(solution)/shard_map/ppermute | solution.py:269
  138.2 1.3 key_grads.1
  139.5 2.5 %collective-permute-start.22 = (bf16[128,1024]{1,0:T(8,128)(2,1)S(1)}, bf16[128,1024]{1,0:T(8,128)(2,1)S(1)}, u32[]{:S(2)}, u32[]{:S(2)}) collective-permute-start(bf16[128,1024]{1,0:T(8,128)(2,1)S(1)} %get-tuple-element.68), channel_id=1, source_target_pairs={{0,192},{8,200},{16,208},{24,216},{32,224},{40,232},{48,240},{56,2... | collective-permute-start | bytes 786440 | tf_op jit(solution)/shard_map/ppermute | solution.py:263
  142.0 0.6 collective-permute-start.23
  142.7 0.5 collective-permute-start.24
  143.2 1.0 add_convert_fusion
  144.2 4.0 %all-to-all-start.2 = ((bf16[4,128,512]{2,1,0:T(8,128)(2,1)}), bf16[4,128,512]{2,1,0:T(8,128)(2,1)S(1)}, u32[]{:S(2)}, u32[]{:S(2)}) async-start(bf16[4,128,512]{2,1,0:T(8,128)(2,1)} %bitcast.38), calls=%async_computation.3 | async-start | bytes 1048576 | tf_op jit(solution)/shard_map/all_to_all | solution.py:373
  148.1 5.1 %collective-permute-done.22 = bf16[128,1024]{1,0:T(8,128)(2,1)S(1)} collective-permute-done((bf16[128,1024]{1,0:T(8,128)(2,1)S(1)}, bf16[128,1024]{1,0:T(8,128)(2,1)S(1)}, u32[]{:S(2)}, u32[]{:S(2)}) %collective-permute-start.22) | collective-permute-done | bytes 262176 | tf_op jit(solution)/shard_map/ppermute | solution.py:263
  153.2 4.2 %collective-permute-done.24 = bf16[128,1024]{1,0:T(8,128)(2,1)S(1)} collective-permute-done((bf16[128,1024]{1,0:T(8,128)(2,1)S(1)}, bf16[128,1024]{1,0:T(8,128)(2,1)S(1)}, u32[]{:S(2)}, u32[]{:S(2)}) %collective-permute-start.24) | collective-permute-done | bytes 262176 | tf_op jit(solution)/shard_map/ppermute | solution.py:263
  157.6 0.7 reshape.135
  158.3 0.7 reshape.134
  159.1 0.7 reshape.133
  (82 shorter events, 2.1 us)
Async XLA Ops:
  7.2 24.6 %copy-start.9 = (s32[128]{0:T(128)S(1)}, s32[128]{0:T(128)}, u32[]{:S(2)}) copy-start(s32[128]{0:T(128)} %param.10) | copy-start | bytes 1540
  7.2 82.6 %reduce-scatter.2.cloned.1.call-start = ((), (), s32[]{:S(2)}) async-start(), calls=%async_computation.4 | async-start | bytes 2359296 | tf_op jit(solution)/shard_map/reduce_scatter | solution.py:326
  10.0 21.8 %collective-permute-start.2 = (bf16[128,512]{1,0:T(8,128)(2,1)S(1)}, bf16[128,512]{1,0:T(8,128)(2,1)S(1)}, u32[]{:S(2)}, u32[]{:S(2)}) collective-permute-start(bf16[128,512]{1,0:T(8,128)(2,1)S(1)} %get-tuple-element.40), channel_id=1, source_target_pairs={{0,192},{8,200},{16,208},{24,216},{32,224},{40,232},{48,240},{56,2... | collective-permute-start | bytes 393224 | tf_op jit(solution)/shard_map/ppermute | solution.py:263
  13.7 18.2 %collective-permute-start.1 = (bf16[128,512]{1,0:T(8,128)(2,1)S(1)}, bf16[128,512]{1,0:T(8,128)(2,1)S(1)}, u32[]{:S(2)}, u32[]{:S(2)}) collective-permute-start(bf16[128,512]{1,0:T(8,128)(2,1)S(1)} %get-tuple-element.40), channel_id=1, source_target_pairs={{0,128},{8,136},{16,144},{24,152},{32,160},{40,168},{48,176},{56,1... | collective-permute-start | bytes 393224 | tf_op jit(solution)/shard_map/ppermute | solution.py:263
  14.0 17.9 %collective-permute-start = (bf16[128,512]{1,0:T(8,128)(2,1)S(1)}, bf16[128,512]{1,0:T(8,128)(2,1)S(1)}, u32[]{:S(2)}, u32[]{:S(2)}) collective-permute-start(bf16[128,512]{1,0:T(8,128)(2,1)S(1)} %get-tuple-element.40), channel_id=1, source_target_pairs={{0,64},{8,72},{16,80},{24,88},{32,96},{40,104},{48,112},{56,120},{... | collective-permute-start | bytes 393224 | tf_op jit(solution)/shard_map/ppermute | solution.py:263
  14.7 13.1 %collective-permute-start.5 = (bf16[128,512]{1,0:T(8,128)(2,1)S(1)}, bf16[128,512]{1,0:T(8,128)(2,1)S(1)}, u32[]{:S(2)}, u32[]{:S(2)}) collective-permute-start(bf16[128,512]{1,0:T(8,128)(2,1)S(1)} %get-tuple-element.39), channel_id=1, source_target_pairs={{0,48},{8,56},{16,0},{24,8},{32,16},{40,24},{48,32},{56,40},{64,11... | collective-permute-start | bytes 393224 | tf_op jit(solution)/shard_map/ppermute | solution.py:266
  17.2 5.3 %collective-permute-start.3 = (bf16[128,512]{1,0:T(8,128)(2,1)S(1)}, bf16[128,512]{1,0:T(8,128)(2,1)S(1)}, u32[]{:S(2)}, u32[]{:S(2)}) collective-permute-start(bf16[128,512]{1,0:T(8,128)(2,1)S(1)} %get-tuple-element.39), channel_id=1, source_target_pairs={{0,16},{8,24},{16,32},{24,40},{32,48},{40,56},{48,0},{56,8},{64,80... | collective-permute-start | bytes 393224 | tf_op jit(solution)/shard_map/ppermute | solution.py:266
  22.5 5.3 %collective-permute-start.4 = (bf16[128,512]{1,0:T(8,128)(2,1)S(1)}, bf16[128,512]{1,0:T(8,128)(2,1)S(1)}, u32[]{:S(2)}, u32[]{:S(2)}) collective-permute-start(bf16[128,512]{1,0:T(8,128)(2,1)S(1)} %get-tuple-element.39), channel_id=1, source_target_pairs={{0,32},{8,40},{16,48},{24,56},{32,0},{40,8},{48,16},{56,24},{64,96... | collective-permute-start | bytes 393224 | tf_op jit(solution)/shard_map/ppermute | solution.py:266
  27.9 5.4 %collective-permute-start.6 = (bf16[4,128,512]{2,1,0:T(8,128)(2,1)S(1)}, bf16[4,128,512]{2,1,0:T(8,128)(2,1)S(1)}, u32[]{:S(2)}, u32[]{:S(2)}) collective-permute-start(bf16[4,128,512]{2,1,0:T(8,128)(2,1)S(1)} %bitcast_dynamic-update-slice_fusion.4), channel_id=1, source_target_pairs={{0,8},{8,0},{16,24},{24,16},{32,40},{40,32},{48,56},{56,48},{64,72... | collective-permute-start | bytes 1572872 | tf_op jit(solution)/shard_map/ppermute | solution.py:269
  31.8 4.0 %copy-start.4 = (pred[16,8,4,128]{3,1,2,0:T(8,128)(4,1)}, pred[16,8,4,128]{3,1,2,0:T(8,128)(4,1)S(1)}, u32[]{:S(2)}) copy-start(pred[16,8,4,128]{3,1,2,0:T(8,128)(4,1)S(1)} %copy.35) | copy-start | bytes 196612
  33.6 2.2 %copy-start.6 = (bf16[128,4,128]{2,1,0:T(4,128)(2,1)S(1)}, bf16[128,4,128]{2,1,0:T(4,128)(2,1)}, u32[]{:S(2)}) copy-start(bf16[128,4,128]{2,1,0:T(4,128)(2,1)} %param.8) | copy-start | bytes 393220
  33.6 2.2 %copy-start.7 = (bf16[128,4,128]{2,1,0:T(4,128)(2,1)S(1)}, bf16[128,4,128]{2,1,0:T(4,128)(2,1)}, u32[]{:S(2)}) copy-start(bf16[128,4,128]{2,1,0:T(4,128)(2,1)} %param.9) | copy-start | bytes 393220
  35.7 94.5 %all-gather.2.cloned.1.call-start = ((), (), s32[]{:S(2)}) async-start(), calls=%async_computation.5 | async-start | bytes 2359296 | tf_op jit(solution)/shard_map/all_gather | solution.py:349
  35.9 4.9 %collective-permute-start.9 = (bf16[128,512]{1,0:T(8,128)(2,1)S(1)}, bf16[128,512]{1,0:T(8,128)(2,1)S(1)}, u32[]{:S(2)}, u32[]{:S(2)}) collective-permute-start(bf16[128,512]{1,0:T(8,128)(2,1)S(1)} %get-tuple-element.44), channel_id=1, source_target_pairs={{0,48},{8,56},{16,0},{24,8},{32,16},{40,24},{48,32},{56,40},{64,11... | collective-permute-start | bytes 393224 | tf_op jit(solution)/shard_map/ppermute | solution.py:266
  36.0 13.0 %collective-permute-start.12 = (bf16[144,512]{1,0:T(8,128)(2,1)S(1)}, bf16[144,512]{1,0:T(8,128)(2,1)}, u32[]{:S(2)}, u32[]{:S(2)}) collective-permute-start(bf16[144,512]{1,0:T(8,128)(2,1)S(1)} %fusion.9), channel_id=1, source_target_pairs={{0,192},{8,200},{16,208},{24,216},{32,224},{40,232},{48,240},{56,2... | collective-permute-start | bytes 442376 | tf_op jit(solution)/shard_map/ppermute | solution.py:263
  38.0 11.0 %collective-permute-start.11 = (bf16[144,512]{1,0:T(8,128)(2,1)S(1)}, bf16[144,512]{1,0:T(8,128)(2,1)}, u32[]{:S(2)}, u32[]{:S(2)}) collective-permute-start(bf16[144,512]{1,0:T(8,128)(2,1)S(1)} %fusion.9), channel_id=1, source_target_pairs={{0,128},{8,136},{16,144},{24,152},{32,160},{40,168},{48,176},{56,1... | collective-permute-start | bytes 442376 | tf_op jit(solution)/shard_map/ppermute | solution.py:263
  39.4 9.6 %collective-permute-start.10 = (bf16[144,512]{1,0:T(8,128)(2,1)S(1)}, bf16[144,512]{1,0:T(8,128)(2,1)S(1)}, u32[]{:S(2)}, u32[]{:S(2)}) collective-permute-start(bf16[144,512]{1,0:T(8,128)(2,1)S(1)} %fusion.9), channel_id=1, source_target_pairs={{0,64},{8,72},{16,80},{24,88},{32,96},{40,104},{48,112},{56,120},{... | collective-permute-start | bytes 442376 | tf_op jit(solution)/shard_map/ppermute | solution.py:263
  39.4 5.7 %collective-permute-start.8 = (bf16[128,512]{1,0:T(8,128)(2,1)S(1)}, bf16[128,512]{1,0:T(8,128)(2,1)S(1)}, u32[]{:S(2)}, u32[]{:S(2)}) collective-permute-start(bf16[128,512]{1,0:T(8,128)(2,1)S(1)} %get-tuple-element.44), channel_id=1, source_target_pairs={{0,32},{8,40},{16,48},{24,56},{32,0},{40,8},{48,16},{56,24},{64,96... | collective-permute-start | bytes 393224 | tf_op jit(solution)/shard_map/ppermute | solution.py:266
  40.8 8.2 %collective-permute-start.7 = (bf16[128,512]{1,0:T(8,128)(2,1)S(1)}, bf16[128,512]{1,0:T(8,128)(2,1)S(1)}, u32[]{:S(2)}, u32[]{:S(2)}) collective-permute-start(bf16[128,512]{1,0:T(8,128)(2,1)S(1)} %get-tuple-element.44), channel_id=1, source_target_pairs={{0,16},{8,24},{16,32},{24,40},{32,48},{40,56},{48,0},{56,8},{64,80... | collective-permute-start | bytes 393224 | tf_op jit(solution)/shard_map/ppermute | solution.py:266
  49.0 0.9 copy-start.8
  49.2 2.6 %collective-permute-start.13 = (bf16[4,128,512]{2,1,0:T(8,128)(2,1)S(1)}, bf16[4,128,512]{2,1,0:T(8,128)(2,1)S(1)}, u32[]{:S(2)}, u32[]{:S(2)}) collective-permute-start(bf16[4,128,512]{2,1,0:T(8,128)(2,1)S(1)} %bitcast_dynamic-update-slice_fusion), channel_id=1, source_target_pairs={{0,8},{8,0},{16,24},{24,16},{32,40},{40,32},{48,56},{56,48},{64,72... | collective-permute-start | bytes 1572872 | tf_op jit(solution)/shard_map/ppermute | solution.py:269
  52.8 1.0 copy-start.3
  54.4 11.9 %collective-permute-start.14 = (bf16[128,512]{1,0:T(8,128)(2,1)}, bf16[128,512]{1,0:T(8,128)(2,1)}, u32[]{:S(2)}, u32[]{:S(2)}) collective-permute-start(bf16[128,512]{1,0:T(8,128)(2,1)} %get-tuple-element.78), channel_id=1, source_target_pairs={{0,1},{1,2},{2,3},{3,4},{4,5},{5,6},{6,7},{7,0},{8,9},{9,10},{10,1... | collective-permute-start | bytes 393224 | tf_op jit(solution)/shard_map/ppermute | solution.py:272
  56.1 11.9 %collective-permute-start.18 = (bf16[128,512]{1,0:T(8,128)(2,1)}, bf16[128,512]{1,0:T(8,128)(2,1)}, u32[]{:S(2)}, u32[]{:S(2)}) collective-permute-start(bf16[128,512]{1,0:T(8,128)(2,1)} %get-tuple-element.77), channel_id=1, source_target_pairs={{0,7},{1,0},{2,1},{3,2},{4,3},{5,4},{6,5},{7,6},{8,15},{9,8},{10,9... | collective-permute-start | bytes 393224 | tf_op jit(solution)/shard_map/ppermute | solution.py:272
  68.0 8.7 %collective-permute-start.15 = (bf16[128,512]{1,0:T(8,128)(2,1)}, bf16[128,512]{1,0:T(8,128)(2,1)}, u32[]{:S(2)}, u32[]{:S(2)}) collective-permute-start(bf16[128,512]{1,0:T(8,128)(2,1)} %fusion.7), channel_id=1, source_target_pairs={{0,1},{1,2},{2,3},{3,4},{4,5},{5,6},{6,7},{7,0},{8,9},{9,10},{10,1... | collective-permute-start | bytes 393224 | tf_op jit(solution)/shard_map/ppermute | solution.py:272
  77.9 3.9 %collective-permute-start.19 = (bf16[128,512]{1,0:T(8,128)(2,1)S(1)}, bf16[128,512]{1,0:T(8,128)(2,1)S(1)}, u32[]{:S(2)}, u32[]{:S(2)}) collective-permute-start(bf16[128,512]{1,0:T(8,128)(2,1)S(1)} %get-tuple-element.75), channel_id=1, source_target_pairs={{0,7},{1,0},{2,1},{3,2},{4,3},{5,4},{6,5},{7,6},{8,15},{9,8},{10,9... | collective-permute-start | bytes 393224 | tf_op jit(solution)/shard_map/ppermute | solution.py:272
  78.5 5.0 %collective-permute-start.16 = (bf16[128,512]{1,0:T(8,128)(2,1)S(1)}, bf16[128,512]{1,0:T(8,128)(2,1)S(1)}, u32[]{:S(2)}, u32[]{:S(2)}) collective-permute-start(bf16[128,512]{1,0:T(8,128)(2,1)S(1)} %get-tuple-element.76), channel_id=1, source_target_pairs={{0,1},{1,2},{2,3},{3,4},{4,5},{5,6},{6,7},{7,0},{8,9},{9,10},{10,1... | collective-permute-start | bytes 393224 | tf_op jit(solution)/shard_map/ppermute | solution.py:272
  84.6 3.9 %collective-permute-start.20 = (bf16[128,512]{1,0:T(8,128)(2,1)S(1)}, bf16[128,512]{1,0:T(8,128)(2,1)S(1)}, u32[]{:S(2)}, u32[]{:S(2)}) collective-permute-start(bf16[128,512]{1,0:T(8,128)(2,1)S(1)} %get-tuple-element.73), channel_id=1, source_target_pairs={{0,7},{1,0},{2,1},{3,2},{4,3},{5,4},{6,5},{7,6},{8,15},{9,8},{10,9... | collective-permute-start | bytes 393224 | tf_op jit(solution)/shard_map/ppermute | solution.py:272
  84.6 5.1 %collective-permute-start.17 = (bf16[128,512]{1,0:T(8,128)(2,1)S(1)}, bf16[128,512]{1,0:T(8,128)(2,1)S(1)}, u32[]{:S(2)}, u32[]{:S(2)}) collective-permute-start(bf16[128,512]{1,0:T(8,128)(2,1)S(1)} %get-tuple-element.74), channel_id=1, source_target_pairs={{0,1},{1,2},{2,3},{3,4},{4,5},{5,6},{6,7},{7,0},{8,9},{9,10},{10,1... | collective-permute-start | bytes 393224 | tf_op jit(solution)/shard_map/ppermute | solution.py:272
  89.8 1.0 copy-start
  109.4 11.4 %all-to-all-start.1 = ((f32[8,2,128]{2,1,0:T(2,128)}), f32[8,2,128]{2,1,0:T(2,128)S(1)}, u32[]{:S(2)}, u32[]{:S(2)}) async-start(f32[8,2,128]{2,1,0:T(2,128)} %broadcast_in_dim.78), calls=%async_computation.2 | async-start | bytes 16384 | tf_op jit(solution)/shard_map/all_to_all | solution.py:277
  115.7 0.7 copy-start.1
  120.8 17.5 %copy-start.2 = (f32[32,1024]{1,0:T(8,128)S(1)}, f32[32,1024]{1,0:T(8,128)}, u32[]{:S(2)}) copy-start(f32[32,1024]{1,0:T(8,128)} %copy-done.1) | copy-start | bytes 393220
  133.8 9.4 %collective-permute-start.21 = (bf16[512,512]{1,0:T(8,128)(2,1)S(1)}, bf16[512,512]{1,0:T(8,128)(2,1)S(1)}, u32[]{:S(2)}, u32[]{:S(2)}) collective-permute-start(bf16[512,512]{1,0:T(8,128)(2,1)S(1)} %get-tuple-element.63), channel_id=1, source_target_pairs={{0,8},{8,0},{16,24},{24,16},{32,40},{40,32},{48,56},{56,48},{64,72... | collective-permute-start | bytes 1572872 | tf_op jit(solution)/shard_map/ppermute | solution.py:269
  139.5 13.7 %collective-permute-start.22 = (bf16[128,1024]{1,0:T(8,128)(2,1)S(1)}, bf16[128,1024]{1,0:T(8,128)(2,1)S(1)}, u32[]{:S(2)}, u32[]{:S(2)}) collective-permute-start(bf16[128,1024]{1,0:T(8,128)(2,1)S(1)} %get-tuple-element.68), channel_id=1, source_target_pairs={{0,192},{8,200},{16,208},{24,216},{32,224},{40,232},{48,240},{56,2... | collective-permute-start | bytes 786440 | tf_op jit(solution)/shard_map/ppermute | solution.py:263
  142.0 11.2 %collective-permute-start.23 = (bf16[128,1024]{1,0:T(8,128)(2,1)S(1)}, bf16[128,1024]{1,0:T(8,128)(2,1)S(1)}, u32[]{:S(2)}, u32[]{:S(2)}) collective-permute-start(bf16[128,1024]{1,0:T(8,128)(2,1)S(1)} %get-tuple-element.69), channel_id=1, source_target_pairs={{0,128},{8,136},{16,144},{24,152},{32,160},{40,168},{48,176},{56,1... | collective-permute-start | bytes 786440 | tf_op jit(solution)/shard_map/ppermute | solution.py:263
  142.7 14.7 %collective-permute-start.24 = (bf16[128,1024]{1,0:T(8,128)(2,1)S(1)}, bf16[128,1024]{1,0:T(8,128)(2,1)S(1)}, u32[]{:S(2)}, u32[]{:S(2)}) collective-permute-start(bf16[128,1024]{1,0:T(8,128)(2,1)S(1)} %get-tuple-element.70), channel_id=1, source_target_pairs={{0,64},{8,72},{16,80},{24,88},{32,96},{40,104},{48,112},{56,120},{... | collective-permute-start | bytes 786440 | tf_op jit(solution)/shard_map/ppermute | solution.py:263
  143.2 14.4 %copy-start.5 = (pred[16,8,4,128]{3,1,2,0:T(8,128)(4,1)S(1)}, pred[16,8,4,128]{3,1,2,0:T(8,128)(4,1)}, u32[]{:S(2)}) copy-start(pred[16,8,4,128]{3,1,2,0:T(8,128)(4,1)} %copy-done.4) | copy-start | bytes 196612
  144.2 14.9 %all-to-all-start.2 = ((bf16[4,128,512]{2,1,0:T(8,128)(2,1)}), bf16[4,128,512]{2,1,0:T(8,128)(2,1)S(1)}, u32[]{:S(2)}, u32[]{:S(2)}) async-start(bf16[4,128,512]{2,1,0:T(8,128)(2,1)} %bitcast.38), calls=%async_computation.3 | async-start | bytes 1048576 | tf_op jit(solution)/shard_map/all_to_all | solution.py:373
Sparse Core Ops, SparseCore 0:
  35.8 40.8 reduce-scatter.1
  91.8 38.3 all-gather.1

commit v10 on v9

--- a/solution.py
+++ b/solution.py
@@ -289,38 +289,46 @@
         flat = jnp.where(keep_flat, table.reshape(rows_dev, flat_width), zero)
         return with_layout_constraint(flat, Layout((0, 1)))
 
-    def key_pieces_of(table):
-        return [table] + [shift_y(table, s) for s in range(1, ys)]
-
-    def query_pieces_of(table):
-        return [table] + [shift_x(table, s) for s in range(1, XS)]
-
-    def query_block(pieces):
+    def wave(first, second, chained):
+        along_x = {s: shift_x(first, s) for s in range(1, XS)}
+        late = second
+        if chained:
+            late, along_x[1] = lax.optimization_barrier((second, along_x[1]))
+        along_y = {s: shift_y(late if s == ys - 1 else second, s) for s in range(1, ys)}
+        return lax.optimization_barrier(
+            (
+                [first] + [along_x[s] for s in range(1, XS)],
+                [second] + [along_y[s] for s in range(1, ys)],
+            )
+        )
+
+    def in_line(pieces):
         line = jnp.zeros((XS, rows_dev, flat_width), queries.dtype)
         for s, piece in enumerate(pieces):
             line = lax.dynamic_update_slice(line, piece[None], ((own_x - s) % XS, 0, 0))
-        other = swap_core(line)
+        return line
+
+    def both_lines(line, other):
         first = jnp.where(own_core == 0, line, other)
         second = jnp.where(own_core == 0, other, line)
         return jnp.stack([first, second], axis=1).reshape(block_rows, flat_width)
 
-    q_flat, k_flat = lax.optimization_barrier((masked(queries), masked(keys)))
-    k_pieces = key_pieces_of(k_flat)
-    q_blk = query_block(query_pieces_of(q_flat))
-    keep_flat, k_pieces = lax.optimization_barrier((keep_flat, k_pieces))
+    q_pieces, k_pieces = wave(*lax.optimization_barrier((masked(queries), masked(keys))), True)
+    q_line = in_line(q_pieces)
+    q_other, keep_flat = lax.optimization_barrier((swap_core(q_line), keep_flat))
+    q_blk = both_lines(q_line, q_other)
     k_blk = jnp.concatenate(k_pieces, axis=0)
     logit_piece = dot_f32(q_blk, k_blk, ROW_PAIR)
     flag_rows = jnp.pad(
         row_keep.astype(jnp.bfloat16)[None, :], ((0, FLAG_ROWS - 1), (0, flat_width - rows_dev))
     )
-    g_pieces, key_pieces = lax.optimization_barrier(
-        (
-            query_pieces_of(masked(out_grad)),
-            key_pieces_of(jnp.concatenate([masked(values), flag_rows], axis=0)),
-        )
+    g_pieces, key_pieces = wave(
+        masked(out_grad), jnp.concatenate([masked(values), flag_rows], axis=0), False
     )
     v_blk = jnp.concatenate([p[:rows_dev] for p in key_pieces], axis=0)
-    g_blk, _ = lax.optimization_barrier((query_block(g_pieces), logit_piece))
+    g_line = in_line(g_pieces)
+    g_blk = both_lines(g_line, swap_core(g_line))
+    g_blk, _ = lax.optimization_barrier((g_blk, logit_piece))
     dprob_piece = dot_f32(g_blk, v_blk, ROW_PAIR).astype(jnp.bfloat16)
     key_flags = jnp.concatenate([p[rows_dev, :rows_dev] for p in key_pieces])[None, :]
     logit_sum = lax.psum_scatter(logit_piece, "col", scatter_dimension=0, tiled=True)

time: 167 us -> 164 us (0.982)
  waiting for transfers between devices: 65.5 us -> 58 us
  starting transfers between devices: 41.4 us -> 45.3 us
    ppermute x6, waiting for transfers between devices: 19.6 us -> 7.42 us  [shift_x(): lax.ppermute(table, 'row', [(at(y, x, c), at(y, x + step, c)) for y, x, c...]
    ppermute x6, starting transfers between devices: 3.08 us -> 7.61 us  [shift_x(): lax.ppermute(table, 'row', [(at(y, x, c), at(y, x + step, c)) for y, x, c...]
    ppermute x9, waiting for transfers between devices: 9.26 us -> 13.4 us  [shift_y(): lax.ppermute(table, 'row', [(at(y, x, c), at(y + step, x, c)) for y, x, c...]
    ppermute x3, starting transfers between devices: 9.08 us -> 7.35 us  [swap_core(): lax.ppermute(table, 'row', [(at(y, x, c), at(y, x, 1 - c)) for y, x, c in...]
  transfers between devices with their start and end apart: 29 -> 29, of which waited for: 16 -> 15; matrix products, arithmetic and copies ran while one was open for 7% -> 8% of each run, Pallas kernels for 2% -> 2%
where the time goes in v10:
time: 164 us; the launch traced here: 163 us
  waiting for transfers between devices  58 us (35%)
  starting transfers between devices  45.3 us (28%)
  blocking collectives  16.2 us (10%)
  between operations  14.5 us (9%)
  local copies, waits for them, and re-layouts  10 us (6%)
  Pallas kernels  8.41 us (5%)
  other arithmetic  8.17 us (5%)
  matrix products  2.82 us (2%)
    ppermute x7, waiting for transfers between devices, shift_z(): return lax.ppermute(table, 'col', [(z, (z + step) % zs) for z in range(zs)])  21.9 us
    all_to_all x1, blocking collectives, share(): lax.all_to_all(copies, axis, split_axis=0, concat_axis=0, tiled=True, axi...  16.2 us
    ppermute x9, waiting for transfers between devices, shift_y(): lax.ppermute(table, 'row', [(at(y, x, c), at(y + step, x, c)) for y, x, c...  13.4 us
    ppermute x9, starting transfers between devices, shift_y(): lax.ppermute(table, 'row', [(at(y, x, c), at(y + step, x, c)) for y, x, c...  12.6 us
    all_gather x1, waiting for transfers between devices, shards(): both = lax.all_gather(both, 'col', axis=0, tiled=True)  9.43 us
    ppermute x7, starting transfers between devices, shift_z(): return lax.ppermute(table, 'col', [(z, (z + step) % zs) for z in range(zs)])  8.65 us
    ppermute x6, starting transfers between devices, shift_x(): lax.ppermute(table, 'row', [(at(y, x, c), at(y, x + step, c)) for y, x, c...  7.61 us
    ppermute x6, waiting for transfers between devices, shift_x(): lax.ppermute(table, 'row', [(at(y, x, c), at(y, x + step, c)) for y, x, c...  7.42 us
  transfers between devices with their start and end apart: 29, of which 15 were waited for; matrix products, arithmetic and copies ran while one was open for 8% of the time, Pallas kernels for 2%

profile of v10, /device:TPU:1, one launch (start us, length us, event | category | flops | bytes accessed | tf_op | source)
XLA Modules:
  0.0 163.5 jit_solution(11417369197481605204)
XLA Ops:
  7.2 0.7 broadcast_compare_fusion
  7.9 0.7 compare_and_fusion
  9.0 1.0 bitcast_select_fusion.3
  10.0 2.1 %collective-permute-start = (bf16[128,512]{1,0:T(8,128)(2,1)S(1)}, bf16[128,512]{1,0:T(8,128)(2,1)S(1)}, u32[]{:S(2)}, u32[]{:S(2)}) collective-permute-start(bf16[128,512]{1,0:T(8,128)(2,1)S(1)} %get-tuple-element.48), channel_id=1, source_target_pairs={{0,16},{8,24},{16,32},{24,40},{32,48},{40,56},{48,0},{56,8},{64,80... | collective-permute-start | bytes 393224 | tf_op jit(solution)/shard_map/ppermute | solution.py:266
  12.1 1.4 collective-permute-start.2
  13.5 1.6 %collective-permute-start.1 = (bf16[128,512]{1,0:T(8,128)(2,1)S(1)}, bf16[128,512]{1,0:T(8,128)(2,1)S(1)}, u32[]{:S(2)}, u32[]{:S(2)}) collective-permute-start(bf16[128,512]{1,0:T(8,128)(2,1)S(1)} %get-tuple-element.48), channel_id=1, source_target_pairs={{0,32},{8,40},{16,48},{24,56},{32,0},{40,8},{48,16},{56,24},{64,96... | collective-permute-start | bytes 393224 | tf_op jit(solution)/shard_map/ppermute | solution.py:266
  15.1 2.9 %collective-permute-start.4 = (bf16[128,512]{1,0:T(8,128)(2,1)S(1)}, bf16[128,512]{1,0:T(8,128)(2,1)S(1)}, u32[]{:S(2)}, u32[]{:S(2)}) collective-permute-start(bf16[128,512]{1,0:T(8,128)(2,1)S(1)} %get-tuple-element.54), channel_id=1, source_target_pairs={{0,128},{8,136},{16,144},{24,152},{32,160},{40,168},{48,176},{56,1... | collective-permute-start | bytes 393224 | tf_op jit(solution)/shard_map/ppermute | solution.py:263
  18.0 0.4 collective-permute-start.3
  18.4 2.3 %collective-permute-start.5 = (bf16[128,512]{1,0:T(8,128)(2,1)S(1)}, bf16[128,512]{1,0:T(8,128)(2,1)S(1)}, u32[]{:S(2)}, u32[]{:S(2)}) collective-permute-start(bf16[128,512]{1,0:T(8,128)(2,1)S(1)} %get-tuple-element.54), channel_id=1, source_target_pairs={{0,192},{8,200},{16,208},{24,216},{32,224},{40,232},{48,240},{56,2... | collective-permute-start | bytes 393224 | tf_op jit(solution)/shard_map/ppermute | solution.py:263
  20.7 3.9 %collective-permute-done.3 = bf16[128,512]{1,0:T(8,128)(2,1)S(1)} collective-permute-done((bf16[128,512]{1,0:T(8,128)(2,1)S(1)}, bf16[128,512]{1,0:T(8,128)(2,1)S(1)}, u32[]{:S(2)}, u32[]{:S(2)}) %collective-permute-start.3) | collective-permute-done | bytes 131104 | tf_op jit(solution)/shard_map/ppermute | solution.py:263
  24.8 1.7 %collective-permute-start.6 = (bf16[4,128,512]{2,1,0:T(8,128)(2,1)S(1)}, bf16[4,128,512]{2,1,0:T(8,128)(2,1)S(1)}, u32[]{:S(2)}, u32[]{:S(2)}) collective-permute-start(bf16[4,128,512]{2,1,0:T(8,128)(2,1)S(1)} %bitcast_dynamic-update-slice_fusion.4), channel_id=1, source_target_pairs={{0,8},{8,0},{16,24},{24,16},{32,40},{40,32},{48,56},{56,48},{64,72... | collective-permute-start | bytes 1572872 | tf_op jit(solution)/shard_map/ppermute | solution.py:269
  26.6 1.4 collective-permute-done.6
  28.3 2.1 %fusion.17 = f32[1024,512]{1,0:T(8,128)} fusion(bf16[1024,512]{1,0:T(8,128)(2,1)S(1)} %bitcast.126, bf16[512,512]{1,0:T(8,128)(2,1)S(1)} %constant_dynamic-update-slice_fusion.k_ref), kind=kOutput, calls=%fused_computation.75 | convolution fusion | flops 536870912 | bytes 3670016 | tf_op jit(solution)/shard_map/dot_general | solution.py:25
  30.6 1.1 collective-permute-start.9
  31.7 2.7 %collective-permute-start.12 = (bf16[144,512]{1,0:T(8,128)(2,1)S(1)}, bf16[144,512]{1,0:T(8,128)(2,1)}, u32[]{:S(2)}, u32[]{:S(2)}) collective-permute-start(bf16[144,512]{1,0:T(8,128)(2,1)S(1)} %fusion.9), channel_id=1, source_target_pairs={{0,192},{8,200},{16,208},{24,216},{32,224},{40,232},{48,240},{56,2... | collective-permute-start | bytes 442376 | tf_op jit(solution)/shard_map/ppermute | solution.py:263
  34.3 0.7 collective-permute-start.10
  35.0 1.2 collective-permute-start.8
  36.5 4.3 %collective-permute-done.8 = bf16[128,512]{1,0:T(8,128)(2,1)S(1)} collective-permute-done((bf16[128,512]{1,0:T(8,128)(2,1)S(1)}, bf16[128,512]{1,0:T(8,128)(2,1)S(1)}, u32[]{:S(2)}, u32[]{:S(2)}) %collective-permute-start.8) | collective-permute-done | bytes 131104 | tf_op jit(solution)/shard_map/ppermute | solution.py:266
  40.7 3.1 %collective-permute-done.7 = bf16[128,512]{1,0:T(8,128)(2,1)S(1)} collective-permute-done((bf16[128,512]{1,0:T(8,128)(2,1)S(1)}, bf16[128,512]{1,0:T(8,128)(2,1)S(1)}, u32[]{:S(2)}, u32[]{:S(2)}) %collective-permute-start.7) | collective-permute-done | bytes 131104 | tf_op jit(solution)/shard_map/ppermute | solution.py:266
  43.9 0.3 collective-permute-done.10
  44.3 1.2 collective-permute-start.13
  45.5 0.9 slice.63
  46.5 0.9 slice.64
  47.6 0.7 convolution_convert_fusion
  48.3 1.0 copy-done.3
  49.3 0.7 dynamic-slice_bitcast_fusion
  50.0 1.6 %collective-permute-start.14 = (bf16[128,512]{1,0:T(8,128)(2,1)}, bf16[128,512]{1,0:T(8,128)(2,1)}, u32[]{:S(2)}, u32[]{:S(2)}) collective-permute-start(bf16[128,512]{1,0:T(8,128)(2,1)} %get-tuple-element.92), channel_id=1, source_target_pairs={{0,1},{1,2},{2,3},{3,4},{4,5},{5,6},{6,7},{7,0},{8,9},{9,10},{10,1... | collective-permute-start | bytes 393224 | tf_op jit(solution)/shard_map/ppermute | solution.py:272
  51.7 3.9 %collective-permute-start.18 = (bf16[128,512]{1,0:T(8,128)(2,1)}, bf16[128,512]{1,0:T(8,128)(2,1)}, u32[]{:S(2)}, u32[]{:S(2)}) collective-permute-start(bf16[128,512]{1,0:T(8,128)(2,1)} %get-tuple-element.91), channel_id=1, source_target_pairs={{0,7},{1,0},{2,1},{3,2},{4,3},{5,4},{6,5},{7,6},{8,15},{9,8},{10,9... | collective-permute-start | bytes 393224 | tf_op jit(solution)/shard_map/ppermute | solution.py:272
  55.6 6.7 %collective-permute-done.14 = bf16[128,512]{1,0:T(8,128)(2,1)} collective-permute-done((bf16[128,512]{1,0:T(8,128)(2,1)}, bf16[128,512]{1,0:T(8,128)(2,1)}, u32[]{:S(2)}, u32[]{:S(2)}) %collective-permute-start.14) | collective-permute-done | bytes 131104 | tf_op jit(solution)/shard_map/ppermute | solution.py:272
  62.3 1.7 %fusion.7 = bf16[128,512]{1,0:T(8,128)(2,1)} fusion(bf16[128,512]{1,0:T(8,128)(2,1)} %collective-permute-done.14, bf16[8,128,512]{2,1,0:T(8,128)(2,1)} %bitcast.135, s32[]{:T(128)S(6)} %select_n.180), kind=kLoop, calls=%fused_computation.25 | loop fusion | flops 262144 | bytes 393220 | tf_op jit(solution)/shard_map/convert_element_type | solution.py:348
  64.0 9.3 %collective-permute-done.15 = bf16[128,512]{1,0:T(8,128)(2,1)} collective-permute-done((bf16[128,512]{1,0:T(8,128)(2,1)}, bf16[128,512]{1,0:T(8,128)(2,1)}, u32[]{:S(2)}, u32[]{:S(2)}) %collective-permute-start.15) | collective-permute-done | bytes 131104 | tf_op jit(solution)/shard_map/ppermute | solution.py:272
  73.3 1.2 fusion.4
  74.5 1.5 collective-permute-start.16
  76.0 0.7 slice_bitcast_fusion.4
  76.6 1.7 %collective-permute-done.19 = bf16[128,512]{1,0:T(8,128)(2,1)S(1)} collective-permute-done((bf16[128,512]{1,0:T(8,128)(2,1)S(1)}, bf16[128,512]{1,0:T(8,128)(2,1)S(1)}, u32[]{:S(2)}, u32[]{:S(2)}) %collective-permute-start.19) | collective-permute-done | bytes 131104 | tf_op jit(solution)/shard_map/ppermute | solution.py:272
  78.3 1.3 collective-permute-done.16
  79.6 1.0 fusion.3
  80.8 1.5 collective-permute-start.17
  82.2 0.7 slice_bitcast_fusion.2
  82.9 1.6 %collective-permute-done.20.back_ref = bf16[128,512]{1,0:T(8,128)(2,1)S(1)} collective-permute-done((bf16[128,512]{1,0:T(8,128)(2,1)S(1)}, bf16[128,512]{1,0:T(8,128)(2,1)S(1)}, u32[]{:S(2)}, u32[]{:S(2)}) %collective-permute-start.20) | collective-permute-done | bytes 131104 | tf_op jit(solution)/shard_map/ppermute | solution.py:272
  84.6 1.3 collective-permute-done.17.forward_ref
  85.9 0.9 copy-done
  86.8 1.0 block_softmax.1
  87.8 1.1 cross_statistics.1
  89.0 16.2 %all_to_all.15.stat_ref = f32[8,16,1024]{2,1,0:T(8,128)S(1)} all-to-all(f32[8,16,1024]{2,1,0:T(8,128)S(1)} %broadcast_in_dim.77), channel_id=1, replica_groups={{0,8,16,24,32,40,48,56},{64,72,80,88,96,104,112,120},{128,136,144,152,1..., dimensions={0} | all-to-all | bytes 1048576 | tf_op jit(solution)/shard_map/all_to_all | solution.py:277
  105.3 0.6 broadcast_in_dim.78
  105.9 5.0 %all-to-all-start.1 = ((f32[8,2,128]{2,1,0:T(2,128)}), f32[8,2,128]{2,1,0:T(2,128)S(1)}, u32[]{:S(2)}, u32[]{:S(2)}) async-start(f32[8,2,128]{2,1,0:T(2,128)} %broadcast_in_dim.78), calls=%async_computation.2 | async-start | bytes 16384 | tf_op jit(solution)/shard_map/all_to_all | solution.py:277
  111.0 1.5 cross_grads.1
  112.6 0.7 copy-done.1
  113.2 4.4 %all-to-all-done.1.scale_ref = f32[8,2,128]{2,1,0:T(2,128)S(1)} async-done(((f32[8,2,128]{2,1,0:T(2,128)}), f32[8,2,128]{2,1,0:T(2,128)S(1)}, u32[]{:S(2)}, u32[]{:S(2)}) %all-to-all-start.1) | async-done | bytes 8224 | tf_op jit(solution)/shard_map/all_to_all | solution.py:277
  117.6 9.4 %all-gather.2.cloned.1.call-done.both_ref = bf16[1024,1024]{1,0:T(8,128)(2,1)} async-done(((bf16[128,1024]{1,0:T(8,128)(2,1)}), bf16[1024,1024]{1,0:T(8,128)(2,1)}) %all-gather.2.cloned.1.call-update) | async-done | bytes 2097168 | tf_op jit(solution)/shard_map/all_gather | solution.py:357
  127.0 3.6 %query_grads.1 = (bf16[1024,512]{1,0:T(8,128)(2,1)S(1)}, bf16[1024,512]{1,0:T(8,128)(2,1)S(1)}, f32[512,512]{1,0:T(8,128)S(1)}, bf16[512,512]{1,0:T(8,128)(2,1)S(1)}) custom-call(s32[2]{0:T(128)S(1)} %pad_add_fusion.place_ref, bf16[1024,1024]{1,0:T(8,128)(2,1)} %all-gather.2.cloned.1.call-done.both_ref, f32[8,2,128]{2,1,0:T(2,128)S(1)} %all-to-all-done.1.scale_ref, ...), custom_call_target="tpu_custom_call" | custom-call | tf_op jit(solution)/shard_map/query_grads/pallas_call | solution.py:192
  130.6 4.4 %collective-permute-start.21 = (bf16[512,512]{1,0:T(8,128)(2,1)S(1)}, bf16[512,512]{1,0:T(8,128)(2,1)S(1)}, u32[]{:S(2)}, u32[]{:S(2)}) collective-permute-start(bf16[512,512]{1,0:T(8,128)(2,1)S(1)} %get-tuple-element.77), channel_id=1, source_target_pairs={{0,8},{8,0},{16,24},{24,16},{32,40},{40,32},{48,56},{56,48},{64,72... | collective-permute-start | bytes 1572872 | tf_op jit(solution)/shard_map/ppermute | solution.py:269
  135.0 1.3 key_grads.1
  136.3 2.5 %collective-permute-start.22 = (bf16[128,1024]{1,0:T(8,128)(2,1)S(1)}, bf16[128,1024]{1,0:T(8,128)(2,1)S(1)}, u32[]{:S(2)}, u32[]{:S(2)}) collective-permute-start(bf16[128,1024]{1,0:T(8,128)(2,1)S(1)} %get-tuple-element.82), channel_id=1, source_target_pairs={{0,192},{8,200},{16,208},{24,216},{32,224},{40,232},{48,240},{56,2... | collective-permute-start | bytes 786440 | tf_op jit(solution)/shard_map/ppermute | solution.py:263
  138.9 0.6 collective-permute-start.23
  139.5 0.5 collective-permute-start.24
  140.0 1.0 add_convert_fusion
  141.0 4.0 %all-to-all-start.2 = ((bf16[4,128,512]{2,1,0:T(8,128)(2,1)}), bf16[4,128,512]{2,1,0:T(8,128)(2,1)S(1)}, u32[]{:S(2)}, u32[]{:S(2)}) async-start(bf16[4,128,512]{2,1,0:T(8,128)(2,1)} %bitcast.38), calls=%async_computation.3 | async-start | bytes 1048576 | tf_op jit(solution)/shard_map/all_to_all | solution.py:381
  144.9 5.1 %collective-permute-done.22 = bf16[128,1024]{1,0:T(8,128)(2,1)S(1)} collective-permute-done((bf16[128,1024]{1,0:T(8,128)(2,1)S(1)}, bf16[128,1024]{1,0:T(8,128)(2,1)S(1)}, u32[]{:S(2)}, u32[]{:S(2)}) %collective-permute-start.22) | collective-permute-done | bytes 262176 | tf_op jit(solution)/shard_map/ppermute | solution.py:263
  150.1 4.2 %collective-permute-done.24 = bf16[128,1024]{1,0:T(8,128)(2,1)S(1)} collective-permute-done((bf16[128,1024]{1,0:T(8,128)(2,1)S(1)}, bf16[128,1024]{1,0:T(8,128)(2,1)S(1)}, u32[]{:S(2)}, u32[]{:S(2)}) %collective-permute-start.24) | collective-permute-done | bytes 262176 | tf_op jit(solution)/shard_map/ppermute | solution.py:263
  154.5 0.7 reshape.135
  155.2 0.7 reshape.134
  155.9 0.7 reshape.133
  (82 shorter events, 2.3 us)
Async XLA Ops:
  7.2 19.3 %copy-start.9 = (s32[128]{0:T(128)S(1)}, s32[128]{0:T(128)}, u32[]{:S(2)}) copy-start(s32[128]{0:T(128)} %param.10) | copy-start | bytes 1540
  7.2 78.7 %reduce-scatter.2.cloned.1.call-start = ((), (), s32[]{:S(2)}) async-start(), calls=%async_computation.4 | async-start | bytes 2359296 | tf_op jit(solution)/shard_map/reduce_scatter | solution.py:334
  10.0 8.4 %collective-permute-start = (bf16[128,512]{1,0:T(8,128)(2,1)S(1)}, bf16[128,512]{1,0:T(8,128)(2,1)S(1)}, u32[]{:S(2)}, u32[]{:S(2)}) collective-permute-start(bf16[128,512]{1,0:T(8,128)(2,1)S(1)} %get-tuple-element.48), channel_id=1, source_target_pairs={{0,16},{8,24},{16,32},{24,40},{32,48},{40,56},{48,0},{56,8},{64,80... | collective-permute-start | bytes 393224 | tf_op jit(solution)/shard_map/ppermute | solution.py:266
  12.1 8.6 %collective-permute-start.2 = (bf16[128,512]{1,0:T(8,128)(2,1)S(1)}, bf16[128,512]{1,0:T(8,128)(2,1)S(1)}, u32[]{:S(2)}, u32[]{:S(2)}) collective-permute-start(bf16[128,512]{1,0:T(8,128)(2,1)S(1)} %get-tuple-element.48), channel_id=1, source_target_pairs={{0,48},{8,56},{16,0},{24,8},{32,16},{40,24},{48,32},{56,40},{64,11... | collective-permute-start | bytes 393224 | tf_op jit(solution)/shard_map/ppermute | solution.py:266
  13.5 7.2 %collective-permute-start.1 = (bf16[128,512]{1,0:T(8,128)(2,1)S(1)}, bf16[128,512]{1,0:T(8,128)(2,1)S(1)}, u32[]{:S(2)}, u32[]{:S(2)}) collective-permute-start(bf16[128,512]{1,0:T(8,128)(2,1)S(1)} %get-tuple-element.48), channel_id=1, source_target_pairs={{0,32},{8,40},{16,48},{24,56},{32,0},{40,8},{48,16},{56,24},{64,96... | collective-permute-start | bytes 393224 | tf_op jit(solution)/shard_map/ppermute | solution.py:266
  15.1 5.6 %collective-permute-start.4 = (bf16[128,512]{1,0:T(8,128)(2,1)S(1)}, bf16[128,512]{1,0:T(8,128)(2,1)S(1)}, u32[]{:S(2)}, u32[]{:S(2)}) collective-permute-start(bf16[128,512]{1,0:T(8,128)(2,1)S(1)} %get-tuple-element.54), channel_id=1, source_target_pairs={{0,128},{8,136},{16,144},{24,152},{32,160},{40,168},{48,176},{56,1... | collective-permute-start | bytes 393224 | tf_op jit(solution)/shard_map/ppermute | solution.py:263
  18.0 6.6 %collective-permute-start.3 = (bf16[128,512]{1,0:T(8,128)(2,1)S(1)}, bf16[128,512]{1,0:T(8,128)(2,1)S(1)}, u32[]{:S(2)}, u32[]{:S(2)}) collective-permute-start(bf16[128,512]{1,0:T(8,128)(2,1)S(1)} %get-tuple-element.54), channel_id=1, source_target_pairs={{0,64},{8,72},{16,80},{24,88},{32,96},{40,104},{48,112},{56,120},{... | collective-permute-start | bytes 393224 | tf_op jit(solution)/shard_map/ppermute | solution.py:263
  18.4 6.2 %collective-permute-start.5 = (bf16[128,512]{1,0:T(8,128)(2,1)S(1)}, bf16[128,512]{1,0:T(8,128)(2,1)S(1)}, u32[]{:S(2)}, u32[]{:S(2)}) collective-permute-start(bf16[128,512]{1,0:T(8,128)(2,1)S(1)} %get-tuple-element.54), channel_id=1, source_target_pairs={{0,192},{8,200},{16,208},{24,216},{32,224},{40,232},{48,240},{56,2... | collective-permute-start | bytes 393224 | tf_op jit(solution)/shard_map/ppermute | solution.py:263
  24.8 3.3 %collective-permute-start.6 = (bf16[4,128,512]{2,1,0:T(8,128)(2,1)S(1)}, bf16[4,128,512]{2,1,0:T(8,128)(2,1)S(1)}, u32[]{:S(2)}, u32[]{:S(2)}) collective-permute-start(bf16[4,128,512]{2,1,0:T(8,128)(2,1)S(1)} %bitcast_dynamic-update-slice_fusion.4), channel_id=1, source_target_pairs={{0,8},{8,0},{16,24},{24,16},{32,40},{40,32},{48,56},{56,48},{64,72... | collective-permute-start | bytes 1572872 | tf_op jit(solution)/shard_map/ppermute | solution.py:269
  26.5 4.0 %copy-start.4 = (pred[16,8,4,128]{3,1,2,0:T(8,128)(4,1)}, pred[16,8,4,128]{3,1,2,0:T(8,128)(4,1)S(1)}, u32[]{:S(2)}) copy-start(pred[16,8,4,128]{3,1,2,0:T(8,128)(4,1)S(1)} %copy.35) | copy-start | bytes 196612
  28.3 2.2 %copy-start.6 = (bf16[128,4,128]{2,1,0:T(4,128)(2,1)S(1)}, bf16[128,4,128]{2,1,0:T(4,128)(2,1)}, u32[]{:S(2)}) copy-start(bf16[128,4,128]{2,1,0:T(4,128)(2,1)} %param.8) | copy-start | bytes 393220
  28.3 2.2 %copy-start.7 = (bf16[128,4,128]{2,1,0:T(4,128)(2,1)S(1)}, bf16[128,4,128]{2,1,0:T(4,128)(2,1)}, u32[]{:S(2)}) copy-start(bf16[128,4,128]{2,1,0:T(4,128)(2,1)} %param.9) | copy-start | bytes 393220
  30.4 96.6 %all-gather.2.cloned.1.call-start = ((), (), s32[]{:S(2)}) async-start(), calls=%async_computation.5 | async-start | bytes 2359296 | tf_op jit(solution)/shard_map/all_gather | solution.py:357
  30.6 5.7 %collective-permute-start.9 = (bf16[128,512]{1,0:T(8,128)(2,1)S(1)}, bf16[128,512]{1,0:T(8,128)(2,1)S(1)}, u32[]{:S(2)}, u32[]{:S(2)}) collective-permute-start(bf16[128,512]{1,0:T(8,128)(2,1)S(1)} %get-tuple-element.58), channel_id=1, source_target_pairs={{0,48},{8,56},{16,0},{24,8},{32,16},{40,24},{48,32},{56,40},{64,11... | collective-permute-start | bytes 393224 | tf_op jit(solution)/shard_map/ppermute | solution.py:266
  31.7 12.2 %collective-permute-start.12 = (bf16[144,512]{1,0:T(8,128)(2,1)S(1)}, bf16[144,512]{1,0:T(8,128)(2,1)}, u32[]{:S(2)}, u32[]{:S(2)}) collective-permute-start(bf16[144,512]{1,0:T(8,128)(2,1)S(1)} %fusion.9), channel_id=1, source_target_pairs={{0,192},{8,200},{16,208},{24,216},{32,224},{40,232},{48,240},{56,2... | collective-permute-start | bytes 442376 | tf_op jit(solution)/shard_map/ppermute | solution.py:263
  34.3 9.5 %collective-permute-start.11 = (bf16[144,512]{1,0:T(8,128)(2,1)S(1)}, bf16[144,512]{1,0:T(8,128)(2,1)}, u32[]{:S(2)}, u32[]{:S(2)}) collective-permute-start(bf16[144,512]{1,0:T(8,128)(2,1)S(1)} %fusion.9), channel_id=1, source_target_pairs={{0,128},{8,136},{16,144},{24,152},{32,160},{40,168},{48,176},{56,1... | collective-permute-start | bytes 442376 | tf_op jit(solution)/shard_map/ppermute | solution.py:263
  34.3 9.8 %collective-permute-start.10 = (bf16[144,512]{1,0:T(8,128)(2,1)S(1)}, bf16[144,512]{1,0:T(8,128)(2,1)S(1)}, u32[]{:S(2)}, u32[]{:S(2)}) collective-permute-start(bf16[144,512]{1,0:T(8,128)(2,1)S(1)} %fusion.9), channel_id=1, source_target_pairs={{0,64},{8,72},{16,80},{24,88},{32,96},{40,104},{48,112},{56,120},{... | collective-permute-start | bytes 442376 | tf_op jit(solution)/shard_map/ppermute | solution.py:263
  35.0 5.7 %collective-permute-start.8 = (bf16[128,512]{1,0:T(8,128)(2,1)S(1)}, bf16[128,512]{1,0:T(8,128)(2,1)S(1)}, u32[]{:S(2)}, u32[]{:S(2)}) collective-permute-start(bf16[128,512]{1,0:T(8,128)(2,1)S(1)} %get-tuple-element.58), channel_id=1, source_target_pairs={{0,32},{8,40},{16,48},{24,56},{32,0},{40,8},{48,16},{56,24},{64,96... | collective-permute-start | bytes 393224 | tf_op jit(solution)/shard_map/ppermute | solution.py:266
  36.3 7.6 %collective-permute-start.7 = (bf16[128,512]{1,0:T(8,128)(2,1)S(1)}, bf16[128,512]{1,0:T(8,128)(2,1)S(1)}, u32[]{:S(2)}, u32[]{:S(2)}) collective-permute-start(bf16[128,512]{1,0:T(8,128)(2,1)S(1)} %get-tuple-element.58), channel_id=1, source_target_pairs={{0,16},{8,24},{16,32},{24,40},{32,48},{40,56},{48,0},{56,8},{64,80... | collective-permute-start | bytes 393224 | tf_op jit(solution)/shard_map/ppermute | solution.py:266
  44.1 1.4 copy-start.8
  44.3 3.1 %collective-permute-start.13 = (bf16[4,128,512]{2,1,0:T(8,128)(2,1)S(1)}, bf16[4,128,512]{2,1,0:T(8,128)(2,1)S(1)}, u32[]{:S(2)}, u32[]{:S(2)}) collective-permute-start(bf16[4,128,512]{2,1,0:T(8,128)(2,1)S(1)} %bitcast_dynamic-update-slice_fusion), channel_id=1, source_target_pairs={{0,8},{8,0},{16,24},{24,16},{32,40},{40,32},{48,56},{56,48},{64,72... | collective-permute-start | bytes 1572872 | tf_op jit(solution)/shard_map/ppermute | solution.py:269
  48.3 1.0 copy-start.3
  50.0 12.3 %collective-permute-start.14 = (bf16[128,512]{1,0:T(8,128)(2,1)}, bf16[128,512]{1,0:T(8,128)(2,1)}, u32[]{:S(2)}, u32[]{:S(2)}) collective-permute-start(bf16[128,512]{1,0:T(8,128)(2,1)} %get-tuple-element.92), channel_id=1, source_target_pairs={{0,1},{1,2},{2,3},{3,4},{4,5},{5,6},{6,7},{7,0},{8,9},{9,10},{10,1... | collective-permute-start | bytes 393224 | tf_op jit(solution)/shard_map/ppermute | solution.py:272
  51.7 12.3 %collective-permute-start.18 = (bf16[128,512]{1,0:T(8,128)(2,1)}, bf16[128,512]{1,0:T(8,128)(2,1)}, u32[]{:S(2)}, u32[]{:S(2)}) collective-permute-start(bf16[128,512]{1,0:T(8,128)(2,1)} %get-tuple-element.91), channel_id=1, source_target_pairs={{0,7},{1,0},{2,1},{3,2},{4,3},{5,4},{6,5},{7,6},{8,15},{9,8},{10,9... | collective-permute-start | bytes 393224 | tf_op jit(solution)/shard_map/ppermute | solution.py:272
  64.0 9.3 %collective-permute-start.15 = (bf16[128,512]{1,0:T(8,128)(2,1)}, bf16[128,512]{1,0:T(8,128)(2,1)}, u32[]{:S(2)}, u32[]{:S(2)}) collective-permute-start(bf16[128,512]{1,0:T(8,128)(2,1)} %fusion.7), channel_id=1, source_target_pairs={{0,1},{1,2},{2,3},{3,4},{4,5},{5,6},{6,7},{7,0},{8,9},{9,10},{10,1... | collective-permute-start | bytes 393224 | tf_op jit(solution)/shard_map/ppermute | solution.py:272
  74.4 3.9 %collective-permute-start.19 = (bf16[128,512]{1,0:T(8,128)(2,1)S(1)}, bf16[128,512]{1,0:T(8,128)(2,1)S(1)}, u32[]{:S(2)}, u32[]{:S(2)}) collective-permute-start(bf16[128,512]{1,0:T(8,128)(2,1)S(1)} %get-tuple-element.89), channel_id=1, source_target_pairs={{0,7},{1,0},{2,1},{3,2},{4,3},{5,4},{6,5},{7,6},{8,15},{9,8},{10,9... | collective-permute-start | bytes 393224 | tf_op jit(solution)/shard_map/ppermute | solution.py:272
  74.5 5.1 %collective-permute-start.16 = (bf16[128,512]{1,0:T(8,128)(2,1)S(1)}, bf16[128,512]{1,0:T(8,128)(2,1)S(1)}, u32[]{:S(2)}, u32[]{:S(2)}) collective-permute-start(bf16[128,512]{1,0:T(8,128)(2,1)S(1)} %get-tuple-element.90), channel_id=1, source_target_pairs={{0,1},{1,2},{2,3},{3,4},{4,5},{5,6},{6,7},{7,0},{8,9},{9,10},{10,1... | collective-permute-start | bytes 393224 | tf_op jit(solution)/shard_map/ppermute | solution.py:272
  80.7 3.9 %collective-permute-start.20 = (bf16[128,512]{1,0:T(8,128)(2,1)S(1)}, bf16[128,512]{1,0:T(8,128)(2,1)S(1)}, u32[]{:S(2)}, u32[]{:S(2)}) collective-permute-start(bf16[128,512]{1,0:T(8,128)(2,1)S(1)} %get-tuple-element.87), channel_id=1, source_target_pairs={{0,7},{1,0},{2,1},{3,2},{4,3},{5,4},{6,5},{7,6},{8,15},{9,8},{10,9... | collective-permute-start | bytes 393224 | tf_op jit(solution)/shard_map/ppermute | solution.py:272
  80.8 5.1 %collective-permute-start.17 = (bf16[128,512]{1,0:T(8,128)(2,1)S(1)}, bf16[128,512]{1,0:T(8,128)(2,1)S(1)}, u32[]{:S(2)}, u32[]{:S(2)}) collective-permute-start(bf16[128,512]{1,0:T(8,128)(2,1)S(1)} %get-tuple-element.88), channel_id=1, source_target_pairs={{0,1},{1,2},{2,3},{3,4},{4,5},{5,6},{6,7},{7,0},{8,9},{9,10},{10,1... | collective-permute-start | bytes 393224 | tf_op jit(solution)/shard_map/ppermute | solution.py:272
  85.9 1.0 copy-start
  105.9 11.7 %all-to-all-start.1 = ((f32[8,2,128]{2,1,0:T(2,128)}), f32[8,2,128]{2,1,0:T(2,128)S(1)}, u32[]{:S(2)}, u32[]{:S(2)}) async-start(f32[8,2,128]{2,1,0:T(2,128)} %broadcast_in_dim.78), calls=%async_computation.2 | async-start | bytes 16384 | tf_op jit(solution)/shard_map/all_to_all | solution.py:277
  112.6 0.7 copy-start.1
  117.6 17.4 %copy-start.2 = (f32[32,1024]{1,0:T(8,128)S(1)}, f32[32,1024]{1,0:T(8,128)}, u32[]{:S(2)}) copy-start(f32[32,1024]{1,0:T(8,128)} %copy-done.1) | copy-start | bytes 393220
  130.6 9.4 %collective-permute-start.21 = (bf16[512,512]{1,0:T(8,128)(2,1)S(1)}, bf16[512,512]{1,0:T(8,128)(2,1)S(1)}, u32[]{:S(2)}, u32[]{:S(2)}) collective-permute-start(bf16[512,512]{1,0:T(8,128)(2,1)S(1)} %get-tuple-element.77), channel_id=1, source_target_pairs={{0,8},{8,0},{16,24},{24,16},{32,40},{40,32},{48,56},{56,48},{64,72... | collective-permute-start | bytes 1572872 | tf_op jit(solution)/shard_map/ppermute | solution.py:269
  136.3 13.7 %collective-permute-start.22 = (bf16[128,1024]{1,0:T(8,128)(2,1)S(1)}, bf16[128,1024]{1,0:T(8,128)(2,1)S(1)}, u32[]{:S(2)}, u32[]{:S(2)}) collective-permute-start(bf16[128,1024]{1,0:T(8,128)(2,1)S(1)} %get-tuple-element.82), channel_id=1, source_target_pairs={{0,192},{8,200},{16,208},{24,216},{32,224},{40,232},{48,240},{56,2... | collective-permute-start | bytes 786440 | tf_op jit(solution)/shard_map/ppermute | solution.py:263
  138.9 11.2 %collective-permute-start.23 = (bf16[128,1024]{1,0:T(8,128)(2,1)S(1)}, bf16[128,1024]{1,0:T(8,128)(2,1)S(1)}, u32[]{:S(2)}, u32[]{:S(2)}) collective-permute-start(bf16[128,1024]{1,0:T(8,128)(2,1)S(1)} %get-tuple-element.83), channel_id=1, source_target_pairs={{0,128},{8,136},{16,144},{24,152},{32,160},{40,168},{48,176},{56,1... | collective-permute-start | bytes 786440 | tf_op jit(solution)/shard_map/ppermute | solution.py:263
  139.5 14.7 %collective-permute-start.24 = (bf16[128,1024]{1,0:T(8,128)(2,1)S(1)}, bf16[128,1024]{1,0:T(8,128)(2,1)S(1)}, u32[]{:S(2)}, u32[]{:S(2)}) collective-permute-start(bf16[128,1024]{1,0:T(8,128)(2,1)S(1)} %get-tuple-element.84), channel_id=1, source_target_pairs={{0,64},{8,72},{16,80},{24,88},{32,96},{40,104},{48,112},{56,120},{... | collective-permute-start | bytes 786440 | tf_op jit(solution)/shard_map/ppermute | solution.py:263
  140.0 14.4 %copy-start.5 = (pred[16,8,4,128]{3,1,2,0:T(8,128)(4,1)S(1)}, pred[16,8,4,128]{3,1,2,0:T(8,128)(4,1)}, u32[]{:S(2)}) copy-start(pred[16,8,4,128]{3,1,2,0:T(8,128)(4,1)} %copy-done.4) | copy-start | bytes 196612
  141.0 14.9 %all-to-all-start.2 = ((bf16[4,128,512]{2,1,0:T(8,128)(2,1)}), bf16[4,128,512]{2,1,0:T(8,128)(2,1)S(1)}, u32[]{:S(2)}, u32[]{:S(2)}) async-start(bf16[4,128,512]{2,1,0:T(8,128)(2,1)} %bitcast.38), calls=%async_computation.3 | async-start | bytes 1048576 | tf_op jit(solution)/shard_map/all_to_all | solution.py:381
Sparse Core Ops, SparseCore 0:
  30.6 43.5 reduce-scatter.1
  87.9 39.0 all-gather.1

commit v11 on v10

--- a/solution.py
+++ b/solution.py
@@ -10,7 +10,6 @@
 
 SUMMARIES = 256
 XS = 4
-FLAG_ROWS = 16
 
 ROW_PAIR = (((1,), (1,)), ((), ()))
 LEAD_PAIR = (((0,), (0,)), ((), ()))
@@ -151,16 +150,16 @@
     )(logit_sum, own, forward, back, key_flags)
 
 
-def query_grads(logit_scale, place, both, scaling, k_blk, cross_dl, sums, chunks):
+def key_grads(logit_scale, both, scaling, q_blk, g_blk, dsum, chunks, pieces):
     block_rows, width = both.shape[0], both.shape[1] // 2
     rows = block_rows // chunks
-    flat_width = k_blk.shape[1]
-    tokens = sums.shape[0]
-    columns = cross_dl.shape[0] // tokens
-    feature = flat_width // columns
-
-    def kernel(place_ref, both_ref, scale_ref, k_ref, dl_ref, sums_ref, p_ref, ds_ref, own_ref, other_ref, dq_ref, held_ref, sems):
-        core = place_ref[0]
+    flat_width = q_blk.shape[1]
+    tokens = dsum.shape[0]
+    group = width // tokens
+    piece = width // pieces
+
+    def kernel(both_ref, scale_ref, q_ref, g_ref, dsum_ref, ds_ref, *refs):
+        out_refs, (p_ref, held_ref, sems) = refs[:pieces], refs[pieces:]
         copies = []
         for i in range(chunks):
             at = pl.ds(i * rows, rows)
@@ -168,53 +167,14 @@
             copies[i].start()
         for i in range(chunks):
             at = slice(i * rows, (i + 1) * rows)
+            weight, offset = upright(scale_ref[i, 0:1, :]), upright(scale_ref[i, 1:2, :])
             copies[i].wait()
-            weight, offset = upright(scale_ref[i, 0:1, :]), upright(scale_ref[i, 1:2, :])
             lifted = held_ref[at, :width].astype(jnp.float32)
             tilted = held_ref[at, width:].astype(jnp.float32)
             p_ref[at, :] = (lifted * weight).astype(jnp.bfloat16)
             ds_ref[at, :] = ((tilted - lifted * offset) * (weight * logit_scale)).astype(
                 jnp.bfloat16
             )
-        dq_ref[...] = dot_f32(ds_ref[...], k_ref[...])
-        for c in range(columns):
-            lanes = slice(c * feature, (c + 1) * feature)
-            dq_ref[:, lanes] += dot_f32(
-                dl_ref[c * tokens : (c + 1) * tokens, :], sums_ref[:, lanes], LEAD_PAIR
-            )
-        for x in range(chunks // 2):
-            to = slice(x * rows, (x + 1) * rows)
-            mine = pl.multiple_of((2 * x + core) * rows, rows)
-            theirs = pl.multiple_of((2 * x + 1 - core) * rows, rows)
-            own_ref[to, :] = dq_ref[pl.ds(mine, rows), :]
-            other_ref[to, :] = dq_ref[pl.ds(theirs, rows), :].astype(jnp.bfloat16)
-
-    return pl.pallas_call(
-        kernel,
-        in_specs=[SMEM, pl.BlockSpec(memory_space=pltpu.HBM)] + [WHOLE] * 4,
-        out_shape=(
-            jax.ShapeDtypeStruct((block_rows, width), jnp.bfloat16),
-            jax.ShapeDtypeStruct((block_rows, width), jnp.bfloat16),
-            jax.ShapeDtypeStruct((block_rows // 2, flat_width), jnp.float32),
-            jax.ShapeDtypeStruct((block_rows // 2, flat_width), jnp.bfloat16),
-        ),
-        scratch_shapes=[
-            pltpu.VMEM((block_rows, flat_width), jnp.float32),
-            pltpu.VMEM((block_rows, 2 * width), jnp.bfloat16),
-            pltpu.SemaphoreType.DMA((chunks,)),
-        ],
-        compiler_params=ROOM,
-        name="query_grads",
-    )(place, pltpu.with_memory_space_constraint(both, pltpu.HBM), scaling, k_blk, cross_dl, sums)
-
-
-def key_grads(prob, dlogit, q_blk, g_blk, dsum, pieces):
-    width, flat_width = prob.shape[1], q_blk.shape[1]
-    tokens = dsum.shape[0]
-    group = width // tokens
-    piece = width // pieces
-
-    def kernel(p_ref, ds_ref, q_ref, g_ref, dsum_ref, *out_refs):
         for half, (w_ref, t_ref) in enumerate(((ds_ref, q_ref), (p_ref, g_ref))):
             lanes = slice(half * flat_width, (half + 1) * flat_width)
             grads = dot_f32(w_ref[...], t_ref[...], LEAD_PAIR)
@@ -226,12 +186,55 @@
 
     return pl.pallas_call(
         kernel,
-        out_shape=tuple(
+        in_specs=[pl.BlockSpec(memory_space=pltpu.HBM)] + [WHOLE] * 4,
+        out_shape=(jax.ShapeDtypeStruct((block_rows, width), jnp.bfloat16),)
+        + tuple(
             jax.ShapeDtypeStruct((piece, 2 * flat_width), jnp.bfloat16) for _ in range(pieces)
         ),
+        scratch_shapes=[
+            pltpu.VMEM((block_rows, width), jnp.bfloat16),
+            pltpu.VMEM((block_rows, 2 * width), jnp.bfloat16),
+            pltpu.SemaphoreType.DMA((chunks,)),
+        ],
         compiler_params=ROOM,
         name="key_grads",
-    )(prob, dlogit, q_blk, g_blk, dsum)
+    )(pltpu.with_memory_space_constraint(both, pltpu.HBM), scaling, q_blk, g_blk, dsum)
+
+
+def query_grads(place, dlogit, k_blk, cross_dl, sums, chunks):
+    block_rows = dlogit.shape[0]
+    rows = block_rows // chunks
+    flat_width = k_blk.shape[1]
+    tokens = sums.shape[0]
+    columns = cross_dl.shape[0] // tokens
+    feature = flat_width // columns
+
+    def kernel(place_ref, ds_ref, k_ref, dl_ref, sums_ref, own_ref, other_ref, dq_ref):
+        core = place_ref[0]
+        dq_ref[...] = dot_f32(ds_ref[...], k_ref[...])
+        for c in range(columns):
+            lanes = slice(c * feature, (c + 1) * feature)
+            dq_ref[:, lanes] += dot_f32(
+                dl_ref[c * tokens : (c + 1) * tokens, :], sums_ref[:, lanes], LEAD_PAIR
+            )
+        for x in range(chunks // 2):
+            to = slice(x * rows, (x + 1) * rows)
+            mine = pl.multiple_of((2 * x + core) * rows, rows)
+            theirs = pl.multiple_of((2 * x + 1 - core) * rows, rows)
+            own_ref[to, :] = dq_ref[pl.ds(mine, rows), :]
+            other_ref[to, :] = dq_ref[pl.ds(theirs, rows), :].astype(jnp.bfloat16)
+
+    return pl.pallas_call(
+        kernel,
+        in_specs=[SMEM] + [WHOLE] * 4,
+        out_shape=(
+            jax.ShapeDtypeStruct((block_rows // 2, flat_width), jnp.float32),
+            jax.ShapeDtypeStruct((block_rows // 2, flat_width), jnp.bfloat16),
+        ),
+        scratch_shapes=[pltpu.VMEM((block_rows, flat_width), jnp.float32)],
+        compiler_params=ROOM,
+        name="query_grads",
+    )(place, dlogit, k_blk, cross_dl, sums)
 
 
 def shards(queries, keys, values, out_grad, row_keep, row_lengths):
@@ -278,8 +281,8 @@
             copies, axis, split_axis=0, concat_axis=0, tiled=True, axis_index_groups=groups
         )
 
-    column_ids = own_z * cols_dev + jnp.arange(cols_dev, dtype=jnp.int32)
-    cell_keep = (row_keep[:, None] == 1) & (column_ids[None, :] < row_lengths[:, None])
+    own_columns = jnp.where(row_keep == 1, row_lengths, 0) - own_z * cols_dev
+    cell_keep = jnp.arange(cols_dev, dtype=jnp.int32)[None, :] < own_columns[:, None]
     keep_flat = jnp.broadcast_to(cell_keep[:, :, None], queries.shape).reshape(
         rows_dev, flat_width
     )
@@ -319,18 +322,16 @@
     q_blk = both_lines(q_line, q_other)
     k_blk = jnp.concatenate(k_pieces, axis=0)
     logit_piece = dot_f32(q_blk, k_blk, ROW_PAIR)
-    flag_rows = jnp.pad(
-        row_keep.astype(jnp.bfloat16)[None, :], ((0, FLAG_ROWS - 1), (0, flat_width - rows_dev))
-    )
-    g_pieces, key_pieces = wave(
-        masked(out_grad), jnp.concatenate([masked(values), flag_rows], axis=0), False
-    )
-    v_blk = jnp.concatenate([p[:rows_dev] for p in key_pieces], axis=0)
+    g_pieces, v_pieces = wave(masked(out_grad), masked(values), False)
+    v_blk = jnp.concatenate(v_pieces, axis=0)
     g_line = in_line(g_pieces)
     g_blk = both_lines(g_line, swap_core(g_line))
     g_blk, _ = lax.optimization_barrier((g_blk, logit_piece))
     dprob_piece = dot_f32(g_blk, v_blk, ROW_PAIR).astype(jnp.bfloat16)
-    key_flags = jnp.concatenate([p[rows_dev, :rows_dev] for p in key_pieces])[None, :]
+    own_flags, _ = lax.optimization_barrier((row_keep.astype(jnp.float32)[None, :], dprob_piece))
+    key_flags = jnp.concatenate(
+        [own_flags] + [shift_y(own_flags, s) for s in range(1, ys)], axis=1
+    )
     logit_sum = lax.psum_scatter(logit_piece, "col", scatter_dimension=0, tiled=True)
 
     dprob_chunks = dprob_piece.reshape(zs, block_rows // zs, block_keys)
@@ -338,18 +339,20 @@
     def part(step):
         return lax.dynamic_index_in_dim(dprob_chunks, (own_z + step) % zs, axis=0, keepdims=False)
 
-    def passed(step, count):
+    def passed(step, count, beside=None):
         moving = part(step * count)
         for left in range(count - 1, -1, -1):
             moving = shift_z(moving, step)
+            if beside is not None and left == count - 1:
+                moving, beside = lax.optimization_barrier((moving, beside))
             if left > 0:
                 moving = (
                     moving.astype(jnp.float32) + part(step * left).astype(jnp.float32)
                 ).astype(jnp.bfloat16)
-        return moving
-
-    dprob_forward = passed(1, zs // 2)
-    dprob_back = passed(-1, zs - 1 - zs // 2)
+        return moving, beside
+
+    dprob_forward, key_flags = passed(1, zs // 2, key_flags)
+    dprob_back, _ = passed(-1, zs - 1 - zs // 2)
 
     both, stats = block_softmax(
         logit_scale, logit_sum, part(0), dprob_forward, dprob_back, key_flags
@@ -369,11 +372,9 @@
     cross_dl, dsum = cross_grads(q_blk, g_blk, sums, all_stats, feature, inv_root)
     both, scaling, cross_dl, dsum = lax.optimization_barrier((both, scaling, cross_dl, dsum))
 
-    prob, dlogit, dq_own, dq_other = query_grads(
-        logit_scale, place, both, scaling, k_blk, cross_dl, sums, zs
-    )
+    dlogit, *key_parts = key_grads(logit_scale, both, scaling, q_blk, g_blk, dsum, zs, ys)
+    dq_own, dq_other = query_grads(place, dlogit, k_blk, cross_dl, sums, near_size)
     dq_swapped = swap_core(dq_other)
-    key_parts = key_grads(prob, dlogit, q_blk, g_blk, dsum, ys)
     key_moved = [shift_y(key_parts[s], -s) for s in range(1, ys)]
     line = (dq_own + dq_swapped.astype(jnp.float32)).astype(jnp.bfloat16)
     line = line.reshape(XS, rows_dev, flat_width)

time: 164 us -> 166 us (1.012)
  waiting for transfers between devices: 58 us -> 53.5 us
  starting transfers between devices: 45.3 us -> 49.5 us
    ppermute x9 -> x12, waiting for transfers between devices: 13.4 us -> 20 us  [shift_y(): lax.ppermute(table, 'row', [(at(y, x, c), at(y + step, x, c)) for y, x, c...]
    ppermute x6, waiting for transfers between devices: 7.42 us -> 1.25 us  [shift_x(): lax.ppermute(table, 'row', [(at(y, x, c), at(y, x + step, c)) for y, x, c...]
    ppermute x9 -> x12, starting transfers between devices: 12.6 us -> 16.7 us  [shift_y(): lax.ppermute(table, 'row', [(at(y, x, c), at(y + step, x, c)) for y, x, c...]
    ppermute x7, waiting for transfers between devices: 21.9 us -> 18 us  [shift_z(): return lax.ppermute(table, 'col', [(z, (z + step) % zs) for z in range(zs)])]
    slice x4 -> x0, local copies, waits for them, and re-layouts: 1.85 us -> none  [shards(): v_blk = jnp.concatenate([p[:rows_dev] for p in key_pieces], axis=0)]
    unnamed x24 -> x25, local copies, waits for them, and re-layouts: 2.67 us -> 4.5 us
  transfers between devices with their start and end apart: 29 -> 32, of which waited for: 15 -> 18; matrix products, arithmetic and copies ran while one was open for 8% -> 7% of each run, Pallas kernels for 2% -> 2%
where the time goes in v11:
time: 166 us; the launch traced here: 165 us
  waiting for transfers between devices  53.5 us (32%)
  starting transfers between devices  49.5 us (30%)
  blocking collectives  17.4 us (10%)
  between operations  14.5 us (9%)
  Pallas kernels  9.8 us (6%)
  other arithmetic  9.08 us (5%)
  local copies, waits for them, and re-layouts  8.45 us (5%)
  matrix products  2.82 us (2%)
    ppermute x12, waiting for transfers between devices, shift_y(): lax.ppermute(table, 'row', [(at(y, x, c), at(y + step, x, c)) for y, x, c...  20 us
    ppermute x7, waiting for transfers between devices, shift_z(): return lax.ppermute(table, 'col', [(z, (z + step) % zs) for z in range(zs)])  18 us
    all_to_all x1, blocking collectives, share(): lax.all_to_all(copies, axis, split_axis=0, concat_axis=0, tiled=True, axi...  17.4 us
    ppermute x12, starting transfers between devices, shift_y(): lax.ppermute(table, 'row', [(at(y, x, c), at(y + step, x, c)) for y, x, c...  16.7 us
    ppermute x7, starting transfers between devices, shift_z(): return lax.ppermute(table, 'col', [(z, (z + step) % zs) for z in range(zs)])  8.67 us
    ppermute x3, starting transfers between devices, swap_core(): lax.ppermute(table, 'row', [(at(y, x, c), at(y, x, 1 - c)) for y, x, c in...  8.55 us
    all_gather x1, waiting for transfers between devices, shards(): both = lax.all_gather(both, 'col', axis=0, tiled=True)  7.83 us
    ppermute x6, starting transfers between devices, shift_x(): lax.ppermute(table, 'row', [(at(y, x, c), at(y, x + step, c)) for y, x, c...  7.49 us
  transfers between devices with their start and end apart: 32, of which 18 were waited for; matrix products, arithmetic and copies ran while one was open for 7% of the time, Pallas kernels for 2%

profile of v11, /device:TPU:1, one launch (start us, length us, event | category | flops | bytes accessed | tf_op | source)
XLA Modules:
  0.0 165.1 jit_solution(4563847417318087872)
XLA Ops:
  7.2 0.7 convert_bitcast_fusion
  8.3 1.0 bitcast_select_fusion.3
  9.3 2.1 %collective-permute-start = (bf16[128,512]{1,0:T(8,128)(2,1)S(1)}, bf16[128,512]{1,0:T(8,128)(2,1)S(1)}, u32[]{:S(2)}, u32[]{:S(2)}) collective-permute-start(bf16[128,512]{1,0:T(8,128)(2,1)S(1)} %get-tuple-element.50), channel_id=1, source_target_pairs={{0,16},{8,24},{16,32},{24,40},{32,48},{40,56},{48,0},{56,8},{64,80... | collective-permute-start | bytes 393224 | tf_op jit(solution)/shard_map/ppermute | solution.py:269
  11.4 1.4 collective-permute-start.2
  12.8 1.6 collective-permute-start.1
  14.4 2.9 %collective-permute-start.4 = (bf16[128,512]{1,0:T(8,128)(2,1)S(1)}, bf16[128,512]{1,0:T(8,128)(2,1)S(1)}, u32[]{:S(2)}, u32[]{:S(2)}) collective-permute-start(bf16[128,512]{1,0:T(8,128)(2,1)S(1)} %get-tuple-element.56), channel_id=1, source_target_pairs={{0,128},{8,136},{16,144},{24,152},{32,160},{40,168},{48,176},{56,1... | collective-permute-start | bytes 393224 | tf_op jit(solution)/shard_map/ppermute | solution.py:266
  17.7 2.3 %collective-permute-start.5 = (bf16[128,512]{1,0:T(8,128)(2,1)S(1)}, bf16[128,512]{1,0:T(8,128)(2,1)S(1)}, u32[]{:S(2)}, u32[]{:S(2)}) collective-permute-start(bf16[128,512]{1,0:T(8,128)(2,1)S(1)} %get-tuple-element.56), channel_id=1, source_target_pairs={{0,192},{8,200},{16,208},{24,216},{32,224},{40,232},{48,240},{56,2... | collective-permute-start | bytes 393224 | tf_op jit(solution)/shard_map/ppermute | solution.py:266
  20.0 3.9 %collective-permute-done.3 = bf16[128,512]{1,0:T(8,128)(2,1)S(1)} collective-permute-done((bf16[128,512]{1,0:T(8,128)(2,1)S(1)}, bf16[128,512]{1,0:T(8,128)(2,1)S(1)}, u32[]{:S(2)}, u32[]{:S(2)}) %collective-permute-start.3) | collective-permute-done | bytes 131104 | tf_op jit(solution)/shard_map/ppermute | solution.py:266
  24.0 1.7 %collective-permute-start.6 = (bf16[4,128,512]{2,1,0:T(8,128)(2,1)S(1)}, bf16[4,128,512]{2,1,0:T(8,128)(2,1)S(1)}, u32[]{:S(2)}, u32[]{:S(2)}) collective-permute-start(bf16[4,128,512]{2,1,0:T(8,128)(2,1)S(1)} %bitcast_dynamic-update-slice_fusion.4), channel_id=1, source_target_pairs={{0,8},{8,0},{16,24},{24,16},{32,40},{40,32},{48,56},{56,48},{64,72... | collective-permute-start | bytes 1572872 | tf_op jit(solution)/shard_map/ppermute | solution.py:272
  25.9 1.4 collective-permute-done.6
  27.6 2.1 %fusion.16 = f32[1024,512]{1,0:T(8,128)} fusion(bf16[1024,512]{1,0:T(8,128)(2,1)S(1)} %bitcast.119, bf16[512,512]{1,0:T(8,128)(2,1)S(1)} %constant_dynamic-update-slice_fusion.k_ref), kind=kOutput, calls=%fused_computation.71 | convolution fusion | flops 536870912 | bytes 3670016 | tf_op jit(solution)/shard_map/dot_general | solution.py:24
  29.9 2.8 %collective-permute-start.12 = (bf16[128,512]{1,0:T(8,128)(2,1)S(1)}, bf16[128,512]{1,0:T(8,128)(2,1)S(1)}, u32[]{:S(2)}, u32[]{:S(2)}) collective-permute-start(bf16[128,512]{1,0:T(8,128)(2,1)S(1)} %get-tuple-element.65), channel_id=1, source_target_pairs={{0,192},{8,200},{16,208},{24,216},{32,224},{40,232},{48,240},{56,2... | collective-permute-start | bytes 393224 | tf_op jit(solution)/shard_map/ppermute | solution.py:266
  32.7 0.7 collective-permute-start.10
  33.3 0.9 collective-permute-start.9
  34.2 1.2 collective-permute-start.8
  35.4 2.6 %collective-permute-done.12 = bf16[128,512]{1,0:T(8,128)(2,1)S(1)} collective-permute-done((bf16[128,512]{1,0:T(8,128)(2,1)S(1)}, bf16[128,512]{1,0:T(8,128)(2,1)S(1)}, u32[]{:S(2)}, u32[]{:S(2)}) %collective-permute-start.12) | collective-permute-done | bytes 131104 | tf_op jit(solution)/shard_map/ppermute | solution.py:266
  38.6 3.2 %collective-permute-done.10 = bf16[128,512]{1,0:T(8,128)(2,1)S(1)} collective-permute-done((bf16[128,512]{1,0:T(8,128)(2,1)S(1)}, bf16[128,512]{1,0:T(8,128)(2,1)S(1)}, u32[]{:S(2)}, u32[]{:S(2)}) %collective-permute-start.10) | collective-permute-done | bytes 131104 | tf_op jit(solution)/shard_map/ppermute | solution.py:266
  41.8 1.2 collective-permute-done.7
  43.2 2.4 %collective-permute-start.13 = (bf16[4,128,512]{2,1,0:T(8,128)(2,1)S(1)}, bf16[4,128,512]{2,1,0:T(8,128)(2,1)S(1)}, u32[]{:S(2)}, u32[]{:S(2)}) collective-permute-start(bf16[4,128,512]{2,1,0:T(8,128)(2,1)S(1)} %bitcast_dynamic-update-slice_fusion), channel_id=1, source_target_pairs={{0,8},{8,0},{16,24},{24,16},{32,40},{40,32},{48,56},{56,48},{64,72... | collective-permute-start | bytes 1572872 | tf_op jit(solution)/shard_map/ppermute | solution.py:272
  45.6 0.9 constant_dynamic-update-slice_fusion.6
  47.3 0.7 convolution_convert_fusion
  48.1 0.9 copy-done.3
  49.0 0.7 dynamic-slice_bitcast_fusion
  49.7 1.6 collective-permute-start.14
  51.3 3.4 %collective-permute-start.17 = (f32[1,128]{1,0:T(1,128)S(1)}, f32[1,128]{1,0:T(1,128)S(1)}, u32[]{:S(2)}, u32[]{:S(2)}) collective-permute-start(f32[1,128]{1,0:T(1,128)S(1)} %get-tuple-element.69), channel_id=1, source_target_pairs={{0,192},{8,200},{16,208},{24,216},{32,224},{40,232},{48,240},{56,2... | collective-permute-start | bytes 1544 | tf_op jit(solution)/shard_map/ppermute | solution.py:266
  54.8 0.6 collective-permute-start.15
  55.3 3.9 %collective-permute-start.21 = (bf16[128,512]{1,0:T(8,128)(2,1)}, bf16[128,512]{1,0:T(8,128)(2,1)}, u32[]{:S(2)}, u32[]{:S(2)}) collective-permute-start(bf16[128,512]{1,0:T(8,128)(2,1)} %get-tuple-element.95), channel_id=1, source_target_pairs={{0,7},{1,0},{2,1},{3,2},{4,3},{5,4},{6,5},{7,6},{8,15},{9,8},{10,9... | collective-permute-start | bytes 393224 | tf_op jit(solution)/shard_map/ppermute | solution.py:275
  59.3 0.7 pad_maximum_fusion.2.flag_ref
  60.0 1.9 %collective-permute-done.14 = bf16[128,512]{1,0:T(8,128)(2,1)S(1)} collective-permute-done((bf16[128,512]{1,0:T(8,128)(2,1)S(1)}, bf16[128,512]{1,0:T(8,128)(2,1)S(1)}, u32[]{:S(2)}, u32[]{:S(2)}) %collective-permute-start.14) | collective-permute-done | bytes 131104 | tf_op jit(solution)/shard_map/ppermute | solution.py:275
  61.9 0.9 fusion.6
  62.9 1.0 collective-permute-done.21
  64.0 6.6 %collective-permute-done.18 = bf16[128,512]{1,0:T(8,128)(2,1)S(1)} collective-permute-done((bf16[128,512]{1,0:T(8,128)(2,1)S(1)}, bf16[128,512]{1,0:T(8,128)(2,1)S(1)}, u32[]{:S(2)}, u32[]{:S(2)}) %collective-permute-start.18) | collective-permute-done | bytes 131104 | tf_op jit(solution)/shard_map/ppermute | solution.py:275
  70.6 1.8 %fusion.3 = (bf16[128,512]{1,0:T(8,128)(2,1)}, bf16[128,512]{1,0:T(8,128)(2,1)S(1)}) fusion(bf16[128,512]{1,0:T(8,128)(2,1)} %collective-permute-done.21, bf16[8,128,512]{2,1,0:T(8,128)(2,1)} %bitcast.129, s32[]{:T(128)S(6)} %select_n.193, s32[]{:T(128)S(6)} %select_n.187, bf16[128,512]{1,0:T(8,128)(2,1)S(1)} %collective-permute-done.18), kind=kLoop, calls=%fused_computation.16 | loop fusion | flops 524288 | bytes 786440 | tf_op jit(solution)/shard_map/convert_element_type | solution.py:351
  72.5 1.3 collective-permute-start.19
  73.8 2.6 %collective-permute-done.22 = bf16[128,512]{1,0:T(8,128)(2,1)S(1)} collective-permute-done((bf16[128,512]{1,0:T(8,128)(2,1)}, bf16[128,512]{1,0:T(8,128)(2,1)S(1)}, u32[]{:S(2)}, u32[]{:S(2)}) %collective-permute-start.22) | collective-permute-done | bytes 131104 | tf_op jit(solution)/shard_map/ppermute | solution.py:275
  76.4 1.3 collective-permute-done.19
  77.6 1.1 fusion.2
  78.7 1.1 collective-permute-start.23
  80.3 2.4 %collective-permute-done.23.back_ref = bf16[128,512]{1,0:T(8,128)(2,1)S(1)} collective-permute-done((bf16[128,512]{1,0:T(8,128)(2,1)S(1)}, bf16[128,512]{1,0:T(8,128)(2,1)S(1)}, u32[]{:S(2)}, u32[]{:S(2)}) %collective-permute-start.23) | collective-permute-done | bytes 131104 | tf_op jit(solution)/shard_map/ppermute | solution.py:275
  82.6 2.3 %collective-permute-done.20.forward_ref = bf16[128,512]{1,0:T(8,128)(2,1)S(1)} collective-permute-done((bf16[128,512]{1,0:T(8,128)(2,1)S(1)}, bf16[128,512]{1,0:T(8,128)(2,1)S(1)}, u32[]{:S(2)}, u32[]{:S(2)}) %collective-permute-start.20) | collective-permute-done | bytes 131104 | tf_op jit(solution)/shard_map/ppermute | solution.py:275
  84.9 0.9 copy-done
  85.9 1.0 block_softmax.1
  86.9 1.1 cross_statistics.1
  88.0 17.4 %all_to_all.15.stat_ref = f32[8,16,1024]{2,1,0:T(8,128)S(1)} all-to-all(f32[8,16,1024]{2,1,0:T(8,128)S(1)} %broadcast_in_dim.77), channel_id=1, replica_groups={{0,8,16,24,32,40,48,56},{64,72,80,88,96,104,112,120},{128,136,144,152,1..., dimensions={0} | all-to-all | bytes 1048576 | tf_op jit(solution)/shard_map/all_to_all | solution.py:280
  105.5 0.6 broadcast_in_dim.78
  106.1 4.4 %all-to-all-start.1 = ((f32[8,2,128]{2,1,0:T(2,128)}), f32[8,2,128]{2,1,0:T(2,128)S(1)}, u32[]{:S(2)}, u32[]{:S(2)}) async-start(f32[8,2,128]{2,1,0:T(2,128)} %broadcast_in_dim.78), calls=%async_computation.2 | async-start | bytes 16384 | tf_op jit(solution)/shard_map/all_to_all | solution.py:280
  110.5 1.5 cross_grads.1
  112.0 0.7 copy-done.1
  112.7 4.4 %all-to-all-done.1.scale_ref = f32[8,2,128]{2,1,0:T(2,128)S(1)} async-done(((f32[8,2,128]{2,1,0:T(2,128)}), f32[8,2,128]{2,1,0:T(2,128)S(1)}, u32[]{:S(2)}, u32[]{:S(2)}) %all-to-all-start.1) | async-done | bytes 8224 | tf_op jit(solution)/shard_map/all_to_all | solution.py:280
  117.1 7.8 %all-gather.2.cloned.1.call-done.both_ref = bf16[1024,1024]{1,0:T(8,128)(2,1)} async-done(((bf16[128,1024]{1,0:T(8,128)(2,1)}), bf16[1024,1024]{1,0:T(8,128)(2,1)}) %all-gather.2.cloned.1.call-update) | async-done | bytes 2097168 | tf_op jit(solution)/shard_map/all_gather | solution.py:360
  124.9 0.9 copy-done.2
  125.8 4.6 %key_grads.1 = (bf16[1024,512]{1,0:T(8,128)(2,1)S(1)}, bf16[128,1024]{1,0:T(8,128)(2,1)S(1)}, bf16[128,1024]{1,0:T(8,128)(2,1)}, bf16[128,1024]{1,0:T(8,128)(2,1)}, bf16[128,1024]{1,0:T(8,128)(2,1)}) custom-call(bf16[1024,1024]{1,0:T(8,128)(2,1)} %all-gather.2.cloned.1.call-done.both_ref, f32[8,2,128]{2,1,0:T(2,128)S(1)} %all-to-all-done.1.scale_ref, ...), custom_call_target="tpu_custom_call" | custom-call | tf_op jit(solution)/shard_map/key_grads/pallas_call | solution.py:187
  130.5 1.6 query_grads.1
  132.1 4.4 %collective-permute-start.24 = (bf16[512,512]{1,0:T(8,128)(2,1)S(1)}, bf16[512,512]{1,0:T(8,128)(2,1)S(1)}, u32[]{:S(2)}, u32[]{:S(2)}) collective-permute-start(bf16[512,512]{1,0:T(8,128)(2,1)S(1)} %get-tuple-element.84), channel_id=1, source_target_pairs={{0,8},{8,0},{16,24},{24,16},{32,40},{40,32},{48,56},{56,48},{64,72... | collective-permute-start | bytes 1572872 | tf_op jit(solution)/shard_map/ppermute | solution.py:272
  136.6 2.6 %collective-permute-start.25 = (bf16[128,1024]{1,0:T(8,128)(2,1)}, bf16[128,1024]{1,0:T(8,128)(2,1)S(1)}, u32[]{:S(2)}, u32[]{:S(2)}) collective-permute-start(bf16[128,1024]{1,0:T(8,128)(2,1)} %get-tuple-element.86), channel_id=1, source_target_pairs={{0,192},{8,200},{16,208},{24,216},{32,224},{40,232},{48,240},{56,2... | collective-permute-start | bytes 786440 | tf_op jit(solution)/shard_map/ppermute | solution.py:266
  139.5 0.7 collective-permute-start.27
  140.2 1.0 add_convert_fusion
  141.2 3.6 %all-to-all-start.2 = ((bf16[4,128,512]{2,1,0:T(8,128)(2,1)}), bf16[4,128,512]{2,1,0:T(8,128)(2,1)S(1)}, u32[]{:S(2)}, u32[]{:S(2)}) async-start(bf16[4,128,512]{2,1,0:T(8,128)(2,1)} %bitcast.34), calls=%async_computation.3 | async-start | bytes 1048576 | tf_op jit(solution)/shard_map/all_to_all | solution.py:382
  144.8 5.8 %collective-permute-done.25 = bf16[128,1024]{1,0:T(8,128)(2,1)S(1)} collective-permute-done((bf16[128,1024]{1,0:T(8,128)(2,1)}, bf16[128,1024]{1,0:T(8,128)(2,1)S(1)}, u32[]{:S(2)}, u32[]{:S(2)}) %collective-permute-start.25) | collective-permute-done | bytes 262176 | tf_op jit(solution)/shard_map/ppermute | solution.py:266
  150.6 4.2 %collective-permute-done.27 = bf16[128,1024]{1,0:T(8,128)(2,1)} collective-permute-done((bf16[128,1024]{1,0:T(8,128)(2,1)}, bf16[128,1024]{1,0:T(8,128)(2,1)}, u32[]{:S(2)}, u32[]{:S(2)}) %collective-permute-start.27) | collective-permute-done | bytes 262176 | tf_op jit(solution)/shard_map/ppermute | solution.py:266
  154.8 1.1 convert_add_fusion
  156.0 0.7 reshape.107
  156.7 0.7 reshape.106
  157.5 0.7 reshape.105
  (78 shorter events, 4.2 us)
Async XLA Ops:
  7.2 77.8 %reduce-scatter.2.cloned.1.call-start = ((), (), s32[]{:S(2)}) async-start(), calls=%async_computation.4 | async-start | bytes 2359296 | tf_op jit(solution)/shard_map/reduce_scatter | solution.py:335
  9.3 8.4 %collective-permute-start = (bf16[128,512]{1,0:T(8,128)(2,1)S(1)}, bf16[128,512]{1,0:T(8,128)(2,1)S(1)}, u32[]{:S(2)}, u32[]{:S(2)}) collective-permute-start(bf16[128,512]{1,0:T(8,128)(2,1)S(1)} %get-tuple-element.50), channel_id=1, source_target_pairs={{0,16},{8,24},{16,32},{24,40},{32,48},{40,56},{48,0},{56,8},{64,80... | collective-permute-start | bytes 393224 | tf_op jit(solution)/shard_map/ppermute | solution.py:269
  11.4 8.6 %collective-permute-start.2 = (bf16[128,512]{1,0:T(8,128)(2,1)S(1)}, bf16[128,512]{1,0:T(8,128)(2,1)S(1)}, u32[]{:S(2)}, u32[]{:S(2)}) collective-permute-start(bf16[128,512]{1,0:T(8,128)(2,1)S(1)} %get-tuple-element.50), channel_id=1, source_target_pairs={{0,48},{8,56},{16,0},{24,8},{32,16},{40,24},{48,32},{56,40},{64,11... | collective-permute-start | bytes 393224 | tf_op jit(solution)/shard_map/ppermute | solution.py:269
  12.8 7.2 %collective-permute-start.1 = (bf16[128,512]{1,0:T(8,128)(2,1)S(1)}, bf16[128,512]{1,0:T(8,128)(2,1)S(1)}, u32[]{:S(2)}, u32[]{:S(2)}) collective-permute-start(bf16[128,512]{1,0:T(8,128)(2,1)S(1)} %get-tuple-element.50), channel_id=1, source_target_pairs={{0,32},{8,40},{16,48},{24,56},{32,0},{40,8},{48,16},{56,24},{64,96... | collective-permute-start | bytes 393224 | tf_op jit(solution)/shard_map/ppermute | solution.py:269
  14.4 5.6 %collective-permute-start.4 = (bf16[128,512]{1,0:T(8,128)(2,1)S(1)}, bf16[128,512]{1,0:T(8,128)(2,1)S(1)}, u32[]{:S(2)}, u32[]{:S(2)}) collective-permute-start(bf16[128,512]{1,0:T(8,128)(2,1)S(1)} %get-tuple-element.56), channel_id=1, source_target_pairs={{0,128},{8,136},{16,144},{24,152},{32,160},{40,168},{48,176},{56,1... | collective-permute-start | bytes 393224 | tf_op jit(solution)/shard_map/ppermute | solution.py:266
  17.3 6.6 %collective-permute-start.3 = (bf16[128,512]{1,0:T(8,128)(2,1)S(1)}, bf16[128,512]{1,0:T(8,128)(2,1)S(1)}, u32[]{:S(2)}, u32[]{:S(2)}) collective-permute-start(bf16[128,512]{1,0:T(8,128)(2,1)S(1)} %get-tuple-element.56), channel_id=1, source_target_pairs={{0,64},{8,72},{16,80},{24,88},{32,96},{40,104},{48,112},{56,120},{... | collective-permute-start | bytes 393224 | tf_op jit(solution)/shard_map/ppermute | solution.py:266
  17.7 6.2 %collective-permute-start.5 = (bf16[128,512]{1,0:T(8,128)(2,1)S(1)}, bf16[128,512]{1,0:T(8,128)(2,1)S(1)}, u32[]{:S(2)}, u32[]{:S(2)}) collective-permute-start(bf16[128,512]{1,0:T(8,128)(2,1)S(1)} %get-tuple-element.56), channel_id=1, source_target_pairs={{0,192},{8,200},{16,208},{24,216},{32,224},{40,232},{48,240},{56,2... | collective-permute-start | bytes 393224 | tf_op jit(solution)/shard_map/ppermute | solution.py:266
  24.0 3.3 %collective-permute-start.6 = (bf16[4,128,512]{2,1,0:T(8,128)(2,1)S(1)}, bf16[4,128,512]{2,1,0:T(8,128)(2,1)S(1)}, u32[]{:S(2)}, u32[]{:S(2)}) collective-permute-start(bf16[4,128,512]{2,1,0:T(8,128)(2,1)S(1)} %bitcast_dynamic-update-slice_fusion.4), channel_id=1, source_target_pairs={{0,8},{8,0},{16,24},{24,16},{32,40},{40,32},{48,56},{56,48},{64,72... | collective-permute-start | bytes 1572872 | tf_op jit(solution)/shard_map/ppermute | solution.py:272
  25.8 4.0 %copy-start.4 = (pred[16,8,4,128]{3,1,2,0:T(8,128)(4,1)}, pred[16,8,4,128]{3,1,2,0:T(8,128)(4,1)S(1)}, u32[]{:S(2)}) copy-start(pred[16,8,4,128]{3,1,2,0:T(8,128)(4,1)S(1)} %copy.31) | copy-start | bytes 196612
  27.6 2.2 %copy-start.7 = (bf16[128,4,128]{2,1,0:T(4,128)(2,1)S(1)}, bf16[128,4,128]{2,1,0:T(4,128)(2,1)}, u32[]{:S(2)}) copy-start(bf16[128,4,128]{2,1,0:T(4,128)(2,1)} %param.8) | copy-start | bytes 393220
  27.6 2.2 %copy-start.8 = (bf16[128,4,128]{2,1,0:T(4,128)(2,1)S(1)}, bf16[128,4,128]{2,1,0:T(4,128)(2,1)}, u32[]{:S(2)}) copy-start(bf16[128,4,128]{2,1,0:T(4,128)(2,1)} %param.9) | copy-start | bytes 393220
  29.7 95.2 %all-gather.2.cloned.1.call-start = ((), (), s32[]{:S(2)}) async-start(), calls=%async_computation.5 | async-start | bytes 2359296 | tf_op jit(solution)/shard_map/all_gather | solution.py:360
  29.9 8.2 %collective-permute-start.12 = (bf16[128,512]{1,0:T(8,128)(2,1)S(1)}, bf16[128,512]{1,0:T(8,128)(2,1)S(1)}, u32[]{:S(2)}, u32[]{:S(2)}) collective-permute-start(bf16[128,512]{1,0:T(8,128)(2,1)S(1)} %get-tuple-element.65), channel_id=1, source_target_pairs={{0,192},{8,200},{16,208},{24,216},{32,224},{40,232},{48,240},{56,2... | collective-permute-start | bytes 393224 | tf_op jit(solution)/shard_map/ppermute | solution.py:266
  32.7 6.0 %collective-permute-start.11 = (bf16[128,512]{1,0:T(8,128)(2,1)S(1)}, bf16[128,512]{1,0:T(8,128)(2,1)S(1)}, u32[]{:S(2)}, u32[]{:S(2)}) collective-permute-start(bf16[128,512]{1,0:T(8,128)(2,1)S(1)} %get-tuple-element.65), channel_id=1, source_target_pairs={{0,128},{8,136},{16,144},{24,152},{32,160},{40,168},{48,176},{56,1... | collective-permute-start | bytes 393224 | tf_op jit(solution)/shard_map/ppermute | solution.py:266
  32.7 9.1 %collective-permute-start.10 = (bf16[128,512]{1,0:T(8,128)(2,1)S(1)}, bf16[128,512]{1,0:T(8,128)(2,1)S(1)}, u32[]{:S(2)}, u32[]{:S(2)}) collective-permute-start(bf16[128,512]{1,0:T(8,128)(2,1)S(1)} %get-tuple-element.65), channel_id=1, source_target_pairs={{0,64},{8,72},{16,80},{24,88},{32,96},{40,104},{48,112},{56,120},{... | collective-permute-start | bytes 393224 | tf_op jit(solution)/shard_map/ppermute | solution.py:266
  33.3 8.5 %collective-permute-start.9 = (bf16[128,512]{1,0:T(8,128)(2,1)S(1)}, bf16[128,512]{1,0:T(8,128)(2,1)S(1)}, u32[]{:S(2)}, u32[]{:S(2)}) collective-permute-start(bf16[128,512]{1,0:T(8,128)(2,1)S(1)} %get-tuple-element.60), channel_id=1, source_target_pairs={{0,48},{8,56},{16,0},{24,8},{32,16},{40,24},{48,32},{56,40},{64,11... | collective-permute-start | bytes 393224 | tf_op jit(solution)/shard_map/ppermute | solution.py:269
  34.2 7.6 %collective-permute-start.8 = (bf16[128,512]{1,0:T(8,128)(2,1)S(1)}, bf16[128,512]{1,0:T(8,128)(2,1)S(1)}, u32[]{:S(2)}, u32[]{:S(2)}) collective-permute-start(bf16[128,512]{1,0:T(8,128)(2,1)S(1)} %get-tuple-element.60), channel_id=1, source_target_pairs={{0,32},{8,40},{16,48},{24,56},{32,0},{40,8},{48,16},{56,24},{64,96... | collective-permute-start | bytes 393224 | tf_op jit(solution)/shard_map/ppermute | solution.py:269
  38.0 5.0 %collective-permute-start.7 = (bf16[128,512]{1,0:T(8,128)(2,1)S(1)}, bf16[128,512]{1,0:T(8,128)(2,1)S(1)}, u32[]{:S(2)}, u32[]{:S(2)}) collective-permute-start(bf16[128,512]{1,0:T(8,128)(2,1)S(1)} %get-tuple-element.60), channel_id=1, source_target_pairs={{0,16},{8,24},{16,32},{24,40},{32,48},{40,56},{48,0},{56,8},{64,80... | collective-permute-start | bytes 393224 | tf_op jit(solution)/shard_map/ppermute | solution.py:269
  41.8 1.4 copy-start.6
  43.2 3.9 %collective-permute-start.13 = (bf16[4,128,512]{2,1,0:T(8,128)(2,1)S(1)}, bf16[4,128,512]{2,1,0:T(8,128)(2,1)S(1)}, u32[]{:S(2)}, u32[]{:S(2)}) collective-permute-start(bf16[4,128,512]{2,1,0:T(8,128)(2,1)S(1)} %bitcast_dynamic-update-slice_fusion), channel_id=1, source_target_pairs={{0,8},{8,0},{16,24},{24,16},{32,40},{40,32},{48,56},{56,48},{64,72... | collective-permute-start | bytes 1572872 | tf_op jit(solution)/shard_map/ppermute | solution.py:272
  48.1 1.0 copy-start.3
  49.7 12.2 %collective-permute-start.14 = (bf16[128,512]{1,0:T(8,128)(2,1)S(1)}, bf16[128,512]{1,0:T(8,128)(2,1)S(1)}, u32[]{:S(2)}, u32[]{:S(2)}) collective-permute-start(bf16[128,512]{1,0:T(8,128)(2,1)S(1)} %get-tuple-element.96), channel_id=1, source_target_pairs={{0,1},{1,2},{2,3},{3,4},{4,5},{5,6},{6,7},{7,0},{8,9},{9,10},{10,1... | collective-permute-start | bytes 393224 | tf_op jit(solution)/shard_map/ppermute | solution.py:275
  51.3 7.9 %collective-permute-start.17 = (f32[1,128]{1,0:T(1,128)S(1)}, f32[1,128]{1,0:T(1,128)S(1)}, u32[]{:S(2)}, u32[]{:S(2)}) collective-permute-start(f32[1,128]{1,0:T(1,128)S(1)} %get-tuple-element.69), channel_id=1, source_target_pairs={{0,192},{8,200},{16,208},{24,216},{32,224},{40,232},{48,240},{56,2... | collective-permute-start | bytes 1544 | tf_op jit(solution)/shard_map/ppermute | solution.py:266
  54.7 4.5 %collective-permute-start.16 = (f32[1,128]{1,0:T(1,128)S(1)}, f32[1,128]{1,0:T(1,128)S(1)}, u32[]{:S(2)}, u32[]{:S(2)}) collective-permute-start(f32[1,128]{1,0:T(1,128)S(1)} %get-tuple-element.69), channel_id=1, source_target_pairs={{0,128},{8,136},{16,144},{24,152},{32,160},{40,168},{48,176},{56,1... | collective-permute-start | bytes 1544 | tf_op jit(solution)/shard_map/ppermute | solution.py:266
  54.8 4.5 %collective-permute-start.15 = (f32[1,128]{1,0:T(1,128)S(1)}, f32[1,128]{1,0:T(1,128)}, u32[]{:S(2)}, u32[]{:S(2)}) collective-permute-start(f32[1,128]{1,0:T(1,128)S(1)} %get-tuple-element.69), channel_id=1, source_target_pairs={{0,64},{8,72},{16,80},{24,88},{32,96},{40,104},{48,112},{56,120},{... | collective-permute-start | bytes 1544 | tf_op jit(solution)/shard_map/ppermute | solution.py:266
  55.3 8.6 %collective-permute-start.21 = (bf16[128,512]{1,0:T(8,128)(2,1)}, bf16[128,512]{1,0:T(8,128)(2,1)}, u32[]{:S(2)}, u32[]{:S(2)}) collective-permute-start(bf16[128,512]{1,0:T(8,128)(2,1)} %get-tuple-element.95), channel_id=1, source_target_pairs={{0,7},{1,0},{2,1},{3,2},{4,3},{5,4},{6,5},{7,6},{8,15},{9,8},{10,9... | collective-permute-start | bytes 393224 | tf_op jit(solution)/shard_map/ppermute | solution.py:275
  62.8 7.8 %collective-permute-start.18 = (bf16[128,512]{1,0:T(8,128)(2,1)S(1)}, bf16[128,512]{1,0:T(8,128)(2,1)S(1)}, u32[]{:S(2)}, u32[]{:S(2)}) collective-permute-start(bf16[128,512]{1,0:T(8,128)(2,1)S(1)} %fusion.6), channel_id=1, source_target_pairs={{0,1},{1,2},{2,3},{3,4},{4,5},{5,6},{6,7},{7,0},{8,9},{9,10},{10,1... | collective-permute-start | bytes 393224 | tf_op jit(solution)/shard_map/ppermute | solution.py:275
  72.3 4.0 %collective-permute-start.22 = (bf16[128,512]{1,0:T(8,128)(2,1)}, bf16[128,512]{1,0:T(8,128)(2,1)S(1)}, u32[]{:S(2)}, u32[]{:S(2)}) collective-permute-start(bf16[128,512]{1,0:T(8,128)(2,1)} %get-tuple-element.93), channel_id=1, source_target_pairs={{0,7},{1,0},{2,1},{3,2},{4,3},{5,4},{6,5},{7,6},{8,15},{9,8},{10,9... | collective-permute-start | bytes 393224 | tf_op jit(solution)/shard_map/ppermute | solution.py:275
  72.5 5.1 %collective-permute-start.19 = (bf16[128,512]{1,0:T(8,128)(2,1)S(1)}, bf16[128,512]{1,0:T(8,128)(2,1)}, u32[]{:S(2)}, u32[]{:S(2)}) collective-permute-start(bf16[128,512]{1,0:T(8,128)(2,1)S(1)} %get-tuple-element.94), channel_id=1, source_target_pairs={{0,1},{1,2},{2,3},{3,4},{4,5},{5,6},{6,7},{7,0},{8,9},{9,10},{10,1... | collective-permute-start | bytes 393224 | tf_op jit(solution)/shard_map/ppermute | solution.py:275
  78.7 3.9 %collective-permute-start.23 = (bf16[128,512]{1,0:T(8,128)(2,1)S(1)}, bf16[128,512]{1,0:T(8,128)(2,1)S(1)}, u32[]{:S(2)}, u32[]{:S(2)}) collective-permute-start(bf16[128,512]{1,0:T(8,128)(2,1)S(1)} %get-tuple-element.91), channel_id=1, source_target_pairs={{0,7},{1,0},{2,1},{3,2},{4,3},{5,4},{6,5},{7,6},{8,15},{9,8},{10,9... | collective-permute-start | bytes 393224 | tf_op jit(solution)/shard_map/ppermute | solution.py:275
  79.9 5.0 %collective-permute-start.20 = (bf16[128,512]{1,0:T(8,128)(2,1)S(1)}, bf16[128,512]{1,0:T(8,128)(2,1)S(1)}, u32[]{:S(2)}, u32[]{:S(2)}) collective-permute-start(bf16[128,512]{1,0:T(8,128)(2,1)S(1)} %get-tuple-element.92), channel_id=1, source_target_pairs={{0,1},{1,2},{2,3},{3,4},{4,5},{5,6},{6,7},{7,0},{8,9},{9,10},{10,1... | collective-permute-start | bytes 393224 | tf_op jit(solution)/shard_map/ppermute | solution.py:275
  84.9 1.0 copy-start
  106.1 11.0 %all-to-all-start.1 = ((f32[8,2,128]{2,1,0:T(2,128)}), f32[8,2,128]{2,1,0:T(2,128)S(1)}, u32[]{:S(2)}, u32[]{:S(2)}) async-start(f32[8,2,128]{2,1,0:T(2,128)} %broadcast_in_dim.78), calls=%async_computation.2 | async-start | bytes 16384 | tf_op jit(solution)/shard_map/all_to_all | solution.py:280
  112.0 0.7 copy-start.1
  124.9 0.9 copy-start.2
  132.1 8.1 %collective-permute-start.24 = (bf16[512,512]{1,0:T(8,128)(2,1)S(1)}, bf16[512,512]{1,0:T(8,128)(2,1)S(1)}, u32[]{:S(2)}, u32[]{:S(2)}) collective-permute-start(bf16[512,512]{1,0:T(8,128)(2,1)S(1)} %get-tuple-element.84), channel_id=1, source_target_pairs={{0,8},{8,0},{16,24},{24,16},{32,40},{40,32},{48,56},{56,48},{64,72... | collective-permute-start | bytes 1572872 | tf_op jit(solution)/shard_map/ppermute | solution.py:272
  136.6 14.1 %collective-permute-start.25 = (bf16[128,1024]{1,0:T(8,128)(2,1)}, bf16[128,1024]{1,0:T(8,128)(2,1)S(1)}, u32[]{:S(2)}, u32[]{:S(2)}) collective-permute-start(bf16[128,1024]{1,0:T(8,128)(2,1)} %get-tuple-element.86), channel_id=1, source_target_pairs={{0,192},{8,200},{16,208},{24,216},{32,224},{40,232},{48,240},{56,2... | collective-permute-start | bytes 786440 | tf_op jit(solution)/shard_map/ppermute | solution.py:266
  139.2 11.4 %collective-permute-start.26 = (bf16[128,1024]{1,0:T(8,128)(2,1)}, bf16[128,1024]{1,0:T(8,128)(2,1)S(1)}, u32[]{:S(2)}, u32[]{:S(2)}) collective-permute-start(bf16[128,1024]{1,0:T(8,128)(2,1)} %get-tuple-element.87), channel_id=1, source_target_pairs={{0,128},{8,136},{16,144},{24,152},{32,160},{40,168},{48,176},{56,1... | collective-permute-start | bytes 786440 | tf_op jit(solution)/shard_map/ppermute | solution.py:266
  139.5 15.3 %collective-permute-start.27 = (bf16[128,1024]{1,0:T(8,128)(2,1)}, bf16[128,1024]{1,0:T(8,128)(2,1)}, u32[]{:S(2)}, u32[]{:S(2)}) collective-permute-start(bf16[128,1024]{1,0:T(8,128)(2,1)} %get-tuple-element.88), channel_id=1, source_target_pairs={{0,64},{8,72},{16,80},{24,88},{32,96},{40,104},{48,112},{56,120},{... | collective-permute-start | bytes 786440 | tf_op jit(solution)/shard_map/ppermute | solution.py:266
  140.2 15.8 %copy-start.5 = (pred[16,8,4,128]{3,1,2,0:T(8,128)(4,1)S(1)}, pred[16,8,4,128]{3,1,2,0:T(8,128)(4,1)}, u32[]{:S(2)}) copy-start(pred[16,8,4,128]{3,1,2,0:T(8,128)(4,1)} %copy-done.4) | copy-start | bytes 196612
  141.2 16.3 %all-to-all-start.2 = ((bf16[4,128,512]{2,1,0:T(8,128)(2,1)}), bf16[4,128,512]{2,1,0:T(8,128)(2,1)S(1)}, u32[]{:S(2)}, u32[]{:S(2)}) async-start(bf16[4,128,512]{2,1,0:T(8,128)(2,1)} %bitcast.34), calls=%async_computation.3 | async-start | bytes 1048576 | tf_op jit(solution)/shard_map/all_to_all | solution.py:382
Sparse Core Ops, SparseCore 0:
  29.8 43.4 reduce-scatter.1
  87.0 37.9 all-gather.1

commit v12 on v10

--- a/solution.py
+++ b/solution.py
@@ -10,7 +10,6 @@
 
 SUMMARIES = 256
 XS = 4
-FLAG_ROWS = 16
 
 ROW_PAIR = (((1,), (1,)), ((), ()))
 LEAD_PAIR = (((0,), (0,)), ((), ()))
@@ -278,8 +277,8 @@
             copies, axis, split_axis=0, concat_axis=0, tiled=True, axis_index_groups=groups
         )
 
-    column_ids = own_z * cols_dev + jnp.arange(cols_dev, dtype=jnp.int32)
-    cell_keep = (row_keep[:, None] == 1) & (column_ids[None, :] < row_lengths[:, None])
+    own_columns = jnp.where(row_keep == 1, row_lengths, 0) - own_z * cols_dev
+    cell_keep = jnp.arange(cols_dev, dtype=jnp.int32)[None, :] < own_columns[:, None]
     keep_flat = jnp.broadcast_to(cell_keep[:, :, None], queries.shape).reshape(
         rows_dev, flat_width
     )
@@ -319,18 +318,12 @@
     q_blk = both_lines(q_line, q_other)
     k_blk = jnp.concatenate(k_pieces, axis=0)
     logit_piece = dot_f32(q_blk, k_blk, ROW_PAIR)
-    flag_rows = jnp.pad(
-        row_keep.astype(jnp.bfloat16)[None, :], ((0, FLAG_ROWS - 1), (0, flat_width - rows_dev))
-    )
-    g_pieces, key_pieces = wave(
-        masked(out_grad), jnp.concatenate([masked(values), flag_rows], axis=0), False
-    )
-    v_blk = jnp.concatenate([p[:rows_dev] for p in key_pieces], axis=0)
+    g_pieces, v_pieces = wave(masked(out_grad), masked(values), False)
+    v_blk = jnp.concatenate(v_pieces, axis=0)
     g_line = in_line(g_pieces)
     g_blk = both_lines(g_line, swap_core(g_line))
     g_blk, _ = lax.optimization_barrier((g_blk, logit_piece))
     dprob_piece = dot_f32(g_blk, v_blk, ROW_PAIR).astype(jnp.bfloat16)
-    key_flags = jnp.concatenate([p[rows_dev, :rows_dev] for p in key_pieces])[None, :]
     logit_sum = lax.psum_scatter(logit_piece, "col", scatter_dimension=0, tiled=True)
 
     dprob_chunks = dprob_piece.reshape(zs, block_rows // zs, block_keys)
@@ -338,18 +331,30 @@
     def part(step):
         return lax.dynamic_index_in_dim(dprob_chunks, (own_z + step) % zs, axis=0, keepdims=False)
 
-    def passed(step, count):
-        moving = part(step * count)
-        for left in range(count - 1, -1, -1):
-            moving = shift_z(moving, step)
-            if left > 0:
-                moving = (
-                    moving.astype(jnp.float32) + part(step * left).astype(jnp.float32)
-                ).astype(jnp.bfloat16)
+    def onward(moving, step, left):
+        if left > 0:
+            moving = (
+                moving.astype(jnp.float32) + part(step * left).astype(jnp.float32)
+            ).astype(jnp.bfloat16)
         return moving
 
-    dprob_forward = passed(1, zs // 2)
-    dprob_back = passed(-1, zs - 1 - zs // 2)
+    def passed(moving, step, left):
+        while left > 0:
+            left -= 1
+            moving = onward(shift_z(moving, step), step, left)
+        return moving
+
+    ahead, behind = zs // 2, zs - 1 - zs // 2
+    dprob_forward = onward(shift_z(part(ahead), 1), 1, ahead - 1)
+    own_flags, dprob_forward = lax.optimization_barrier(
+        (row_keep.astype(jnp.float32)[None, :], dprob_forward)
+    )
+    key_flags = jnp.concatenate(
+        [own_flags] + [shift_y(own_flags, s) for s in range(1, ys)], axis=1
+    )
+    dprob_forward, key_flags = lax.optimization_barrier((shift_z(dprob_forward, 1), key_flags))
+    dprob_forward = passed(onward(dprob_forward, 1, ahead - 2), 1, ahead - 2)
+    dprob_back = passed(part(-behind), -1, behind)
 
     both, stats = block_softmax(
         logit_scale, logit_sum, part(0), dprob_forward, dprob_back, key_flags

time: 164 us -> 166 us (1.012)
  starting transfers between devices: 45.3 us -> 49 us
  local copies, waits for them, and re-layouts: 10 us -> 7.6 us
    ppermute x9 -> x12, waiting for transfers between devices: 13.4 us -> 23 us  [shift_y(): lax.ppermute(table, 'row', [(at(y, x, c), at(y + step, x, c)) for y, x, c...]
    ppermute x6, waiting for transfers between devices: 7.42 us -> 1.25 us  [shift_x(): lax.ppermute(table, 'row', [(at(y, x, c), at(y, x + step, c)) for y, x, c...]
    ppermute x9 -> x12, starting transfers between devices: 12.6 us -> 16.8 us  [shift_y(): lax.ppermute(table, 'row', [(at(y, x, c), at(y + step, x, c)) for y, x, c...]
    ppermute x7, waiting for transfers between devices: 21.9 us -> 17.9 us  [shift_z(): return lax.ppermute(table, 'col', [(z, (z + step) % zs) for z in range(zs)])]
    slice x4 -> x0, local copies, waits for them, and re-layouts: 1.85 us -> none  [shards(): v_blk = jnp.concatenate([p[:rows_dev] for p in key_pieces], axis=0)]
  transfers between devices with their start and end apart: 29 -> 32, of which waited for: 15 -> 19; matrix products, arithmetic and copies ran while one was open for 8% -> 8% of each run, Pallas kernels for 2% -> 2%
where the time goes in v12:
time: 166 us; the launch traced here: 165 us
  waiting for transfers between devices  56.4 us (34%)
  starting transfers between devices  49 us (30%)
  blocking collectives  17.4 us (10%)
  between operations  14.4 us (9%)
  Pallas kernels  8.4 us (5%)
  other arithmetic  8.16 us (5%)
  local copies, waits for them, and re-layouts  7.6 us (5%)
  matrix products  3.79 us (2%)
    ppermute x12, waiting for transfers between devices, shift_y(): lax.ppermute(table, 'row', [(at(y, x, c), at(y + step, x, c)) for y, x, c...  23 us
    ppermute x7, waiting for transfers between devices, shift_z(): return lax.ppermute(table, 'col', [(z, (z + step) % zs) for z in range(zs)])  17.9 us
    all_to_all x1, blocking collectives, share(): lax.all_to_all(copies, axis, split_axis=0, concat_axis=0, tiled=True, axi...  17.4 us
    ppermute x12, starting transfers between devices, shift_y(): lax.ppermute(table, 'row', [(at(y, x, c), at(y + step, x, c)) for y, x, c...  16.8 us
    ppermute x3, starting transfers between devices, swap_core(): lax.ppermute(table, 'row', [(at(y, x, c), at(y, x, 1 - c)) for y, x, c in...  8.78 us
    all_gather x1, waiting for transfers between devices, shards(): both = lax.all_gather(both, 'col', axis=0, tiled=True)  7.81 us
    ppermute x6, starting transfers between devices, shift_x(): lax.ppermute(table, 'row', [(at(y, x, c), at(y, x + step, c)) for y, x, c...  7.49 us
    ppermute x7, starting transfers between devices, shift_z(): return lax.ppermute(table, 'col', [(z, (z + step) % zs) for z in range(zs)])  7.38 us
  transfers between devices with their start and end apart: 32, of which 19 were waited for; matrix products, arithmetic and copies ran while one was open for 8% of the time, Pallas kernels for 2%

profile of v12, /device:TPU:1, one launch (start us, length us, event | category | flops | bytes accessed | tf_op | source)
XLA Modules:
  0.0 165.1 jit_solution(13593120218276762220)
XLA Ops:
  7.2 0.7 convert_bitcast_fusion
  8.3 1.0 bitcast_select_fusion.3
  9.3 2.1 %collective-permute-start = (bf16[128,512]{1,0:T(8,128)(2,1)S(1)}, bf16[128,512]{1,0:T(8,128)(2,1)S(1)}, u32[]{:S(2)}, u32[]{:S(2)}) collective-permute-start(bf16[128,512]{1,0:T(8,128)(2,1)S(1)} %get-tuple-element.52), channel_id=1, source_target_pairs={{0,16},{8,24},{16,32},{24,40},{32,48},{40,56},{48,0},{56,8},{64,80... | collective-permute-start | bytes 393224 | tf_op jit(solution)/shard_map/ppermute | solution.py:265
  11.4 1.4 collective-permute-start.2
  12.8 1.6 collective-permute-start.1
  14.4 2.9 %collective-permute-start.4 = (bf16[128,512]{1,0:T(8,128)(2,1)S(1)}, bf16[128,512]{1,0:T(8,128)(2,1)S(1)}, u32[]{:S(2)}, u32[]{:S(2)}) collective-permute-start(bf16[128,512]{1,0:T(8,128)(2,1)S(1)} %get-tuple-element.58), channel_id=1, source_target_pairs={{0,128},{8,136},{16,144},{24,152},{32,160},{40,168},{48,176},{56,1... | collective-permute-start | bytes 393224 | tf_op jit(solution)/shard_map/ppermute | solution.py:262
  17.3 0.4 collective-permute-start.3
  17.7 2.3 %collective-permute-start.5 = (bf16[128,512]{1,0:T(8,128)(2,1)S(1)}, bf16[128,512]{1,0:T(8,128)(2,1)S(1)}, u32[]{:S(2)}, u32[]{:S(2)}) collective-permute-start(bf16[128,512]{1,0:T(8,128)(2,1)S(1)} %get-tuple-element.58), channel_id=1, source_target_pairs={{0,192},{8,200},{16,208},{24,216},{32,224},{40,232},{48,240},{56,2... | collective-permute-start | bytes 393224 | tf_op jit(solution)/shard_map/ppermute | solution.py:262
  20.0 3.9 %collective-permute-done.3 = bf16[128,512]{1,0:T(8,128)(2,1)S(1)} collective-permute-done((bf16[128,512]{1,0:T(8,128)(2,1)S(1)}, bf16[128,512]{1,0:T(8,128)(2,1)S(1)}, u32[]{:S(2)}, u32[]{:S(2)}) %collective-permute-start.3) | collective-permute-done | bytes 131104 | tf_op jit(solution)/shard_map/ppermute | solution.py:262
  24.0 1.7 %collective-permute-start.6 = (bf16[4,128,512]{2,1,0:T(8,128)(2,1)S(1)}, bf16[4,128,512]{2,1,0:T(8,128)(2,1)S(1)}, u32[]{:S(2)}, u32[]{:S(2)}) collective-permute-start(bf16[4,128,512]{2,1,0:T(8,128)(2,1)S(1)} %bitcast_dynamic-update-slice_fusion.4), channel_id=1, source_target_pairs={{0,8},{8,0},{16,24},{24,16},{32,40},{40,32},{48,56},{56,48},{64,72... | collective-permute-start | bytes 1572872 | tf_op jit(solution)/shard_map/ppermute | solution.py:268
  25.9 1.4 collective-permute-done.6
  27.6 2.1 %fusion.16 = f32[1024,512]{1,0:T(8,128)} fusion(bf16[1024,512]{1,0:T(8,128)(2,1)S(1)} %bitcast.119, bf16[512,512]{1,0:T(8,128)(2,1)S(1)} %constant_dynamic-update-slice_fusion.k_ref), kind=kOutput, calls=%fused_computation.71 | convolution fusion | flops 536870912 | bytes 3670016 | tf_op jit(solution)/shard_map/dot_general | solution.py:24
  29.8 2.8 %collective-permute-start.12 = (bf16[128,512]{1,0:T(8,128)(2,1)S(1)}, bf16[128,512]{1,0:T(8,128)(2,1)S(1)}, u32[]{:S(2)}, u32[]{:S(2)}) collective-permute-start(bf16[128,512]{1,0:T(8,128)(2,1)S(1)} %get-tuple-element.67), channel_id=1, source_target_pairs={{0,192},{8,200},{16,208},{24,216},{32,224},{40,232},{48,240},{56,2... | collective-permute-start | bytes 393224 | tf_op jit(solution)/shard_map/ppermute | solution.py:262
  32.6 0.7 collective-permute-start.10
  33.3 0.9 collective-permute-start.9
  34.2 1.2 collective-permute-start.8
  35.4 2.6 %collective-permute-done.12 = bf16[128,512]{1,0:T(8,128)(2,1)S(1)} collective-permute-done((bf16[128,512]{1,0:T(8,128)(2,1)S(1)}, bf16[128,512]{1,0:T(8,128)(2,1)S(1)}, u32[]{:S(2)}, u32[]{:S(2)}) %collective-permute-start.12) | collective-permute-done | bytes 131104 | tf_op jit(solution)/shard_map/ppermute | solution.py:262
  38.3 0.4 collective-permute-done.11
  38.6 3.2 %collective-permute-done.10 = bf16[128,512]{1,0:T(8,128)(2,1)S(1)} collective-permute-done((bf16[128,512]{1,0:T(8,128)(2,1)S(1)}, bf16[128,512]{1,0:T(8,128)(2,1)S(1)}, u32[]{:S(2)}, u32[]{:S(2)}) %collective-permute-start.10) | collective-permute-done | bytes 131104 | tf_op jit(solution)/shard_map/ppermute | solution.py:262
  41.8 1.2 collective-permute-done.7
  43.2 2.4 %collective-permute-start.13 = (bf16[4,128,512]{2,1,0:T(8,128)(2,1)S(1)}, bf16[4,128,512]{2,1,0:T(8,128)(2,1)S(1)}, u32[]{:S(2)}, u32[]{:S(2)}) collective-permute-start(bf16[4,128,512]{2,1,0:T(8,128)(2,1)S(1)} %bitcast_dynamic-update-slice_fusion), channel_id=1, source_target_pairs={{0,8},{8,0},{16,24},{24,16},{32,40},{40,32},{48,56},{56,48},{64,72... | collective-permute-start | bytes 1572872 | tf_op jit(solution)/shard_map/ppermute | solution.py:268
  45.6 0.9 constant_dynamic-update-slice_fusion.6
  46.5 0.6 collective-permute-done.13
  47.3 1.7 %convolution_convert_fusion = bf16[1024,512]{1,0:T(8,128)(2,1)} fusion(bf16[1024,512]{1,0:T(8,128)(2,1)S(1)} %bitcast.123, bf16[512,512]{1,0:T(8,128)(2,1)S(1)} %constant_dynamic-update-slice_fusion.4.v_ref), kind=kOutput, calls=%fused_computation | convolution fusion | flops 537395200 | bytes 2621440 | tf_op jit(solution)/shard_map/dot_general | solution.py:24
  49.0 1.7 %dynamic-slice_bitcast_fusion = (bf16[128,512]{1,0:T(8,128)(2,1)}, bf16[128,512]{1,0:T(8,128)(2,1)S(1)}, bf16[128,512]{1,0:T(8,128)(2,1)S(1)}) fusion(bf16[8,128,512]{2,1,0:T(8,128)(2,1)} %bitcast.17, s32[]{:T(128)S(6)} %select_n.191, s32[]{:T(128)S(6)} %select_n.183, s32[]{:T(128)S(6)} %select_n.181), kind=kLoop, calls=%fused_computation.38 | loop fusion | bytes 786444 | tf_op jit(solution)/shard_map/jit(dynamic_index_in_dim)/squeeze | solution.py:332
  50.7 1.6 collective-permute-start.14
  52.3 10.5 %collective-permute-done.14 = bf16[128,512]{1,0:T(8,128)(2,1)S(1)} collective-permute-done((bf16[128,512]{1,0:T(8,128)(2,1)S(1)}, bf16[128,512]{1,0:T(8,128)(2,1)S(1)}, u32[]{:S(2)}, u32[]{:S(2)}) %collective-permute-start.14) | collective-permute-done | bytes 131104 | tf_op jit(solution)/shard_map/ppermute | solution.py:271
  62.8 0.9 fusion.6
  63.9 2.7 %collective-permute-start.21 = (bf16[128,512]{1,0:T(8,128)(2,1)}, bf16[128,512]{1,0:T(8,128)(2,1)}, u32[]{:S(2)}, u32[]{:S(2)}) collective-permute-start(bf16[128,512]{1,0:T(8,128)(2,1)} %get-tuple-element.99), channel_id=1, source_target_pairs={{0,7},{1,0},{2,1},{3,2},{4,3},{5,4},{6,5},{7,6},{8,15},{9,8},{10,9... | collective-permute-start | bytes 393224 | tf_op jit(solution)/shard_map/ppermute | solution.py:271
  66.5 3.5 %collective-permute-start.18 = (f32[1,128]{1,0:T(1,128)S(1)}, f32[1,128]{1,0:T(1,128)S(1)}, u32[]{:S(2)}, u32[]{:S(2)}) collective-permute-start(f32[1,128]{1,0:T(1,128)S(1)} %get-tuple-element.72), channel_id=1, source_target_pairs={{0,192},{8,200},{16,208},{24,216},{32,224},{40,232},{48,240},{56,2... | collective-permute-start | bytes 1544 | tf_op jit(solution)/shard_map/ppermute | solution.py:262
  70.0 0.6 collective-permute-start.16
  70.7 3.2 %collective-permute-done.17 = f32[1,128]{1,0:T(1,128)S(1)} collective-permute-done((f32[1,128]{1,0:T(1,128)S(1)}, f32[1,128]{1,0:T(1,128)S(1)}, u32[]{:S(2)}, u32[]{:S(2)}) %collective-permute-start.17) | collective-permute-done | bytes 544 | tf_op jit(solution)/shard_map/ppermute | solution.py:262
  74.0 0.7 pad_maximum_fusion.2.flag_ref
  74.7 1.8 %fusion.3 = (bf16[128,512]{1,0:T(8,128)(2,1)}, bf16[128,512]{1,0:T(8,128)(2,1)S(1)}) fusion(bf16[128,512]{1,0:T(8,128)(2,1)} %collective-permute-done.21, bf16[8,128,512]{2,1,0:T(8,128)(2,1)} %bitcast.17, s32[]{:T(128)S(6)} %select_n.193, s32[]{:T(128)S(6)} %select_n.187, bf16[128,512]{1,0:T(8,128)(2,1)S(1)} %collective-permute-done.15), kind=kLoop, calls=%fused_computation.16 | loop fusion | flops 524288 | bytes 786440 | tf_op jit(solution)/shard_map/convert_element_type | solution.py:338
  76.5 1.4 collective-permute-start.19
  77.9 2.6 %collective-permute-done.22 = bf16[128,512]{1,0:T(8,128)(2,1)S(1)} collective-permute-done((bf16[128,512]{1,0:T(8,128)(2,1)}, bf16[128,512]{1,0:T(8,128)(2,1)S(1)}, u32[]{:S(2)}, u32[]{:S(2)}) %collective-permute-start.22) | collective-permute-done | bytes 131104 | tf_op jit(solution)/shard_map/ppermute | solution.py:271
  80.5 1.2 collective-permute-done.19
  81.7 1.1 fusion.2
  83.0 1.4 collective-permute-start.20
  84.3 2.4 %collective-permute-done.23.back_ref = bf16[128,512]{1,0:T(8,128)(2,1)S(1)} collective-permute-done((bf16[128,512]{1,0:T(8,128)(2,1)S(1)}, bf16[128,512]{1,0:T(8,128)(2,1)S(1)}, u32[]{:S(2)}, u32[]{:S(2)}) %collective-permute-start.23) | collective-permute-done | bytes 131104 | tf_op jit(solution)/shard_map/ppermute | solution.py:271
  86.7 1.3 collective-permute-done.20.forward_ref
  88.0 0.9 copy-done
  88.9 1.0 block_softmax.1
  89.9 1.1 cross_statistics.1
  91.0 17.4 %all_to_all.15.stat_ref = f32[8,16,1024]{2,1,0:T(8,128)S(1)} all-to-all(f32[8,16,1024]{2,1,0:T(8,128)S(1)} %broadcast_in_dim.77), channel_id=1, replica_groups={{0,8,16,24,32,40,48,56},{64,72,80,88,96,104,112,120},{128,136,144,152,1..., dimensions={0} | all-to-all | bytes 1048576 | tf_op jit(solution)/shard_map/all_to_all | solution.py:276
  108.5 0.6 broadcast_in_dim.78
  109.1 4.8 %all-to-all-start.1 = ((f32[8,2,128]{2,1,0:T(2,128)}), f32[8,2,128]{2,1,0:T(2,128)S(1)}, u32[]{:S(2)}, u32[]{:S(2)}) async-start(f32[8,2,128]{2,1,0:T(2,128)} %broadcast_in_dim.78), calls=%async_computation.2 | async-start | bytes 16384 | tf_op jit(solution)/shard_map/all_to_all | solution.py:276
  114.0 1.5 cross_grads.1
  115.5 0.7 copy-done.1
  116.2 4.4 %all-to-all-done.1.scale_ref = f32[8,2,128]{2,1,0:T(2,128)S(1)} async-done(((f32[8,2,128]{2,1,0:T(2,128)}), f32[8,2,128]{2,1,0:T(2,128)S(1)}, u32[]{:S(2)}, u32[]{:S(2)}) %all-to-all-start.1) | async-done | bytes 8224 | tf_op jit(solution)/shard_map/all_to_all | solution.py:276
  120.6 7.8 %all-gather.2.cloned.1.call-done.both_ref = bf16[1024,1024]{1,0:T(8,128)(2,1)} async-done(((bf16[128,1024]{1,0:T(8,128)(2,1)}), bf16[1024,1024]{1,0:T(8,128)(2,1)}) %all-gather.2.cloned.1.call-update) | async-done | bytes 2097168 | tf_op jit(solution)/shard_map/all_gather | solution.py:362
  128.4 3.6 %query_grads.1 = (bf16[1024,512]{1,0:T(8,128)(2,1)S(1)}, bf16[1024,512]{1,0:T(8,128)(2,1)S(1)}, f32[512,512]{1,0:T(8,128)S(1)}, bf16[512,512]{1,0:T(8,128)(2,1)S(1)}) custom-call(s32[2]{0:T(128)S(1)} %pad_add_fusion.place_ref, bf16[1024,1024]{1,0:T(8,128)(2,1)} %all-gather.2.cloned.1.call-done.both_ref, f32[8,2,128]{2,1,0:T(2,128)S(1)} %all-to-all-done.1.scale_ref, ...), custom_call_target="tpu_custom_call" | custom-call | tf_op jit(solution)/shard_map/query_grads/pallas_call | solution.py:191
  132.0 4.7 %collective-permute-start.24 = (bf16[512,512]{1,0:T(8,128)(2,1)S(1)}, bf16[512,512]{1,0:T(8,128)(2,1)S(1)}, u32[]{:S(2)}, u32[]{:S(2)}) collective-permute-start(bf16[512,512]{1,0:T(8,128)(2,1)S(1)} %get-tuple-element.85), channel_id=1, source_target_pairs={{0,8},{8,0},{16,24},{24,16},{32,40},{40,32},{48,56},{56,48},{64,72... | collective-permute-start | bytes 1572872 | tf_op jit(solution)/shard_map/ppermute | solution.py:268
  136.7 1.3 key_grads.1
  138.0 2.6 %collective-permute-start.25 = (bf16[128,1024]{1,0:T(8,128)(2,1)S(1)}, bf16[128,1024]{1,0:T(8,128)(2,1)S(1)}, u32[]{:S(2)}, u32[]{:S(2)}) collective-permute-start(bf16[128,1024]{1,0:T(8,128)(2,1)S(1)} %get-tuple-element.90), channel_id=1, source_target_pairs={{0,192},{8,200},{16,208},{24,216},{32,224},{40,232},{48,240},{56,2... | collective-permute-start | bytes 786440 | tf_op jit(solution)/shard_map/ppermute | solution.py:262
  140.5 0.5 collective-permute-start.26
  141.0 0.7 collective-permute-start.27
  141.6 1.0 add_convert_fusion
  142.6 3.7 %all-to-all-start.2 = ((bf16[4,128,512]{2,1,0:T(8,128)(2,1)}), bf16[4,128,512]{2,1,0:T(8,128)(2,1)S(1)}, u32[]{:S(2)}, u32[]{:S(2)}) async-start(bf16[4,128,512]{2,1,0:T(8,128)(2,1)} %bitcast.34), calls=%async_computation.3 | async-start | bytes 1048576 | tf_op jit(solution)/shard_map/all_to_all | solution.py:386
  146.3 5.4 %collective-permute-done.25 = bf16[128,1024]{1,0:T(8,128)(2,1)S(1)} collective-permute-done((bf16[128,1024]{1,0:T(8,128)(2,1)S(1)}, bf16[128,1024]{1,0:T(8,128)(2,1)S(1)}, u32[]{:S(2)}, u32[]{:S(2)}) %collective-permute-start.25) | collective-permute-done | bytes 262176 | tf_op jit(solution)/shard_map/ppermute | solution.py:262
  151.7 4.2 %collective-permute-done.27 = bf16[128,1024]{1,0:T(8,128)(2,1)S(1)} collective-permute-done((bf16[128,1024]{1,0:T(8,128)(2,1)S(1)}, bf16[128,1024]{1,0:T(8,128)(2,1)S(1)}, u32[]{:S(2)}, u32[]{:S(2)}) %collective-permute-start.27) | collective-permute-done | bytes 262176 | tf_op jit(solution)/shard_map/ppermute | solution.py:262
  156.1 0.7 reshape.107
  156.8 0.7 reshape.106
  157.6 0.7 reshape.105
  (76 shorter events, 2.7 us)
Async XLA Ops:
  7.2 80.8 %reduce-scatter.2.cloned.1.call-start = ((), (), s32[]{:S(2)}) async-start(), calls=%async_computation.4 | async-start | bytes 2359296 | tf_op jit(solution)/shard_map/reduce_scatter | solution.py:327
  9.3 8.4 %collective-permute-start = (bf16[128,512]{1,0:T(8,128)(2,1)S(1)}, bf16[128,512]{1,0:T(8,128)(2,1)S(1)}, u32[]{:S(2)}, u32[]{:S(2)}) collective-permute-start(bf16[128,512]{1,0:T(8,128)(2,1)S(1)} %get-tuple-element.52), channel_id=1, source_target_pairs={{0,16},{8,24},{16,32},{24,40},{32,48},{40,56},{48,0},{56,8},{64,80... | collective-permute-start | bytes 393224 | tf_op jit(solution)/shard_map/ppermute | solution.py:265
  11.4 8.6 %collective-permute-start.2 = (bf16[128,512]{1,0:T(8,128)(2,1)S(1)}, bf16[128,512]{1,0:T(8,128)(2,1)S(1)}, u32[]{:S(2)}, u32[]{:S(2)}) collective-permute-start(bf16[128,512]{1,0:T(8,128)(2,1)S(1)} %get-tuple-element.52), channel_id=1, source_target_pairs={{0,48},{8,56},{16,0},{24,8},{32,16},{40,24},{48,32},{56,40},{64,11... | collective-permute-start | bytes 393224 | tf_op jit(solution)/shard_map/ppermute | solution.py:265
  12.8 7.2 %collective-permute-start.1 = (bf16[128,512]{1,0:T(8,128)(2,1)S(1)}, bf16[128,512]{1,0:T(8,128)(2,1)S(1)}, u32[]{:S(2)}, u32[]{:S(2)}) collective-permute-start(bf16[128,512]{1,0:T(8,128)(2,1)S(1)} %get-tuple-element.52), channel_id=1, source_target_pairs={{0,32},{8,40},{16,48},{24,56},{32,0},{40,8},{48,16},{56,24},{64,96... | collective-permute-start | bytes 393224 | tf_op jit(solution)/shard_map/ppermute | solution.py:265
  14.4 5.6 %collective-permute-start.4 = (bf16[128,512]{1,0:T(8,128)(2,1)S(1)}, bf16[128,512]{1,0:T(8,128)(2,1)S(1)}, u32[]{:S(2)}, u32[]{:S(2)}) collective-permute-start(bf16[128,512]{1,0:T(8,128)(2,1)S(1)} %get-tuple-element.58), channel_id=1, source_target_pairs={{0,128},{8,136},{16,144},{24,152},{32,160},{40,168},{48,176},{56,1... | collective-permute-start | bytes 393224 | tf_op jit(solution)/shard_map/ppermute | solution.py:262
  17.3 6.6 %collective-permute-start.3 = (bf16[128,512]{1,0:T(8,128)(2,1)S(1)}, bf16[128,512]{1,0:T(8,128)(2,1)S(1)}, u32[]{:S(2)}, u32[]{:S(2)}) collective-permute-start(bf16[128,512]{1,0:T(8,128)(2,1)S(1)} %get-tuple-element.58), channel_id=1, source_target_pairs={{0,64},{8,72},{16,80},{24,88},{32,96},{40,104},{48,112},{56,120},{... | collective-permute-start | bytes 393224 | tf_op jit(solution)/shard_map/ppermute | solution.py:262
  17.7 6.2 %collective-permute-start.5 = (bf16[128,512]{1,0:T(8,128)(2,1)S(1)}, bf16[128,512]{1,0:T(8,128)(2,1)S(1)}, u32[]{:S(2)}, u32[]{:S(2)}) collective-permute-start(bf16[128,512]{1,0:T(8,128)(2,1)S(1)} %get-tuple-element.58), channel_id=1, source_target_pairs={{0,192},{8,200},{16,208},{24,216},{32,224},{40,232},{48,240},{56,2... | collective-permute-start | bytes 393224 | tf_op jit(solution)/shard_map/ppermute | solution.py:262
  24.0 3.3 %collective-permute-start.6 = (bf16[4,128,512]{2,1,0:T(8,128)(2,1)S(1)}, bf16[4,128,512]{2,1,0:T(8,128)(2,1)S(1)}, u32[]{:S(2)}, u32[]{:S(2)}) collective-permute-start(bf16[4,128,512]{2,1,0:T(8,128)(2,1)S(1)} %bitcast_dynamic-update-slice_fusion.4), channel_id=1, source_target_pairs={{0,8},{8,0},{16,24},{24,16},{32,40},{40,32},{48,56},{56,48},{64,72... | collective-permute-start | bytes 1572872 | tf_op jit(solution)/shard_map/ppermute | solution.py:268
  25.8 3.9 %copy-start.3 = (pred[16,8,4,128]{3,1,2,0:T(8,128)(4,1)}, pred[16,8,4,128]{3,1,2,0:T(8,128)(4,1)S(1)}, u32[]{:S(2)}) copy-start(pred[16,8,4,128]{3,1,2,0:T(8,128)(4,1)S(1)} %copy.31) | copy-start | bytes 196612
  27.6 2.2 %copy-start.6 = (bf16[128,4,128]{2,1,0:T(4,128)(2,1)S(1)}, bf16[128,4,128]{2,1,0:T(4,128)(2,1)}, u32[]{:S(2)}) copy-start(bf16[128,4,128]{2,1,0:T(4,128)(2,1)} %param.8) | copy-start | bytes 393220
  27.6 2.2 %copy-start.7 = (bf16[128,4,128]{2,1,0:T(4,128)(2,1)S(1)}, bf16[128,4,128]{2,1,0:T(4,128)(2,1)}, u32[]{:S(2)}) copy-start(bf16[128,4,128]{2,1,0:T(4,128)(2,1)} %param.9) | copy-start | bytes 393220
  29.7 98.7 %all-gather.2.cloned.1.call-start = ((), (), s32[]{:S(2)}) async-start(), calls=%async_computation.5 | async-start | bytes 2359296 | tf_op jit(solution)/shard_map/all_gather | solution.py:362
  29.8 8.2 %collective-permute-start.12 = (bf16[128,512]{1,0:T(8,128)(2,1)S(1)}, bf16[128,512]{1,0:T(8,128)(2,1)S(1)}, u32[]{:S(2)}, u32[]{:S(2)}) collective-permute-start(bf16[128,512]{1,0:T(8,128)(2,1)S(1)} %get-tuple-element.67), channel_id=1, source_target_pairs={{0,192},{8,200},{16,208},{24,216},{32,224},{40,232},{48,240},{56,2... | collective-permute-start | bytes 393224 | tf_op jit(solution)/shard_map/ppermute | solution.py:262
  32.6 6.0 %collective-permute-start.11 = (bf16[128,512]{1,0:T(8,128)(2,1)S(1)}, bf16[128,512]{1,0:T(8,128)(2,1)S(1)}, u32[]{:S(2)}, u32[]{:S(2)}) collective-permute-start(bf16[128,512]{1,0:T(8,128)(2,1)S(1)} %get-tuple-element.67), channel_id=1, source_target_pairs={{0,128},{8,136},{16,144},{24,152},{32,160},{40,168},{48,176},{56,1... | collective-permute-start | bytes 393224 | tf_op jit(solution)/shard_map/ppermute | solution.py:262
  32.6 9.1 %collective-permute-start.10 = (bf16[128,512]{1,0:T(8,128)(2,1)S(1)}, bf16[128,512]{1,0:T(8,128)(2,1)S(1)}, u32[]{:S(2)}, u32[]{:S(2)}) collective-permute-start(bf16[128,512]{1,0:T(8,128)(2,1)S(1)} %get-tuple-element.67), channel_id=1, source_target_pairs={{0,64},{8,72},{16,80},{24,88},{32,96},{40,104},{48,112},{56,120},{... | collective-permute-start | bytes 393224 | tf_op jit(solution)/shard_map/ppermute | solution.py:262
  33.3 8.5 %collective-permute-start.9 = (bf16[128,512]{1,0:T(8,128)(2,1)S(1)}, bf16[128,512]{1,0:T(8,128)(2,1)S(1)}, u32[]{:S(2)}, u32[]{:S(2)}) collective-permute-start(bf16[128,512]{1,0:T(8,128)(2,1)S(1)} %get-tuple-element.62), channel_id=1, source_target_pairs={{0,48},{8,56},{16,0},{24,8},{32,16},{40,24},{48,32},{56,40},{64,11... | collective-permute-start | bytes 393224 | tf_op jit(solution)/shard_map/ppermute | solution.py:265
  34.2 7.6 %collective-permute-start.8 = (bf16[128,512]{1,0:T(8,128)(2,1)S(1)}, bf16[128,512]{1,0:T(8,128)(2,1)S(1)}, u32[]{:S(2)}, u32[]{:S(2)}) collective-permute-start(bf16[128,512]{1,0:T(8,128)(2,1)S(1)} %get-tuple-element.62), channel_id=1, source_target_pairs={{0,32},{8,40},{16,48},{24,56},{32,0},{40,8},{48,16},{56,24},{64,96... | collective-permute-start | bytes 393224 | tf_op jit(solution)/shard_map/ppermute | solution.py:265
  38.0 5.0 %collective-permute-start.7 = (bf16[128,512]{1,0:T(8,128)(2,1)S(1)}, bf16[128,512]{1,0:T(8,128)(2,1)S(1)}, u32[]{:S(2)}, u32[]{:S(2)}) collective-permute-start(bf16[128,512]{1,0:T(8,128)(2,1)S(1)} %get-tuple-element.62), channel_id=1, source_target_pairs={{0,16},{8,24},{16,32},{24,40},{32,48},{40,56},{48,0},{56,8},{64,80... | collective-permute-start | bytes 393224 | tf_op jit(solution)/shard_map/ppermute | solution.py:265
  41.8 3.8 %copy-start.5 = (bf16[128,512]{1,0:T(8,128)(2,1)}, bf16[128,512]{1,0:T(8,128)(2,1)S(1)}, u32[]{:S(2)}) copy-start(bf16[128,512]{1,0:T(8,128)(2,1)S(1)} %collective-permute-done.10) | copy-start | bytes 393220
  43.2 3.9 %collective-permute-start.13 = (bf16[4,128,512]{2,1,0:T(8,128)(2,1)S(1)}, bf16[4,128,512]{2,1,0:T(8,128)(2,1)S(1)}, u32[]{:S(2)}, u32[]{:S(2)}) collective-permute-start(bf16[4,128,512]{2,1,0:T(8,128)(2,1)S(1)} %bitcast_dynamic-update-slice_fusion), channel_id=1, source_target_pairs={{0,8},{8,0},{16,24},{24,16},{32,40},{40,32},{48,56},{56,48},{64,72... | collective-permute-start | bytes 1572872 | tf_op jit(solution)/shard_map/ppermute | solution.py:268
  50.7 12.1 %collective-permute-start.14 = (bf16[128,512]{1,0:T(8,128)(2,1)S(1)}, bf16[128,512]{1,0:T(8,128)(2,1)S(1)}, u32[]{:S(2)}, u32[]{:S(2)}) collective-permute-start(bf16[128,512]{1,0:T(8,128)(2,1)S(1)} %get-tuple-element.100), channel_id=1, source_target_pairs={{0,1},{1,2},{2,3},{3,4},{4,5},{5,6},{6,7},{7,0},{8,9},{9,10},{10,1... | collective-permute-start | bytes 393224 | tf_op jit(solution)/shard_map/ppermute | solution.py:271
  63.8 10.9 %collective-permute-start.15 = (bf16[128,512]{1,0:T(8,128)(2,1)S(1)}, bf16[128,512]{1,0:T(8,128)(2,1)S(1)}, u32[]{:S(2)}, u32[]{:S(2)}) collective-permute-start(bf16[128,512]{1,0:T(8,128)(2,1)S(1)} %fusion.6), channel_id=1, source_target_pairs={{0,1},{1,2},{2,3},{3,4},{4,5},{5,6},{6,7},{7,0},{8,9},{9,10},{10,1... | collective-permute-start | bytes 393224 | tf_op jit(solution)/shard_map/ppermute | solution.py:271
  63.9 10.8 %collective-permute-start.21 = (bf16[128,512]{1,0:T(8,128)(2,1)}, bf16[128,512]{1,0:T(8,128)(2,1)}, u32[]{:S(2)}, u32[]{:S(2)}) collective-permute-start(bf16[128,512]{1,0:T(8,128)(2,1)} %get-tuple-element.99), channel_id=1, source_target_pairs={{0,7},{1,0},{2,1},{3,2},{4,3},{5,4},{6,5},{7,6},{8,15},{9,8},{10,9... | collective-permute-start | bytes 393224 | tf_op jit(solution)/shard_map/ppermute | solution.py:271
  66.5 4.2 %collective-permute-start.18 = (f32[1,128]{1,0:T(1,128)S(1)}, f32[1,128]{1,0:T(1,128)S(1)}, u32[]{:S(2)}, u32[]{:S(2)}) collective-permute-start(f32[1,128]{1,0:T(1,128)S(1)} %get-tuple-element.72), channel_id=1, source_target_pairs={{0,192},{8,200},{16,208},{24,216},{32,224},{40,232},{48,240},{56,2... | collective-permute-start | bytes 1544 | tf_op jit(solution)/shard_map/ppermute | solution.py:262
  70.0 3.9 %collective-permute-start.17 = (f32[1,128]{1,0:T(1,128)S(1)}, f32[1,128]{1,0:T(1,128)S(1)}, u32[]{:S(2)}, u32[]{:S(2)}) collective-permute-start(f32[1,128]{1,0:T(1,128)S(1)} %get-tuple-element.72), channel_id=1, source_target_pairs={{0,128},{8,136},{16,144},{24,152},{32,160},{40,168},{48,176},{56,1... | collective-permute-start | bytes 1544 | tf_op jit(solution)/shard_map/ppermute | solution.py:262
  70.0 4.0 %collective-permute-start.16 = (f32[1,128]{1,0:T(1,128)S(1)}, f32[1,128]{1,0:T(1,128)}, u32[]{:S(2)}, u32[]{:S(2)}) collective-permute-start(f32[1,128]{1,0:T(1,128)S(1)} %get-tuple-element.72), channel_id=1, source_target_pairs={{0,64},{8,72},{16,80},{24,88},{32,96},{40,104},{48,112},{56,120},{... | collective-permute-start | bytes 1544 | tf_op jit(solution)/shard_map/ppermute | solution.py:262
  76.4 4.0 %collective-permute-start.22 = (bf16[128,512]{1,0:T(8,128)(2,1)}, bf16[128,512]{1,0:T(8,128)(2,1)S(1)}, u32[]{:S(2)}, u32[]{:S(2)}) collective-permute-start(bf16[128,512]{1,0:T(8,128)(2,1)} %get-tuple-element.97), channel_id=1, source_target_pairs={{0,7},{1,0},{2,1},{3,2},{4,3},{5,4},{6,5},{7,6},{8,15},{9,8},{10,9... | collective-permute-start | bytes 393224 | tf_op jit(solution)/shard_map/ppermute | solution.py:271
  76.5 5.1 %collective-permute-start.19 = (bf16[128,512]{1,0:T(8,128)(2,1)S(1)}, bf16[128,512]{1,0:T(8,128)(2,1)}, u32[]{:S(2)}, u32[]{:S(2)}) collective-permute-start(bf16[128,512]{1,0:T(8,128)(2,1)S(1)} %get-tuple-element.98), channel_id=1, source_target_pairs={{0,1},{1,2},{2,3},{3,4},{4,5},{5,6},{6,7},{7,0},{8,9},{9,10},{10,1... | collective-permute-start | bytes 393224 | tf_op jit(solution)/shard_map/ppermute | solution.py:271
  82.8 3.9 %collective-permute-start.23 = (bf16[128,512]{1,0:T(8,128)(2,1)S(1)}, bf16[128,512]{1,0:T(8,128)(2,1)S(1)}, u32[]{:S(2)}, u32[]{:S(2)}) collective-permute-start(bf16[128,512]{1,0:T(8,128)(2,1)S(1)} %get-tuple-element.95), channel_id=1, source_target_pairs={{0,7},{1,0},{2,1},{3,2},{4,3},{5,4},{6,5},{7,6},{8,15},{9,8},{10,9... | collective-permute-start | bytes 393224 | tf_op jit(solution)/shard_map/ppermute | solution.py:271
  83.0 5.0 %collective-permute-start.20 = (bf16[128,512]{1,0:T(8,128)(2,1)S(1)}, bf16[128,512]{1,0:T(8,128)(2,1)S(1)}, u32[]{:S(2)}, u32[]{:S(2)}) collective-permute-start(bf16[128,512]{1,0:T(8,128)(2,1)S(1)} %get-tuple-element.96), channel_id=1, source_target_pairs={{0,1},{1,2},{2,3},{3,4},{4,5},{5,6},{6,7},{7,0},{8,9},{9,10},{10,1... | collective-permute-start | bytes 393224 | tf_op jit(solution)/shard_map/ppermute | solution.py:271
  88.0 1.0 copy-start
  109.1 11.5 %all-to-all-start.1 = ((f32[8,2,128]{2,1,0:T(2,128)}), f32[8,2,128]{2,1,0:T(2,128)S(1)}, u32[]{:S(2)}, u32[]{:S(2)}) async-start(f32[8,2,128]{2,1,0:T(2,128)} %broadcast_in_dim.78), calls=%async_computation.2 | async-start | bytes 16384 | tf_op jit(solution)/shard_map/all_to_all | solution.py:276
  115.5 0.7 copy-start.1
  120.6 16.1 %copy-start.2 = (f32[32,1024]{1,0:T(8,128)S(1)}, f32[32,1024]{1,0:T(8,128)}, u32[]{:S(2)}) copy-start(f32[32,1024]{1,0:T(8,128)} %copy-done.1) | copy-start | bytes 393220
  132.0 9.6 %collective-permute-start.24 = (bf16[512,512]{1,0:T(8,128)(2,1)S(1)}, bf16[512,512]{1,0:T(8,128)(2,1)S(1)}, u32[]{:S(2)}, u32[]{:S(2)}) collective-permute-start(bf16[512,512]{1,0:T(8,128)(2,1)S(1)} %get-tuple-element.85), channel_id=1, source_target_pairs={{0,8},{8,0},{16,24},{24,16},{32,40},{40,32},{48,56},{56,48},{64,72... | collective-permute-start | bytes 1572872 | tf_op jit(solution)/shard_map/ppermute | solution.py:268
  138.0 13.7 %collective-permute-start.25 = (bf16[128,1024]{1,0:T(8,128)(2,1)S(1)}, bf16[128,1024]{1,0:T(8,128)(2,1)S(1)}, u32[]{:S(2)}, u32[]{:S(2)}) collective-permute-start(bf16[128,1024]{1,0:T(8,128)(2,1)S(1)} %get-tuple-element.90), channel_id=1, source_target_pairs={{0,192},{8,200},{16,208},{24,216},{32,224},{40,232},{48,240},{56,2... | collective-permute-start | bytes 786440 | tf_op jit(solution)/shard_map/ppermute | solution.py:262
  140.5 11.2 %collective-permute-start.26 = (bf16[128,1024]{1,0:T(8,128)(2,1)S(1)}, bf16[128,1024]{1,0:T(8,128)(2,1)S(1)}, u32[]{:S(2)}, u32[]{:S(2)}) collective-permute-start(bf16[128,1024]{1,0:T(8,128)(2,1)S(1)} %get-tuple-element.91), channel_id=1, source_target_pairs={{0,128},{8,136},{16,144},{24,152},{32,160},{40,168},{48,176},{56,1... | collective-permute-start | bytes 786440 | tf_op jit(solution)/shard_map/ppermute | solution.py:262
  141.0 14.9 %collective-permute-start.27 = (bf16[128,1024]{1,0:T(8,128)(2,1)S(1)}, bf16[128,1024]{1,0:T(8,128)(2,1)S(1)}, u32[]{:S(2)}, u32[]{:S(2)}) collective-permute-start(bf16[128,1024]{1,0:T(8,128)(2,1)S(1)} %get-tuple-element.92), channel_id=1, source_target_pairs={{0,64},{8,72},{16,80},{24,88},{32,96},{40,104},{48,112},{56,120},{... | collective-permute-start | bytes 786440 | tf_op jit(solution)/shard_map/ppermute | solution.py:262
  141.6 14.4 %copy-start.4 = (pred[16,8,4,128]{3,1,2,0:T(8,128)(4,1)S(1)}, pred[16,8,4,128]{3,1,2,0:T(8,128)(4,1)}, u32[]{:S(2)}) copy-start(pred[16,8,4,128]{3,1,2,0:T(8,128)(4,1)} %copy-done.3) | copy-start | bytes 196612
  142.6 14.9 %all-to-all-start.2 = ((bf16[4,128,512]{2,1,0:T(8,128)(2,1)}), bf16[4,128,512]{2,1,0:T(8,128)(2,1)S(1)}, u32[]{:S(2)}, u32[]{:S(2)}) async-start(bf16[4,128,512]{2,1,0:T(8,128)(2,1)} %bitcast.34), calls=%async_computation.3 | async-start | bytes 1048576 | tf_op jit(solution)/shard_map/all_to_all | solution.py:386
Sparse Core Ops, SparseCore 0:
  29.8 42.6 reduce-scatter.1
  90.0 38.3 all-gather.1

commit v13 on v10

--- a/solution.py
+++ b/solution.py
@@ -122,13 +122,18 @@
 def block_softmax(logit_scale, logit_sum, own, forward, back, key_flags):
     rows, width = logit_sum.shape
 
-    def kernel(logit_ref, own_ref, forward_ref, back_ref, flag_ref, both_ref, stat_ref):
+    def kernel(
+        logit_ref, own_ref, forward_ref, back_ref, flag_ref, both_ref, stat_ref, held_ref, sem
+    ):
+        copy = pltpu.make_async_copy(logit_ref, held_ref, sem)
+        copy.start()
         dprob = (
             own_ref[...].astype(jnp.float32)
             + forward_ref[...].astype(jnp.float32)
             + back_ref[...].astype(jnp.float32)
         )
-        logits = jnp.where(flag_ref[...] > 0, logit_ref[...] * logit_scale, -1e30)
+        copy.wait()
+        logits = jnp.where(flag_ref[...] > 0, held_ref[...] * logit_scale, -1e30)
         peak = jnp.max(logits, axis=1, keepdims=True)
         lifted = jnp.exp(logits - peak)
         total = jnp.sum(lifted, axis=1, keepdims=True)
@@ -146,9 +151,13 @@
             jax.ShapeDtypeStruct((rows, 2 * width), jnp.bfloat16),
             jax.ShapeDtypeStruct((8, rows), jnp.float32),
         ),
+        in_specs=[pl.BlockSpec(memory_space=pltpu.HBM)] + [WHOLE] * 4,
+        scratch_shapes=[pltpu.VMEM((rows, width), jnp.float32), pltpu.SemaphoreType.DMA],
         compiler_params=ROOM,
         name="block_softmax",
-    )(logit_sum, own, forward, back, key_flags)
+    )(
+        pltpu.with_memory_space_constraint(logit_sum, pltpu.HBM), own, forward, back, key_flags
+    )
 
 
 def query_grads(logit_scale, place, both, scaling, k_blk, cross_dl, sums, chunks):
@@ -278,8 +287,8 @@
             copies, axis, split_axis=0, concat_axis=0, tiled=True, axis_index_groups=groups
         )
 
-    column_ids = own_z * cols_dev + jnp.arange(cols_dev, dtype=jnp.int32)
-    cell_keep = (row_keep[:, None] == 1) & (column_ids[None, :] < row_lengths[:, None])
+    own_columns = jnp.where(row_keep == 1, row_lengths, 0) - own_z * cols_dev
+    cell_keep = jnp.arange(cols_dev, dtype=jnp.int32)[None, :] < own_columns[:, None]
     keep_flat = jnp.broadcast_to(cell_keep[:, :, None], queries.shape).reshape(
         rows_dev, flat_width
     )
@@ -386,8 +395,6 @@
         return sum(p.astype(jnp.float32) for p in parts)
 
     grad_q = added([line[x] for x in range(XS)])
-    grad_kv = added([key_parts[0]] + key_moved)
-
     def finished(rows):
         return (
             jnp.where(keep_flat, rows, 0.0)
@@ -395,11 +402,9 @@
             .reshape(rows_dev, cols_dev, feature)
         )
 
-    return (
-        finished(grad_q),
-        finished(grad_kv[:, :flat_width]),
-        finished(grad_kv[:, flat_width:]),
-    )
+    grad_q = finished(grad_q)
+    grad_kv = added([key_parts[0]] + key_moved)
+    return (grad_q, finished(grad_kv[:, :flat_width]), finished(grad_kv[:, flat_width:]))
 
 
 def solution(mesh):

time: 164 us -> 163 us (level)
  no operation moved by 1% of the time
where the time goes in v13:
time: 163 us
  waiting for transfers between devices  57.4 us (35%)
  starting transfers between devices  45.4 us (28%)
  blocking collectives  16.5 us (10%)
  between operations  14.5 us (9%)
  Pallas kernels  9.37 us (6%)
  local copies, waits for them, and re-layouts  8.92 us (5%)
  other arithmetic  7.61 us (5%)
  matrix products  2.81 us (2%)
    ppermute x7, waiting for transfers between devices, shift_z(): return lax.ppermute(table, 'col', [(z, (z + step) % zs) for z in range(zs)])  21.6 us
    all_to_all x1, blocking collectives, share(): lax.all_to_all(copies, axis, split_axis=0, concat_axis=0, tiled=True, axi...  16.5 us
    ppermute x9, waiting for transfers between devices, shift_y(): lax.ppermute(table, 'row', [(at(y, x, c), at(y + step, x, c)) for y, x, c...  13.4 us
    ppermute x9, starting transfers between devices, shift_y(): lax.ppermute(table, 'row', [(at(y, x, c), at(y + step, x, c)) for y, x, c...  12.5 us
    all_gather x1, waiting for transfers between devices, shards(): both = lax.all_gather(both, 'col', axis=0, tiled=True)  9.17 us
    ppermute x7, starting transfers between devices, shift_z(): return lax.ppermute(table, 'col', [(z, (z + step) % zs) for z in range(zs)])  8.66 us
    ppermute x6, starting transfers between devices, shift_x(): lax.ppermute(table, 'row', [(at(y, x, c), at(y, x + step, c)) for y, x, c...  7.62 us
    ppermute x6, waiting for transfers between devices, shift_x(): lax.ppermute(table, 'row', [(at(y, x, c), at(y, x + step, c)) for y, x, c...  7.42 us
  transfers between devices with their start and end apart: 29, of which 15 were waited for; matrix products, arithmetic and copies ran while one was open for 8% of the time, Pallas kernels for 2%

profile of v13, /device:TPU:1, one launch (start us, length us, event | category | flops | bytes accessed | tf_op | source)
XLA Modules:
  0.0 162.5 jit_solution(11171034445096827281)
XLA Ops:
  7.2 0.7 convert_bitcast_fusion
  8.0 0.2 broadcast_in_dim.69
  8.3 1.0 bitcast_select_fusion.3
  9.3 2.1 %collective-permute-start = (bf16[128,512]{1,0:T(8,128)(2,1)S(1)}, bf16[128,512]{1,0:T(8,128)(2,1)S(1)}, u32[]{:S(2)}, u32[]{:S(2)}) collective-permute-start(bf16[128,512]{1,0:T(8,128)(2,1)S(1)} %get-tuple-element.48), channel_id=1, source_target_pairs={{0,16},{8,24},{16,32},{24,40},{32,48},{40,56},{48,0},{56,8},{64,80... | collective-permute-start | bytes 393224 | tf_op jit(solution)/shard_map/ppermute | solution.py:275
  11.4 1.4 collective-permute-start.2
  12.8 1.6 %collective-permute-start.1 = (bf16[128,512]{1,0:T(8,128)(2,1)S(1)}, bf16[128,512]{1,0:T(8,128)(2,1)S(1)}, u32[]{:S(2)}, u32[]{:S(2)}) collective-permute-start(bf16[128,512]{1,0:T(8,128)(2,1)S(1)} %get-tuple-element.48), channel_id=1, source_target_pairs={{0,32},{8,40},{16,48},{24,56},{32,0},{40,8},{48,16},{56,24},{64,96... | collective-permute-start | bytes 393224 | tf_op jit(solution)/shard_map/ppermute | solution.py:275
  14.4 2.9 %collective-permute-start.4 = (bf16[128,512]{1,0:T(8,128)(2,1)S(1)}, bf16[128,512]{1,0:T(8,128)(2,1)S(1)}, u32[]{:S(2)}, u32[]{:S(2)}) collective-permute-start(bf16[128,512]{1,0:T(8,128)(2,1)S(1)} %get-tuple-element.54), channel_id=1, source_target_pairs={{0,128},{8,136},{16,144},{24,152},{32,160},{40,168},{48,176},{56,1... | collective-permute-start | bytes 393224 | tf_op jit(solution)/shard_map/ppermute | solution.py:272
  17.3 0.4 collective-permute-start.3
  17.7 2.3 %collective-permute-start.5 = (bf16[128,512]{1,0:T(8,128)(2,1)S(1)}, bf16[128,512]{1,0:T(8,128)(2,1)S(1)}, u32[]{:S(2)}, u32[]{:S(2)}) collective-permute-start(bf16[128,512]{1,0:T(8,128)(2,1)S(1)} %get-tuple-element.54), channel_id=1, source_target_pairs={{0,192},{8,200},{16,208},{24,216},{32,224},{40,232},{48,240},{56,2... | collective-permute-start | bytes 393224 | tf_op jit(solution)/shard_map/ppermute | solution.py:272
  20.0 3.9 %collective-permute-done.3 = bf16[128,512]{1,0:T(8,128)(2,1)S(1)} collective-permute-done((bf16[128,512]{1,0:T(8,128)(2,1)S(1)}, bf16[128,512]{1,0:T(8,128)(2,1)S(1)}, u32[]{:S(2)}, u32[]{:S(2)}) %collective-permute-start.3) | collective-permute-done | bytes 131104 | tf_op jit(solution)/shard_map/ppermute | solution.py:272
  24.0 1.7 %collective-permute-start.6 = (bf16[4,128,512]{2,1,0:T(8,128)(2,1)S(1)}, bf16[4,128,512]{2,1,0:T(8,128)(2,1)S(1)}, u32[]{:S(2)}, u32[]{:S(2)}) collective-permute-start(bf16[4,128,512]{2,1,0:T(8,128)(2,1)S(1)} %bitcast_dynamic-update-slice_fusion.4), channel_id=1, source_target_pairs={{0,8},{8,0},{16,24},{24,16},{32,40},{40,32},{48,56},{56,48},{64,72... | collective-permute-start | bytes 1572872 | tf_op jit(solution)/shard_map/ppermute | solution.py:278
  25.9 1.4 collective-permute-done.6
  27.6 2.1 %fusion.18 = f32[1024,512]{1,0:T(8,128)} fusion(bf16[1024,512]{1,0:T(8,128)(2,1)S(1)} %bitcast.126, bf16[512,512]{1,0:T(8,128)(2,1)S(1)} %constant_dynamic-update-slice_fusion.k_ref), kind=kOutput, calls=%fused_computation.75 | convolution fusion | flops 536870912 | bytes 3670016 | tf_op jit(solution)/shard_map/dot_general | solution.py:25
  29.8 1.1 collective-permute-start.9
  30.9 2.7 %collective-permute-start.12 = (bf16[144,512]{1,0:T(8,128)(2,1)S(1)}, bf16[144,512]{1,0:T(8,128)(2,1)}, u32[]{:S(2)}, u32[]{:S(2)}) collective-permute-start(bf16[144,512]{1,0:T(8,128)(2,1)S(1)} %fusion.9), channel_id=1, source_target_pairs={{0,192},{8,200},{16,208},{24,216},{32,224},{40,232},{48,240},{56,2... | collective-permute-start | bytes 442376 | tf_op jit(solution)/shard_map/ppermute | solution.py:272
  33.6 0.7 collective-permute-start.10
  34.3 1.2 collective-permute-start.8
  35.7 4.3 %collective-permute-done.8 = bf16[128,512]{1,0:T(8,128)(2,1)S(1)} collective-permute-done((bf16[128,512]{1,0:T(8,128)(2,1)S(1)}, bf16[128,512]{1,0:T(8,128)(2,1)S(1)}, u32[]{:S(2)}, u32[]{:S(2)}) %collective-permute-start.8) | collective-permute-done | bytes 131104 | tf_op jit(solution)/shard_map/ppermute | solution.py:275
  40.0 3.1 %collective-permute-done.7 = bf16[128,512]{1,0:T(8,128)(2,1)S(1)} collective-permute-done((bf16[128,512]{1,0:T(8,128)(2,1)S(1)}, bf16[128,512]{1,0:T(8,128)(2,1)S(1)}, u32[]{:S(2)}, u32[]{:S(2)}) %collective-permute-start.7) | collective-permute-done | bytes 131104 | tf_op jit(solution)/shard_map/ppermute | solution.py:275
  43.1 0.3 collective-permute-done.10
  43.5 1.2 collective-permute-start.13
  44.8 0.9 slice.63
  45.7 0.9 slice.64
  46.8 0.7 convolution_convert_fusion
  47.6 1.0 copy-done.2
  48.6 0.7 dynamic-slice_bitcast_fusion
  49.3 1.6 %collective-permute-start.14 = (bf16[128,512]{1,0:T(8,128)(2,1)}, bf16[128,512]{1,0:T(8,128)(2,1)}, u32[]{:S(2)}, u32[]{:S(2)}) collective-permute-start(bf16[128,512]{1,0:T(8,128)(2,1)} %get-tuple-element.92), channel_id=1, source_target_pairs={{0,1},{1,2},{2,3},{3,4},{4,5},{5,6},{6,7},{7,0},{8,9},{9,10},{10,1... | collective-permute-start | bytes 393224 | tf_op jit(solution)/shard_map/ppermute | solution.py:281
  50.9 3.9 %collective-permute-start.18 = (bf16[128,512]{1,0:T(8,128)(2,1)}, bf16[128,512]{1,0:T(8,128)(2,1)}, u32[]{:S(2)}, u32[]{:S(2)}) collective-permute-start(bf16[128,512]{1,0:T(8,128)(2,1)} %get-tuple-element.91), channel_id=1, source_target_pairs={{0,7},{1,0},{2,1},{3,2},{4,3},{5,4},{6,5},{7,6},{8,15},{9,8},{10,9... | collective-permute-start | bytes 393224 | tf_op jit(solution)/shard_map/ppermute | solution.py:281
  54.9 6.7 %collective-permute-done.14 = bf16[128,512]{1,0:T(8,128)(2,1)} collective-permute-done((bf16[128,512]{1,0:T(8,128)(2,1)}, bf16[128,512]{1,0:T(8,128)(2,1)}, u32[]{:S(2)}, u32[]{:S(2)}) %collective-permute-start.14) | collective-permute-done | bytes 131104 | tf_op jit(solution)/shard_map/ppermute | solution.py:281
  61.6 1.7 %fusion.7 = bf16[128,512]{1,0:T(8,128)(2,1)} fusion(bf16[128,512]{1,0:T(8,128)(2,1)} %collective-permute-done.14, bf16[8,128,512]{2,1,0:T(8,128)(2,1)} %bitcast.135, s32[]{:T(128)S(6)} %select_n.185), kind=kLoop, calls=%fused_computation.25 | loop fusion | flops 262144 | bytes 393220 | tf_op jit(solution)/shard_map/convert_element_type | solution.py:357
  63.3 8.9 %collective-permute-done.15 = bf16[128,512]{1,0:T(8,128)(2,1)} collective-permute-done((bf16[128,512]{1,0:T(8,128)(2,1)}, bf16[128,512]{1,0:T(8,128)(2,1)}, u32[]{:S(2)}, u32[]{:S(2)}) %collective-permute-start.15) | collective-permute-done | bytes 131104 | tf_op jit(solution)/shard_map/ppermute | solution.py:281
  72.1 1.2 fusion.4
  73.3 0.2 collective-permute-start.19
  73.5 1.3 collective-permute-start.16
  74.9 0.7 slice_bitcast_fusion.4
  75.5 1.7 %collective-permute-done.19 = bf16[128,512]{1,0:T(8,128)(2,1)S(1)} collective-permute-done((bf16[128,512]{1,0:T(8,128)(2,1)S(1)}, bf16[128,512]{1,0:T(8,128)(2,1)S(1)}, u32[]{:S(2)}, u32[]{:S(2)}) %collective-permute-start.19) | collective-permute-done | bytes 131104 | tf_op jit(solution)/shard_map/ppermute | solution.py:281
  77.2 1.3 collective-permute-done.16
  78.6 1.0 fusion.3
  79.7 1.5 collective-permute-start.17
  81.1 0.7 slice_bitcast_fusion.2
  81.8 1.6 %collective-permute-done.20.back_ref = bf16[128,512]{1,0:T(8,128)(2,1)S(1)} collective-permute-done((bf16[128,512]{1,0:T(8,128)(2,1)S(1)}, bf16[128,512]{1,0:T(8,128)(2,1)S(1)}, u32[]{:S(2)}, u32[]{:S(2)}) %collective-permute-start.20) | collective-permute-done | bytes 131104 | tf_op jit(solution)/shard_map/ppermute | solution.py:281
  83.5 1.3 collective-permute-done.17.forward_ref
  84.8 1.9 %block_softmax.1 = (bf16[128,1024]{1,0:T(8,128)(2,1)}, f32[8,128]{1,0:T(8,128)S(1)}) custom-call(f32[128,512]{1,0:T(8,128)} %reduce-scatter.2.cloned.1.call-done.logit_ref, bf16[128,512]{1,0:T(8,128)(2,1)S(1)} %get-tuple-element.93.own_ref, bf16[128,512]{1,0:T(8,128)(2,1)S(1)} %collective-permute-done.17.forward_ref, ...), custom_call_target="tpu_custom_call" | custom-call | tf_op jit(solution)/shard_map/block_softmax/pallas_call | solution.py:148
  86.8 1.1 cross_statistics.1
  87.9 16.5 %all_to_all.15.stat_ref = f32[8,16,1024]{2,1,0:T(8,128)S(1)} all-to-all(f32[8,16,1024]{2,1,0:T(8,128)S(1)} %broadcast_in_dim.81), channel_id=1, replica_groups={{0,8,16,24,32,40,48,56},{64,72,80,88,96,104,112,120},{128,136,144,152,1..., dimensions={0} | all-to-all | bytes 1048576 | tf_op jit(solution)/shard_map/all_to_all | solution.py:286
  104.5 0.6 broadcast_in_dim.82
  105.1 5.2 %all-to-all-start.1 = ((f32[8,2,128]{2,1,0:T(2,128)}), f32[8,2,128]{2,1,0:T(2,128)S(1)}, u32[]{:S(2)}, u32[]{:S(2)}) async-start(f32[8,2,128]{2,1,0:T(2,128)} %broadcast_in_dim.82), calls=%async_computation.2 | async-start | bytes 16384 | tf_op jit(solution)/shard_map/all_to_all | solution.py:286
  110.4 1.5 cross_grads.1
  111.9 0.7 copy-done
  112.6 4.4 %all-to-all-done.1.scale_ref = f32[8,2,128]{2,1,0:T(2,128)S(1)} async-done(((f32[8,2,128]{2,1,0:T(2,128)}), f32[8,2,128]{2,1,0:T(2,128)S(1)}, u32[]{:S(2)}, u32[]{:S(2)}) %all-to-all-start.1) | async-done | bytes 8224 | tf_op jit(solution)/shard_map/all_to_all | solution.py:286
  117.0 9.2 %all-gather.2.cloned.1.call-done.both_ref = bf16[1024,1024]{1,0:T(8,128)(2,1)} async-done(((bf16[128,1024]{1,0:T(8,128)(2,1)}), bf16[1024,1024]{1,0:T(8,128)(2,1)}) %all-gather.2.cloned.1.call-update) | async-done | bytes 2097168 | tf_op jit(solution)/shard_map/all_gather | solution.py:366
  126.1 3.6 %query_grads.1 = (bf16[1024,512]{1,0:T(8,128)(2,1)S(1)}, bf16[1024,512]{1,0:T(8,128)(2,1)S(1)}, f32[512,512]{1,0:T(8,128)S(1)}, bf16[512,512]{1,0:T(8,128)(2,1)S(1)}) custom-call(s32[2]{0:T(128)S(1)} %pad_add_fusion.place_ref, bf16[1024,1024]{1,0:T(8,128)(2,1)} %all-gather.2.cloned.1.call-done.both_ref, f32[8,2,128]{2,1,0:T(2,128)S(1)} %all-to-all-done.1.scale_ref, ...), custom_call_target="tpu_custom_call" | custom-call | tf_op jit(solution)/shard_map/query_grads/pallas_call | solution.py:201
  129.7 4.5 %collective-permute-start.21 = (bf16[512,512]{1,0:T(8,128)(2,1)S(1)}, bf16[512,512]{1,0:T(8,128)(2,1)S(1)}, u32[]{:S(2)}, u32[]{:S(2)}) collective-permute-start(bf16[512,512]{1,0:T(8,128)(2,1)S(1)} %get-tuple-element.77), channel_id=1, source_target_pairs={{0,8},{8,0},{16,24},{24,16},{32,40},{40,32},{48,56},{56,48},{64,72... | collective-permute-start | bytes 1572872 | tf_op jit(solution)/shard_map/ppermute | solution.py:278
  134.2 1.3 key_grads.1
  135.5 2.4 %collective-permute-start.22 = (bf16[128,1024]{1,0:T(8,128)(2,1)S(1)}, bf16[128,1024]{1,0:T(8,128)(2,1)S(1)}, u32[]{:S(2)}, u32[]{:S(2)}) collective-permute-start(bf16[128,1024]{1,0:T(8,128)(2,1)S(1)} %get-tuple-element.82), channel_id=1, source_target_pairs={{0,192},{8,200},{16,208},{24,216},{32,224},{40,232},{48,240},{56,2... | collective-permute-start | bytes 786440 | tf_op jit(solution)/shard_map/ppermute | solution.py:272
  137.9 0.9 collective-permute-start.23
  138.8 0.3 collective-permute-start.24
  139.0 1.0 add_convert_fusion
  140.0 4.0 %all-to-all-start.2 = ((bf16[4,128,512]{2,1,0:T(8,128)(2,1)}), bf16[4,128,512]{2,1,0:T(8,128)(2,1)S(1)}, u32[]{:S(2)}, u32[]{:S(2)}) async-start(bf16[4,128,512]{2,1,0:T(8,128)(2,1)} %bitcast.38), calls=%async_computation.3 | async-start | bytes 1048576 | tf_op jit(solution)/shard_map/all_to_all | solution.py:390
  144.0 5.1 %collective-permute-done.22 = bf16[128,1024]{1,0:T(8,128)(2,1)S(1)} collective-permute-done((bf16[128,1024]{1,0:T(8,128)(2,1)S(1)}, bf16[128,1024]{1,0:T(8,128)(2,1)S(1)}, u32[]{:S(2)}, u32[]{:S(2)}) %collective-permute-start.22) | collective-permute-done | bytes 262176 | tf_op jit(solution)/shard_map/ppermute | solution.py:272
  149.1 4.2 %collective-permute-done.24 = bf16[128,1024]{1,0:T(8,128)(2,1)S(1)} collective-permute-done((bf16[128,1024]{1,0:T(8,128)(2,1)S(1)}, bf16[128,1024]{1,0:T(8,128)(2,1)S(1)}, u32[]{:S(2)}, u32[]{:S(2)}) %collective-permute-start.24) | collective-permute-done | bytes 262176 | tf_op jit(solution)/shard_map/ppermute | solution.py:272
  153.5 0.7 reshape.107
  154.2 0.7 reshape.106
  155.0 0.7 reshape.105
  (75 shorter events, 1.9 us)
Async XLA Ops:
  7.2 77.6 %reduce-scatter.2.cloned.1.call-start = ((), (), s32[]{:S(2)}) async-start(), calls=%async_computation.4 | async-start | bytes 2359296 | tf_op jit(solution)/shard_map/reduce_scatter | solution.py:343
  9.3 8.4 %collective-permute-start = (bf16[128,512]{1,0:T(8,128)(2,1)S(1)}, bf16[128,512]{1,0:T(8,128)(2,1)S(1)}, u32[]{:S(2)}, u32[]{:S(2)}) collective-permute-start(bf16[128,512]{1,0:T(8,128)(2,1)S(1)} %get-tuple-element.48), channel_id=1, source_target_pairs={{0,16},{8,24},{16,32},{24,40},{32,48},{40,56},{48,0},{56,8},{64,80... | collective-permute-start | bytes 393224 | tf_op jit(solution)/shard_map/ppermute | solution.py:275
  11.4 8.6 %collective-permute-start.2 = (bf16[128,512]{1,0:T(8,128)(2,1)S(1)}, bf16[128,512]{1,0:T(8,128)(2,1)S(1)}, u32[]{:S(2)}, u32[]{:S(2)}) collective-permute-start(bf16[128,512]{1,0:T(8,128)(2,1)S(1)} %get-tuple-element.48), channel_id=1, source_target_pairs={{0,48},{8,56},{16,0},{24,8},{32,16},{40,24},{48,32},{56,40},{64,11... | collective-permute-start | bytes 393224 | tf_op jit(solution)/shard_map/ppermute | solution.py:275
  12.8 7.2 %collective-permute-start.1 = (bf16[128,512]{1,0:T(8,128)(2,1)S(1)}, bf16[128,512]{1,0:T(8,128)(2,1)S(1)}, u32[]{:S(2)}, u32[]{:S(2)}) collective-permute-start(bf16[128,512]{1,0:T(8,128)(2,1)S(1)} %get-tuple-element.48), channel_id=1, source_target_pairs={{0,32},{8,40},{16,48},{24,56},{32,0},{40,8},{48,16},{56,24},{64,96... | collective-permute-start | bytes 393224 | tf_op jit(solution)/shard_map/ppermute | solution.py:275
  14.4 5.6 %collective-permute-start.4 = (bf16[128,512]{1,0:T(8,128)(2,1)S(1)}, bf16[128,512]{1,0:T(8,128)(2,1)S(1)}, u32[]{:S(2)}, u32[]{:S(2)}) collective-permute-start(bf16[128,512]{1,0:T(8,128)(2,1)S(1)} %get-tuple-element.54), channel_id=1, source_target_pairs={{0,128},{8,136},{16,144},{24,152},{32,160},{40,168},{48,176},{56,1... | collective-permute-start | bytes 393224 | tf_op jit(solution)/shard_map/ppermute | solution.py:272
  17.3 6.6 %collective-permute-start.3 = (bf16[128,512]{1,0:T(8,128)(2,1)S(1)}, bf16[128,512]{1,0:T(8,128)(2,1)S(1)}, u32[]{:S(2)}, u32[]{:S(2)}) collective-permute-start(bf16[128,512]{1,0:T(8,128)(2,1)S(1)} %get-tuple-element.54), channel_id=1, source_target_pairs={{0,64},{8,72},{16,80},{24,88},{32,96},{40,104},{48,112},{56,120},{... | collective-permute-start | bytes 393224 | tf_op jit(solution)/shard_map/ppermute | solution.py:272
  17.7 6.2 %collective-permute-start.5 = (bf16[128,512]{1,0:T(8,128)(2,1)S(1)}, bf16[128,512]{1,0:T(8,128)(2,1)S(1)}, u32[]{:S(2)}, u32[]{:S(2)}) collective-permute-start(bf16[128,512]{1,0:T(8,128)(2,1)S(1)} %get-tuple-element.54), channel_id=1, source_target_pairs={{0,192},{8,200},{16,208},{24,216},{32,224},{40,232},{48,240},{56,2... | collective-permute-start | bytes 393224 | tf_op jit(solution)/shard_map/ppermute | solution.py:272
  24.0 3.3 %collective-permute-start.6 = (bf16[4,128,512]{2,1,0:T(8,128)(2,1)S(1)}, bf16[4,128,512]{2,1,0:T(8,128)(2,1)S(1)}, u32[]{:S(2)}, u32[]{:S(2)}) collective-permute-start(bf16[4,128,512]{2,1,0:T(8,128)(2,1)S(1)} %bitcast_dynamic-update-slice_fusion.4), channel_id=1, source_target_pairs={{0,8},{8,0},{16,24},{24,16},{32,40},{40,32},{48,56},{56,48},{64,72... | collective-permute-start | bytes 1572872 | tf_op jit(solution)/shard_map/ppermute | solution.py:278
  25.8 4.0 %copy-start.3 = (pred[16,8,4,128]{3,1,2,0:T(8,128)(4,1)}, pred[16,8,4,128]{3,1,2,0:T(8,128)(4,1)S(1)}, u32[]{:S(2)}) copy-start(pred[16,8,4,128]{3,1,2,0:T(8,128)(4,1)S(1)} %copy.31) | copy-start | bytes 196612
  27.6 2.2 %copy-start.5 = (bf16[128,4,128]{2,1,0:T(4,128)(2,1)S(1)}, bf16[128,4,128]{2,1,0:T(4,128)(2,1)}, u32[]{:S(2)}) copy-start(bf16[128,4,128]{2,1,0:T(4,128)(2,1)} %param.8) | copy-start | bytes 393220
  27.6 2.2 %copy-start.6 = (bf16[128,4,128]{2,1,0:T(4,128)(2,1)S(1)}, bf16[128,4,128]{2,1,0:T(4,128)(2,1)}, u32[]{:S(2)}) copy-start(bf16[128,4,128]{2,1,0:T(4,128)(2,1)} %param.9) | copy-start | bytes 393220
  29.7 96.4 %all-gather.2.cloned.1.call-start = ((), (), s32[]{:S(2)}) async-start(), calls=%async_computation.5 | async-start | bytes 2359296 | tf_op jit(solution)/shard_map/all_gather | solution.py:366
  29.8 5.7 %collective-permute-start.9 = (bf16[128,512]{1,0:T(8,128)(2,1)S(1)}, bf16[128,512]{1,0:T(8,128)(2,1)S(1)}, u32[]{:S(2)}, u32[]{:S(2)}) collective-permute-start(bf16[128,512]{1,0:T(8,128)(2,1)S(1)} %get-tuple-element.58), channel_id=1, source_target_pairs={{0,48},{8,56},{16,0},{24,8},{32,16},{40,24},{48,32},{56,40},{64,11... | collective-permute-start | bytes 393224 | tf_op jit(solution)/shard_map/ppermute | solution.py:275
  30.9 12.2 %collective-permute-start.12 = (bf16[144,512]{1,0:T(8,128)(2,1)S(1)}, bf16[144,512]{1,0:T(8,128)(2,1)}, u32[]{:S(2)}, u32[]{:S(2)}) collective-permute-start(bf16[144,512]{1,0:T(8,128)(2,1)S(1)} %fusion.9), channel_id=1, source_target_pairs={{0,192},{8,200},{16,208},{24,216},{32,224},{40,232},{48,240},{56,2... | collective-permute-start | bytes 442376 | tf_op jit(solution)/shard_map/ppermute | solution.py:272
  33.6 9.5 %collective-permute-start.11 = (bf16[144,512]{1,0:T(8,128)(2,1)S(1)}, bf16[144,512]{1,0:T(8,128)(2,1)}, u32[]{:S(2)}, u32[]{:S(2)}) collective-permute-start(bf16[144,512]{1,0:T(8,128)(2,1)S(1)} %fusion.9), channel_id=1, source_target_pairs={{0,128},{8,136},{16,144},{24,152},{32,160},{40,168},{48,176},{56,1... | collective-permute-start | bytes 442376 | tf_op jit(solution)/shard_map/ppermute | solution.py:272
  33.6 9.8 %collective-permute-start.10 = (bf16[144,512]{1,0:T(8,128)(2,1)S(1)}, bf16[144,512]{1,0:T(8,128)(2,1)S(1)}, u32[]{:S(2)}, u32[]{:S(2)}) collective-permute-start(bf16[144,512]{1,0:T(8,128)(2,1)S(1)} %fusion.9), channel_id=1, source_target_pairs={{0,64},{8,72},{16,80},{24,88},{32,96},{40,104},{48,112},{56,120},{... | collective-permute-start | bytes 442376 | tf_op jit(solution)/shard_map/ppermute | solution.py:272
  34.3 5.7 %collective-permute-start.8 = (bf16[128,512]{1,0:T(8,128)(2,1)S(1)}, bf16[128,512]{1,0:T(8,128)(2,1)S(1)}, u32[]{:S(2)}, u32[]{:S(2)}) collective-permute-start(bf16[128,512]{1,0:T(8,128)(2,1)S(1)} %get-tuple-element.58), channel_id=1, source_target_pairs={{0,32},{8,40},{16,48},{24,56},{32,0},{40,8},{48,16},{56,24},{64,96... | collective-permute-start | bytes 393224 | tf_op jit(solution)/shard_map/ppermute | solution.py:275
  35.5 7.6 %collective-permute-start.7 = (bf16[128,512]{1,0:T(8,128)(2,1)S(1)}, bf16[128,512]{1,0:T(8,128)(2,1)S(1)}, u32[]{:S(2)}, u32[]{:S(2)}) collective-permute-start(bf16[128,512]{1,0:T(8,128)(2,1)S(1)} %get-tuple-element.58), channel_id=1, source_target_pairs={{0,16},{8,24},{16,32},{24,40},{32,48},{40,56},{48,0},{56,8},{64,80... | collective-permute-start | bytes 393224 | tf_op jit(solution)/shard_map/ppermute | solution.py:275
  43.4 1.4 copy-start.7
  43.5 3.1 %collective-permute-start.13 = (bf16[4,128,512]{2,1,0:T(8,128)(2,1)S(1)}, bf16[4,128,512]{2,1,0:T(8,128)(2,1)S(1)}, u32[]{:S(2)}, u32[]{:S(2)}) collective-permute-start(bf16[4,128,512]{2,1,0:T(8,128)(2,1)S(1)} %bitcast_dynamic-update-slice_fusion), channel_id=1, source_target_pairs={{0,8},{8,0},{16,24},{24,16},{32,40},{40,32},{48,56},{56,48},{64,72... | collective-permute-start | bytes 1572872 | tf_op jit(solution)/shard_map/ppermute | solution.py:278
  47.6 1.0 copy-start.2
  49.3 12.3 %collective-permute-start.14 = (bf16[128,512]{1,0:T(8,128)(2,1)}, bf16[128,512]{1,0:T(8,128)(2,1)}, u32[]{:S(2)}, u32[]{:S(2)}) collective-permute-start(bf16[128,512]{1,0:T(8,128)(2,1)} %get-tuple-element.92), channel_id=1, source_target_pairs={{0,1},{1,2},{2,3},{3,4},{4,5},{5,6},{6,7},{7,0},{8,9},{9,10},{10,1... | collective-permute-start | bytes 393224 | tf_op jit(solution)/shard_map/ppermute | solution.py:281
  50.9 12.3 %collective-permute-start.18 = (bf16[128,512]{1,0:T(8,128)(2,1)}, bf16[128,512]{1,0:T(8,128)(2,1)}, u32[]{:S(2)}, u32[]{:S(2)}) collective-permute-start(bf16[128,512]{1,0:T(8,128)(2,1)} %get-tuple-element.91), channel_id=1, source_target_pairs={{0,7},{1,0},{2,1},{3,2},{4,3},{5,4},{6,5},{7,6},{8,15},{9,8},{10,9... | collective-permute-start | bytes 393224 | tf_op jit(solution)/shard_map/ppermute | solution.py:281
  63.3 8.9 %collective-permute-start.15 = (bf16[128,512]{1,0:T(8,128)(2,1)}, bf16[128,512]{1,0:T(8,128)(2,1)}, u32[]{:S(2)}, u32[]{:S(2)}) collective-permute-start(bf16[128,512]{1,0:T(8,128)(2,1)} %fusion.7), channel_id=1, source_target_pairs={{0,1},{1,2},{2,3},{3,4},{4,5},{5,6},{6,7},{7,0},{8,9},{9,10},{10,1... | collective-permute-start | bytes 393224 | tf_op jit(solution)/shard_map/ppermute | solution.py:281
  73.3 3.9 %collective-permute-start.19 = (bf16[128,512]{1,0:T(8,128)(2,1)S(1)}, bf16[128,512]{1,0:T(8,128)(2,1)S(1)}, u32[]{:S(2)}, u32[]{:S(2)}) collective-permute-start(bf16[128,512]{1,0:T(8,128)(2,1)S(1)} %get-tuple-element.89), channel_id=1, source_target_pairs={{0,7},{1,0},{2,1},{3,2},{4,3},{5,4},{6,5},{7,6},{8,15},{9,8},{10,9... | collective-permute-start | bytes 393224 | tf_op jit(solution)/shard_map/ppermute | solution.py:281
  73.5 5.0 %collective-permute-start.16 = (bf16[128,512]{1,0:T(8,128)(2,1)S(1)}, bf16[128,512]{1,0:T(8,128)(2,1)S(1)}, u32[]{:S(2)}, u32[]{:S(2)}) collective-permute-start(bf16[128,512]{1,0:T(8,128)(2,1)S(1)} %get-tuple-element.90), channel_id=1, source_target_pairs={{0,1},{1,2},{2,3},{3,4},{4,5},{5,6},{6,7},{7,0},{8,9},{9,10},{10,1... | collective-permute-start | bytes 393224 | tf_op jit(solution)/shard_map/ppermute | solution.py:281
  79.6 3.9 %collective-permute-start.20 = (bf16[128,512]{1,0:T(8,128)(2,1)S(1)}, bf16[128,512]{1,0:T(8,128)(2,1)S(1)}, u32[]{:S(2)}, u32[]{:S(2)}) collective-permute-start(bf16[128,512]{1,0:T(8,128)(2,1)S(1)} %get-tuple-element.87), channel_id=1, source_target_pairs={{0,7},{1,0},{2,1},{3,2},{4,3},{5,4},{6,5},{7,6},{8,15},{9,8},{10,9... | collective-permute-start | bytes 393224 | tf_op jit(solution)/shard_map/ppermute | solution.py:281
  79.7 5.1 %collective-permute-start.17 = (bf16[128,512]{1,0:T(8,128)(2,1)S(1)}, bf16[128,512]{1,0:T(8,128)(2,1)S(1)}, u32[]{:S(2)}, u32[]{:S(2)}) collective-permute-start(bf16[128,512]{1,0:T(8,128)(2,1)S(1)} %get-tuple-element.88), channel_id=1, source_target_pairs={{0,1},{1,2},{2,3},{3,4},{4,5},{5,6},{6,7},{7,0},{8,9},{9,10},{10,1... | collective-permute-start | bytes 393224 | tf_op jit(solution)/shard_map/ppermute | solution.py:281
  105.1 11.9 %all-to-all-start.1 = ((f32[8,2,128]{2,1,0:T(2,128)}), f32[8,2,128]{2,1,0:T(2,128)S(1)}, u32[]{:S(2)}, u32[]{:S(2)}) async-start(f32[8,2,128]{2,1,0:T(2,128)} %broadcast_in_dim.82), calls=%async_computation.2 | async-start | bytes 16384 | tf_op jit(solution)/shard_map/all_to_all | solution.py:286
  111.9 0.7 copy-start
  117.0 17.2 %copy-start.1 = (f32[32,1024]{1,0:T(8,128)S(1)}, f32[32,1024]{1,0:T(8,128)}, u32[]{:S(2)}) copy-start(f32[32,1024]{1,0:T(8,128)} %copy-done) | copy-start | bytes 393220
  129.7 9.3 %collective-permute-start.21 = (bf16[512,512]{1,0:T(8,128)(2,1)S(1)}, bf16[512,512]{1,0:T(8,128)(2,1)S(1)}, u32[]{:S(2)}, u32[]{:S(2)}) collective-permute-start(bf16[512,512]{1,0:T(8,128)(2,1)S(1)} %get-tuple-element.77), channel_id=1, source_target_pairs={{0,8},{8,0},{16,24},{24,16},{32,40},{40,32},{48,56},{56,48},{64,72... | collective-permute-start | bytes 1572872 | tf_op jit(solution)/shard_map/ppermute | solution.py:278
  135.5 13.6 %collective-permute-start.22 = (bf16[128,1024]{1,0:T(8,128)(2,1)S(1)}, bf16[128,1024]{1,0:T(8,128)(2,1)S(1)}, u32[]{:S(2)}, u32[]{:S(2)}) collective-permute-start(bf16[128,1024]{1,0:T(8,128)(2,1)S(1)} %get-tuple-element.82), channel_id=1, source_target_pairs={{0,192},{8,200},{16,208},{24,216},{32,224},{40,232},{48,240},{56,2... | collective-permute-start | bytes 786440 | tf_op jit(solution)/shard_map/ppermute | solution.py:272
  137.9 11.2 %collective-permute-start.23 = (bf16[128,1024]{1,0:T(8,128)(2,1)S(1)}, bf16[128,1024]{1,0:T(8,128)(2,1)S(1)}, u32[]{:S(2)}, u32[]{:S(2)}) collective-permute-start(bf16[128,1024]{1,0:T(8,128)(2,1)S(1)} %get-tuple-element.83), channel_id=1, source_target_pairs={{0,128},{8,136},{16,144},{24,152},{32,160},{40,168},{48,176},{56,1... | collective-permute-start | bytes 786440 | tf_op jit(solution)/shard_map/ppermute | solution.py:272
  138.8 14.5 %collective-permute-start.24 = (bf16[128,1024]{1,0:T(8,128)(2,1)S(1)}, bf16[128,1024]{1,0:T(8,128)(2,1)S(1)}, u32[]{:S(2)}, u32[]{:S(2)}) collective-permute-start(bf16[128,1024]{1,0:T(8,128)(2,1)S(1)} %get-tuple-element.84), channel_id=1, source_target_pairs={{0,64},{8,72},{16,80},{24,88},{32,96},{40,104},{48,112},{56,120},{... | collective-permute-start | bytes 786440 | tf_op jit(solution)/shard_map/ppermute | solution.py:272
  139.0 14.4 %copy-start.4 = (pred[16,8,4,128]{3,1,2,0:T(8,128)(4,1)S(1)}, pred[16,8,4,128]{3,1,2,0:T(8,128)(4,1)}, u32[]{:S(2)}) copy-start(pred[16,8,4,128]{3,1,2,0:T(8,128)(4,1)} %copy-done.3) | copy-start | bytes 196612
  140.0 14.9 %all-to-all-start.2 = ((bf16[4,128,512]{2,1,0:T(8,128)(2,1)}), bf16[4,128,512]{2,1,0:T(8,128)(2,1)S(1)}, u32[]{:S(2)}, u32[]{:S(2)}) async-start(bf16[4,128,512]{2,1,0:T(8,128)(2,1)} %bitcast.38), calls=%async_computation.3 | async-start | bytes 1048576 | tf_op jit(solution)/shard_map/all_to_all | solution.py:390
Sparse Core Ops, SparseCore 0:
  29.8 43.0 reduce-scatter.1
  86.9 39.2 all-gather.1

commit v14 on v13

--- a/solution.py
+++ b/solution.py
@@ -322,24 +322,22 @@
         second = jnp.where(own_core == 0, other, line)
         return jnp.stack([first, second], axis=1).reshape(block_rows, flat_width)
 
-    q_pieces, k_pieces = wave(*lax.optimization_barrier((masked(queries), masked(keys))), True)
-    q_line = in_line(q_pieces)
-    q_other, keep_flat = lax.optimization_barrier((swap_core(q_line), keep_flat))
-    q_blk = both_lines(q_line, q_other)
-    k_blk = jnp.concatenate(k_pieces, axis=0)
-    logit_piece = dot_f32(q_blk, k_blk, ROW_PAIR)
     flag_rows = jnp.pad(
         row_keep.astype(jnp.bfloat16)[None, :], ((0, FLAG_ROWS - 1), (0, flat_width - rows_dev))
     )
-    g_pieces, key_pieces = wave(
-        masked(out_grad), jnp.concatenate([masked(values), flag_rows], axis=0), False
-    )
-    v_blk = jnp.concatenate([p[:rows_dev] for p in key_pieces], axis=0)
-    g_line = in_line(g_pieces)
+    query_rows = jnp.concatenate([masked(queries), masked(out_grad)], axis=0)
+    key_rows = jnp.concatenate([masked(keys), masked(values), flag_rows], axis=0)
+    query_pieces, key_pieces = wave(*lax.optimization_barrier((query_rows, key_rows)), False)
+    q_line = in_line([p[:rows_dev] for p in query_pieces])
+    g_line = in_line([p[rows_dev:] for p in query_pieces])
+    q_blk = both_lines(q_line, swap_core(q_line))
+    k_blk = jnp.concatenate([p[:rows_dev] for p in key_pieces], axis=0)
+    logit_piece = dot_f32(q_blk, k_blk, ROW_PAIR)
+    v_blk = jnp.concatenate([p[rows_dev : 2 * rows_dev] for p in key_pieces], axis=0)
     g_blk = both_lines(g_line, swap_core(g_line))
     g_blk, _ = lax.optimization_barrier((g_blk, logit_piece))
     dprob_piece = dot_f32(g_blk, v_blk, ROW_PAIR).astype(jnp.bfloat16)
-    key_flags = jnp.concatenate([p[rows_dev, :rows_dev] for p in key_pieces])[None, :]
+    key_flags = jnp.concatenate([p[2 * rows_dev, :rows_dev] for p in key_pieces])[None, :]
     logit_sum = lax.psum_scatter(logit_piece, "col", scatter_dimension=0, tiled=True)
 
     dprob_chunks = dprob_piece.reshape(zs, block_rows // zs, block_keys)

time: 163 us -> 164 us (level)
  starting transfers between devices: 45.4 us -> 36.2 us
  waiting for transfers between devices: 57.4 us -> 62.5 us
  other arithmetic: 7.61 us -> 9.57 us
    ppermute x9 -> x6, starting transfers between devices: 12.5 us -> 7.62 us  [shift_y(): lax.ppermute(table, 'row', [(at(y, x, c), at(y + step, x, c)) for y, x, c...]
    ppermute x6 -> x3, waiting for transfers between devices: 7.42 us -> 11.2 us  [shift_x(): lax.ppermute(table, 'row', [(at(y, x, c), at(y, x + step, c)) for y, x, c...]
    ppermute x7, waiting for transfers between devices: 21.6 us -> 24.4 us  [shift_z(): return lax.ppermute(table, 'col', [(z, (z + step) % zs) for z in range(zs)])]
    ppermute x6 -> x3, starting transfers between devices: 7.62 us -> 4.84 us  [shift_x(): lax.ppermute(table, 'row', [(at(y, x, c), at(y, x + step, c)) for y, x, c...]
    ppermute x9 -> x6, waiting for transfers between devices: 13.4 us -> 10.9 us  [shift_y(): lax.ppermute(table, 'row', [(at(y, x, c), at(y + step, x, c)) for y, x, c...]
  transfers between devices with their start and end apart: 29 -> 23, of which waited for: 15 -> 16; matrix products, arithmetic and copies ran while one was open for 8% -> 10% of each run, Pallas kernels for 2% -> 2%
where the time goes in v14:
time: 164 us; the launch traced here: 163 us
  waiting for transfers between devices  62.5 us (38%)
  starting transfers between devices  36.2 us (22%)
  blocking collectives  17.4 us (11%)
  between operations  14.4 us (9%)
  local copies, waits for them, and re-layouts  10.2 us (6%)
  other arithmetic  9.57 us (6%)
  Pallas kernels  9.37 us (6%)
  matrix products  3.81 us (2%)
    ppermute x7, waiting for transfers between devices, shift_z(): return lax.ppermute(table, 'col', [(z, (z + step) % zs) for z in range(zs)])  24.4 us
    all_to_all x1, blocking collectives, share(): lax.all_to_all(copies, axis, split_axis=0, concat_axis=0, tiled=True, axi...  17.4 us
    ppermute x3, waiting for transfers between devices, shift_x(): lax.ppermute(table, 'row', [(at(y, x, c), at(y, x + step, c)) for y, x, c...  11.2 us
    ppermute x6, waiting for transfers between devices, shift_y(): lax.ppermute(table, 'row', [(at(y, x, c), at(y + step, x, c)) for y, x, c...  10.9 us
    ppermute x7, starting transfers between devices, shift_z(): return lax.ppermute(table, 'col', [(z, (z + step) % zs) for z in range(zs)])  8.85 us
    all_gather x1, waiting for transfers between devices, shards(): both = lax.all_gather(both, 'col', axis=0, tiled=True)  8.8 us
    ppermute x6, starting transfers between devices, shift_y(): lax.ppermute(table, 'row', [(at(y, x, c), at(y + step, x, c)) for y, x, c...  7.62 us
    ppermute x3, starting transfers between devices, swap_core(): lax.ppermute(table, 'row', [(at(y, x, c), at(y, x, 1 - c)) for y, x, c in...  7.17 us
  transfers between devices with their start and end apart: 23, of which 16 were waited for; matrix products, arithmetic and copies ran while one was open for 10% of the time, Pallas kernels for 2%

profile of v14, /device:TPU:1, one launch (start us, length us, event | category | flops | bytes accessed | tf_op | source)
XLA Modules:
  0.0 163.5 jit_solution(467599131074265326)
XLA Ops:
  7.2 0.7 convert_bitcast_fusion
  8.1 0.2 broadcast_in_dim.71
  8.3 0.4 copy-done.7
  8.6 1.2 bitcast_select_fusion.1
  9.9 3.4 %collective-permute-start.2 = (bf16[256,512]{1,0:T(8,128)(2,1)S(1)}, bf16[256,512]{1,0:T(8,128)(2,1)S(1)}, u32[]{:S(2)}, u32[]{:S(2)}) collective-permute-start(bf16[256,512]{1,0:T(8,128)(2,1)S(1)} %pad_maximum_fusion.4), channel_id=1, source_target_pairs={{0,48},{8,56},{16,0},{24,8},{32,16},{40,24},{48,32},{56,40},{64,11... | collective-permute-start | bytes 786440 | tf_op jit(solution)/shard_map/ppermute | solution.py:275
  13.3 2.7 %collective-permute-start.5 = (bf16[272,512]{1,0:T(8,128)(2,1)S(1)}, bf16[272,512]{1,0:T(8,128)(2,1)S(1)}, u32[]{:S(2)}, u32[]{:S(2)}) collective-permute-start(bf16[272,512]{1,0:T(8,128)(2,1)S(1)} %fusion.1), channel_id=1, source_target_pairs={{0,192},{8,200},{16,208},{24,216},{32,224},{40,232},{48,240},{56,2... | collective-permute-start | bytes 835592 | tf_op jit(solution)/shard_map/ppermute | solution.py:272
  16.0 0.3 collective-permute-start.4
  16.4 0.7 collective-permute-start.3
  17.1 0.5 collective-permute-start.1
  17.6 0.7 collective-permute-done.2
  18.3 0.9 collective-permute-start
  19.2 5.4 %collective-permute-done.1 = bf16[256,512]{1,0:T(8,128)(2,1)S(1)} collective-permute-done((bf16[256,512]{1,0:T(8,128)(2,1)S(1)}, bf16[256,512]{1,0:T(8,128)(2,1)S(1)}, u32[]{:S(2)}, u32[]{:S(2)}) %collective-permute-start.1) | collective-permute-done | bytes 262176 | tf_op jit(solution)/shard_map/ppermute | solution.py:275
  24.6 5.1 %collective-permute-done = bf16[256,512]{1,0:T(8,128)(2,1)S(1)} collective-permute-done((bf16[256,512]{1,0:T(8,128)(2,1)S(1)}, bf16[256,512]{1,0:T(8,128)(2,1)S(1)}, u32[]{:S(2)}, u32[]{:S(2)}) %collective-permute-start) | collective-permute-done | bytes 262176 | tf_op jit(solution)/shard_map/ppermute | solution.py:275
  29.7 0.7 copy-done.5
  30.4 1.6 collective-permute-done.3
  32.3 2.2 %collective-permute-start.6 = (bf16[4,128,512]{2,1,0:T(8,128)(2,1)S(1)}, bf16[4,128,512]{2,1,0:T(8,128)(2,1)S(1)}, u32[]{:S(2)}, u32[]{:S(2)}) collective-permute-start(bf16[4,128,512]{2,1,0:T(8,128)(2,1)S(1)} %get-tuple-element.85), channel_id=1, source_target_pairs={{0,8},{8,0},{16,24},{24,16},{32,40},{40,32},{48,56},{56,48},{64,72... | collective-permute-start | bytes 1572872 | tf_op jit(solution)/shard_map/ppermute | solution.py:278
  34.5 1.0 fusion.18
  35.5 1.8 %fusion.20 = (bf16[128,512]{1,0:T(8,128)(2,1)S(1)}, bf16[128,512]{1,0:T(8,128)(2,1)S(1)}, bf16[128,512]{1,0:T(8,128)(2,1)S(1)}, bf16[128,512]{1,0:T(8,128)(2,1)}) fusion(bf16[272,512]{1,0:T(8,128)(2,1)} %copy-done.5, bf16[272,512]{1,0:T(8,128)(2,1)} %copy-done.4), kind=kLoop, calls=%fused_computation.75 | loop fusion | bytes 1048576 | tf_op jit(solution)/shard_map/slice | solution.py:336
  37.6 2.1 %fusion.17 = f32[1024,512]{1,0:T(8,128)} fusion(bf16[1024,512]{1,0:T(8,128)(2,1)S(1)} %bitcast.121, bf16[128,512]{1,0:T(8,128)(2,1)S(1)} %get-tuple-element.104, bf16[128,512]{1,0:T(8,128)(2,1)S(1)} %get-tuple-element.81, bf16[128,512]{1,0:T(8,128)(2,1)S(1)} %get-tuple-element.102, bf16[128,512]{1,0:T(8,128)(2,1)S(1)} %get-tuple-element.77), kind=kOutput, calls=%fused_computation.72 | convolution fusion | flops 538968064 | bytes 3670016 | tf_op jit(solution)/shard_map/dot_general | solution.py:25
  39.8 0.5 collective-permute-start.7
  40.2 1.5 collective-permute-done.7
  42.0 1.7 %convolution_convert_fusion = bf16[1024,512]{1,0:T(8,128)(2,1)} fusion(bf16[1024,512]{1,0:T(8,128)(2,1)S(1)} %bitcast.125, bf16[128,512]{1,0:T(8,128)(2,1)S(1)} %copy-done.3, bf16[128,512]{1,0:T(8,128)(2,1)S(1)} %get-tuple-element.80, bf16[128,512]{1,0:T(8,128)(2,1)S(1)} %get-tuple-element.103, bf16[128,512]{1,0:T(8,128)(2,1)S(1)} %get-tuple-element.76), kind=kOutput, calls=%fused_computation | convolution fusion | flops 539492352 | bytes 2621440 | tf_op jit(solution)/shard_map/dot_general | solution.py:25
  43.7 1.8 %dynamic-slice_bitcast_fusion = (bf16[128,512]{1,0:T(8,128)(2,1)}, bf16[128,512]{1,0:T(8,128)(2,1)}, bf16[128,512]{1,0:T(8,128)(2,1)S(1)}) fusion(bf16[8,128,512]{2,1,0:T(8,128)(2,1)} %bitcast.18, s32[]{:T(128)S(6)} %select_n.192, s32[]{:T(128)S(6)} %select_n.184, s32[]{:T(128)S(6)} %select_n.182), kind=kLoop, calls=%fused_computation.43 | loop fusion | bytes 786444 | tf_op jit(solution)/shard_map/jit(dynamic_index_in_dim)/squeeze | solution.py:346
  45.4 1.6 %collective-permute-start.8 = (bf16[128,512]{1,0:T(8,128)(2,1)}, bf16[128,512]{1,0:T(8,128)(2,1)}, u32[]{:S(2)}, u32[]{:S(2)}) collective-permute-start(bf16[128,512]{1,0:T(8,128)(2,1)} %get-tuple-element.68), channel_id=1, source_target_pairs={{0,1},{1,2},{2,3},{3,4},{4,5},{5,6},{6,7},{7,0},{8,9},{9,10},{10,1... | collective-permute-start | bytes 393224 | tf_op jit(solution)/shard_map/ppermute | solution.py:281
  47.1 3.9 %collective-permute-start.12 = (bf16[128,512]{1,0:T(8,128)(2,1)}, bf16[128,512]{1,0:T(8,128)(2,1)}, u32[]{:S(2)}, u32[]{:S(2)}) collective-permute-start(bf16[128,512]{1,0:T(8,128)(2,1)} %get-tuple-element.67), channel_id=1, source_target_pairs={{0,7},{1,0},{2,1},{3,2},{4,3},{5,4},{6,5},{7,6},{8,15},{9,8},{10,9... | collective-permute-start | bytes 393224 | tf_op jit(solution)/shard_map/ppermute | solution.py:281
  51.0 3.9 %collective-permute-done.8 = bf16[128,512]{1,0:T(8,128)(2,1)} collective-permute-done((bf16[128,512]{1,0:T(8,128)(2,1)}, bf16[128,512]{1,0:T(8,128)(2,1)}, u32[]{:S(2)}, u32[]{:S(2)}) %collective-permute-start.8) | collective-permute-done | bytes 131104 | tf_op jit(solution)/shard_map/ppermute | solution.py:281
  54.9 1.7 %fusion.8 = bf16[128,512]{1,0:T(8,128)(2,1)} fusion(bf16[128,512]{1,0:T(8,128)(2,1)} %collective-permute-done.8, bf16[8,128,512]{2,1,0:T(8,128)(2,1)} %bitcast.18, s32[]{:T(128)S(6)} %select_n.186), kind=kLoop, calls=%fused_computation.28 | loop fusion | flops 262144 | bytes 393220 | tf_op jit(solution)/shard_map/convert_element_type | solution.py:355
  56.6 8.1 %collective-permute-done.9 = bf16[128,512]{1,0:T(8,128)(2,1)} collective-permute-done((bf16[128,512]{1,0:T(8,128)(2,1)}, bf16[128,512]{1,0:T(8,128)(2,1)}, u32[]{:S(2)}, u32[]{:S(2)}) %collective-permute-start.9) | collective-permute-done | bytes 131104 | tf_op jit(solution)/shard_map/ppermute | solution.py:281
  64.7 1.2 fusion.5
  65.9 0.8 collective-permute-start.13
  66.7 0.7 collective-permute-start.10
  67.4 0.7 slice_bitcast_fusion.4
  68.1 4.3 %collective-permute-done.13 = bf16[128,512]{1,0:T(8,128)(2,1)S(1)} collective-permute-done((bf16[128,512]{1,0:T(8,128)(2,1)S(1)}, bf16[128,512]{1,0:T(8,128)(2,1)S(1)}, u32[]{:S(2)}, u32[]{:S(2)}) %collective-permute-start.13) | collective-permute-done | bytes 131104 | tf_op jit(solution)/shard_map/ppermute | solution.py:281
  72.4 1.8 %collective-permute-done.10 = bf16[128,512]{1,0:T(8,128)(2,1)S(1)} collective-permute-done((bf16[128,512]{1,0:T(8,128)(2,1)S(1)}, bf16[128,512]{1,0:T(8,128)(2,1)S(1)}, u32[]{:S(2)}, u32[]{:S(2)}) %collective-permute-start.10) | collective-permute-done | bytes 131104 | tf_op jit(solution)/shard_map/ppermute | solution.py:281
  74.2 1.0 fusion.4
  75.2 0.9 collective-permute-start.14
  76.1 0.9 collective-permute-start.11
  77.0 0.7 slice_bitcast_fusion.2
  77.6 4.5 %collective-permute-done.14.back_ref = bf16[128,512]{1,0:T(8,128)(2,1)S(1)} collective-permute-done((bf16[128,512]{1,0:T(8,128)(2,1)S(1)}, bf16[128,512]{1,0:T(8,128)(2,1)S(1)}, u32[]{:S(2)}, u32[]{:S(2)}) %collective-permute-start.14) | collective-permute-done | bytes 131104 | tf_op jit(solution)/shard_map/ppermute | solution.py:281
  82.1 1.8 %collective-permute-done.11.forward_ref = bf16[128,512]{1,0:T(8,128)(2,1)S(1)} collective-permute-done((bf16[128,512]{1,0:T(8,128)(2,1)S(1)}, bf16[128,512]{1,0:T(8,128)(2,1)S(1)}, u32[]{:S(2)}, u32[]{:S(2)}) %collective-permute-start.11) | collective-permute-done | bytes 131104 | tf_op jit(solution)/shard_map/ppermute | solution.py:281
  83.9 1.3 reduce-scatter.2.cloned.1.call-done.logit_ref
  85.3 1.9 %block_softmax.1 = (bf16[128,1024]{1,0:T(8,128)(2,1)}, f32[8,128]{1,0:T(8,128)S(1)}) custom-call(f32[128,512]{1,0:T(8,128)} %reduce-scatter.2.cloned.1.call-done.logit_ref, bf16[128,512]{1,0:T(8,128)(2,1)S(1)} %get-tuple-element.69.own_ref, bf16[128,512]{1,0:T(8,128)(2,1)S(1)} %collective-permute-done.11.forward_ref, ...), custom_call_target="tpu_custom_call" | custom-call | tf_op jit(solution)/shard_map/block_softmax/pallas_call | solution.py:148
  87.3 1.0 pad_maximum_fusion.3.v_ref
  88.3 1.1 cross_statistics.1
  89.4 17.4 %all_to_all.15.stat_ref = f32[8,16,1024]{2,1,0:T(8,128)S(1)} all-to-all(f32[8,16,1024]{2,1,0:T(8,128)S(1)} %broadcast_in_dim.83), channel_id=1, replica_groups={{0,8,16,24,32,40,48,56},{64,72,80,88,96,104,112,120},{128,136,144,152,1..., dimensions={0} | all-to-all | bytes 1048576 | tf_op jit(solution)/shard_map/all_to_all | solution.py:286
  106.9 0.6 broadcast_in_dim.84
  107.5 3.7 %all-to-all-start.1 = ((f32[8,2,128]{2,1,0:T(2,128)}), f32[8,2,128]{2,1,0:T(2,128)S(1)}, u32[]{:S(2)}, u32[]{:S(2)}) async-start(f32[8,2,128]{2,1,0:T(2,128)} %broadcast_in_dim.84), calls=%async_computation.2 | async-start | bytes 16384 | tf_op jit(solution)/shard_map/all_to_all | solution.py:286
  111.3 1.5 cross_grads.1
  112.8 0.7 copy-done
  113.5 4.4 %all-to-all-done.1.scale_ref = f32[8,2,128]{2,1,0:T(2,128)S(1)} async-done(((f32[8,2,128]{2,1,0:T(2,128)}), f32[8,2,128]{2,1,0:T(2,128)S(1)}, u32[]{:S(2)}, u32[]{:S(2)}) %all-to-all-start.1) | async-done | bytes 8224 | tf_op jit(solution)/shard_map/all_to_all | solution.py:286
  117.8 8.8 %all-gather.2.cloned.1.call-done.both_ref = bf16[1024,1024]{1,0:T(8,128)(2,1)} async-done(((bf16[128,1024]{1,0:T(8,128)(2,1)}), bf16[1024,1024]{1,0:T(8,128)(2,1)}) %all-gather.2.cloned.1.call-update) | async-done | bytes 2097168 | tf_op jit(solution)/shard_map/all_gather | solution.py:364
  126.6 3.6 %query_grads.1 = (bf16[1024,512]{1,0:T(8,128)(2,1)S(1)}, bf16[1024,512]{1,0:T(8,128)(2,1)S(1)}, f32[512,512]{1,0:T(8,128)S(1)}, bf16[512,512]{1,0:T(8,128)(2,1)S(1)}) custom-call(s32[2]{0:T(128)S(1)} %pad_add_fusion.place_ref, bf16[1024,1024]{1,0:T(8,128)(2,1)} %all-gather.2.cloned.1.call-done.both_ref, f32[8,2,128]{2,1,0:T(2,128)S(1)} %all-to-all-done.1.scale_ref, ...), custom_call_target="tpu_custom_call" | custom-call | tf_op jit(solution)/shard_map/query_grads/pallas_call | solution.py:201
  130.2 4.5 %collective-permute-start.15 = (bf16[512,512]{1,0:T(8,128)(2,1)S(1)}, bf16[512,512]{1,0:T(8,128)(2,1)S(1)}, u32[]{:S(2)}, u32[]{:S(2)}) collective-permute-start(bf16[512,512]{1,0:T(8,128)(2,1)S(1)} %get-tuple-element.53), channel_id=1, source_target_pairs={{0,8},{8,0},{16,24},{24,16},{32,40},{40,32},{48,56},{56,48},{64,72... | collective-permute-start | bytes 1572872 | tf_op jit(solution)/shard_map/ppermute | solution.py:278
  134.7 1.3 key_grads.1
  136.0 2.7 %collective-permute-start.16 = (bf16[128,1024]{1,0:T(8,128)(2,1)S(1)}, bf16[128,1024]{1,0:T(8,128)(2,1)S(1)}, u32[]{:S(2)}, u32[]{:S(2)}) collective-permute-start(bf16[128,1024]{1,0:T(8,128)(2,1)S(1)} %get-tuple-element.58), channel_id=1, source_target_pairs={{0,192},{8,200},{16,208},{24,216},{32,224},{40,232},{48,240},{56,2... | collective-permute-start | bytes 786440 | tf_op jit(solution)/shard_map/ppermute | solution.py:272
  138.7 0.4 collective-permute-start.17
  139.1 0.8 collective-permute-start.18
  139.9 1.0 add_convert_fusion
  140.8 4.0 %all-to-all-start.2 = ((bf16[4,128,512]{2,1,0:T(8,128)(2,1)}), bf16[4,128,512]{2,1,0:T(8,128)(2,1)S(1)}, u32[]{:S(2)}, u32[]{:S(2)}) async-start(bf16[4,128,512]{2,1,0:T(8,128)(2,1)} %bitcast.38), calls=%async_computation.3 | async-start | bytes 1048576 | tf_op jit(solution)/shard_map/all_to_all | solution.py:388
  144.8 5.1 %collective-permute-done.16 = bf16[128,1024]{1,0:T(8,128)(2,1)S(1)} collective-permute-done((bf16[128,1024]{1,0:T(8,128)(2,1)S(1)}, bf16[128,1024]{1,0:T(8,128)(2,1)S(1)}, u32[]{:S(2)}, u32[]{:S(2)}) %collective-permute-start.16) | collective-permute-done | bytes 262176 | tf_op jit(solution)/shard_map/ppermute | solution.py:272
  149.9 4.2 %collective-permute-done.18 = bf16[128,1024]{1,0:T(8,128)(2,1)S(1)} collective-permute-done((bf16[128,1024]{1,0:T(8,128)(2,1)S(1)}, bf16[128,1024]{1,0:T(8,128)(2,1)S(1)}, u32[]{:S(2)}, u32[]{:S(2)}) %collective-permute-start.18) | collective-permute-done | bytes 262176 | tf_op jit(solution)/shard_map/ppermute | solution.py:272
  154.3 0.7 reshape.108
  155.0 0.7 reshape.107
  155.8 0.9 select_convert_fusion
  (57 shorter events, 1.5 us)
Async XLA Ops:
  7.2 78.1 %reduce-scatter.2.cloned.1.call-start = ((), (), s32[]{:S(2)}) async-start(), calls=%async_computation.4 | async-start | bytes 2359296 | tf_op jit(solution)/shard_map/reduce_scatter | solution.py:341
  8.0 0.6 copy-start.7
  9.9 8.4 %collective-permute-start.2 = (bf16[256,512]{1,0:T(8,128)(2,1)S(1)}, bf16[256,512]{1,0:T(8,128)(2,1)S(1)}, u32[]{:S(2)}, u32[]{:S(2)}) collective-permute-start(bf16[256,512]{1,0:T(8,128)(2,1)S(1)} %pad_maximum_fusion.4), channel_id=1, source_target_pairs={{0,48},{8,56},{16,0},{24,8},{32,16},{40,24},{48,32},{56,40},{64,11... | collective-permute-start | bytes 786440 | tf_op jit(solution)/shard_map/ppermute | solution.py:275
  13.3 16.4 %collective-permute-start.5 = (bf16[272,512]{1,0:T(8,128)(2,1)S(1)}, bf16[272,512]{1,0:T(8,128)(2,1)S(1)}, u32[]{:S(2)}, u32[]{:S(2)}) collective-permute-start(bf16[272,512]{1,0:T(8,128)(2,1)S(1)} %fusion.1), channel_id=1, source_target_pairs={{0,192},{8,200},{16,208},{24,216},{32,224},{40,232},{48,240},{56,2... | collective-permute-start | bytes 835592 | tf_op jit(solution)/shard_map/ppermute | solution.py:272
  16.0 13.7 %collective-permute-start.4 = (bf16[272,512]{1,0:T(8,128)(2,1)S(1)}, bf16[272,512]{1,0:T(8,128)(2,1)S(1)}, u32[]{:S(2)}, u32[]{:S(2)}) collective-permute-start(bf16[272,512]{1,0:T(8,128)(2,1)S(1)} %fusion.1), channel_id=1, source_target_pairs={{0,128},{8,136},{16,144},{24,152},{32,160},{40,168},{48,176},{56,1... | collective-permute-start | bytes 835592 | tf_op jit(solution)/shard_map/ppermute | solution.py:272
  16.4 15.7 %collective-permute-start.3 = (bf16[272,512]{1,0:T(8,128)(2,1)S(1)}, bf16[272,512]{1,0:T(8,128)(2,1)S(1)}, u32[]{:S(2)}, u32[]{:S(2)}) collective-permute-start(bf16[272,512]{1,0:T(8,128)(2,1)S(1)} %fusion.1), channel_id=1, source_target_pairs={{0,64},{8,72},{16,80},{24,88},{32,96},{40,104},{48,112},{56,120},{... | collective-permute-start | bytes 835592 | tf_op jit(solution)/shard_map/ppermute | solution.py:272
  17.1 7.5 %collective-permute-start.1 = (bf16[256,512]{1,0:T(8,128)(2,1)S(1)}, bf16[256,512]{1,0:T(8,128)(2,1)S(1)}, u32[]{:S(2)}, u32[]{:S(2)}) collective-permute-start(bf16[256,512]{1,0:T(8,128)(2,1)S(1)} %pad_maximum_fusion.4), channel_id=1, source_target_pairs={{0,32},{8,40},{16,48},{24,56},{32,0},{40,8},{48,16},{56,24},{64,96... | collective-permute-start | bytes 786440 | tf_op jit(solution)/shard_map/ppermute | solution.py:275
  18.3 11.4 %collective-permute-start = (bf16[256,512]{1,0:T(8,128)(2,1)S(1)}, bf16[256,512]{1,0:T(8,128)(2,1)S(1)}, u32[]{:S(2)}, u32[]{:S(2)}) collective-permute-start(bf16[256,512]{1,0:T(8,128)(2,1)S(1)} %pad_maximum_fusion.4), channel_id=1, source_target_pairs={{0,16},{8,24},{16,32},{24,40},{32,48},{40,56},{48,0},{56,8},{64,80... | collective-permute-start | bytes 786440 | tf_op jit(solution)/shard_map/ppermute | solution.py:275
  29.7 2.4 %copy-start.4 = (bf16[272,512]{1,0:T(8,128)(2,1)}, bf16[272,512]{1,0:T(8,128)(2,1)S(1)}, u32[]{:S(2)}) copy-start(bf16[272,512]{1,0:T(8,128)(2,1)S(1)} %collective-permute-done.5) | copy-start | bytes 835588
  29.7 0.7 copy-start.5
  32.1 2.5 %copy-start.6 = (bf16[272,512]{1,0:T(8,128)(2,1)}, bf16[272,512]{1,0:T(8,128)(2,1)S(1)}, u32[]{:S(2)}) copy-start(bf16[272,512]{1,0:T(8,128)(2,1)S(1)} %collective-permute-done.3) | copy-start | bytes 835588
  32.3 5.0 %collective-permute-start.6 = (bf16[4,128,512]{2,1,0:T(8,128)(2,1)S(1)}, bf16[4,128,512]{2,1,0:T(8,128)(2,1)S(1)}, u32[]{:S(2)}, u32[]{:S(2)}) collective-permute-start(bf16[4,128,512]{2,1,0:T(8,128)(2,1)S(1)} %get-tuple-element.85), channel_id=1, source_target_pairs={{0,8},{8,0},{16,24},{24,16},{32,40},{40,32},{48,56},{56,48},{64,72... | collective-permute-start | bytes 1572872 | tf_op jit(solution)/shard_map/ppermute | solution.py:278
  37.3 4.6 %copy-start.2 = (bf16[128,512]{1,0:T(8,128)(2,1)}, bf16[128,512]{1,0:T(8,128)(2,1)S(1)}, u32[]{:S(2)}) copy-start(bf16[128,512]{1,0:T(8,128)(2,1)S(1)} %get-tuple-element.80) | copy-start | bytes 393220
  39.7 86.9 %all-gather.2.cloned.1.call-start = ((), (), s32[]{:S(2)}) async-start(), calls=%async_computation.5 | async-start | bytes 2359296 | tf_op jit(solution)/shard_map/all_gather | solution.py:364
  39.8 2.0 %collective-permute-start.7 = (bf16[4,128,512]{2,1,0:T(8,128)(2,1)S(1)}, bf16[4,128,512]{2,1,0:T(8,128)(2,1)S(1)}, u32[]{:S(2)}, u32[]{:S(2)}) collective-permute-start(bf16[4,128,512]{2,1,0:T(8,128)(2,1)S(1)} %get-tuple-element.84), channel_id=1, source_target_pairs={{0,8},{8,0},{16,24},{24,16},{32,40},{40,32},{48,56},{56,48},{64,72... | collective-permute-start | bytes 1572872 | tf_op jit(solution)/shard_map/ppermute | solution.py:278
  40.2 1.7 %copy-start.3 = (bf16[128,512]{1,0:T(8,128)(2,1)S(1)}, bf16[128,512]{1,0:T(8,128)(2,1)}, u32[]{:S(2)}) copy-start(bf16[128,512]{1,0:T(8,128)(2,1)} %get-tuple-element.105) | copy-start | bytes 393220
  45.4 9.5 %collective-permute-start.8 = (bf16[128,512]{1,0:T(8,128)(2,1)}, bf16[128,512]{1,0:T(8,128)(2,1)}, u32[]{:S(2)}, u32[]{:S(2)}) collective-permute-start(bf16[128,512]{1,0:T(8,128)(2,1)} %get-tuple-element.68), channel_id=1, source_target_pairs={{0,1},{1,2},{2,3},{3,4},{4,5},{5,6},{6,7},{7,0},{8,9},{9,10},{10,1... | collective-permute-start | bytes 393224 | tf_op jit(solution)/shard_map/ppermute | solution.py:281
  47.1 9.5 %collective-permute-start.12 = (bf16[128,512]{1,0:T(8,128)(2,1)}, bf16[128,512]{1,0:T(8,128)(2,1)}, u32[]{:S(2)}, u32[]{:S(2)}) collective-permute-start(bf16[128,512]{1,0:T(8,128)(2,1)} %get-tuple-element.67), channel_id=1, source_target_pairs={{0,7},{1,0},{2,1},{3,2},{4,3},{5,4},{6,5},{7,6},{8,15},{9,8},{10,9... | collective-permute-start | bytes 393224 | tf_op jit(solution)/shard_map/ppermute | solution.py:281
  56.6 8.1 %collective-permute-start.9 = (bf16[128,512]{1,0:T(8,128)(2,1)}, bf16[128,512]{1,0:T(8,128)(2,1)}, u32[]{:S(2)}, u32[]{:S(2)}) collective-permute-start(bf16[128,512]{1,0:T(8,128)(2,1)} %fusion.8), channel_id=1, source_target_pairs={{0,1},{1,2},{2,3},{3,4},{4,5},{5,6},{6,7},{7,0},{8,9},{9,10},{10,1... | collective-permute-start | bytes 393224 | tf_op jit(solution)/shard_map/ppermute | solution.py:281
  65.9 6.6 %collective-permute-start.13 = (bf16[128,512]{1,0:T(8,128)(2,1)S(1)}, bf16[128,512]{1,0:T(8,128)(2,1)S(1)}, u32[]{:S(2)}, u32[]{:S(2)}) collective-permute-start(bf16[128,512]{1,0:T(8,128)(2,1)S(1)} %get-tuple-element.65), channel_id=1, source_target_pairs={{0,7},{1,0},{2,1},{3,2},{4,3},{5,4},{6,5},{7,6},{8,15},{9,8},{10,9... | collective-permute-start | bytes 393224 | tf_op jit(solution)/shard_map/ppermute | solution.py:281
  66.7 7.5 %collective-permute-start.10 = (bf16[128,512]{1,0:T(8,128)(2,1)S(1)}, bf16[128,512]{1,0:T(8,128)(2,1)S(1)}, u32[]{:S(2)}, u32[]{:S(2)}) collective-permute-start(bf16[128,512]{1,0:T(8,128)(2,1)S(1)} %get-tuple-element.66), channel_id=1, source_target_pairs={{0,1},{1,2},{2,3},{3,4},{4,5},{5,6},{6,7},{7,0},{8,9},{9,10},{10,1... | collective-permute-start | bytes 393224 | tf_op jit(solution)/shard_map/ppermute | solution.py:281
  75.2 6.9 %collective-permute-start.14 = (bf16[128,512]{1,0:T(8,128)(2,1)S(1)}, bf16[128,512]{1,0:T(8,128)(2,1)S(1)}, u32[]{:S(2)}, u32[]{:S(2)}) collective-permute-start(bf16[128,512]{1,0:T(8,128)(2,1)S(1)} %get-tuple-element.63), channel_id=1, source_target_pairs={{0,7},{1,0},{2,1},{3,2},{4,3},{5,4},{6,5},{7,6},{8,15},{9,8},{10,9... | collective-permute-start | bytes 393224 | tf_op jit(solution)/shard_map/ppermute | solution.py:281
  76.1 7.9 %collective-permute-start.11 = (bf16[128,512]{1,0:T(8,128)(2,1)S(1)}, bf16[128,512]{1,0:T(8,128)(2,1)S(1)}, u32[]{:S(2)}, u32[]{:S(2)}) collective-permute-start(bf16[128,512]{1,0:T(8,128)(2,1)S(1)} %get-tuple-element.64), channel_id=1, source_target_pairs={{0,1},{1,2},{2,3},{3,4},{4,5},{5,6},{6,7},{7,0},{8,9},{9,10},{10,1... | collective-permute-start | bytes 393224 | tf_op jit(solution)/shard_map/ppermute | solution.py:281
  107.5 10.3 %all-to-all-start.1 = ((f32[8,2,128]{2,1,0:T(2,128)}), f32[8,2,128]{2,1,0:T(2,128)S(1)}, u32[]{:S(2)}, u32[]{:S(2)}) async-start(f32[8,2,128]{2,1,0:T(2,128)} %broadcast_in_dim.84), calls=%async_computation.2 | async-start | bytes 16384 | tf_op jit(solution)/shard_map/all_to_all | solution.py:286
  112.8 0.7 copy-start
  117.8 16.9 %copy-start.1 = (f32[32,1024]{1,0:T(8,128)S(1)}, f32[32,1024]{1,0:T(8,128)}, u32[]{:S(2)}) copy-start(f32[32,1024]{1,0:T(8,128)} %copy-done) | copy-start | bytes 393220
  130.2 9.6 %collective-permute-start.15 = (bf16[512,512]{1,0:T(8,128)(2,1)S(1)}, bf16[512,512]{1,0:T(8,128)(2,1)S(1)}, u32[]{:S(2)}, u32[]{:S(2)}) collective-permute-start(bf16[512,512]{1,0:T(8,128)(2,1)S(1)} %get-tuple-element.53), channel_id=1, source_target_pairs={{0,8},{8,0},{16,24},{24,16},{32,40},{40,32},{48,56},{56,48},{64,72... | collective-permute-start | bytes 1572872 | tf_op jit(solution)/shard_map/ppermute | solution.py:278
  136.0 13.9 %collective-permute-start.16 = (bf16[128,1024]{1,0:T(8,128)(2,1)S(1)}, bf16[128,1024]{1,0:T(8,128)(2,1)S(1)}, u32[]{:S(2)}, u32[]{:S(2)}) collective-permute-start(bf16[128,1024]{1,0:T(8,128)(2,1)S(1)} %get-tuple-element.58), channel_id=1, source_target_pairs={{0,192},{8,200},{16,208},{24,216},{32,224},{40,232},{48,240},{56,2... | collective-permute-start | bytes 786440 | tf_op jit(solution)/shard_map/ppermute | solution.py:272
  138.7 11.2 %collective-permute-start.17 = (bf16[128,1024]{1,0:T(8,128)(2,1)S(1)}, bf16[128,1024]{1,0:T(8,128)(2,1)S(1)}, u32[]{:S(2)}, u32[]{:S(2)}) collective-permute-start(bf16[128,1024]{1,0:T(8,128)(2,1)S(1)} %get-tuple-element.59), channel_id=1, source_target_pairs={{0,128},{8,136},{16,144},{24,152},{32,160},{40,168},{48,176},{56,1... | collective-permute-start | bytes 786440 | tf_op jit(solution)/shard_map/ppermute | solution.py:272
  139.1 14.9 %collective-permute-start.18 = (bf16[128,1024]{1,0:T(8,128)(2,1)S(1)}, bf16[128,1024]{1,0:T(8,128)(2,1)S(1)}, u32[]{:S(2)}, u32[]{:S(2)}) collective-permute-start(bf16[128,1024]{1,0:T(8,128)(2,1)S(1)} %get-tuple-element.60), channel_id=1, source_target_pairs={{0,64},{8,72},{16,80},{24,88},{32,96},{40,104},{48,112},{56,120},{... | collective-permute-start | bytes 786440 | tf_op jit(solution)/shard_map/ppermute | solution.py:272
  140.8 15.0 %copy-start.8 = (pred[128,4]{1,0:T(8,128)(4,1)S(1)}, pred[128,4]{1,0:T(8,128)(4,1)}, u32[]{:S(2)}) copy-start(pred[128,4]{1,0:T(8,128)(4,1)} %copy-done.7) | copy-start | bytes 1540
  140.8 14.8 %all-to-all-start.2 = ((bf16[4,128,512]{2,1,0:T(8,128)(2,1)}), bf16[4,128,512]{2,1,0:T(8,128)(2,1)S(1)}, u32[]{:S(2)}, u32[]{:S(2)}) async-start(bf16[4,128,512]{2,1,0:T(8,128)(2,1)} %bitcast.38), calls=%async_computation.3 | async-start | bytes 1048576 | tf_op jit(solution)/shard_map/all_to_all | solution.py:388
Sparse Core Ops, SparseCore 0:
  39.8 45.3 reduce-scatter.1
  87.3 39.2 all-gather.1

commit v15 on v13

--- a/solution.py
+++ b/solution.py
@@ -344,8 +344,11 @@
 
     dprob_chunks = dprob_piece.reshape(zs, block_rows // zs, block_keys)
 
+    back_chunks = lax.optimization_barrier(dprob_chunks)
+
     def part(step):
-        return lax.dynamic_index_in_dim(dprob_chunks, (own_z + step) % zs, axis=0, keepdims=False)
+        chunks = back_chunks if step < 0 else dprob_chunks
+        return lax.dynamic_index_in_dim(chunks, (own_z + step) % zs, axis=0, keepdims=False)
 
     def passed(step, count):
         moving = part(step * count)

time: 163 us -> 162 us (level)
  waiting for transfers between devices: 57.4 us -> 52.1 us
  starting transfers between devices: 45.4 us -> 48.9 us
  other arithmetic: 7.61 us -> 4.92 us
  local copies, waits for them, and re-layouts: 8.92 us -> 11 us
    ppermute x6, waiting for transfers between devices: 7.42 us -> 1.72 us  [shift_x(): lax.ppermute(table, 'row', [(at(y, x, c), at(y, x + step, c)) for y, x, c...]
    ppermute x9, waiting for transfers between devices: 13.4 us -> 17.4 us  [shift_y(): lax.ppermute(table, 'row', [(at(y, x, c), at(y + step, x, c)) for y, x, c...]
    ppermute x7, starting transfers between devices: 8.66 us -> 12.4 us  [shift_z(): return lax.ppermute(table, 'col', [(z, (z + step) % zs) for z in range(zs)])]
    convert_element_type x3 -> x5, other arithmetic: 3.86 us -> 0.19 us  [passed(): moving = (moving.astype(jnp.float32) + part(step * left).astype(jnp.float...]
    all_gather x1, waiting for transfers between devices: 9.17 us -> 6.85 us  [shards(): both = lax.all_gather(both, 'col', axis=0, tiled=True)]
    dynamic_update_slice x8, local copies, waits for them, and re-layouts: 0.13 us -> 1.93 us  [in_line(): line = lax.dynamic_update_slice(line, piece[None], ((own_x - s) % XS, 0, 0))]
  transfers between devices with their start and end apart: 29 -> 29, of which waited for: 15 -> 13; matrix products, arithmetic and copies ran while one was open for 8% -> 9% of each run, Pallas kernels for 2% -> 2%
where the time goes in v15:
time: 162 us
  waiting for transfers between devices  52.1 us (32%)
  starting transfers between devices  48.9 us (30%)
  blocking collectives  17.5 us (11%)
  between operations  14.5 us (9%)
  local copies, waits for them, and re-layouts  11 us (7%)
  Pallas kernels  9.35 us (6%)
  other arithmetic  4.92 us (3%)
  matrix products  3.79 us (2%)
    ppermute x7, waiting for transfers between devices, shift_z(): return lax.ppermute(table, 'col', [(z, (z + step) % zs) for z in range(zs)])  20.2 us
    all_to_all x1, blocking collectives, share(): lax.all_to_all(copies, axis, split_axis=0, concat_axis=0, tiled=True, axi...  17.5 us
    ppermute x9, waiting for transfers between devices, shift_y(): lax.ppermute(table, 'row', [(at(y, x, c), at(y + step, x, c)) for y, x, c...  17.4 us
    ppermute x7, starting transfers between devices, shift_z(): return lax.ppermute(table, 'col', [(z, (z + step) % zs) for z in range(zs)])  12.4 us
    ppermute x9, starting transfers between devices, shift_y(): lax.ppermute(table, 'row', [(at(y, x, c), at(y + step, x, c)) for y, x, c...  12.4 us
    ppermute x6, starting transfers between devices, shift_x(): lax.ppermute(table, 'row', [(at(y, x, c), at(y, x + step, c)) for y, x, c...  7.81 us
    ppermute x3, starting transfers between devices, swap_core(): lax.ppermute(table, 'row', [(at(y, x, c), at(y, x, 1 - c)) for y, x, c in...  7.75 us
    all_gather x1, waiting for transfers between devices, shards(): both = lax.all_gather(both, 'col', axis=0, tiled=True)  6.85 us
  transfers between devices with their start and end apart: 29, of which 13 were waited for; matrix products, arithmetic and copies ran while one was open for 9% of the time, Pallas kernels for 2%

profile of v15, /device:TPU:1, one launch (start us, length us, event | category | flops | bytes accessed | tf_op | source)
XLA Modules:
  0.0 161.9 jit_solution(15679403398134434887)
XLA Ops:
  7.2 0.7 convert_bitcast_fusion
  8.1 0.2 broadcast_in_dim.69
  8.3 1.0 bitcast_select_fusion.3
  9.3 2.1 %collective-permute-start = (bf16[128,512]{1,0:T(8,128)(2,1)S(1)}, bf16[128,512]{1,0:T(8,128)(2,1)S(1)}, u32[]{:S(2)}, u32[]{:S(2)}) collective-permute-start(bf16[128,512]{1,0:T(8,128)(2,1)S(1)} %get-tuple-element.48), channel_id=1, source_target_pairs={{0,16},{8,24},{16,32},{24,40},{32,48},{40,56},{48,0},{56,8},{64,80... | collective-permute-start | bytes 393224 | tf_op jit(solution)/shard_map/ppermute | solution.py:275
  11.4 1.4 collective-permute-start.2
  12.8 1.6 %collective-permute-start.1 = (bf16[128,512]{1,0:T(8,128)(2,1)S(1)}, bf16[128,512]{1,0:T(8,128)(2,1)S(1)}, u32[]{:S(2)}, u32[]{:S(2)}) collective-permute-start(bf16[128,512]{1,0:T(8,128)(2,1)S(1)} %get-tuple-element.48), channel_id=1, source_target_pairs={{0,32},{8,40},{16,48},{24,56},{32,0},{40,8},{48,16},{56,24},{64,96... | collective-permute-start | bytes 393224 | tf_op jit(solution)/shard_map/ppermute | solution.py:275
  14.4 2.9 %collective-permute-start.4 = (bf16[128,512]{1,0:T(8,128)(2,1)S(1)}, bf16[128,512]{1,0:T(8,128)(2,1)S(1)}, u32[]{:S(2)}, u32[]{:S(2)}) collective-permute-start(bf16[128,512]{1,0:T(8,128)(2,1)S(1)} %get-tuple-element.54), channel_id=1, source_target_pairs={{0,128},{8,136},{16,144},{24,152},{32,160},{40,168},{48,176},{56,1... | collective-permute-start | bytes 393224 | tf_op jit(solution)/shard_map/ppermute | solution.py:272
  17.4 0.4 collective-permute-start.3
  17.8 2.3 %collective-permute-start.5 = (bf16[128,512]{1,0:T(8,128)(2,1)S(1)}, bf16[128,512]{1,0:T(8,128)(2,1)S(1)}, u32[]{:S(2)}, u32[]{:S(2)}) collective-permute-start(bf16[128,512]{1,0:T(8,128)(2,1)S(1)} %get-tuple-element.54), channel_id=1, source_target_pairs={{0,192},{8,200},{16,208},{24,216},{32,224},{40,232},{48,240},{56,2... | collective-permute-start | bytes 393224 | tf_op jit(solution)/shard_map/ppermute | solution.py:272
  20.0 3.9 %collective-permute-done.3 = bf16[128,512]{1,0:T(8,128)(2,1)S(1)} collective-permute-done((bf16[128,512]{1,0:T(8,128)(2,1)S(1)}, bf16[128,512]{1,0:T(8,128)(2,1)S(1)}, u32[]{:S(2)}, u32[]{:S(2)}) %collective-permute-start.3) | collective-permute-done | bytes 131104 | tf_op jit(solution)/shard_map/ppermute | solution.py:272
  24.1 1.7 %collective-permute-start.6 = (bf16[4,128,512]{2,1,0:T(8,128)(2,1)S(1)}, bf16[4,128,512]{2,1,0:T(8,128)(2,1)S(1)}, u32[]{:S(2)}, u32[]{:S(2)}) collective-permute-start(bf16[4,128,512]{2,1,0:T(8,128)(2,1)S(1)} %bitcast_dynamic-update-slice_fusion.4), channel_id=1, source_target_pairs={{0,8},{8,0},{16,24},{24,16},{32,40},{40,32},{48,56},{56,48},{64,72... | collective-permute-start | bytes 1572872 | tf_op jit(solution)/shard_map/ppermute | solution.py:278
  25.9 1.4 collective-permute-done.6
  27.4 1.1 collective-permute-start.9
  28.4 1.2 collective-permute-start.8
  29.7 0.4 collective-permute-start.7
  30.1 2.5 %collective-permute-start.12 = (bf16[144,512]{1,0:T(8,128)(2,1)S(1)}, bf16[144,512]{1,0:T(8,128)(2,1)}, u32[]{:S(2)}, u32[]{:S(2)}) collective-permute-start(bf16[144,512]{1,0:T(8,128)(2,1)S(1)} %fusion.9), channel_id=1, source_target_pairs={{0,192},{8,200},{16,208},{24,216},{32,224},{40,232},{48,240},{56,2... | collective-permute-start | bytes 442376 | tf_op jit(solution)/shard_map/ppermute | solution.py:272
  32.9 0.6 copy-done.2
  33.5 0.7 collective-permute-start.10
  34.2 2.1 %fusion.18 = f32[1024,512]{1,0:T(8,128)} fusion(bf16[1024,512]{1,0:T(8,128)(2,1)S(1)} %bitcast.126, bf16[512,512]{1,0:T(8,128)(2,1)S(1)} %constant_dynamic-update-slice_fusion.k_ref), kind=kOutput, calls=%fused_computation.75 | convolution fusion | flops 536870912 | bytes 3670016 | tf_op jit(solution)/shard_map/dot_general | solution.py:25
  36.4 1.7 %collective-permute-done.7 = bf16[128,512]{1,0:T(8,128)(2,1)} collective-permute-done((bf16[128,512]{1,0:T(8,128)(2,1)S(1)}, bf16[128,512]{1,0:T(8,128)(2,1)}, u32[]{:S(2)}, u32[]{:S(2)}) %collective-permute-start.7) | collective-permute-done | bytes 131104 | tf_op jit(solution)/shard_map/ppermute | solution.py:275
  38.1 0.2 collective-permute-done.11
  38.3 4.0 %collective-permute-done.10 = bf16[144,512]{1,0:T(8,128)(2,1)S(1)} collective-permute-done((bf16[144,512]{1,0:T(8,128)(2,1)S(1)}, bf16[144,512]{1,0:T(8,128)(2,1)S(1)}, u32[]{:S(2)}, u32[]{:S(2)}) %collective-permute-start.10) | collective-permute-done | bytes 147488 | tf_op jit(solution)/shard_map/ppermute | solution.py:272
  42.4 0.9 bitcast_dynamic-update-slice_fusion.2
  43.3 0.9 bitcast_dynamic-update-slice_fusion.1
  44.3 1.3 collective-permute-start.13
  45.6 1.6 slice.63
  47.1 1.6 slice.64
  48.8 0.1 pad_maximum_fusion.1
  48.9 1.7 %convolution_convert_fusion = bf16[1024,512]{1,0:T(8,128)(2,1)S(1)} fusion(bf16[1024,512]{1,0:T(8,128)(2,1)S(1)} %bitcast.130, bf16[128,512]{1,0:T(8,128)(2,1)} %slice.64, bf16[128,512]{1,0:T(8,128)(2,1)} %slice.63, bf16[128,512]{1,0:T(8,128)(2,1)S(1)} %slice.62, bf16[128,512]{1,0:T(8,128)(2,1)S(1)} %slice.61), kind=kOutput, calls=%fused_computation | convolution fusion | flops 539492352 | bytes 2621440 | tf_op jit(solution)/shard_map/dot_general | solution.py:25
  50.7 1.9 %collective-permute-start.14 = (bf16[128,512]{1,0:T(8,128)(2,1)S(1)}, bf16[128,512]{1,0:T(8,128)(2,1)S(1)}, u32[]{:S(2)}, u32[]{:S(2)}) collective-permute-start(bf16[128,512]{1,0:T(8,128)(2,1)S(1)} %get-tuple-element.87), channel_id=1, source_target_pairs={{0,1},{1,2},{2,3},{3,4},{4,5},{5,6},{6,7},{7,0},{8,9},{9,10},{10,1... | collective-permute-start | bytes 393224 | tf_op jit(solution)/shard_map/ppermute | solution.py:281
  52.6 0.7 slice_bitcast_fusion.4
  53.2 4.0 %collective-permute-start.18 = (bf16[128,512]{1,0:T(8,128)(2,1)S(1)}, bf16[128,512]{1,0:T(8,128)(2,1)S(1)}, u32[]{:S(2)}, u32[]{:S(2)}) collective-permute-start(bf16[128,512]{1,0:T(8,128)(2,1)S(1)} %dynamic-slice_bitcast_fusion), channel_id=1, source_target_pairs={{0,7},{1,0},{2,1},{3,2},{4,3},{5,4},{6,5},{7,6},{8,15},{9,8},{10,9... | collective-permute-start | bytes 393224 | tf_op jit(solution)/shard_map/ppermute | solution.py:281
  57.3 5.7 %collective-permute-done.14 = bf16[128,512]{1,0:T(8,128)(2,1)S(1)} collective-permute-done((bf16[128,512]{1,0:T(8,128)(2,1)S(1)}, bf16[128,512]{1,0:T(8,128)(2,1)S(1)}, u32[]{:S(2)}, u32[]{:S(2)}) %collective-permute-start.14) | collective-permute-done | bytes 131104 | tf_op jit(solution)/shard_map/ppermute | solution.py:281
  63.2 3.5 %collective-permute-start.19 = (bf16[128,512]{1,0:T(8,128)(2,1)S(1)}, bf16[128,512]{1,0:T(8,128)(2,1)S(1)}, u32[]{:S(2)}, u32[]{:S(2)}) collective-permute-start(bf16[128,512]{1,0:T(8,128)(2,1)S(1)} %fusion.4), channel_id=1, source_target_pairs={{0,7},{1,0},{2,1},{3,2},{4,3},{5,4},{6,5},{7,6},{8,15},{9,8},{10,9... | collective-permute-start | bytes 393224 | tf_op jit(solution)/shard_map/ppermute | solution.py:281
  66.7 4.7 %collective-permute-done.15 = bf16[128,512]{1,0:T(8,128)(2,1)S(1)} collective-permute-done((bf16[128,512]{1,0:T(8,128)(2,1)S(1)}, bf16[128,512]{1,0:T(8,128)(2,1)S(1)}, u32[]{:S(2)}, u32[]{:S(2)}) %collective-permute-start.15) | collective-permute-done | bytes 131104 | tf_op jit(solution)/shard_map/ppermute | solution.py:281
  71.5 2.8 %collective-permute-start.20 = (bf16[128,512]{1,0:T(8,128)(2,1)S(1)}, bf16[128,512]{1,0:T(8,128)(2,1)S(1)}, u32[]{:S(2)}, u32[]{:S(2)}) collective-permute-start(bf16[128,512]{1,0:T(8,128)(2,1)S(1)} %fusion.3), channel_id=1, source_target_pairs={{0,7},{1,0},{2,1},{3,2},{4,3},{5,4},{6,5},{7,6},{8,15},{9,8},{10,9... | collective-permute-start | bytes 393224 | tf_op jit(solution)/shard_map/ppermute | solution.py:281
  74.3 4.7 %collective-permute-done.16 = bf16[128,512]{1,0:T(8,128)(2,1)S(1)} collective-permute-done((bf16[128,512]{1,0:T(8,128)(2,1)S(1)}, bf16[128,512]{1,0:T(8,128)(2,1)S(1)}, u32[]{:S(2)}, u32[]{:S(2)}) %collective-permute-start.16) | collective-permute-done | bytes 131104 | tf_op jit(solution)/shard_map/ppermute | solution.py:281
  79.2 0.7 slice_bitcast_fusion.2
  79.9 5.1 %collective-permute-done.17.forward_ref = bf16[128,512]{1,0:T(8,128)(2,1)S(1)} collective-permute-done((bf16[128,512]{1,0:T(8,128)(2,1)S(1)}, bf16[128,512]{1,0:T(8,128)(2,1)S(1)}, u32[]{:S(2)}, u32[]{:S(2)}) %collective-permute-start.17) | collective-permute-done | bytes 131104 | tf_op jit(solution)/shard_map/ppermute | solution.py:281
  85.0 1.9 %block_softmax.1 = (bf16[128,1024]{1,0:T(8,128)(2,1)}, f32[8,128]{1,0:T(8,128)S(1)}) custom-call(f32[128,512]{1,0:T(8,128)} %reduce-scatter.2.cloned.1.call-done.logit_ref, bf16[128,512]{1,0:T(8,128)(2,1)S(1)} %get-tuple-element.88.own_ref, bf16[128,512]{1,0:T(8,128)(2,1)S(1)} %collective-permute-done.17.forward_ref, ...), custom_call_target="tpu_custom_call" | custom-call | tf_op jit(solution)/shard_map/block_softmax/pallas_call | solution.py:148
  87.0 1.0 pad_maximum_fusion.2.v_ref
  88.0 1.1 cross_statistics.1
  89.1 17.5 %all_to_all.15.stat_ref = f32[8,16,1024]{2,1,0:T(8,128)S(1)} all-to-all(f32[8,16,1024]{2,1,0:T(8,128)S(1)} %broadcast_in_dim.81), channel_id=1, replica_groups={{0,8,16,24,32,40,48,56},{64,72,80,88,96,104,112,120},{128,136,144,152,1..., dimensions={0} | all-to-all | bytes 1048576 | tf_op jit(solution)/shard_map/all_to_all | solution.py:286
  106.7 0.6 broadcast_in_dim.82
  107.3 4.5 %all-to-all-start.1 = ((f32[8,2,128]{2,1,0:T(2,128)}), f32[8,2,128]{2,1,0:T(2,128)S(1)}, u32[]{:S(2)}, u32[]{:S(2)}) async-start(f32[8,2,128]{2,1,0:T(2,128)} %broadcast_in_dim.82), calls=%async_computation.2 | async-start | bytes 16384 | tf_op jit(solution)/shard_map/all_to_all | solution.py:286
  111.9 1.5 cross_grads.1
  113.4 0.7 copy-done
  114.1 4.4 %all-to-all-done.1.scale_ref = f32[8,2,128]{2,1,0:T(2,128)S(1)} async-done(((f32[8,2,128]{2,1,0:T(2,128)}), f32[8,2,128]{2,1,0:T(2,128)S(1)}, u32[]{:S(2)}, u32[]{:S(2)}) %all-to-all-start.1) | async-done | bytes 8224 | tf_op jit(solution)/shard_map/all_to_all | solution.py:286
  118.5 6.9 %all-gather.2.cloned.1.call-done.both_ref = bf16[1024,1024]{1,0:T(8,128)(2,1)} async-done(((bf16[128,1024]{1,0:T(8,128)(2,1)}), bf16[1024,1024]{1,0:T(8,128)(2,1)}) %all-gather.2.cloned.1.call-update) | async-done | bytes 2097168 | tf_op jit(solution)/shard_map/all_gather | solution.py:369
  125.3 3.6 %query_grads.1 = (bf16[1024,512]{1,0:T(8,128)(2,1)S(1)}, bf16[1024,512]{1,0:T(8,128)(2,1)S(1)}, f32[512,512]{1,0:T(8,128)S(1)}, bf16[512,512]{1,0:T(8,128)(2,1)S(1)}) custom-call(s32[2]{0:T(128)S(1)} %pad_add_fusion.place_ref, bf16[1024,1024]{1,0:T(8,128)(2,1)} %all-gather.2.cloned.1.call-done.both_ref, f32[8,2,128]{2,1,0:T(2,128)S(1)} %all-to-all-done.1.scale_ref, ...), custom_call_target="tpu_custom_call" | custom-call | tf_op jit(solution)/shard_map/query_grads/pallas_call | solution.py:201
  128.9 4.7 %collective-permute-start.21 = (bf16[512,512]{1,0:T(8,128)(2,1)S(1)}, bf16[512,512]{1,0:T(8,128)(2,1)S(1)}, u32[]{:S(2)}, u32[]{:S(2)}) collective-permute-start(bf16[512,512]{1,0:T(8,128)(2,1)S(1)} %get-tuple-element.77), channel_id=1, source_target_pairs={{0,8},{8,0},{16,24},{24,16},{32,40},{40,32},{48,56},{56,48},{64,72... | collective-permute-start | bytes 1572872 | tf_op jit(solution)/shard_map/ppermute | solution.py:278
  133.7 1.3 key_grads.1
  135.0 2.4 %collective-permute-start.22 = (bf16[128,1024]{1,0:T(8,128)(2,1)S(1)}, bf16[128,1024]{1,0:T(8,128)(2,1)S(1)}, u32[]{:S(2)}, u32[]{:S(2)}) collective-permute-start(bf16[128,1024]{1,0:T(8,128)(2,1)S(1)} %get-tuple-element.82), channel_id=1, source_target_pairs={{0,192},{8,200},{16,208},{24,216},{32,224},{40,232},{48,240},{56,2... | collective-permute-start | bytes 786440 | tf_op jit(solution)/shard_map/ppermute | solution.py:272
  137.3 0.6 collective-permute-start.23
  137.9 0.7 collective-permute-start.24
  138.6 1.0 add_convert_fusion
  139.6 3.9 %all-to-all-start.2 = ((bf16[4,128,512]{2,1,0:T(8,128)(2,1)}), bf16[4,128,512]{2,1,0:T(8,128)(2,1)S(1)}, u32[]{:S(2)}, u32[]{:S(2)}) async-start(bf16[4,128,512]{2,1,0:T(8,128)(2,1)} %bitcast.38), calls=%async_computation.3 | async-start | bytes 1048576 | tf_op jit(solution)/shard_map/all_to_all | solution.py:393
  143.4 5.1 %collective-permute-done.22 = bf16[128,1024]{1,0:T(8,128)(2,1)S(1)} collective-permute-done((bf16[128,1024]{1,0:T(8,128)(2,1)S(1)}, bf16[128,1024]{1,0:T(8,128)(2,1)S(1)}, u32[]{:S(2)}, u32[]{:S(2)}) %collective-permute-start.22) | collective-permute-done | bytes 262176 | tf_op jit(solution)/shard_map/ppermute | solution.py:272
  148.5 4.2 %collective-permute-done.24 = bf16[128,1024]{1,0:T(8,128)(2,1)S(1)} collective-permute-done((bf16[128,1024]{1,0:T(8,128)(2,1)S(1)}, bf16[128,1024]{1,0:T(8,128)(2,1)S(1)}, u32[]{:S(2)}, u32[]{:S(2)}) %collective-permute-start.24) | collective-permute-done | bytes 262176 | tf_op jit(solution)/shard_map/ppermute | solution.py:272
  152.7 0.2 convert_add_fusion
  152.9 0.7 reshape.107
  153.6 0.7 reshape.106
  154.3 0.1 fusion.8
  154.4 0.7 reshape.105
  (76 shorter events, 1.7 us)
Async XLA Ops:
  7.2 20.2 %copy-start.5 = (bf16[128,4,128]{2,1,0:T(4,128)(2,1)S(1)}, bf16[128,4,128]{2,1,0:T(4,128)(2,1)}, u32[]{:S(2)}) copy-start(bf16[128,4,128]{2,1,0:T(4,128)(2,1)} %param.9) | copy-start | bytes 393220
  7.2 20.2 %copy-start.4 = (bf16[128,4,128]{2,1,0:T(4,128)(2,1)S(1)}, bf16[128,4,128]{2,1,0:T(4,128)(2,1)}, u32[]{:S(2)}) copy-start(bf16[128,4,128]{2,1,0:T(4,128)(2,1)} %param.8) | copy-start | bytes 393220
  7.2 77.8 %reduce-scatter.2.cloned.1.call-start = ((), (), s32[]{:S(2)}) async-start(), calls=%async_computation.4 | async-start | bytes 2359296 | tf_op jit(solution)/shard_map/reduce_scatter | solution.py:343
  9.3 8.4 %collective-permute-start = (bf16[128,512]{1,0:T(8,128)(2,1)S(1)}, bf16[128,512]{1,0:T(8,128)(2,1)S(1)}, u32[]{:S(2)}, u32[]{:S(2)}) collective-permute-start(bf16[128,512]{1,0:T(8,128)(2,1)S(1)} %get-tuple-element.48), channel_id=1, source_target_pairs={{0,16},{8,24},{16,32},{24,40},{32,48},{40,56},{48,0},{56,8},{64,80... | collective-permute-start | bytes 393224 | tf_op jit(solution)/shard_map/ppermute | solution.py:275
  11.4 8.6 %collective-permute-start.2 = (bf16[128,512]{1,0:T(8,128)(2,1)S(1)}, bf16[128,512]{1,0:T(8,128)(2,1)S(1)}, u32[]{:S(2)}, u32[]{:S(2)}) collective-permute-start(bf16[128,512]{1,0:T(8,128)(2,1)S(1)} %get-tuple-element.48), channel_id=1, source_target_pairs={{0,48},{8,56},{16,0},{24,8},{32,16},{40,24},{48,32},{56,40},{64,11... | collective-permute-start | bytes 393224 | tf_op jit(solution)/shard_map/ppermute | solution.py:275
  12.8 7.2 %collective-permute-start.1 = (bf16[128,512]{1,0:T(8,128)(2,1)S(1)}, bf16[128,512]{1,0:T(8,128)(2,1)S(1)}, u32[]{:S(2)}, u32[]{:S(2)}) collective-permute-start(bf16[128,512]{1,0:T(8,128)(2,1)S(1)} %get-tuple-element.48), channel_id=1, source_target_pairs={{0,32},{8,40},{16,48},{24,56},{32,0},{40,8},{48,16},{56,24},{64,96... | collective-permute-start | bytes 393224 | tf_op jit(solution)/shard_map/ppermute | solution.py:275
  14.4 5.6 %collective-permute-start.4 = (bf16[128,512]{1,0:T(8,128)(2,1)S(1)}, bf16[128,512]{1,0:T(8,128)(2,1)S(1)}, u32[]{:S(2)}, u32[]{:S(2)}) collective-permute-start(bf16[128,512]{1,0:T(8,128)(2,1)S(1)} %get-tuple-element.54), channel_id=1, source_target_pairs={{0,128},{8,136},{16,144},{24,152},{32,160},{40,168},{48,176},{56,1... | collective-permute-start | bytes 393224 | tf_op jit(solution)/shard_map/ppermute | solution.py:272
  17.4 6.6 %collective-permute-start.3 = (bf16[128,512]{1,0:T(8,128)(2,1)S(1)}, bf16[128,512]{1,0:T(8,128)(2,1)S(1)}, u32[]{:S(2)}, u32[]{:S(2)}) collective-permute-start(bf16[128,512]{1,0:T(8,128)(2,1)S(1)} %get-tuple-element.54), channel_id=1, source_target_pairs={{0,64},{8,72},{16,80},{24,88},{32,96},{40,104},{48,112},{56,120},{... | collective-permute-start | bytes 393224 | tf_op jit(solution)/shard_map/ppermute | solution.py:272
  17.8 6.2 %collective-permute-start.5 = (bf16[128,512]{1,0:T(8,128)(2,1)S(1)}, bf16[128,512]{1,0:T(8,128)(2,1)S(1)}, u32[]{:S(2)}, u32[]{:S(2)}) collective-permute-start(bf16[128,512]{1,0:T(8,128)(2,1)S(1)} %get-tuple-element.54), channel_id=1, source_target_pairs={{0,192},{8,200},{16,208},{24,216},{32,224},{40,232},{48,240},{56,2... | collective-permute-start | bytes 393224 | tf_op jit(solution)/shard_map/ppermute | solution.py:272
  24.1 3.3 %collective-permute-start.6 = (bf16[4,128,512]{2,1,0:T(8,128)(2,1)S(1)}, bf16[4,128,512]{2,1,0:T(8,128)(2,1)S(1)}, u32[]{:S(2)}, u32[]{:S(2)}) collective-permute-start(bf16[4,128,512]{2,1,0:T(8,128)(2,1)S(1)} %bitcast_dynamic-update-slice_fusion.4), channel_id=1, source_target_pairs={{0,8},{8,0},{16,24},{24,16},{32,40},{40,32},{48,56},{56,48},{64,72... | collective-permute-start | bytes 1572872 | tf_op jit(solution)/shard_map/ppermute | solution.py:278
  27.4 5.5 %collective-permute-start.9 = (bf16[128,512]{1,0:T(8,128)(2,1)S(1)}, bf16[128,512]{1,0:T(8,128)(2,1)S(1)}, u32[]{:S(2)}, u32[]{:S(2)}) collective-permute-start(bf16[128,512]{1,0:T(8,128)(2,1)S(1)} %get-tuple-element.58), channel_id=1, source_target_pairs={{0,48},{8,56},{16,0},{24,8},{32,16},{40,24},{48,32},{56,40},{64,11... | collective-permute-start | bytes 393224 | tf_op jit(solution)/shard_map/ppermute | solution.py:275
  28.4 7.9 %collective-permute-start.8 = (bf16[128,512]{1,0:T(8,128)(2,1)S(1)}, bf16[128,512]{1,0:T(8,128)(2,1)}, u32[]{:S(2)}, u32[]{:S(2)}) collective-permute-start(bf16[128,512]{1,0:T(8,128)(2,1)S(1)} %get-tuple-element.58), channel_id=1, source_target_pairs={{0,32},{8,40},{16,48},{24,56},{32,0},{40,8},{48,16},{56,24},{64,96... | collective-permute-start | bytes 393224 | tf_op jit(solution)/shard_map/ppermute | solution.py:275
  29.7 8.4 %collective-permute-start.7 = (bf16[128,512]{1,0:T(8,128)(2,1)S(1)}, bf16[128,512]{1,0:T(8,128)(2,1)}, u32[]{:S(2)}, u32[]{:S(2)}) collective-permute-start(bf16[128,512]{1,0:T(8,128)(2,1)S(1)} %get-tuple-element.58), channel_id=1, source_target_pairs={{0,16},{8,24},{16,32},{24,40},{32,48},{40,56},{48,0},{56,8},{64,80... | collective-permute-start | bytes 393224 | tf_op jit(solution)/shard_map/ppermute | solution.py:275
  30.1 8.0 %collective-permute-start.12 = (bf16[144,512]{1,0:T(8,128)(2,1)S(1)}, bf16[144,512]{1,0:T(8,128)(2,1)}, u32[]{:S(2)}, u32[]{:S(2)}) collective-permute-start(bf16[144,512]{1,0:T(8,128)(2,1)S(1)} %fusion.9), channel_id=1, source_target_pairs={{0,192},{8,200},{16,208},{24,216},{32,224},{40,232},{48,240},{56,2... | collective-permute-start | bytes 442376 | tf_op jit(solution)/shard_map/ppermute | solution.py:272
  32.6 5.7 %collective-permute-start.11 = (bf16[144,512]{1,0:T(8,128)(2,1)S(1)}, bf16[144,512]{1,0:T(8,128)(2,1)}, u32[]{:S(2)}, u32[]{:S(2)}) collective-permute-start(bf16[144,512]{1,0:T(8,128)(2,1)S(1)} %fusion.9), channel_id=1, source_target_pairs={{0,128},{8,136},{16,144},{24,152},{32,160},{40,168},{48,176},{56,1... | collective-permute-start | bytes 442376 | tf_op jit(solution)/shard_map/ppermute | solution.py:272
  32.9 0.7 copy-start.2
  33.5 8.8 %collective-permute-start.10 = (bf16[144,512]{1,0:T(8,128)(2,1)S(1)}, bf16[144,512]{1,0:T(8,128)(2,1)S(1)}, u32[]{:S(2)}, u32[]{:S(2)}) collective-permute-start(bf16[144,512]{1,0:T(8,128)(2,1)S(1)} %fusion.9), channel_id=1, source_target_pairs={{0,64},{8,72},{16,80},{24,88},{32,96},{40,104},{48,112},{56,120},{... | collective-permute-start | bytes 442376 | tf_op jit(solution)/shard_map/ppermute | solution.py:272
  36.3 8.0 %copy-start.3 = (bf16[128,512]{1,0:T(8,128)(2,1)S(1)}, bf16[128,512]{1,0:T(8,128)(2,1)}, u32[]{:S(2)}) copy-start(bf16[128,512]{1,0:T(8,128)(2,1)} %copy-done.2) | copy-start | bytes 393220
  36.3 89.0 %all-gather.2.cloned.1.call-start = ((), (), s32[]{:S(2)}) async-start(), calls=%async_computation.5 | async-start | bytes 2359296 | tf_op jit(solution)/shard_map/all_gather | solution.py:369
  42.3 6.5 %copy-start.6 = (bf16[144,512]{1,0:T(8,128)(2,1)}, bf16[144,512]{1,0:T(8,128)(2,1)S(1)}, u32[]{:S(2)}) copy-start(bf16[144,512]{1,0:T(8,128)(2,1)S(1)} %collective-permute-done.10) | copy-start | bytes 442372
  44.3 4.4 %collective-permute-start.13 = (bf16[4,128,512]{2,1,0:T(8,128)(2,1)S(1)}, bf16[4,128,512]{2,1,0:T(8,128)(2,1)S(1)}, u32[]{:S(2)}, u32[]{:S(2)}) collective-permute-start(bf16[4,128,512]{2,1,0:T(8,128)(2,1)S(1)} %bitcast_dynamic-update-slice_fusion), channel_id=1, source_target_pairs={{0,8},{8,0},{16,24},{24,16},{32,40},{40,32},{48,56},{56,48},{64,72... | collective-permute-start | bytes 1572872 | tf_op jit(solution)/shard_map/ppermute | solution.py:278
  50.7 12.3 %collective-permute-start.14 = (bf16[128,512]{1,0:T(8,128)(2,1)S(1)}, bf16[128,512]{1,0:T(8,128)(2,1)S(1)}, u32[]{:S(2)}, u32[]{:S(2)}) collective-permute-start(bf16[128,512]{1,0:T(8,128)(2,1)S(1)} %get-tuple-element.87), channel_id=1, source_target_pairs={{0,1},{1,2},{2,3},{3,4},{4,5},{5,6},{6,7},{7,0},{8,9},{9,10},{10,1... | collective-permute-start | bytes 393224 | tf_op jit(solution)/shard_map/ppermute | solution.py:281
  53.2 9.9 %collective-permute-start.18 = (bf16[128,512]{1,0:T(8,128)(2,1)S(1)}, bf16[128,512]{1,0:T(8,128)(2,1)S(1)}, u32[]{:S(2)}, u32[]{:S(2)}) collective-permute-start(bf16[128,512]{1,0:T(8,128)(2,1)S(1)} %dynamic-slice_bitcast_fusion), channel_id=1, source_target_pairs={{0,7},{1,0},{2,1},{3,2},{4,3},{5,4},{6,5},{7,6},{8,15},{9,8},{10,9... | collective-permute-start | bytes 393224 | tf_op jit(solution)/shard_map/ppermute | solution.py:281
  63.0 8.3 %collective-permute-start.15 = (bf16[128,512]{1,0:T(8,128)(2,1)S(1)}, bf16[128,512]{1,0:T(8,128)(2,1)S(1)}, u32[]{:S(2)}, u32[]{:S(2)}) collective-permute-start(bf16[128,512]{1,0:T(8,128)(2,1)S(1)} %fusion.7), channel_id=1, source_target_pairs={{0,1},{1,2},{2,3},{3,4},{4,5},{5,6},{6,7},{7,0},{8,9},{9,10},{10,1... | collective-permute-start | bytes 393224 | tf_op jit(solution)/shard_map/ppermute | solution.py:281
  63.2 8.3 %collective-permute-start.19 = (bf16[128,512]{1,0:T(8,128)(2,1)S(1)}, bf16[128,512]{1,0:T(8,128)(2,1)S(1)}, u32[]{:S(2)}, u32[]{:S(2)}) collective-permute-start(bf16[128,512]{1,0:T(8,128)(2,1)S(1)} %fusion.4), channel_id=1, source_target_pairs={{0,7},{1,0},{2,1},{3,2},{4,3},{5,4},{6,5},{7,6},{8,15},{9,8},{10,9... | collective-permute-start | bytes 393224 | tf_op jit(solution)/shard_map/ppermute | solution.py:281
  71.4 7.6 %collective-permute-start.16 = (bf16[128,512]{1,0:T(8,128)(2,1)S(1)}, bf16[128,512]{1,0:T(8,128)(2,1)S(1)}, u32[]{:S(2)}, u32[]{:S(2)}) collective-permute-start(bf16[128,512]{1,0:T(8,128)(2,1)S(1)} %fusion.6), channel_id=1, source_target_pairs={{0,1},{1,2},{2,3},{3,4},{4,5},{5,6},{6,7},{7,0},{8,9},{9,10},{10,1... | collective-permute-start | bytes 393224 | tf_op jit(solution)/shard_map/ppermute | solution.py:281
  71.5 8.3 %collective-permute-start.20 = (bf16[128,512]{1,0:T(8,128)(2,1)S(1)}, bf16[128,512]{1,0:T(8,128)(2,1)S(1)}, u32[]{:S(2)}, u32[]{:S(2)}) collective-permute-start(bf16[128,512]{1,0:T(8,128)(2,1)S(1)} %fusion.3), channel_id=1, source_target_pairs={{0,7},{1,0},{2,1},{3,2},{4,3},{5,4},{6,5},{7,6},{8,15},{9,8},{10,9... | collective-permute-start | bytes 393224 | tf_op jit(solution)/shard_map/ppermute | solution.py:281
  79.1 6.0 %collective-permute-start.17 = (bf16[128,512]{1,0:T(8,128)(2,1)S(1)}, bf16[128,512]{1,0:T(8,128)(2,1)S(1)}, u32[]{:S(2)}, u32[]{:S(2)}) collective-permute-start(bf16[128,512]{1,0:T(8,128)(2,1)S(1)} %fusion.5), channel_id=1, source_target_pairs={{0,1},{1,2},{2,3},{3,4},{4,5},{5,6},{6,7},{7,0},{8,9},{9,10},{10,1... | collective-permute-start | bytes 393224 | tf_op jit(solution)/shard_map/ppermute | solution.py:281
  107.3 11.2 %all-to-all-start.1 = ((f32[8,2,128]{2,1,0:T(2,128)}), f32[8,2,128]{2,1,0:T(2,128)S(1)}, u32[]{:S(2)}, u32[]{:S(2)}) async-start(f32[8,2,128]{2,1,0:T(2,128)} %broadcast_in_dim.82), calls=%async_computation.2 | async-start | bytes 16384 | tf_op jit(solution)/shard_map/all_to_all | solution.py:286
  113.4 0.7 copy-start
  118.5 15.2 %copy-start.1 = (f32[32,1024]{1,0:T(8,128)S(1)}, f32[32,1024]{1,0:T(8,128)}, u32[]{:S(2)}) copy-start(f32[32,1024]{1,0:T(8,128)} %copy-done) | copy-start | bytes 393220
  128.9 9.7 %collective-permute-start.21 = (bf16[512,512]{1,0:T(8,128)(2,1)S(1)}, bf16[512,512]{1,0:T(8,128)(2,1)S(1)}, u32[]{:S(2)}, u32[]{:S(2)}) collective-permute-start(bf16[512,512]{1,0:T(8,128)(2,1)S(1)} %get-tuple-element.77), channel_id=1, source_target_pairs={{0,8},{8,0},{16,24},{24,16},{32,40},{40,32},{48,56},{56,48},{64,72... | collective-permute-start | bytes 1572872 | tf_op jit(solution)/shard_map/ppermute | solution.py:278
  135.0 13.5 %collective-permute-start.22 = (bf16[128,1024]{1,0:T(8,128)(2,1)S(1)}, bf16[128,1024]{1,0:T(8,128)(2,1)S(1)}, u32[]{:S(2)}, u32[]{:S(2)}) collective-permute-start(bf16[128,1024]{1,0:T(8,128)(2,1)S(1)} %get-tuple-element.82), channel_id=1, source_target_pairs={{0,192},{8,200},{16,208},{24,216},{32,224},{40,232},{48,240},{56,2... | collective-permute-start | bytes 786440 | tf_op jit(solution)/shard_map/ppermute | solution.py:272
  137.3 11.2 %collective-permute-start.23 = (bf16[128,1024]{1,0:T(8,128)(2,1)S(1)}, bf16[128,1024]{1,0:T(8,128)(2,1)S(1)}, u32[]{:S(2)}, u32[]{:S(2)}) collective-permute-start(bf16[128,1024]{1,0:T(8,128)(2,1)S(1)} %get-tuple-element.83), channel_id=1, source_target_pairs={{0,128},{8,136},{16,144},{24,152},{32,160},{40,168},{48,176},{56,1... | collective-permute-start | bytes 786440 | tf_op jit(solution)/shard_map/ppermute | solution.py:272
  137.9 14.7 %collective-permute-start.24 = (bf16[128,1024]{1,0:T(8,128)(2,1)S(1)}, bf16[128,1024]{1,0:T(8,128)(2,1)S(1)}, u32[]{:S(2)}, u32[]{:S(2)}) collective-permute-start(bf16[128,1024]{1,0:T(8,128)(2,1)S(1)} %get-tuple-element.84), channel_id=1, source_target_pairs={{0,64},{8,72},{16,80},{24,88},{32,96},{40,104},{48,112},{56,120},{... | collective-permute-start | bytes 786440 | tf_op jit(solution)/shard_map/ppermute | solution.py:272
  139.6 14.7 %all-to-all-start.2 = ((bf16[4,128,512]{2,1,0:T(8,128)(2,1)}), bf16[4,128,512]{2,1,0:T(8,128)(2,1)S(1)}, u32[]{:S(2)}, u32[]{:S(2)}) async-start(bf16[4,128,512]{2,1,0:T(8,128)(2,1)} %bitcast.38), calls=%async_computation.3 | async-start | bytes 1048576 | tf_op jit(solution)/shard_map/all_to_all | solution.py:393
Sparse Core Ops, SparseCore 0:
  36.4 47.1 reduce-scatter.1
  87.1 38.1 all-gather.1
